TPU v7x, 128 devices: a whole 4x4x4 slice. The times are simulated.
128 devices in a mesh: slab: 4 (over z), grp: 32 (over y, x, core).
Axes of the slice: x: 4, y: 4, z: 4, core: 2. Of those that a mesh axis runs over, the one named last changes fastest.
Arguments:
- samples: float32 [131072, 6, 128], P(('slab', 'grp')), as said below
- block_ids: int32 [131072], P(('slab', 'grp')), may hold values from 0 to 131071, as said below
- tile_counts: int32 [131072], P(('slab', 'grp')), may hold values from 0 to 128
- occupied: int32 [8, 64, 256], P('slab', 'grp'), may hold values 0 or 1
- coupling: float32 [27, 64, 64], replicated, may hold values from -0.06 to 0.06
Outputs:
- solution_field: float32 [64, 8, 64, 256], P(None, 'slab', 'grp')
- residual: float32 [64, 8, 64, 256], P(None, 'slab', 'grp')
Inputs may be any that keep to these rules, and one draw needn't show every extreme that they name: `samples`: the first three components of every sample lie in [0, 1). `block_ids`: slot j * 8 + c of a device's slots (c below 8) carries a block whose x // 2 is the slab index and y // 2 the grp index of the device of linear index j over slab then grp; ids number blocks as (x * 64 + y) * 256 + z; every block is named by exactly one slot over all devices.
All inputs are finite; a program needn't handle non-finite values. No bound on the sum of `occupied` on one device may be relied on, other than what follows from the above.
Results may differ from a plain program's by a relative error of at most 0.0003.
Values sent between devices are 32-bit elements; how exact they have to be, the bound alone decides.
No kernel may reach another device: no remote copies, remote signals or barrier semaphores. Data moves between devices by JAX's collectives and lax.ppermute only.
A program may use at most 128 MiB of HBM per device.

v0:
```python
import math

import jax
import jax.numpy as jnp
from jax import lax
from jax.sharding import PartitionSpec as P

ITERS = 3


HIGH = lax.Precision.HIGHEST


def with_halo(block, sides, width):
    for axis, dim in sides:
        count = lax.axis_size(axis)
        forward = [(i, i + 1) for i in range(count - 1)]
        backward = [(target, source) for source, target in forward]
        low = lax.ppermute(
            lax.slice_in_dim(block, block.shape[dim] - width, None, axis=dim), axis, forward
        )
        high = lax.ppermute(lax.slice_in_dim(block, 0, width, axis=dim), axis, backward)
        block = jnp.concatenate([low, block, high], axis=dim)
    return block


def bspline_value(diff):
    mag = jnp.abs(diff)
    return jnp.where(mag < 0.5, 0.75 - mag * mag, jnp.where(mag < 1.5, 0.5 * (1.5 - mag) ** 2, 0.0))


def bspline_slope(diff):
    mag = jnp.abs(diff)
    outer = -(1.5 - mag) * diff / jnp.maximum(mag, 0.5)
    return jnp.where(mag < 0.5, -2.0 * diff, jnp.where(mag < 1.5, outer, 0.0))


def splat_tiles(tile_data, counts):
    slots = tile_data.shape[0]
    width = tile_data.shape[2]
    lanes = jnp.arange(width, dtype=jnp.int32)[None, :]
    valid = (lanes < counts[:, None]).astype(jnp.float32)
    centres = jnp.arange(4, dtype=jnp.float32) + 0.5
    diff = 4.0 * tile_data[:, 0:3, :][:, :, None, :] - centres[None, None, :, None]
    values = bspline_value(diff)
    slopes = 4.0 * bspline_slope(diff)
    normals = tile_data[:, 3:6, :] * valid[:, None, :]
    pair_val = (values[:, 1][:, :, None, :] * values[:, 2][:, None, :, :]).reshape(slots, 16, width)
    pair_dy = (slopes[:, 1][:, :, None, :] * values[:, 2][:, None, :, :]).reshape(slots, 16, width)
    pair_dz = (values[:, 1][:, :, None, :] * slopes[:, 2][:, None, :, :]).reshape(slots, 16, width)
    term_x = jnp.einsum(
        "tis,tks->tik", slopes[:, 0] * normals[:, 0][:, None, :], pair_val, precision=HIGH
    )
    term_y = jnp.einsum(
        "tis,tks->tik", values[:, 0] * normals[:, 1][:, None, :], pair_dy, precision=HIGH
    )
    term_z = jnp.einsum(
        "tis,tks->tik", values[:, 0] * normals[:, 2][:, None, :], pair_dz, precision=HIGH
    )
    dens = jnp.einsum("tis,tks->tik", values[:, 0] * valid[:, None, :], pair_val, precision=HIGH)
    rhs = (term_x + term_y + term_z).reshape(slots, 64)
    return jnp.concatenate([rhs, dens.reshape(slots, 64)], axis=1)


def splat_blocks(tile_data, counts):
    total = tile_data.shape[0]
    group = math.gcd(total, 512)
    batches = total // group
    stacked = tile_data.reshape(batches, group, tile_data.shape[1], tile_data.shape[2])
    stacked_counts = counts.reshape(batches, group)
    result = lax.map(lambda pair: splat_tiles(pair[0], pair[1]), (stacked, stacked_counts))
    return result.reshape(total, 128)


def symmetric_blocks(coupling):
    coupled = 0.5 * (coupling + jnp.transpose(jnp.flip(coupling, 0), (0, 2, 1)))
    rowabs = jnp.sum(jnp.abs(coupled), axis=(0, 2))
    return (coupled, rowabs)


def apply_stiffness(field, coupled, diag, mask):
    nodes, size_x, size_y, size_z = field.shape
    framed = with_halo(field * mask, (("slab", 1), ("grp", 2)), 1)
    padded = jnp.pad(framed, ((0, 0), (0, 0), (0, 0), (1, 1)))
    total = jnp.zeros((nodes, size_x * size_y * size_z), jnp.float32)
    for offset in range(27):
        shift_x = offset // 9
        shift_y = offset // 3 % 3
        shift_z = offset % 3
        piece = padded[
            :, shift_x : shift_x + size_x, shift_y : shift_y + size_y, shift_z : shift_z + size_z
        ]
        total = total + jnp.dot(coupled[offset], piece.reshape(nodes, -1), precision=HIGH)
    return diag * field - mask * total.reshape(field.shape)


def squares(residual):
    return lax.psum(jnp.sum(residual * residual), ("slab", "grp"))


def on_device(samples, block_ids, tile_counts, occupied, coupling):
    size_x, size_y, size_z = occupied.shape
    span_y = size_y * lax.axis_size("grp")
    arrived, arrived_ids, arrived_counts = (
        lax.all_to_all(samples, ("slab", "grp"), split_axis=0, concat_axis=0, tiled=True),
        lax.all_to_all(block_ids, ("slab", "grp"), split_axis=0, concat_axis=0, tiled=True),
        lax.all_to_all(tile_counts, ("slab", "grp"), split_axis=0, concat_axis=0, tiled=True),
    )
    contrib = splat_blocks(arrived, arrived_counts)
    block_x = arrived_ids // (span_y * size_z)
    block_y = arrived_ids // size_z % span_y
    block_z = arrived_ids % size_z
    local_ids = (block_x % size_x * size_y + block_y % size_y) * size_z + block_z
    summed = jax.ops.segment_sum(contrib, local_ids, num_segments=size_x * size_y * size_z)
    grid = summed.T.reshape(2, 64, size_x, size_y, size_z)
    right_side = grid[0]
    density = grid[1]
    coupled, rowabs = symmetric_blocks(coupling)
    diag = rowabs[:, None, None, None] + 0.5 + 4.0 * density
    mask = occupied.astype(jnp.float32)[None]
    solution_field = jnp.zeros_like(right_side)
    residual = right_side
    direction = right_side
    norm_now = squares(residual)
    for step in range(ITERS):
        image = apply_stiffness(direction, coupled, diag, mask)
        alpha = norm_now / lax.psum(jnp.sum(direction * image), ("slab", "grp"))
        solution_field = solution_field + alpha * direction
        residual = residual - alpha * image
        norm_next = squares(residual)
        direction = residual + norm_next / norm_now * direction
        norm_now = norm_next
    return (solution_field, residual)


def solution(mesh):
    placed = (
        P(("slab", "grp"), None, None),
        P(("slab", "grp")),
        P(("slab", "grp")),
        P("slab", "grp", None),
        P(),
    )
    return jax.shard_map(
        on_device,
        mesh=mesh,
        in_specs=placed,
        out_specs=(P(None, "slab", "grp", None), P(None, "slab", "grp", None)),
        check_vma=False,
    )
```

profile of v0, /device:TPU:1, one launch (start us, length us, event | category | flops | bytes accessed | tf_op | source)
XLA Modules:
  0.0 903.6 jit_solution(11653452664829850402)
XLA Ops:
  2.0 11.5 %all-to-all-start.2 = ((s32[128,8,1]{1,2,0:T(1,128)}), s32[128,8,1]{1,2,0:T(1,128)S(1)}, u32[]{:S(2)}, u32[]{:S(2)}) async-start(s32[128,8,1]{1,2,0:T(1,128)} %bitcast.20), calls=%async_computation.2 | async-start | bytes 131072 | tf_op jit(solution)/shard_map/all_to_all | solution.py:107
  14.9 8.2 all-to-all-done.2
  27.6 5.8 copy.23
  37.1 6.5 all-to-all-start.1
  47.4 48.8 %all-to-all-done.1 = f32[1024,6,128]{2,1,0:T(8,128)} async-done(((f32[1024,6,128]{2,1,0:T(8,128)}), f32[1024,6,128]{2,1,0:T(8,128)}, u32[]{:S(2)}, u32[]{:S(2)}) %all-to-all-start.1) | async-done | bytes 3145760 | tf_op jit(solution)/shard_map/all_to_all | solution.py:105
  100.7 104.5 %while.10 = (s32[]{:T(128)}, f32[2,512,128]{2,1,0:T(8,128)}, f32[2,512,6,128]{3,1,2,0:T(8,128)}, s32[2,512]{1,0:T(2,128)S(1)}, s32[]{:T(128)}) while((s32[]{:T(128)}, f32[2,512,128]{2,1,0:T(8,128)}, f32[2,512,6,128]{3,1,2,0:T(8,128)}, s32[2,512]{1,0:T(2,128)S(1)}, s32[]{:T(128)}) %tuple.132), condition=%wide.region_1.2_spmd, body=%wide.region_0.1_spmd.sunk | while | flops 221118464 | bytes 88348856 | solution.py:71
  127.2 6.6 fusion.272
  133.8 6.6 convolution_add_fusion.7
  140.5 7.7 convolution_add_fusion.8
  149.7 9.2 %fusion.271 = f32[512,4,16]{2,1,0:T(4,128)} fusion(f32[512,16,128]{2,1,0:T(8,128)} %bitcast.316, f32[512,3,4,128]{3,2,0,1:T(4,128)S(1)} %get-tuple-element.216, f32[512,128]{1,0:T(8,128)S(1)} %fusion.269), kind=kOutput, calls=%fused_computation.33.clone.1 | convolution fusion | flops 50593792 | bytes 5636096 | tf_op jit(solution)/shard_map/while/body/eval_jaxpr/tis,tks->tik/dot_general | solution.py:60
  170.5 6.6 fusion.272
  177.2 6.6 convolution_add_fusion.7
  183.8 7.7 convolution_add_fusion.8
  193.1 9.2 %fusion.271 = f32[512,4,16]{2,1,0:T(4,128)} fusion(f32[512,16,128]{2,1,0:T(8,128)} %bitcast.316, f32[512,3,4,128]{3,2,0,1:T(4,128)S(1)} %get-tuple-element.216, f32[512,128]{1,0:T(8,128)S(1)} %fusion.269), kind=kOutput, calls=%fused_computation.33.clone.1 | convolution fusion | flops 50593792 | bytes 5636096 | tf_op jit(solution)/shard_map/while/body/eval_jaxpr/tis,tks->tik/dot_general | solution.py:60
  205.2 6.5 scatter_custom_fusion
  235.8 4.6 fusion.160
  320.7 67.3 %all-reduce.3 = (f32[]{:T(128)}, f32[]{:T(128)}) all-reduce(f32[]{:T(128)} %get-tuple-element.38, f32[]{:T(128)} %get-tuple-element.37), channel_id=1, replica_groups=mesh['slab'=4,'grp'=32] {'slab','grp'}, use_global_device_ids=true, to_apply=%region_4.5 | all-reduce | flops 2 | bytes 16 | tf_op jit(solution)/shard_map/psum | solution.py:98
  390.1 62.5 %psum.44 = f32[]{:T(128)} all-reduce(f32[]{:T(128)} %get-tuple-element.55), channel_id=1, replica_groups=mesh['slab'=4,'grp'=32] {'slab','grp'}, use_global_device_ids=true, to_apply=%region_9.10 | all-reduce | flops 1 | bytes 8 | tf_op jit(solution)/shard_map/psum | solution.py:98
  508.2 4.7 fusion.159
  582.9 4.9 multiply_reduce_fusion.2
  587.8 66.0 %psum.45 = f32[]{:T(128)} all-reduce(f32[]{:T(128)} %get-tuple-element.51), channel_id=1, replica_groups=mesh['slab'=4,'grp'=32] {'slab','grp'}, use_global_device_ids=true, to_apply=%region_11.12 | all-reduce | flops 1 | bytes 8 | tf_op jit(solution)/shard_map/psum | solution.py:127
  657.7 62.9 %psum.46 = f32[]{:T(128)} all-reduce(f32[]{:T(128)} %multiply_reduce_fusion.1), channel_id=1, replica_groups=mesh['slab'=4,'grp'=32] {'slab','grp'}, use_global_device_ids=true, to_apply=%region_13.14 | all-reduce | flops 1 | bytes 8 | tf_op jit(solution)/shard_map/psum | solution.py:98
  763.2 4.8 fusion.158
  834.6 66.0 %psum.47 = f32[]{:T(128)} all-reduce(f32[]{:T(128)} %get-tuple-element.173), channel_id=1, replica_groups=mesh['slab'=4,'grp'=32] {'slab','grp'}, use_global_device_ids=true, to_apply=%region_15.16 | all-reduce | flops 1 | bytes 8 | tf_op jit(solution)/shard_map/psum | solution.py:127
  (312 shorter events, 385.8 us)
Async XLA Ops:
  2.0 21.1 %all-to-all-start.2 = ((s32[128,8,1]{1,2,0:T(1,128)}), s32[128,8,1]{1,2,0:T(1,128)S(1)}, u32[]{:S(2)}, u32[]{:S(2)}) async-start(s32[128,8,1]{1,2,0:T(1,128)} %bitcast.20), calls=%async_computation.2 | async-start | bytes 131072 | tf_op jit(solution)/shard_map/all_to_all | solution.py:107
  23.1 14.1 %all-to-all-start = ((s32[128,8,1]{1,2,0:T(1,128)}), s32[128,8,1]{1,2,0:T(1,128)S(1)}, u32[]{:S(2)}, u32[]{:S(2)}) async-start(s32[128,8,1]{1,2,0:T(1,128)} %bitcast.17), calls=%async_computation | async-start | bytes 131072 | tf_op jit(solution)/shard_map/all_to_all | solution.py:106
  33.4 10.3 %copy-start.1 = (f32[27,64,64]{2,1,0:T(8,128)S(1)}, f32[27,64,64]{2,1,0:T(8,128)}, u32[]{:S(2)}) copy-start(f32[27,64,64]{2,1,0:T(8,128)} %param.11) | copy-start | bytes 1327108
  37.1 59.1 %all-to-all-start.1 = ((f32[1024,6,128]{2,1,0:T(8,128)}), f32[1024,6,128]{2,1,0:T(8,128)}, u32[]{:S(2)}, u32[]{:S(2)}) async-start(f32[1024,6,128]{2,1,0:T(8,128)} %copy.23), calls=%async_computation.1 | async-start | bytes 8388608 | tf_op jit(solution)/shard_map/all_to_all | solution.py:105
  127.1 6.7 copy-start
  170.5 6.7 copy-start
  212.4 4.1 collective-permute-start
  213.7 5.7 collective-permute-start.1
  220.1 7.5 collective-permute-start.2
  224.3 7.7 collective-permute-start.3
  454.7 4.8 collective-permute-start.4
  457.6 5.7 collective-permute-start.5
  464.6 6.9 collective-permute-start.6
  469.2 24.4 %collective-permute-start.7 = (f32[64,4,1,256]{3,2,1,0:T(1,128)}, f32[64,4,1,256]{3,2,1,0:T(1,128)}, u32[]{:S(2)}, u32[]{:S(2)}) collective-permute-start(f32[64,4,1,256]{3,2,1,0:T(1,128)} %get-tuple-element.152), channel_id=1, source_target_pairs={{1,0},{2,1},{3,2},{4,3},{5,4},{6,5},{7,6},{8,7},{9,8},{10,9},{11,1... | collective-permute-start | bytes 786440 | tf_op jit(solution)/shard_map/ppermute | solution.py:22
  572.1 10.7 %copy-start.7 = (f32[64,1024]{1,0:T(8,128)S(1)}, f32[64,1024]{1,0:T(8,128)}, u32[]{:S(2)}) copy-start(f32[64,1024]{1,0:T(8,128)} %fusion.66) | copy-start | bytes 786436
  724.3 4.8 collective-permute-start.8
  727.1 5.7 collective-permute-start.9
  729.1 11.9 %copy-start.3 = (f32[64,1,2,256]{3,2,1,0:T(2,128)}, f32[64,1,2,256]{3,2,1,0:T(2,128)S(1)}, u32[]{:S(2)}) copy-start(f32[64,1,2,256]{3,2,1,0:T(2,128)S(1)} %collective-permute-done.8) | copy-start | bytes 393220
  732.9 8.1 copy-start.5
  734.2 6.7 collective-permute-start.10
  738.8 14.2 %collective-permute-start.11 = (f32[64,4,1,256]{3,2,1,0:T(1,128)}, f32[64,4,1,256]{3,2,1,0:T(1,128)S(1)}, u32[]{:S(2)}, u32[]{:S(2)}) collective-permute-start(f32[64,4,1,256]{3,2,1,0:T(1,128)} %get-tuple-element.150), channel_id=1, source_target_pairs={{1,0},{2,1},{3,2},{4,3},{5,4},{6,5},{7,6},{8,7},{9,8},{10,9},{11,1... | collective-permute-start | bytes 786440 | tf_op jit(solution)/shard_map/ppermute | solution.py:22
  746.3 6.8 copy-start.4
  746.3 6.8 copy-start.6
  830.4 71.7 %copy-start.8 = (f32[64,2,2,256]{3,2,1,0:T(2,128)S(1)}, f32[64,2,2,256]{3,2,1,0:T(2,128)}, u32[]{:S(2)}) copy-start(f32[64,2,2,256]{3,2,1,0:T(2,128)} %get-tuple-element.50) | copy-start | bytes 786436
  (17 other events, 40.0 us)
where the time goes:
time: 913 us; the launch traced here: 904 us
  blocking collectives  325 us (36%)
  matrix products  208 us (23%)
  local copies, waits for them, and re-layouts  163 us (18%)
  waiting for transfers between devices  77.1 us (8%)
  other arithmetic  52.9 us (6%)
  starting transfers between devices  50.9 us (6%)
  loops' own time  18.1 us (2%)
    psum x3, blocking collectives, squares(): return lax.psum(jnp.sum(residual * residual), ('slab', 'grp'))  193 us
    dot_general x81, matrix products, apply_stiffness(): jnp.dot(coupled[offset], piece.reshape(nodes, -1), precision=HIGH)  148 us
    psum x2, blocking collectives, on_device(): alpha = norm_now / lax.psum(jnp.sum(direction * image), ('slab', 'grp'))  132 us
    reshape x78, local copies, waits for them, and re-layouts, apply_stiffness(): piece.reshape(nodes, -1)  115 us
    all_to_all x1, waiting for transfers between devices, on_device(): lax.all_to_all(samples, ('slab', 'grp'), split_axis=0, concat_axis=0, til...  48.8 us
    dot_general x2, matrix products, splat_tiles(): jnp.einsum('tis,tks->tik', values[:, 0] * valid[:, None, :], pair_val, pr...  18.4 us
  transfers between devices with their start and end apart: 15, of which 10 were waited for; matrix products, arithmetic and copies ran while one was open for 5% of the time, Pallas kernels for 0%

commit v1 on v0

v1 whole, which is shorter than its diff:
```python
import functools

import jax
import jax.numpy as jnp
from jax import lax
from jax.experimental import pallas as pl
from jax.experimental.pallas import tpu as pltpu
from jax.sharding import PartitionSpec as P

AXES = ("slab", "grp")
F32 = jnp.float32
BF16 = jnp.bfloat16
N_COLS = 4
BZ = 256
NODES = 64
SENDERS = 128
CAP = 8
ROWS = CAP + 1


def lane_iota(shape):
    return lax.broadcasted_iota(jnp.int32, shape, len(shape) - 1)


def row_iota(shape):
    return lax.broadcasted_iota(jnp.int32, shape, 0)


def basis_of(pos):
    u = 4.0 * pos
    cell = jnp.floor(u)
    w = u - cell
    rest = 1.0 - w
    low = 0.5 * (rest * rest)
    high = 0.5 * (w * w)
    off = w - 0.5
    mid = 0.75 - off * off
    slow = -4.0 * rest
    shigh = 4.0 * w
    smid = -8.0 * off
    at = [cell == float(i) for i in range(4)]
    zero = jnp.zeros_like(u)
    values, slopes = [], []
    for i in range(4):
        val, slo = zero, zero
        if i + 1 < 4:
            val = jnp.where(at[i + 1], low, val)
            slo = jnp.where(at[i + 1], slow, slo)
        if i - 1 >= 0:
            val = jnp.where(at[i - 1], high, val)
            slo = jnp.where(at[i - 1], shigh, slo)
        values.append(jnp.where(at[i], mid, val))
        slopes.append(jnp.where(at[i], smid, slo))
    return values, slopes


def splat_kernel(samp_ref, cnt_ref, ids_ref, out_ref, flip, basis, acc, stats):
    step = pl.program_id(0)
    last = pl.num_programs(0) - 1

    @pl.when(step == 0)
    def _():
        stats[...] = jnp.zeros_like(stats)

    for k in range(6):
        flip[k] = samp_ref[k].T
    counts = cnt_ref[pl.ds(step, 1), :]

    def evaluate(group, carry):
        rows = pl.ds(pl.multiple_of(group * 8, 8), 8)
        valid = (row_iota((8, 128)) + group * 8 < counts).astype(F32)
        n0 = flip[3, rows, :] * valid
        n1 = flip[4, rows, :] * valid
        n2 = flip[5, rows, :] * valid
        val, slo = basis_of(flip[0, rows, :])
        for i in range(4):
            basis[i, rows, :] = slo[i] * n0
            basis[4 + i, rows, :] = val[i] * n1
            basis[8 + i, rows, :] = val[i] * n2
            basis[12 + i, rows, :] = val[i] * valid
        for d in (1, 2):
            val, slo = basis_of(flip[d, rows, :])
            for i in range(4):
                basis[8 + 8 * d + i, rows, :] = val[i]
                basis[12 + 8 * d + i, rows, :] = slo[i]
        return carry

    lax.fori_loop(0, 16, evaluate, 0, unroll=2)

    for i in range(4):
        def add_group(group, sums, i=i):
            rows = pl.ds(pl.multiple_of(group * 8, 8), 8)
            a = basis[i, rows, :]
            b = basis[4 + i, rows, :]
            c = basis[8 + i, rows, :]
            d = basis[12 + i, rows, :]
            v2 = [basis[24 + l, rows, :] for l in range(4)]
            s2 = [basis[28 + l, rows, :] for l in range(4)]
            out = list(sums)
            for j in range(4):
                v1 = basis[16 + j, rows, :]
                s1 = basis[20 + j, rows, :]
                first = a * v1 + b * s1
                second = c * v1
                dens = d * v1
                for l in range(4):
                    at = j * 4 + l
                    out[at] = out[at] + (first * v2[l] + second * s2[l])
                    out[16 + at] = out[16 + at] + dens * v2[l]
            return tuple(out)

        zero = jnp.zeros((8, 128), F32)
        sums = lax.fori_loop(0, 16, add_group, (zero,) * 32, unroll=2)
        for at in range(16):
            acc[pl.ds((i * 16 + at) * 8, 8), :] = sums[at]
            acc[pl.ds((64 + i * 16 + at) * 8, 8), :] = sums[16 + at]

    total = acc[pl.ds(0, 128, stride=8), :]
    for s in range(1, 8):
        total = total + acc[pl.ds(s, 128, stride=8), :]
    square = total[:64] * total[:64]
    weighted = total[64:] * square
    part, wpart = square[:8], weighted[:8]
    for k in range(1, 8):
        part = part + square[8 * k : 8 * k + 8]
        wpart = wpart + weighted[8 * k : 8 * k + 8]
    stats[0] = stats[0] + part
    stats[1] = stats[1] + wpart
    by_tile = total.T
    for d in range(16):
        out_ref[step, pl.ds(ROWS * d, 8), :] = by_tile[8 * d : 8 * d + 8]

    @pl.when(step == last)
    def _():
        ids = ids_ref[...]
        local = ((ids >> 14) & 1) * 512 + ((ids >> 8) & 1) * 256 + (ids & 255)
        local = local.astype(F32)
        sum0 = jnp.sum(stats[0], keepdims=True)
        sum1 = jnp.sum(stats[1], keepdims=True)
        lanes = lane_iota((1, 128))
        both = jnp.where(lanes % 2 == 0, sum0, sum1)
        for g in range(8):
            for d in range(16):
                row = jnp.where(lanes // 8 == d, local[g : g + 1], both)
                out_ref[g, pl.ds(ROWS * d + CAP, 1), :] = row


def splat(samples, counts, ids):
    tiles = samples.shape[0]
    groups = tiles // 128
    return pl.pallas_call(
        splat_kernel,
        name="splat",
        grid=(groups,),
        in_specs=[
            pl.BlockSpec((6, 128, 128), lambda g: (0, g, 0)),
            pl.BlockSpec((groups, 128), lambda g: (0, 0)),
            pl.BlockSpec((groups, 128), lambda g: (0, 0)),
        ],
        out_specs=pl.BlockSpec((groups, 16 * ROWS, 128), lambda g: (0, 0, 0)),
        out_shape=jax.ShapeDtypeStruct((groups, 16 * ROWS, 128), F32),
        scratch_shapes=[
            pltpu.VMEM((6, 128, 128), F32),
            pltpu.VMEM((32, 128, 128), F32),
            pltpu.VMEM((1024, 128), F32),
            pltpu.VMEM((2, 8, 128), F32),
        ],
    )(jnp.transpose(samples, (1, 0, 2)), counts.reshape(groups, 128), ids.reshape(groups, 128))


def assemble_kernel(seat_ref, recv_ref, mask_ref, rowabs_ref, v_ref, mv_ref, diag_ref, maskc_ref, c_ref, turned):
    seat = seat_ref[0]
    turned[...] = recv_ref[pl.ds(CAP, SENDERS, stride=ROWS), :].T
    where = turned[pl.ds(pl.multiple_of(seat * 8, 8), 8), :].astype(jnp.int32)
    other = lax.rem(seat + 1, 16)
    sums = turned[pl.ds(pl.multiple_of(other * 8, 8), 8), :]
    sum0 = jnp.sum(sums[0:1, :], keepdims=True)
    sum1 = jnp.sum(sums[1:2, :], keepdims=True)
    rowabs = rowabs_ref[...]
    mean = jnp.sum(rowabs[:, 0:1], keepdims=True) * (1.0 / NODES)
    centre = mean + 0.5 + 4.0 * (sum1 / sum0)
    inverse = 1.0 / centre
    c_ref[...] = jnp.broadcast_to(centre, (8, 128))
    tiles = []
    for c in range(CAP):
        block = recv_ref[pl.ds(c, SENDERS, stride=ROWS), :]
        high = block.astype(BF16)
        low = (block - high.astype(F32)).astype(BF16)
        tiles.append(jnp.concatenate([high, low], axis=1))
    table = jnp.concatenate(tiles, axis=0)
    for col in range(N_COLS):
        picks = []
        for c in range(CAP):
            hit = row_iota((BZ, SENDERS)) + col * BZ == where[c : c + 1, :]
            picks.append(hit.astype(F32).astype(BF16))
        pick = jnp.concatenate(picks, axis=1)
        both = jnp.dot(pick, table, preferred_element_type=F32)
        ordered = (both[:, :128] + both[:, 128:]).T
        rhs = ordered[:NODES]
        dens = ordered[NODES:]
        lanes = pl.ds(col * BZ, BZ)
        mask = mask_ref[0:1, lanes]
        v_ref[:, lanes] = rhs
        mv_ref[:, lanes] = rhs * mask
        diag = rowabs[:, 0:1] + 0.5 + 4.0 * dens
        diag_ref[:, lanes] = (diag - centre) * inverse
        maskc_ref[:, lanes] = jnp.broadcast_to(mask * inverse, (8, BZ))


def assemble(seat, recv, mask, rowabs):
    blocks = N_COLS * BZ
    field = jax.ShapeDtypeStruct((NODES, blocks), F32)
    return pl.pallas_call(
        assemble_kernel,
        name="assemble",
        in_specs=[pl.BlockSpec(memory_space=pltpu.SMEM)] + [pl.BlockSpec(memory_space=pltpu.VMEM)] * 3,
        out_specs=[pl.BlockSpec(memory_space=pltpu.VMEM)] * 5,
        out_shape=[field, field, field, jax.ShapeDtypeStruct((8, blocks), F32), jax.ShapeDtypeStruct((8, 128), F32)],
        scratch_shapes=[pltpu.VMEM((128, 128), F32)],
    )(seat, recv, mask, rowabs)


def apply_kernel(first, flag_ref, v_ref, mv_ref, diag_ref, mask_ref, maskc_ref, xl_ref, xh_ref, yl_ref, yh_ref,
                 w_ref, mom_ref, o_ref, mo_ref, mo_mom_ref, high, low):
    edges = [flag_ref[k] for k in range(4)]
    for px in range(4):
        for py in range(4):
            if py in (0, 3):
                src = (yl_ref if py == 0 else yh_ref)[:, pl.ds(px * BZ, BZ)]
                src = src * edges[2 if py == 0 else 3]
            elif px in (0, 3):
                src = (xl_ref if px == 0 else xh_ref)[:, pl.ds((py - 1) * BZ, BZ)]
            else:
                src = mv_ref[:, pl.ds(((px - 1) * 2 + py - 1) * BZ, BZ)]
            if px in (0, 3):
                src = src * edges[0 if px == 0 else 1]
            top = src.astype(BF16)
            rows = pl.ds((px * 4 + py) * NODES, NODES)
            high[rows, :] = top
            low[rows, :] = (src - top.astype(F32)).astype(BF16)
    lanes = lane_iota((NODES, BZ))
    sq = jnp.zeros((NODES, BZ), F32)
    cross = jnp.zeros((NODES, BZ), F32)
    for ox in range(2):
        for oy in range(2):
            full = jnp.zeros((6 * NODES, BZ), F32)
            half = jnp.zeros((3 * NODES, BZ), F32)
            for dx in range(3):
                rows = pl.ds(((ox + dx) * 4 + oy) * NODES, 3 * NODES)
                cols = pl.ds(dx * 3 * NODES, 3 * NODES)
                full = full + jnp.dot(w_ref[dx], high[rows, :], preferred_element_type=F32)
                half = half + jnp.dot(w_ref[dx, 0 : 3 * NODES, :], low[rows, :], preferred_element_type=F32)
            part = full[: 3 * NODES] + full[3 * NODES :] + half
            before = jnp.where(lanes == 0, 0.0, pltpu.roll(part[:NODES], 1, 1))
            after = jnp.where(lanes == BZ - 1, 0.0, pltpu.roll(part[2 * NODES :], BZ - 1, 1))
            total = part[NODES : 2 * NODES] + before + after
            at = pl.ds((ox * 2 + oy) * BZ, BZ)
            v = v_ref[:, at]
            new = diag_ref[:, at] * v - maskc_ref[0:1, at] * total
            o_ref[:, at] = new
            mo_ref[:, at] = new * mask_ref[0:1, at]
            sq = sq + v * v
            cross = cross + v * new
    sq = jnp.sum(sq, keepdims=True)
    cross = jnp.sum(cross, keepdims=True)
    spot = lane_iota((1, 128))
    mom = jnp.where(spot == first, sq, jnp.where(spot == first + 1, cross, mom_ref[0:1, :]))
    mo_mom_ref[...] = jnp.broadcast_to(mom, mo_mom_ref.shape)


def apply_stiffness(order, flags, v, mv, diag, mask, maskc, halos, weights, moments):
    blocks = N_COLS * BZ
    field = jax.ShapeDtypeStruct((NODES, blocks), F32)
    moment_rows = SENDERS if order == 2 else 8
    return pl.pallas_call(
        functools.partial(apply_kernel, 2 * order),
        name="stiffness",
        in_specs=[pl.BlockSpec(memory_space=pltpu.SMEM)] + [pl.BlockSpec(memory_space=pltpu.VMEM)] * 11,
        out_specs=[pl.BlockSpec(memory_space=pltpu.VMEM)] * 3,
        out_shape=[field, field, jax.ShapeDtypeStruct((moment_rows, 128), F32)],
        scratch_shapes=[pltpu.VMEM((16 * NODES, BZ), BF16), pltpu.VMEM((16 * NODES, BZ), BF16)],
    )(flags, v, mv, diag, mask, maskc, *halos, weights, moments)


def finish_kernel(mom_ref, c_ref, v0_ref, v1_ref, v2_ref, v3_ref, x_ref, r_ref):
    row = jnp.sum(mom_ref[...], axis=0, keepdims=True)
    lanes = lane_iota((1, 128))
    m = [jnp.sum(jnp.where(lanes == k, row, 0.0), keepdims=True) for k in range(6)]
    zero = jnp.zeros((1, 1), F32)
    one = jnp.ones((1, 1), F32)

    def inner(f, g):
        total = zero
        for i, a in enumerate(f):
            for j, b in enumerate(g):
                if a is not None and b is not None:
                    total = total + a * b * m[i + j]
        return total

    r = [one, None, None, None]
    p = [one, None, None, None]
    x = [None, None, None]
    norm = m[0]

    def plus(a, b):
        if a is None:
            return b
        return a if b is None else a + b

    for step in range(3):
        image = [plus(p[k], p[k - 1] if k else None) for k in range(4)]
        alpha = norm / inner(p, image)
        for k in range(3):
            if p[k] is not None:
                x[k] = plus(x[k], alpha * p[k])
        for k in range(4):
            if image[k] is not None:
                r[k] = plus(r[k], -(alpha * image[k]))
        if step < 2:
            new = inner(r, r)
            beta = new / norm
            p = [plus(r[k], None if p[k] is None else beta * p[k]) for k in range(4)]
            norm = new
    inverse = 1.0 / c_ref[0:1, 0:1]
    x = [value * inverse for value in x]
    for chunk in range(8):
        bx, by, zt = chunk // 4, chunk // 2 % 2, chunk % 2
        spot = bx * 4 + zt * 2 + by
        at = pl.ds(chunk * 128, 128)
        v0, v1, v2, v3 = v0_ref[:, at], v1_ref[:, at], v2_ref[:, at], v3_ref[:, at]
        x_ref[:, spot, :] = x[0] * v0 + x[1] * v1 + x[2] * v2
        r_ref[:, spot, :] = r[0] * v0 + r[1] * v1 + r[2] * v2 + r[3] * v3


def finish(moments, centre, fields):
    out = jax.ShapeDtypeStruct((NODES, 8, 128), F32)
    return pl.pallas_call(
        finish_kernel,
        name="finish",
        in_specs=[pl.BlockSpec(memory_space=pltpu.VMEM)] * 6,
        out_specs=[pl.BlockSpec(memory_space=pltpu.VMEM)] * 2,
        out_shape=[out, out],
    )(moments, centre, *fields)


def stencil_weights(coupling):
    coupled = 0.5 * (coupling + jnp.transpose(jnp.flip(coupling, 0), (0, 2, 1)))
    rowabs = jnp.sum(jnp.abs(coupled), axis=(0, 2))
    stacked = jnp.transpose(coupled.reshape(3, 3, 3, NODES, NODES), (0, 2, 3, 1, 4))
    stacked = stacked.reshape(3, 3 * NODES, 3 * NODES)
    high = lax.reduce_precision(stacked, 8, 7)
    both = jnp.concatenate([high, stacked - high], axis=1).astype(BF16)
    return both, jnp.broadcast_to(rowabs[:, None], (NODES, 128))


def ring(axis, move):
    count = lax.axis_size(axis)
    return [(i, (i + move) % count) for i in range(count)]


def exchange(field):
    half = field.shape[1] // 2
    xl = lax.ppermute(field[:, half:], "slab", ring("slab", 1))
    xh = lax.ppermute(field[:, :half], "slab", ring("slab", -1))
    first = jnp.concatenate([xl[:, :BZ], field[:, :BZ], field[:, half : half + BZ], xh[:, :BZ]], axis=1)
    final = jnp.concatenate([xl[:, BZ:], field[:, BZ:half], field[:, half + BZ :], xh[:, BZ:]], axis=1)
    yh = lax.ppermute(first, "grp", ring("grp", -1))
    yl = lax.ppermute(final, "grp", ring("grp", 1))
    return xl, xh, yl, yh


def on_device(samples, block_ids, tile_counts, occupied, coupling):
    slab, grp = lax.axis_index("slab"), lax.axis_index("grp")
    payload = splat(samples, tile_counts, block_ids)
    recv = lax.all_to_all(payload.reshape(SENDERS, 1, ROWS * 128), AXES, split_axis=0, concat_axis=0, tiled=True)
    weights, rowabs = stencil_weights(coupling)
    mask = jnp.broadcast_to(occupied.astype(F32).reshape(1, N_COLS * BZ), (8, N_COLS * BZ))
    flags = jnp.stack([slab > 0, slab < lax.axis_size("slab") - 1, grp > 0, grp < lax.axis_size("grp") - 1]).astype(F32)
    seat = (grp % 16).astype(jnp.int32).reshape(1)
    v, mv, diag, maskc, centre = assemble(seat, recv.reshape(SENDERS * ROWS, 128), mask, rowabs)
    fields = [v]
    moments = jnp.zeros((8, 128), F32)
    for order in range(3):
        v, mv, moments = apply_stiffness(order, flags, v, mv, diag, mask, maskc, exchange(mv), weights, moments)
        fields.append(v)
    shared = lax.all_to_all(moments.reshape(SENDERS, 1, 128), AXES, split_axis=0, concat_axis=0, tiled=True)
    outs = finish(shared.reshape(SENDERS, 128), centre, fields)

    def place(out):
        out = out.reshape(NODES, 2, 2, 2, 128)
        return jnp.transpose(out, (0, 1, 3, 2, 4)).reshape(NODES, 2, 2, BZ)

    return place(outs[0]), place(outs[1])


def solution(mesh):
    placed = (P(AXES, None, None), P(AXES), P(AXES), P("slab", "grp", None), P())
    return jax.shard_map(
        on_device,
        mesh=mesh,
        in_specs=placed,
        out_specs=(P(None, "slab", "grp", None), P(None, "slab", "grp", None)),
        check_vma=False,
    )
```

time: 913 us -> 132 us (0.14)
  blocking collectives: 325 us -> 20 us
  matrix products: 208 us -> 0 us
  local copies, waits for them, and re-layouts: 163 us -> 11 us
  waiting for transfers between devices: 77.1 us -> 25.4 us
  other arithmetic: 52.9 us -> 2.01 us
  Pallas kernels: 0 us -> 35.8 us
  loops' own time: 18.1 us -> 0 us
  starting transfers between devices: 50.9 us -> 36.3 us
    psum x5 -> x0, blocking collectives: 325 us -> none  [the longest x3 193 us: squares(): return lax.psum(jnp.sum(residual * residual), ('slab', 'grp'))]
    dot_general x89 -> x0, matrix products: 208 us -> none  [the longest x81 148 us: apply_stiffness(): jnp.dot(coupled[offset], piece.reshape(nodes, -1), precision=HIGH)]
    reshape x82 -> x2, local copies, waits for them, and re-layouts: 118 us -> 1.24 us  [the longest x1 0.62 us: stencil_weights(): stacked = stacked.reshape(3, 3 * NODES, 3 * NODES)]
    all_to_all x3 -> x1, waiting for transfers between devices: 60.7 us -> 12.4 us  [on_device(): lax.all_to_all(payload.reshape(SENDERS, 1, ROWS * 128), AXES, split_axis=...]
    pallas_call x0 -> x6, Pallas kernels: none -> 35.8 us  [the longest x1 19.5 us: splat(): pl.pallas_call(splat_kernel, name='splat', grid=(groups,), in_specs=[pl.B...]
    all_to_all x0 -> x1, blocking collectives: none -> 20 us  [on_device(): lax.all_to_all(moments.reshape(SENDERS, 1, 128), AXES, split_axis=0, conc...]
    another operation x1 -> x0, loops' own time: 18.1 us -> none  [splat_blocks(): lax.map(lambda pair: splat_tiles(pair[0], pair[1]), (stacked, stacked_cou...]
    mul x9 -> x0, other arithmetic: 16.6 us -> none  [the longest x2 8.6 us: splat_tiles(): slopes = 4.0 * bspline_slope(diff)]
  transfers between devices with their start and end apart: 15 -> 13, of which waited for: 10 -> 9; matrix products, arithmetic and copies ran while one was open for 5% -> 5% of each run, Pallas kernels for 0% -> 0%
where the time goes in v1:
time: 132 us; the launch traced here: 131 us
  starting transfers between devices  36.3 us (27%)
  Pallas kernels  35.8 us (27%)
  waiting for transfers between devices  25.4 us (19%)
  blocking collectives  20 us (15%)
  local copies, waits for them, and re-layouts  11 us (8%)
  other arithmetic  2.01 us (2%)
    all_to_all x1, blocking collectives, on_device(): lax.all_to_all(moments.reshape(SENDERS, 1, 128), AXES, split_axis=0, conc...  20 us
    pallas_call x1, Pallas kernels, splat(): pl.pallas_call(splat_kernel, name='splat', grid=(groups,), in_specs=[pl.B...  19.5 us
    ppermute x3, starting transfers between devices, exchange(): yh = lax.ppermute(first, 'grp', ring('grp', -1))  15.5 us
    all_to_all x1, waiting for transfers between devices, on_device(): lax.all_to_all(payload.reshape(SENDERS, 1, ROWS * 128), AXES, split_axis=...  12.4 us
    all_to_all x1, starting transfers between devices, on_device(): lax.all_to_all(payload.reshape(SENDERS, 1, ROWS * 128), AXES, split_axis=...  11.5 us
    pallas_call x3, Pallas kernels, apply_stiffness(): pl.pallas_call(functools.partial(apply_kernel, 2 * order), name='stiffnes...  10.8 us
    ppermute x3, starting transfers between devices, exchange(): xh = lax.ppermute(field[:, :half], 'slab', ring('slab', -1))  8.14 us
    ppermute x3, waiting for transfers between devices, exchange(): yl = lax.ppermute(final, 'grp', ring('grp', 1))  4.5 us
  transfers between devices with their start and end apart: 13, of which 9 were waited for; matrix products, arithmetic and copies ran while one was open for 5% of the time, Pallas kernels for 0%

profile of v1, /device:TPU:1, one launch (start us, length us, event | category | flops | bytes accessed | tf_op | source)
XLA Modules:
  0.0 131.3 jit_solution(2828313442664251633)
XLA Ops:
  0.6 19.5 %splat.1 = f32[8,144,128]{2,1,0:T(8,128)} custom-call(f32[6,1024,128]{2,1,0:T(8,128)} %bitcast.38, s32[8,128]{1,0:T(8,128)} %bitcast.44, s32[8,128]{1,0:T(8,128)} %bitcast.45), custom_call_target="tpu_custom_call" | custom-call | tf_op jit(solution)/shard_map/splat/pallas_call | solution.py:151
  20.2 11.5 %all-to-all-start = ((f32[128,1,1152]{2,1,0:T(1,128)}), f32[128,1,1152]{2,1,0:T(1,128)S(1)}, u32[]{:S(2)}, u32[]{:S(2)}) async-start(f32[128,1,1152]{2,1,0:T(1,128)} %bitcast.39), calls=%async_computation | async-start | bytes 1179648 | tf_op jit(solution)/shard_map/all_to_all | solution.py:375
  33.5 12.4 %all-to-all-done = f32[128,1,1152]{2,1,0:T(1,128)S(1)} async-done(((f32[128,1,1152]{2,1,0:T(1,128)}), f32[128,1,1152]{2,1,0:T(1,128)S(1)}, u32[]{:S(2)}, u32[]{:S(2)}) %all-to-all-start) | async-done | bytes 589856 | tf_op jit(solution)/shard_map/all_to_all | solution.py:375
  47.3 2.9 %assemble.1 = (f32[64,1024]{1,0:T(8,128)}, f32[64,1024]{1,0:T(8,128)}, f32[64,1024]{1,0:T(8,128)}, f32[8,1024]{1,0:T(8,128)}, f32[8,128]{1,0:T(8,128)}) custom-call(s32[1]{0:T(128)} %bitcast.4.seat_ref, f32[1152,128]{1,0:T(8,128)} %bitcast.40, f32[8,1024]{1,0:T(8,128)} %broadcast_in_dim.17.mask_ref, f32[64,128]{1,0:T(8,128)} %broadcast_in_dim.18.rowabs_ref), custom_call_target="tpu_custom_call" | custom-call | tf_op jit(solution)/shard_map/assemble/pallas_call | solution.py:213
  50.1 1.0 fusion.8
  51.2 2.7 %collective-permute-start.1 = (f32[64,512]{1,0:T(8,128)S(1)}, f32[64,512]{1,0:T(8,128)S(1)}, u32[]{:S(2)}, u32[]{:S(2)}) collective-permute-start(f32[64,512]{1,0:T(8,128)S(1)} %get-tuple-element.52), channel_id=1, source_target_pairs={{0,96},{32,0},{64,32},{96,64},{1,97},{33,1},{65,33},{97,65},{2,98}... | collective-permute-start | bytes 393224 | tf_op jit(solution)/shard_map/ppermute | solution.py:364
  54.8 1.4 %collective-permute-done.xl_ref = f32[64,512]{1,0:T(8,128)S(1)} collective-permute-done((f32[64,512]{1,0:T(8,128)S(1)}, f32[64,512]{1,0:T(8,128)S(1)}, u32[]{:S(2)}, u32[]{:S(2)}) %collective-permute-start) | collective-permute-done | bytes 131104 | tf_op jit(solution)/shard_map/ppermute | solution.py:363
  56.3 2.2 %collective-permute-start.3 = (f32[64,1024]{1,0:T(8,128)S(1)}, f32[64,1024]{1,0:T(8,128)S(1)}, u32[]{:S(2)}, u32[]{:S(2)}) collective-permute-start(f32[64,1024]{1,0:T(8,128)S(1)} %pad_maximum_fusion.2), channel_id=1, source_target_pairs={{0,31},{1,0},{2,1},{3,2},{4,3},{5,4},{6,5},{7,6},{8,7},{9,8},{10,9... | collective-permute-start | bytes 786440 | tf_op jit(solution)/shard_map/ppermute | solution.py:367
  60.4 2.3 %collective-permute-done.3.yh_ref = f32[64,1024]{1,0:T(8,128)S(1)} collective-permute-done((f32[64,1024]{1,0:T(8,128)S(1)}, f32[64,1024]{1,0:T(8,128)S(1)}, u32[]{:S(2)}, u32[]{:S(2)}) %collective-permute-start.3) | collective-permute-done | bytes 262176 | tf_op jit(solution)/shard_map/ppermute | solution.py:367
  63.5 3.6 %stiffness.3 = (f32[64,1024]{1,0:T(8,128)}, f32[64,1024]{1,0:T(8,128)}, f32[8,128]{1,0:T(8,128)}) custom-call(f32[4]{0:T(128)} %add_convert_fusion.flag_ref, f32[64,1024]{1,0:T(8,128)} %get-tuple-element.17.v_ref.v0_ref, f32[64,1024]{1,0:T(8,128)} %get-tuple-element.18.mv_ref, f32[64,1024]{1,0:T(8,128)} %get-tuple-element.19.diag_ref, ...), custom_call_target="tpu_custom_call" | custom-call | tf_op jit(solution)/shard_map/stiffness/pallas_call | solution.py:275
  68.2 3.0 %collective-permute-start.5 = (f32[64,512]{1,0:T(8,128)S(1)}, f32[64,512]{1,0:T(8,128)S(1)}, u32[]{:S(2)}, u32[]{:S(2)}) collective-permute-start(f32[64,512]{1,0:T(8,128)S(1)} %get-tuple-element.46), channel_id=1, source_target_pairs={{0,96},{32,0},{64,32},{96,64},{1,97},{33,1},{65,33},{97,65},{2,98}... | collective-permute-start | bytes 393224 | tf_op jit(solution)/shard_map/ppermute | solution.py:364
  72.1 1.3 %collective-permute-done.4.xl_ref = f32[64,512]{1,0:T(8,128)S(1)} collective-permute-done((f32[64,512]{1,0:T(8,128)S(1)}, f32[64,512]{1,0:T(8,128)S(1)}, u32[]{:S(2)}, u32[]{:S(2)}) %collective-permute-start.4) | collective-permute-done | bytes 131104 | tf_op jit(solution)/shard_map/ppermute | solution.py:363
  73.5 6.5 %collective-permute-start.7 = (f32[64,1024]{1,0:T(8,128)S(1)}, f32[64,1024]{1,0:T(8,128)S(1)}, u32[]{:S(2)}, u32[]{:S(2)}) collective-permute-start(f32[64,1024]{1,0:T(8,128)S(1)} %pad_maximum_fusion.4), channel_id=1, source_target_pairs={{0,31},{1,0},{2,1},{3,2},{4,3},{5,4},{6,5},{7,6},{8,7},{9,8},{10,9... | collective-permute-start | bytes 786440 | tf_op jit(solution)/shard_map/ppermute | solution.py:367
  80.1 1.1 collective-permute-done.7.yh_ref
  81.2 2.2 %collective-permute-done.6.yl_ref = f32[64,1024]{1,0:T(8,128)S(1)} collective-permute-done((f32[64,1024]{1,0:T(8,128)S(1)}, f32[64,1024]{1,0:T(8,128)S(1)}, u32[]{:S(2)}, u32[]{:S(2)}) %collective-permute-start.6) | collective-permute-done | bytes 262176 | tf_op jit(solution)/shard_map/ppermute | solution.py:368
  84.1 3.6 %stiffness.4 = (f32[64,1024]{1,0:T(8,128)}, f32[64,1024]{1,0:T(8,128)}, f32[8,128]{1,0:T(8,128)}) custom-call(f32[4]{0:T(128)} %add_convert_fusion.flag_ref, f32[64,1024]{1,0:T(8,128)} %get-tuple-element.21.v_ref.v1_ref, f32[64,1024]{1,0:T(8,128)} %get-tuple-element.22.mv_ref, f32[64,1024]{1,0:T(8,128)} %get-tuple-element.19.diag_ref, ...), custom_call_target="tpu_custom_call" | custom-call | tf_op jit(solution)/shard_map/stiffness/pallas_call | solution.py:275
  89.3 2.5 %collective-permute-start.9 = (f32[64,512]{1,0:T(8,128)S(1)}, f32[64,512]{1,0:T(8,128)S(1)}, u32[]{:S(2)}, u32[]{:S(2)}) collective-permute-start(f32[64,512]{1,0:T(8,128)S(1)} %get-tuple-element.40), channel_id=1, source_target_pairs={{0,96},{32,0},{64,32},{96,64},{1,97},{33,1},{65,33},{97,65},{2,98}... | collective-permute-start | bytes 393224 | tf_op jit(solution)/shard_map/ppermute | solution.py:364
  92.7 1.3 %collective-permute-done.8.xl_ref = f32[64,512]{1,0:T(8,128)S(1)} collective-permute-done((f32[64,512]{1,0:T(8,128)S(1)}, f32[64,512]{1,0:T(8,128)S(1)}, u32[]{:S(2)}, u32[]{:S(2)}) %collective-permute-start.8) | collective-permute-done | bytes 131104 | tf_op jit(solution)/shard_map/ppermute | solution.py:363
  94.1 6.8 %collective-permute-start.11 = (f32[64,1024]{1,0:T(8,128)S(1)}, f32[64,1024]{1,0:T(8,128)S(1)}, u32[]{:S(2)}, u32[]{:S(2)}) collective-permute-start(f32[64,1024]{1,0:T(8,128)S(1)} %pad_maximum_fusion.6), channel_id=1, source_target_pairs={{0,31},{1,0},{2,1},{3,2},{4,3},{5,4},{6,5},{7,6},{8,7},{9,8},{10,9... | collective-permute-start | bytes 786440 | tf_op jit(solution)/shard_map/ppermute | solution.py:367
  101.0 1.1 collective-permute-done.11.yh_ref
  102.1 2.2 %collective-permute-done.10.yl_ref = f32[64,1024]{1,0:T(8,128)S(1)} collective-permute-done((f32[64,1024]{1,0:T(8,128)S(1)}, f32[64,1024]{1,0:T(8,128)S(1)}, u32[]{:S(2)}, u32[]{:S(2)}) %collective-permute-start.10) | collective-permute-done | bytes 262176 | tf_op jit(solution)/shard_map/ppermute | solution.py:368
  105.0 3.6 %stiffness.5 = (f32[64,1024]{1,0:T(8,128)}, f32[64,1024]{1,0:T(8,128)}, f32[128,128]{1,0:T(8,128)}) custom-call(f32[4]{0:T(128)} %add_convert_fusion.flag_ref, f32[64,1024]{1,0:T(8,128)} %get-tuple-element.24.v_ref.v2_ref, f32[64,1024]{1,0:T(8,128)} %get-tuple-element.25.mv_ref, f32[64,1024]{1,0:T(8,128)} %get-tuple-element.19.diag_ref, ...), custom_call_target="tpu_custom_call" | custom-call | tf_op jit(solution)/shard_map/stiffness/pallas_call | solution.py:275
  108.7 20.0 %all_to_all.10 = f32[128,1,128]{2,1,0:T(1,128)} all-to-all(f32[128,1,128]{2,1,0:T(1,128)} %bitcast.42), channel_id=1, replica_groups=mesh['slab'=4,'grp'=32] {'slab','grp'}, dimensions={0} | all-to-all | bytes 131072 | tf_op jit(solution)/shard_map/all_to_all | solution.py:386
  128.7 2.6 %finish.1 = (f32[64,8,128]{2,1,0:T(8,128)}, f32[64,8,128]{2,1,0:T(8,128)}) custom-call(f32[128,128]{1,0:T(8,128)} %bitcast.41, f32[8,128]{1,0:T(8,128)} %get-tuple-element.28.c_ref, f32[64,1024]{1,0:T(8,128)} %get-tuple-element.17.v_ref.v0_ref, f32[64,1024]{1,0:T(8,128)} %get-tuple-element.21.v_ref.v1_ref, f32[64,1024]{1,0:T(8,128)} %get-tuple-element.24.v_ref.v2_ref, ...), custom_call_target="tpu_custom_call" | custom-call | tf_op jit(solution)/shard_map/finish/pallas_call | solution.py:337
  (69 shorter events, 13.1 us)
Async XLA Ops:
  20.1 11.5 %copy-start.14 = (s32[2,2,256]{2,1,0:T(2,128)S(1)}, s32[2,2,256]{2,1,0:T(2,128)}, u32[]{:S(2)}) copy-start(s32[2,2,256]{2,1,0:T(2,128)} %param.8) | copy-start | bytes 12292
  20.1 11.5 %copy-start = (f32[27,64,64]{2,1,0:T(8,128)S(1)}, f32[27,64,64]{2,1,0:T(8,128)}, u32[]{:S(2)}) copy-start(f32[27,64,64]{2,1,0:T(8,128)} %param.9) | copy-start | bytes 1327108
  20.2 25.8 %all-to-all-start = ((f32[128,1,1152]{2,1,0:T(1,128)}), f32[128,1,1152]{2,1,0:T(1,128)S(1)}, u32[]{:S(2)}, u32[]{:S(2)}) async-start(f32[128,1,1152]{2,1,0:T(1,128)} %bitcast.39), calls=%async_computation | async-start | bytes 1179648 | tf_op jit(solution)/shard_map/all_to_all | solution.py:375
  46.0 1.3 %copy-start.1 = (f32[128,1,1152]{2,1,0:T(1,128)}, f32[128,1,1152]{2,1,0:T(1,128)S(1)}, u32[]{:S(2)}) copy-start(f32[128,1,1152]{2,1,0:T(1,128)S(1)} %all-to-all-done) | copy-start | bytes 1769476
  51.1 5.1 %collective-permute-start = (f32[64,512]{1,0:T(8,128)S(1)}, f32[64,512]{1,0:T(8,128)S(1)}, u32[]{:S(2)}, u32[]{:S(2)}) collective-permute-start(f32[64,512]{1,0:T(8,128)S(1)} %get-tuple-element.53), channel_id=1, source_target_pairs={{0,32},{32,64},{64,96},{96,0},{1,33},{33,65},{65,97},{97,1},{2,34}... | collective-permute-start | bytes 393224 | tf_op jit(solution)/shard_map/ppermute | solution.py:363
  51.2 5.0 %collective-permute-start.1 = (f32[64,512]{1,0:T(8,128)S(1)}, f32[64,512]{1,0:T(8,128)S(1)}, u32[]{:S(2)}, u32[]{:S(2)}) collective-permute-start(f32[64,512]{1,0:T(8,128)S(1)} %get-tuple-element.52), channel_id=1, source_target_pairs={{0,96},{32,0},{64,32},{96,64},{1,97},{33,1},{65,33},{97,65},{2,98}... | collective-permute-start | bytes 393224 | tf_op jit(solution)/shard_map/ppermute | solution.py:364
  56.2 2.7 %copy-start.2 = (f32[64,512]{1,0:T(8,128)}, f32[64,512]{1,0:T(8,128)S(1)}, u32[]{:S(2)}) copy-start(f32[64,512]{1,0:T(8,128)S(1)} %collective-permute-done.xl_ref) | copy-start | bytes 393220
  56.2 2.6 %copy-start.3 = (f32[64,512]{1,0:T(8,128)}, f32[64,512]{1,0:T(8,128)S(1)}, u32[]{:S(2)}) copy-start(f32[64,512]{1,0:T(8,128)S(1)} %collective-permute-done.1.xh_ref) | copy-start | bytes 393220
  56.3 6.4 %collective-permute-start.3 = (f32[64,1024]{1,0:T(8,128)S(1)}, f32[64,1024]{1,0:T(8,128)S(1)}, u32[]{:S(2)}, u32[]{:S(2)}) collective-permute-start(f32[64,1024]{1,0:T(8,128)S(1)} %pad_maximum_fusion.2), channel_id=1, source_target_pairs={{0,31},{1,0},{2,1},{3,2},{4,3},{5,4},{6,5},{7,6},{8,7},{9,8},{10,9... | collective-permute-start | bytes 786440 | tf_op jit(solution)/shard_map/ppermute | solution.py:367
  58.5 4.2 %collective-permute-start.2 = (f32[64,1024]{1,0:T(8,128)S(1)}, f32[64,1024]{1,0:T(8,128)S(1)}, u32[]{:S(2)}, u32[]{:S(2)}) collective-permute-start(f32[64,1024]{1,0:T(8,128)S(1)} %pad_maximum_fusion.1), channel_id=1, source_target_pairs={{0,1},{1,2},{2,3},{3,4},{4,5},{5,6},{6,7},{7,8},{8,9},{9,10},{10,1... | collective-permute-start | bytes 786440 | tf_op jit(solution)/shard_map/ppermute | solution.py:368
  68.1 5.3 %collective-permute-start.4 = (f32[64,512]{1,0:T(8,128)S(1)}, f32[64,512]{1,0:T(8,128)S(1)}, u32[]{:S(2)}, u32[]{:S(2)}) collective-permute-start(f32[64,512]{1,0:T(8,128)S(1)} %get-tuple-element.47), channel_id=1, source_target_pairs={{0,32},{32,64},{64,96},{96,0},{1,33},{33,65},{65,97},{97,1},{2,34}... | collective-permute-start | bytes 393224 | tf_op jit(solution)/shard_map/ppermute | solution.py:363
  68.2 5.3 %collective-permute-start.5 = (f32[64,512]{1,0:T(8,128)S(1)}, f32[64,512]{1,0:T(8,128)S(1)}, u32[]{:S(2)}, u32[]{:S(2)}) collective-permute-start(f32[64,512]{1,0:T(8,128)S(1)} %get-tuple-element.46), channel_id=1, source_target_pairs={{0,96},{32,0},{64,32},{96,64},{1,97},{33,1},{65,33},{97,65},{2,98}... | collective-permute-start | bytes 393224 | tf_op jit(solution)/shard_map/ppermute | solution.py:364
  73.4 10.0 %copy-start.6 = (f32[64,512]{1,0:T(8,128)}, f32[64,512]{1,0:T(8,128)S(1)}, u32[]{:S(2)}) copy-start(f32[64,512]{1,0:T(8,128)S(1)} %collective-permute-done.4.xl_ref) | copy-start | bytes 393220
  73.5 10.0 %copy-start.7 = (f32[64,512]{1,0:T(8,128)}, f32[64,512]{1,0:T(8,128)S(1)}, u32[]{:S(2)}) copy-start(f32[64,512]{1,0:T(8,128)S(1)} %collective-permute-done.5.xh_ref) | copy-start | bytes 393220
  73.5 7.7 %collective-permute-start.7 = (f32[64,1024]{1,0:T(8,128)S(1)}, f32[64,1024]{1,0:T(8,128)S(1)}, u32[]{:S(2)}, u32[]{:S(2)}) collective-permute-start(f32[64,1024]{1,0:T(8,128)S(1)} %pad_maximum_fusion.4), channel_id=1, source_target_pairs={{0,31},{1,0},{2,1},{3,2},{4,3},{5,4},{6,5},{7,6},{8,7},{9,8},{10,9... | collective-permute-start | bytes 786440 | tf_op jit(solution)/shard_map/ppermute | solution.py:367
  80.1 3.4 %collective-permute-start.6 = (f32[64,1024]{1,0:T(8,128)S(1)}, f32[64,1024]{1,0:T(8,128)S(1)}, u32[]{:S(2)}, u32[]{:S(2)}) collective-permute-start(f32[64,1024]{1,0:T(8,128)S(1)} %pad_maximum_fusion.3), channel_id=1, source_target_pairs={{0,1},{1,2},{2,3},{3,4},{4,5},{5,6},{6,7},{7,8},{8,9},{9,10},{10,1... | collective-permute-start | bytes 786440 | tf_op jit(solution)/shard_map/ppermute | solution.py:368
  81.2 2.3 %copy-start.11 = (f32[64,1024]{1,0:T(8,128)}, f32[64,1024]{1,0:T(8,128)S(1)}, u32[]{:S(2)}) copy-start(f32[64,1024]{1,0:T(8,128)S(1)} %collective-permute-done.7.yh_ref) | copy-start | bytes 786436
  88.7 5.3 %collective-permute-start.8 = (f32[64,512]{1,0:T(8,128)S(1)}, f32[64,512]{1,0:T(8,128)S(1)}, u32[]{:S(2)}, u32[]{:S(2)}) collective-permute-start(f32[64,512]{1,0:T(8,128)S(1)} %get-tuple-element.41), channel_id=1, source_target_pairs={{0,32},{32,64},{64,96},{96,0},{1,33},{33,65},{65,97},{97,1},{2,34}... | collective-permute-start | bytes 393224 | tf_op jit(solution)/shard_map/ppermute | solution.py:363
  89.3 4.8 %collective-permute-start.9 = (f32[64,512]{1,0:T(8,128)S(1)}, f32[64,512]{1,0:T(8,128)S(1)}, u32[]{:S(2)}, u32[]{:S(2)}) collective-permute-start(f32[64,512]{1,0:T(8,128)S(1)} %get-tuple-element.40), channel_id=1, source_target_pairs={{0,96},{32,0},{64,32},{96,64},{1,97},{33,1},{65,33},{97,65},{2,98}... | collective-permute-start | bytes 393224 | tf_op jit(solution)/shard_map/ppermute | solution.py:364
  94.1 10.3 %copy-start.4 = (f32[64,512]{1,0:T(8,128)}, f32[64,512]{1,0:T(8,128)S(1)}, u32[]{:S(2)}) copy-start(f32[64,512]{1,0:T(8,128)S(1)} %collective-permute-done.8.xl_ref) | copy-start | bytes 393220
  94.1 10.3 %copy-start.5 = (f32[64,512]{1,0:T(8,128)}, f32[64,512]{1,0:T(8,128)S(1)}, u32[]{:S(2)}) copy-start(f32[64,512]{1,0:T(8,128)S(1)} %collective-permute-done.9.xh_ref) | copy-start | bytes 393220
  94.1 8.0 %collective-permute-start.11 = (f32[64,1024]{1,0:T(8,128)S(1)}, f32[64,1024]{1,0:T(8,128)S(1)}, u32[]{:S(2)}, u32[]{:S(2)}) collective-permute-start(f32[64,1024]{1,0:T(8,128)S(1)} %pad_maximum_fusion.6), channel_id=1, source_target_pairs={{0,31},{1,0},{2,1},{3,2},{4,3},{5,4},{6,5},{7,6},{8,7},{9,8},{10,9... | collective-permute-start | bytes 786440 | tf_op jit(solution)/shard_map/ppermute | solution.py:367
  101.0 3.4 %collective-permute-start.10 = (f32[64,1024]{1,0:T(8,128)S(1)}, f32[64,1024]{1,0:T(8,128)S(1)}, u32[]{:S(2)}, u32[]{:S(2)}) collective-permute-start(f32[64,1024]{1,0:T(8,128)S(1)} %pad_maximum_fusion.5), channel_id=1, source_target_pairs={{0,1},{1,2},{2,3},{3,4},{4,5},{5,6},{6,7},{7,8},{8,9},{9,10},{10,1... | collective-permute-start | bytes 786440 | tf_op jit(solution)/shard_map/ppermute | solution.py:368
  102.1 2.3 %copy-start.10 = (f32[64,1024]{1,0:T(8,128)}, f32[64,1024]{1,0:T(8,128)S(1)}, u32[]{:S(2)}) copy-start(f32[64,1024]{1,0:T(8,128)S(1)} %collective-permute-done.11.yh_ref) | copy-start | bytes 786436
  (4 other events, 2.9 us)

commit v2 on v1

--- a/solution.py
+++ b/solution.py
@@ -89,7 +89,7 @@
 
     for i in range(4):
         def add_group(group, sums, i=i):
-            rows = pl.ds(pl.multiple_of(group * 8, 8), 8)
+            rows = pl.ds(group * 8, 8)
             a = basis[i, rows, :]
             b = basis[4 + i, rows, :]
             c = basis[8 + i, rows, :]
@@ -110,7 +110,9 @@
             return tuple(out)
 
         zero = jnp.zeros((8, 128), F32)
-        sums = lax.fori_loop(0, 16, add_group, (zero,) * 32, unroll=2)
+        sums = (zero,) * 32
+        for group in range(16):
+            sums = add_group(group, sums)
         for at in range(16):
             acc[pl.ds((i * 16 + at) * 8, 8), :] = sums[at]
             acc[pl.ds((64 + i * 16 + at) * 8, 8), :] = sums[16 + at]
@@ -168,8 +170,84 @@
     )(jnp.transpose(samples, (1, 0, 2)), counts.reshape(groups, 128), ids.reshape(groups, 128))
 
 
-def assemble_kernel(seat_ref, recv_ref, mask_ref, rowabs_ref, v_ref, mv_ref, diag_ref, maskc_ref, c_ref, turned):
-    seat = seat_ref[0]
+def vmem(x):
+    return pltpu.with_memory_space_constraint(x, pltpu.VMEM)
+
+
+def parity_weights(place_ref):
+    slab, grp = place_ref[0], place_ref[1]
+    slabs, grps = place_ref[2], place_ref[3]
+
+    def pick(cond):
+        return jnp.where(cond, 1.0, 0.0).astype(F32)
+
+    def sides(at, count):
+        odd = at % 2 == 1
+        low = (pick(odd), pick(jnp.logical_and(jnp.logical_not(odd), at > 0)))
+        high = (pick(jnp.logical_not(odd)), pick(jnp.logical_and(odd, at < count - 1)))
+        return low, high
+
+    return sides(slab, slabs), sides(grp, grps)
+
+
+def blend(pair, a, b):
+    return a * pair[0] + b * pair[1]
+
+
+def column(x, y):
+    return pl.ds((x * 2 + y) * BZ, BZ)
+
+
+def store_edges(place_ref, masked, ea_ref, eb_ref, oa_ref, ob_ref):
+    up_slab = place_ref[0] % 2 == 0
+    up_grp = place_ref[1] % 2 == 0
+    for k in range(2):
+        at = pl.ds(k * BZ, BZ)
+        ea_ref[:, at] = jnp.where(up_slab, masked[1][k], masked[0][k])
+        eb_ref[:, at] = jnp.where(up_slab, masked[0][k], masked[1][k])
+        oa_ref[:, at] = jnp.where(up_grp, masked[k][1], masked[k][0])
+        ob_ref[:, at] = jnp.where(up_grp, masked[k][0], masked[k][1])
+
+
+def prepare_kernel(coupling_ref, occ_ref, w_ref, rowabs_ref, mask_ref):
+    total = jnp.zeros((NODES, NODES), F32)
+    for dx in range(3):
+        for dz in range(3):
+            parts = []
+            for dy in range(3):
+                k = (dx * 3 + dy) * 3 + dz
+                coupled = 0.5 * (coupling_ref[k] + coupling_ref[26 - k].T)
+                total = total + jnp.abs(coupled)
+                parts.append(coupled)
+            wide = jnp.concatenate(parts, axis=1)
+            high = wide.astype(BF16)
+            w_ref[dx, pl.ds(dz * NODES, NODES), :] = high
+            w_ref[dx, pl.ds((3 + dz) * NODES, NODES), :] = (wide - high.astype(F32)).astype(BF16)
+    rowabs_ref[...] = jnp.broadcast_to(jnp.sum(total, axis=1, keepdims=True), (NODES, 128))
+    for x in range(2):
+        for y in range(2):
+            mask_ref[:, column(x, y)] = jnp.broadcast_to(occ_ref[x, y : y + 1, :].astype(F32), (8, BZ))
+
+
+def prepare(coupling, occupied):
+    return pl.pallas_call(
+        prepare_kernel,
+        name="prepare",
+        in_specs=[pl.BlockSpec(memory_space=pltpu.VMEM)] * 2,
+        out_specs=[pl.BlockSpec(memory_space=pltpu.VMEM)] * 3,
+        out_shape=[
+            pltpu.VMEM((3, 6 * NODES, 3 * NODES), BF16),
+            pltpu.VMEM((NODES, 128), F32),
+            pltpu.VMEM((8, N_COLS * BZ), F32),
+        ],
+        compiler_params=pltpu.CompilerParams(vmem_limit_bytes=8 << 20),
+        cost_estimate=pl.CostEstimate(flops=10**7, transcendentals=0, bytes_accessed=4 * 10**6),
+    )(coupling, occupied)
+
+
+def assemble_kernel(place_ref, recv_ref, mask_ref, rowabs_ref, v_ref, diag_ref, maskc_ref, c_ref,
+                    ea_ref, eb_ref, oa_ref, ob_ref, turned):
+    seat = place_ref[1] % 16
     turned[...] = recv_ref[pl.ds(CAP, SENDERS, stride=ROWS), :].T
     where = turned[pl.ds(pl.multiple_of(seat * 8, 8), 8), :].astype(jnp.int32)
     other = lax.rem(seat + 1, 16)
@@ -188,98 +266,125 @@
         low = (block - high.astype(F32)).astype(BF16)
         tiles.append(jnp.concatenate([high, low], axis=1))
     table = jnp.concatenate(tiles, axis=0)
-    for col in range(N_COLS):
-        picks = []
-        for c in range(CAP):
-            hit = row_iota((BZ, SENDERS)) + col * BZ == where[c : c + 1, :]
-            picks.append(hit.astype(F32).astype(BF16))
-        pick = jnp.concatenate(picks, axis=1)
-        both = jnp.dot(pick, table, preferred_element_type=F32)
-        ordered = (both[:, :128] + both[:, 128:]).T
-        rhs = ordered[:NODES]
-        dens = ordered[NODES:]
-        lanes = pl.ds(col * BZ, BZ)
-        mask = mask_ref[0:1, lanes]
-        v_ref[:, lanes] = rhs
-        mv_ref[:, lanes] = rhs * mask
-        diag = rowabs[:, 0:1] + 0.5 + 4.0 * dens
-        diag_ref[:, lanes] = (diag - centre) * inverse
-        maskc_ref[:, lanes] = jnp.broadcast_to(mask * inverse, (8, BZ))
-
-
-def assemble(seat, recv, mask, rowabs):
-    blocks = N_COLS * BZ
-    field = jax.ShapeDtypeStruct((NODES, blocks), F32)
+    masked = []
+    for x in range(2):
+        masked.append([])
+        for y in range(2):
+            picks = []
+            for c in range(CAP):
+                hit = row_iota((BZ, SENDERS)) + (x * 2 + y) * BZ == where[c : c + 1, :]
+                picks.append(hit.astype(F32).astype(BF16))
+            pick = jnp.concatenate(picks, axis=1)
+            both = jnp.dot(pick, table, preferred_element_type=F32)
+            ordered = (both[:, :128] + both[:, 128:]).T
+            rhs = ordered[:NODES]
+            dens = ordered[NODES:]
+            mask = mask_ref[0:1, column(x, y)]
+            v_ref[:, column(x, y)] = rhs
+            diag = rowabs[:, 0:1] + 0.5 + 4.0 * dens
+            diag_ref[:, column(x, y)] = (diag - centre) * inverse
+            maskc_ref[:, column(x, y)] = jnp.broadcast_to(mask * inverse, (8, BZ))
+            masked[x].append(rhs * mask)
+    store_edges(place_ref, masked, ea_ref, eb_ref, oa_ref, ob_ref)
+
+
+FIELD = pltpu.VMEM((NODES, N_COLS * BZ), F32)
+EDGE = pltpu.VMEM((NODES, 2 * BZ), F32)
+
+
+def in_specs(count):
+    return [pl.BlockSpec(memory_space=pltpu.SMEM)] + [pl.BlockSpec(memory_space=pltpu.VMEM)] * count
+
+
+def assemble(place, recv, mask, rowabs):
     return pl.pallas_call(
         assemble_kernel,
         name="assemble",
-        in_specs=[pl.BlockSpec(memory_space=pltpu.SMEM)] + [pl.BlockSpec(memory_space=pltpu.VMEM)] * 3,
-        out_specs=[pl.BlockSpec(memory_space=pltpu.VMEM)] * 5,
-        out_shape=[field, field, field, jax.ShapeDtypeStruct((8, blocks), F32), jax.ShapeDtypeStruct((8, 128), F32)],
+        in_specs=in_specs(3),
+        out_specs=[pl.BlockSpec(memory_space=pltpu.VMEM)] * 8,
+        out_shape=[FIELD, FIELD, pltpu.VMEM((8, N_COLS * BZ), F32), pltpu.VMEM((8, 128), F32), EDGE, EDGE, EDGE, EDGE],
         scratch_shapes=[pltpu.VMEM((128, 128), F32)],
-    )(seat, recv, mask, rowabs)
-
-
-def apply_kernel(first, flag_ref, v_ref, mv_ref, diag_ref, mask_ref, maskc_ref, xl_ref, xh_ref, yl_ref, yh_ref,
-                 w_ref, mom_ref, o_ref, mo_ref, mo_mom_ref, high, low):
-    edges = [flag_ref[k] for k in range(4)]
-    for px in range(4):
-        for py in range(4):
-            if py in (0, 3):
-                src = (yl_ref if py == 0 else yh_ref)[:, pl.ds(px * BZ, BZ)]
-                src = src * edges[2 if py == 0 else 3]
-            elif px in (0, 3):
-                src = (xl_ref if px == 0 else xh_ref)[:, pl.ds((py - 1) * BZ, BZ)]
-            else:
-                src = mv_ref[:, pl.ds(((px - 1) * 2 + py - 1) * BZ, BZ)]
-            if px in (0, 3):
-                src = src * edges[0 if px == 0 else 1]
-            top = src.astype(BF16)
-            rows = pl.ds((px * 4 + py) * NODES, NODES)
-            high[rows, :] = top
-            low[rows, :] = (src - top.astype(F32)).astype(BF16)
+        compiler_params=pltpu.CompilerParams(vmem_limit_bytes=16 << 20),
+    )(place, vmem(recv), vmem(mask), vmem(rowabs))
+
+
+def apply_kernel(order, place_ref, v_ref, diag_ref, mask_ref, maskc_ref, ra_ref, rb_ref, ga_ref, gb_ref, w_ref, *rest):
+    rest = list(rest)
+    mom_ref = rest.pop(0) if order else None
+    o_ref, mom_out = rest[:2]
+    edges = rest[2:-2]
+    high, low = rest[-2:]
+    (x_low, x_high), (y_low, y_high) = parity_weights(place_ref)
+    last = len(edges) == 0
+
+    def put(px, py, src):
+        top = src.astype(BF16)
+        rows = pl.ds((px * 4 + py) * NODES, NODES)
+        high[rows, :] = top
+        low[rows, :] = (src - top.astype(F32)).astype(BF16)
+
+    for x in range(2):
+        for y in range(2):
+            put(x + 1, y + 1, v_ref[:, column(x, y)] * mask_ref[0:1, column(x, y)])
+    for y in range(2):
+        at = pl.ds(y * BZ, BZ)
+        put(0, y + 1, blend(x_low, ra_ref[:, at], rb_ref[:, at]))
+        put(3, y + 1, blend(x_high, ra_ref[:, at], rb_ref[:, at]))
+    for py, pair in ((0, y_low), (3, y_high)):
+        line = [blend(pair, ga_ref[:, pl.ds(k * BZ, BZ)], gb_ref[:, pl.ds(k * BZ, BZ)]) for k in range(4)]
+        put(1, py, line[1])
+        put(2, py, line[2])
+        put(0, py, blend(x_low, line[0], line[3]))
+        put(3, py, blend(x_high, line[0], line[3]))
     lanes = lane_iota((NODES, BZ))
     sq = jnp.zeros((NODES, BZ), F32)
     cross = jnp.zeros((NODES, BZ), F32)
-    for ox in range(2):
-        for oy in range(2):
+    masked = []
+    for x in range(2):
+        masked.append([])
+        for y in range(2):
             full = jnp.zeros((6 * NODES, BZ), F32)
             half = jnp.zeros((3 * NODES, BZ), F32)
             for dx in range(3):
-                rows = pl.ds(((ox + dx) * 4 + oy) * NODES, 3 * NODES)
-                cols = pl.ds(dx * 3 * NODES, 3 * NODES)
+                rows = pl.ds(((x + dx) * 4 + y) * NODES, 3 * NODES)
                 full = full + jnp.dot(w_ref[dx], high[rows, :], preferred_element_type=F32)
                 half = half + jnp.dot(w_ref[dx, 0 : 3 * NODES, :], low[rows, :], preferred_element_type=F32)
             part = full[: 3 * NODES] + full[3 * NODES :] + half
             before = jnp.where(lanes == 0, 0.0, pltpu.roll(part[:NODES], 1, 1))
             after = jnp.where(lanes == BZ - 1, 0.0, pltpu.roll(part[2 * NODES :], BZ - 1, 1))
             total = part[NODES : 2 * NODES] + before + after
-            at = pl.ds((ox * 2 + oy) * BZ, BZ)
+            at = column(x, y)
             v = v_ref[:, at]
             new = diag_ref[:, at] * v - maskc_ref[0:1, at] * total
             o_ref[:, at] = new
-            mo_ref[:, at] = new * mask_ref[0:1, at]
+            masked[x].append(new * mask_ref[0:1, at])
             sq = sq + v * v
             cross = cross + v * new
+    if not last:
+        store_edges(place_ref, masked, *edges)
     sq = jnp.sum(sq, keepdims=True)
     cross = jnp.sum(cross, keepdims=True)
     spot = lane_iota((1, 128))
-    mom = jnp.where(spot == first, sq, jnp.where(spot == first + 1, cross, mom_ref[0:1, :]))
-    mo_mom_ref[...] = jnp.broadcast_to(mom, mo_mom_ref.shape)
-
-
-def apply_stiffness(order, flags, v, mv, diag, mask, maskc, halos, weights, moments):
-    blocks = N_COLS * BZ
-    field = jax.ShapeDtypeStruct((NODES, blocks), F32)
-    moment_rows = SENDERS if order == 2 else 8
+    before = mom_ref[0:1, :] if order else jnp.zeros((1, 128), F32)
+    mom = jnp.where(spot == 2 * order, sq, jnp.where(spot == 2 * order + 1, cross, before))
+    mom_out[...] = jnp.broadcast_to(mom, mom_out.shape)
+
+
+def apply_stiffness(order, place, v, diag, mask, maskc, halos, weights, moments):
+    more = [] if moments is None else [moments]
+    last = order == 2
+    moment = jax.ShapeDtypeStruct((SENDERS, 128), F32) if last else pltpu.VMEM((8, 128), F32)
+    shapes = [FIELD, moment] + ([] if last else [EDGE] * 4)
+    operands = [v, diag, mask, maskc, *halos, weights] + more
     return pl.pallas_call(
-        functools.partial(apply_kernel, 2 * order),
+        functools.partial(apply_kernel, order),
         name="stiffness",
-        in_specs=[pl.BlockSpec(memory_space=pltpu.SMEM)] + [pl.BlockSpec(memory_space=pltpu.VMEM)] * 11,
-        out_specs=[pl.BlockSpec(memory_space=pltpu.VMEM)] * 3,
-        out_shape=[field, field, jax.ShapeDtypeStruct((moment_rows, 128), F32)],
+        in_specs=in_specs(len(operands)),
+        out_specs=[pl.BlockSpec(memory_space=pltpu.VMEM)] * len(shapes),
+        out_shape=shapes,
         scratch_shapes=[pltpu.VMEM((16 * NODES, BZ), BF16), pltpu.VMEM((16 * NODES, BZ), BF16)],
-    )(flags, v, mv, diag, mask, maskc, *halos, weights, moments)
+        compiler_params=pltpu.CompilerParams(vmem_limit_bytes=16 << 20),
+    )(place, *[vmem(x) for x in operands])
 
 
 def finish_kernel(mom_ref, c_ref, v0_ref, v1_ref, v2_ref, v3_ref, x_ref, r_ref):
@@ -340,57 +445,55 @@
         in_specs=[pl.BlockSpec(memory_space=pltpu.VMEM)] * 6,
         out_specs=[pl.BlockSpec(memory_space=pltpu.VMEM)] * 2,
         out_shape=[out, out],
-    )(moments, centre, *fields)
-
-
-def stencil_weights(coupling):
-    coupled = 0.5 * (coupling + jnp.transpose(jnp.flip(coupling, 0), (0, 2, 1)))
-    rowabs = jnp.sum(jnp.abs(coupled), axis=(0, 2))
-    stacked = jnp.transpose(coupled.reshape(3, 3, 3, NODES, NODES), (0, 2, 3, 1, 4))
-    stacked = stacked.reshape(3, 3 * NODES, 3 * NODES)
-    high = lax.reduce_precision(stacked, 8, 7)
-    both = jnp.concatenate([high, stacked - high], axis=1).astype(BF16)
-    return both, jnp.broadcast_to(rowabs[:, None], (NODES, 128))
-
-
-def ring(axis, move):
+        compiler_params=pltpu.CompilerParams(vmem_limit_bytes=16 << 20),
+    )(moments, *[vmem(x) for x in (centre, *fields)])
+
+
+def swap(axis, first):
     count = lax.axis_size(axis)
-    return [(i, (i + move) % count) for i in range(count)]
-
-
-def exchange(field):
-    half = field.shape[1] // 2
-    xl = lax.ppermute(field[:, half:], "slab", ring("slab", 1))
-    xh = lax.ppermute(field[:, :half], "slab", ring("slab", -1))
-    first = jnp.concatenate([xl[:, :BZ], field[:, :BZ], field[:, half : half + BZ], xh[:, :BZ]], axis=1)
-    final = jnp.concatenate([xl[:, BZ:], field[:, BZ:half], field[:, half + BZ :], xh[:, BZ:]], axis=1)
-    yh = lax.ppermute(first, "grp", ring("grp", -1))
-    yl = lax.ppermute(final, "grp", ring("grp", 1))
-    return xl, xh, yl, yh
+    pairs = []
+    for i in range(count):
+        j = i + 1 if (i - first) % 2 == 0 else i - 1
+        pairs.append((i, j if 0 <= j < count else i))
+    return pairs
+
+
+def exchange(grp, ea, eb, oa, ob):
+    ra = lax.ppermute(ea, "slab", swap("slab", 0))
+    rb = lax.ppermute(eb, "slab", swap("slab", 1))
+    up = grp % 2 == 0
+
+    def line(own, upper):
+        take = [jnp.where(upper, r[:, BZ:], r[:, :BZ]) for r in (ra, rb)]
+        return jnp.concatenate([take[0], own, take[1]], axis=1)
+
+    gb = lax.ppermute(line(ob, jnp.logical_not(up)), "grp", swap("grp", 1))
+    ga = lax.ppermute(line(oa, up), "grp", swap("grp", 0))
+    return ra, rb, ga, gb
 
 
 def on_device(samples, block_ids, tile_counts, occupied, coupling):
     slab, grp = lax.axis_index("slab"), lax.axis_index("grp")
+    place = jnp.stack([slab, grp, lax.axis_size("slab"), lax.axis_size("grp")]).astype(jnp.int32)
     payload = splat(samples, tile_counts, block_ids)
     recv = lax.all_to_all(payload.reshape(SENDERS, 1, ROWS * 128), AXES, split_axis=0, concat_axis=0, tiled=True)
-    weights, rowabs = stencil_weights(coupling)
-    mask = jnp.broadcast_to(occupied.astype(F32).reshape(1, N_COLS * BZ), (8, N_COLS * BZ))
-    flags = jnp.stack([slab > 0, slab < lax.axis_size("slab") - 1, grp > 0, grp < lax.axis_size("grp") - 1]).astype(F32)
-    seat = (grp % 16).astype(jnp.int32).reshape(1)
-    v, mv, diag, maskc, centre = assemble(seat, recv.reshape(SENDERS * ROWS, 128), mask, rowabs)
+    weights, rowabs, mask = prepare(coupling, occupied)
+    v, diag, maskc, centre, *edges = assemble(place, recv.reshape(SENDERS * ROWS, 128), mask, rowabs)
     fields = [v]
-    moments = jnp.zeros((8, 128), F32)
+    moments = None
     for order in range(3):
-        v, mv, moments = apply_stiffness(order, flags, v, mv, diag, mask, maskc, exchange(mv), weights, moments)
+        v, moments, *edges = apply_stiffness(
+            order, place, v, diag, mask, maskc, exchange(grp, *edges), weights, moments
+        )
         fields.append(v)
     shared = lax.all_to_all(moments.reshape(SENDERS, 1, 128), AXES, split_axis=0, concat_axis=0, tiled=True)
     outs = finish(shared.reshape(SENDERS, 128), centre, fields)
 
-    def place(out):
+    def settle(out):
         out = out.reshape(NODES, 2, 2, 2, 128)
         return jnp.transpose(out, (0, 1, 3, 2, 4)).reshape(NODES, 2, 2, BZ)
 
-    return place(outs[0]), place(outs[1])
+    return settle(outs[0]), settle(outs[1])
 
 
 def solution(mesh):

time: 132 us -> 117 us (0.89)
  local copies, waits for them, and re-layouts: 11 us -> 0.01 us
  Pallas kernels: 35.8 us -> 25.4 us
  waiting for transfers between devices: 25.4 us -> 33.9 us
  other arithmetic: 2.01 us -> 0.27 us
    ppermute x12, waiting for transfers between devices: 13 us -> 20.1 us  [the longest x3 13.6 us: exchange(): gb = lax.ppermute(line(ob, jnp.logical_not(up)), 'grp', swap('grp', 1))]
    pallas_call x4 -> x5, Pallas kernels: 13.6 us -> 7.46 us  [the longest x3 5.56 us: apply_stiffness(): pl.pallas_call(functools.partial(apply_kernel, order), name='stiffness',...]
    slice x12 -> x0, local copies, waits for them, and re-layouts: 5.88 us -> none  [the longest x3 2.96 us: exchange(): xh = lax.ppermute(field[:, :half], 'slab', ring('slab', -1))]
    pallas_call x1, Pallas kernels: 19.5 us -> 16.6 us  [splat(): pl.pallas_call(splat_kernel, name='splat', grid=(groups,), in_specs=[pl.B...]
    broadcast_in_dim x3 -> x0, local copies, waits for them, and re-layouts: 1.94 us -> none  [the longest x1 0.67 us: stencil_weights(): return (both, jnp.broadcast_to(rowabs[:, None], (NODES, 128)))]
    unnamed x32 -> x4, local copies, waits for them, and re-layouts: 1.91 us -> 0.01 us
    all_to_all x1, waiting for transfers between devices: 12.4 us -> 13.8 us  [on_device(): lax.all_to_all(payload.reshape(SENDERS, 1, ROWS * 128), AXES, split_axis=...]
  transfers between devices with their start and end apart: 13 -> 13, of which waited for: 9 -> 7; matrix products, arithmetic and copies ran while one was open for 5% -> 0% of each run, Pallas kernels for 0% -> 0%
where the time goes in v2:
time: 117 us; the launch traced here: 116 us
  starting transfers between devices  35 us (30%)
  waiting for transfers between devices  33.9 us (29%)
  Pallas kernels  25.4 us (22%)
  blocking collectives  20.7 us (18%)
    all_to_all x1, blocking collectives, on_device(): lax.all_to_all(moments.reshape(SENDERS, 1, 128), AXES, split_axis=0, conc...  20.7 us
    pallas_call x1, Pallas kernels, splat(): pl.pallas_call(splat_kernel, name='splat', grid=(groups,), in_specs=[pl.B...  16.6 us
    all_to_all x1, waiting for transfers between devices, on_device(): lax.all_to_all(payload.reshape(SENDERS, 1, ROWS * 128), AXES, split_axis=...  13.8 us
    ppermute x3, waiting for transfers between devices, exchange(): gb = lax.ppermute(line(ob, jnp.logical_not(up)), 'grp', swap('grp', 1))  13.6 us
    ppermute x3, starting transfers between devices, exchange(): gb = lax.ppermute(line(ob, jnp.logical_not(up)), 'grp', swap('grp', 1))  11.5 us
    all_to_all x1, starting transfers between devices, on_device(): lax.all_to_all(payload.reshape(SENDERS, 1, ROWS * 128), AXES, split_axis=...  11.5 us
    ppermute x3, starting transfers between devices, exchange(): ra = lax.ppermute(ea, 'slab', swap('slab', 0))  7.68 us
    ppermute x3, waiting for transfers between devices, exchange(): ra = lax.ppermute(ea, 'slab', swap('slab', 0))  6.5 us
  transfers between devices with their start and end apart: 13, of which 7 were waited for; matrix products, arithmetic and copies ran while one was open for 0% of the time, Pallas kernels for 0%

profile of v2, /device:TPU:1, one launch (start us, length us, event | category | flops | bytes accessed | tf_op | source)
XLA Modules:
  0.0 116.3 jit_solution(18387532147959215105)
XLA Ops:
  0.7 16.6 %splat.1 = f32[8,144,128]{2,1,0:T(8,128)} custom-call(f32[6,1024,128]{2,1,0:T(8,128)} %bitcast.24, s32[8,128]{1,0:T(8,128)} %bitcast.26, s32[8,128]{1,0:T(8,128)} %bitcast.27), custom_call_target="tpu_custom_call" | custom-call | tf_op jit(solution)/shard_map/splat/pallas_call | solution.py:153
  17.2 11.5 %all-to-all-start = ((f32[128,1,1152]{2,1,0:T(1,128)}), f32[128,1,1152]{2,1,0:T(1,128)S(1)}, u32[]{:S(2)}, u32[]{:S(2)}) async-start(f32[128,1,1152]{2,1,0:T(1,128)} %bitcast.25), calls=%async_computation | async-start | bytes 1179648 | tf_op jit(solution)/shard_map/all_to_all | solution.py:479
  29.3 13.8 %all-to-all-done = f32[128,1,1152]{2,1,0:T(1,128)S(1)} async-done(((f32[128,1,1152]{2,1,0:T(1,128)}), f32[128,1,1152]{2,1,0:T(1,128)S(1)}, u32[]{:S(2)}, u32[]{:S(2)}) %all-to-all-start) | async-done | bytes 589856 | tf_op jit(solution)/shard_map/all_to_all | solution.py:479
  43.0 1.5 %assemble.1 = (f32[64,1024]{1,0:T(8,128)S(1)}, f32[64,1024]{1,0:T(8,128)S(1)}, f32[8,1024]{1,0:T(8,128)S(1)}, f32[8,128]{1,0:T(8,128)S(1)}, f32[64,512]{1,0:T(8,...) custom-call(s32[4]{0:T(128)S(1)} %pad_add_fusion.place_ref, ...), custom_call_target="tpu_custom_call" | custom-call | tf_op jit(solution)/shard_map/assemble/pallas_call | solution.py:300
  44.6 0.7 collective-permute-start.1
  45.3 3.1 %collective-permute-done.ra_ref = f32[64,512]{1,0:T(8,128)S(1)} collective-permute-done((f32[64,512]{1,0:T(8,128)S(1)}, f32[64,512]{1,0:T(8,128)S(1)}, u32[]{:S(2)}, u32[]{:S(2)}) %collective-permute-start) | collective-permute-done | bytes 131104 | tf_op jit(solution)/shard_map/ppermute | solution.py:462
  48.5 2.2 %collective-permute-start.2 = (f32[64,1024]{1,0:T(8,128)S(1)}, f32[64,1024]{1,0:T(8,128)S(1)}, u32[]{:S(2)}, u32[]{:S(2)}) collective-permute-start(f32[64,1024]{1,0:T(8,128)S(1)} %pad_maximum_fusion), channel_id=1, source_target_pairs={{0,1},{1,0},{2,3},{3,2},{4,5},{5,4},{6,7},{7,6},{8,9},{9,8},{10,11... | collective-permute-start | bytes 786440 | tf_op jit(solution)/shard_map/ppermute | solution.py:471
  50.7 2.1 %collective-permute-start.3 = (f32[64,1024]{1,0:T(8,128)S(1)}, f32[64,1024]{1,0:T(8,128)S(1)}, u32[]{:S(2)}, u32[]{:S(2)}) collective-permute-start(f32[64,1024]{1,0:T(8,128)S(1)} %pad_maximum_fusion.1), channel_id=1, source_target_pairs={{0,0},{1,2},{2,1},{3,4},{4,3},{5,6},{6,5},{7,8},{8,7},{9,10},{10,9... | collective-permute-start | bytes 786440 | tf_op jit(solution)/shard_map/ppermute | solution.py:470
  52.8 5.6 %collective-permute-done.3.gb_ref = f32[64,1024]{1,0:T(8,128)S(1)} collective-permute-done((f32[64,1024]{1,0:T(8,128)S(1)}, f32[64,1024]{1,0:T(8,128)S(1)}, u32[]{:S(2)}, u32[]{:S(2)}) %collective-permute-start.3) | collective-permute-done | bytes 262176 | tf_op jit(solution)/shard_map/ppermute | solution.py:470
  58.4 1.9 %stiffness.3 = (f32[64,1024]{1,0:T(8,128)S(1)}, f32[8,128]{1,0:T(8,128)S(1)}, f32[64,512]{1,0:T(8,128)S(1)}, f32[64,512]{1,0:T(8,128)S(1)}, f32[64,512]{1,0:T(8,128)S(1)}, /*index=5*/f32[64,512]{1,0:T(8,128)S(1)}) custom-call(s32[4]{0:T(128)S(1)} %pad_add_fusion.place_ref, f32[64,1024]{1,0:T(8,128)S(1)} %get-tuple-element.31.v_ref.v0_ref, ...), custom_call_target="tpu_custom_call" | custom-call | tf_op jit(solution)/shard_map/stiffness/pallas_call | solution.py:379
  60.2 4.0 %collective-permute-start.4 = (f32[64,512]{1,0:T(8,128)S(1)}, f32[64,512]{1,0:T(8,128)S(1)}, u32[]{:S(2)}, u32[]{:S(2)}) collective-permute-start(f32[64,512]{1,0:T(8,128)S(1)} %get-tuple-element.40), channel_id=1, source_target_pairs={{0,32},{32,0},{64,96},{96,64},{1,33},{33,1},{65,97},{97,65},{2,34}... | collective-permute-start | bytes 393224 | tf_op jit(solution)/shard_map/ppermute | solution.py:462
  64.2 0.7 collective-permute-start.5
  64.9 1.7 %collective-permute-done.4.ra_ref = f32[64,512]{1,0:T(8,128)S(1)} collective-permute-done((f32[64,512]{1,0:T(8,128)S(1)}, f32[64,512]{1,0:T(8,128)S(1)}, u32[]{:S(2)}, u32[]{:S(2)}) %collective-permute-start.4) | collective-permute-done | bytes 131104 | tf_op jit(solution)/shard_map/ppermute | solution.py:462
  66.8 3.9 %collective-permute-start.7 = (f32[64,1024]{1,0:T(8,128)S(1)}, f32[64,1024]{1,0:T(8,128)S(1)}, u32[]{:S(2)}, u32[]{:S(2)}) collective-permute-start(f32[64,1024]{1,0:T(8,128)S(1)} %pad_maximum_fusion.3), channel_id=1, source_target_pairs={{0,0},{1,2},{2,1},{3,4},{4,3},{5,6},{6,5},{7,8},{8,7},{9,10},{10,9... | collective-permute-start | bytes 786440 | tf_op jit(solution)/shard_map/ppermute | solution.py:470
  70.7 4.0 %collective-permute-done.7.gb_ref = f32[64,1024]{1,0:T(8,128)S(1)} collective-permute-done((f32[64,1024]{1,0:T(8,128)S(1)}, f32[64,1024]{1,0:T(8,128)S(1)}, u32[]{:S(2)}, u32[]{:S(2)}) %collective-permute-start.7) | collective-permute-done | bytes 262176 | tf_op jit(solution)/shard_map/ppermute | solution.py:470
  74.7 1.9 %stiffness.4 = (f32[64,1024]{1,0:T(8,128)S(1)}, f32[8,128]{1,0:T(8,128)S(1)}, f32[64,512]{1,0:T(8,128)S(1)}, f32[64,512]{1,0:T(8,128)S(1)}, f32[64,512]{1,0:T(8,128)S(1)}, /*index=5*/f32[64,512]{1,0:T(8,128)S(1)}) custom-call(s32[4]{0:T(128)S(1)} %pad_add_fusion.place_ref, f32[64,1024]{1,0:T(8,128)S(1)} %get-tuple-element.39.v_ref.v1_ref, ...), custom_call_target="tpu_custom_call" | custom-call | tf_op jit(solution)/shard_map/stiffness/pallas_call | solution.py:379
  76.6 3.6 %collective-permute-start.8 = (f32[64,512]{1,0:T(8,128)S(1)}, f32[64,512]{1,0:T(8,128)S(1)}, u32[]{:S(2)}, u32[]{:S(2)}) collective-permute-start(f32[64,512]{1,0:T(8,128)S(1)} %get-tuple-element.46), channel_id=1, source_target_pairs={{0,32},{32,0},{64,96},{96,64},{1,33},{33,1},{65,97},{97,65},{2,34}... | collective-permute-start | bytes 393224 | tf_op jit(solution)/shard_map/ppermute | solution.py:462
  80.2 0.7 collective-permute-start.9
  80.9 1.7 %collective-permute-done.8.ra_ref = f32[64,512]{1,0:T(8,128)S(1)} collective-permute-done((f32[64,512]{1,0:T(8,128)S(1)}, f32[64,512]{1,0:T(8,128)S(1)}, u32[]{:S(2)}, u32[]{:S(2)}) %collective-permute-start.8) | collective-permute-done | bytes 131104 | tf_op jit(solution)/shard_map/ppermute | solution.py:462
  82.7 5.5 %collective-permute-start.11 = (f32[64,1024]{1,0:T(8,128)S(1)}, f32[64,1024]{1,0:T(8,128)S(1)}, u32[]{:S(2)}, u32[]{:S(2)}) collective-permute-start(f32[64,1024]{1,0:T(8,128)S(1)} %pad_maximum_fusion.5), channel_id=1, source_target_pairs={{0,0},{1,2},{2,1},{3,4},{4,3},{5,6},{6,5},{7,8},{8,7},{9,10},{10,9... | collective-permute-start | bytes 786440 | tf_op jit(solution)/shard_map/ppermute | solution.py:470
  88.3 4.0 %collective-permute-done.11.gb_ref = f32[64,1024]{1,0:T(8,128)S(1)} collective-permute-done((f32[64,1024]{1,0:T(8,128)S(1)}, f32[64,1024]{1,0:T(8,128)S(1)}, u32[]{:S(2)}, u32[]{:S(2)}) %collective-permute-start.11) | collective-permute-done | bytes 262176 | tf_op jit(solution)/shard_map/ppermute | solution.py:470
  92.3 1.8 %stiffness.5 = (f32[64,1024]{1,0:T(8,128)S(1)}, f32[128,128]{1,0:T(8,128)S(1)}) custom-call(s32[4]{0:T(128)S(1)} %pad_add_fusion.place_ref, f32[64,1024]{1,0:T(8,128)S(1)} %get-tuple-element.45.v_ref.v2_ref, f32[64,1024]{1,0:T(8,128)S(1)} %get-tuple-element.32.diag_ref, f32[8,1024]{1,0:T(8,128)S(1)} %get-tuple-element.29.mask_ref, ...), custom_call_target="tpu_custom_call" | custom-call | tf_op jit(solution)/shard_map/stiffness/pallas_call | solution.py:379
  94.2 20.7 %all_to_all.10 = f32[128,1,128]{2,1,0:T(1,128)S(1)} all-to-all(f32[128,1,128]{2,1,0:T(1,128)S(1)} %bitcast.23), channel_id=1, replica_groups=mesh['slab'=4,'grp'=32] {'slab','grp'}, dimensions={0} | all-to-all | bytes 131072 | tf_op jit(solution)/shard_map/all_to_all | solution.py:489
  114.9 1.4 %finish.1 = (f32[64,8,128]{2,1,0:T(8,128)}, f32[64,8,128]{2,1,0:T(8,128)}) custom-call(f32[128,128]{1,0:T(8,128)S(1)} %bitcast.22, f32[8,128]{1,0:T(8,128)S(1)} %get-tuple-element.52.c_ref, f32[64,1024]{1,0:T(8,128)S(1)} %get-tuple-element.31.v_ref.v0_ref, f32[64,1024]{1,0:T(8,128)S(1)} %get-tuple-element.39.v_ref.v1_ref, ...), custom_call_target="tpu_custom_call" | custom-call | tf_op jit(solution)/shard_map/finish/pallas_call | solution.py:442
  (27 shorter events, 1.0 us)
Async XLA Ops:
  0.6 28.1 %copy-start = (f32[27,64,64]{2,1,0:T(8,128)S(1)}, f32[27,64,64]{2,1,0:T(8,128)}, u32[]{:S(2)}) copy-start(f32[27,64,64]{2,1,0:T(8,128)} %coupling_ref.1) | copy-start | bytes 1327108
  0.6 28.1 %copy-start.1 = (s32[2,2,256]{2,1,0:T(2,128)S(1)}, s32[2,2,256]{2,1,0:T(2,128)}, u32[]{:S(2)}) copy-start(s32[2,2,256]{2,1,0:T(2,128)} %occ_ref.1) | copy-start | bytes 12292
  17.2 25.8 %all-to-all-start = ((f32[128,1,1152]{2,1,0:T(1,128)}), f32[128,1,1152]{2,1,0:T(1,128)S(1)}, u32[]{:S(2)}, u32[]{:S(2)}) async-start(f32[128,1,1152]{2,1,0:T(1,128)} %bitcast.25), calls=%async_computation | async-start | bytes 1179648 | tf_op jit(solution)/shard_map/all_to_all | solution.py:479
  44.5 3.9 %collective-permute-start = (f32[64,512]{1,0:T(8,128)S(1)}, f32[64,512]{1,0:T(8,128)S(1)}, u32[]{:S(2)}, u32[]{:S(2)}) collective-permute-start(f32[64,512]{1,0:T(8,128)S(1)} %get-tuple-element.34), channel_id=1, source_target_pairs={{0,32},{32,0},{64,96},{96,64},{1,33},{33,1},{65,97},{97,65},{2,34}... | collective-permute-start | bytes 393224 | tf_op jit(solution)/shard_map/ppermute | solution.py:462
  44.6 3.8 %collective-permute-start.1 = (f32[64,512]{1,0:T(8,128)S(1)}, f32[64,512]{1,0:T(8,128)S(1)}, u32[]{:S(2)}, u32[]{:S(2)}) collective-permute-start(f32[64,512]{1,0:T(8,128)S(1)} %get-tuple-element.35), channel_id=1, source_target_pairs={{0,0},{32,64},{64,32},{96,96},{1,1},{33,65},{65,33},{97,97},{2,2},... | collective-permute-start | bytes 393224 | tf_op jit(solution)/shard_map/ppermute | solution.py:463
  48.5 4.3 %collective-permute-start.2 = (f32[64,1024]{1,0:T(8,128)S(1)}, f32[64,1024]{1,0:T(8,128)S(1)}, u32[]{:S(2)}, u32[]{:S(2)}) collective-permute-start(f32[64,1024]{1,0:T(8,128)S(1)} %pad_maximum_fusion), channel_id=1, source_target_pairs={{0,1},{1,0},{2,3},{3,2},{4,5},{5,4},{6,7},{7,6},{8,9},{9,8},{10,11... | collective-permute-start | bytes 786440 | tf_op jit(solution)/shard_map/ppermute | solution.py:471
  50.7 7.7 %collective-permute-start.3 = (f32[64,1024]{1,0:T(8,128)S(1)}, f32[64,1024]{1,0:T(8,128)S(1)}, u32[]{:S(2)}, u32[]{:S(2)}) collective-permute-start(f32[64,1024]{1,0:T(8,128)S(1)} %pad_maximum_fusion.1), channel_id=1, source_target_pairs={{0,0},{1,2},{2,1},{3,4},{4,3},{5,6},{6,5},{7,8},{8,7},{9,10},{10,9... | collective-permute-start | bytes 786440 | tf_op jit(solution)/shard_map/ppermute | solution.py:470
  60.2 6.3 %collective-permute-start.4 = (f32[64,512]{1,0:T(8,128)S(1)}, f32[64,512]{1,0:T(8,128)S(1)}, u32[]{:S(2)}, u32[]{:S(2)}) collective-permute-start(f32[64,512]{1,0:T(8,128)S(1)} %get-tuple-element.40), channel_id=1, source_target_pairs={{0,32},{32,0},{64,96},{96,64},{1,33},{33,1},{65,97},{97,65},{2,34}... | collective-permute-start | bytes 393224 | tf_op jit(solution)/shard_map/ppermute | solution.py:462
  64.2 2.4 %collective-permute-start.5 = (f32[64,512]{1,0:T(8,128)S(1)}, f32[64,512]{1,0:T(8,128)S(1)}, u32[]{:S(2)}, u32[]{:S(2)}) collective-permute-start(f32[64,512]{1,0:T(8,128)S(1)} %get-tuple-element.41), channel_id=1, source_target_pairs={{0,0},{32,64},{64,32},{96,96},{1,1},{33,65},{65,33},{97,97},{2,2},... | collective-permute-start | bytes 393224 | tf_op jit(solution)/shard_map/ppermute | solution.py:463
  66.6 4.0 %collective-permute-start.6 = (f32[64,1024]{1,0:T(8,128)S(1)}, f32[64,1024]{1,0:T(8,128)S(1)}, u32[]{:S(2)}, u32[]{:S(2)}) collective-permute-start(f32[64,1024]{1,0:T(8,128)S(1)} %pad_maximum_fusion.2), channel_id=1, source_target_pairs={{0,1},{1,0},{2,3},{3,2},{4,5},{5,4},{6,7},{7,6},{8,9},{9,8},{10,11... | collective-permute-start | bytes 786440 | tf_op jit(solution)/shard_map/ppermute | solution.py:471
  66.8 7.9 %collective-permute-start.7 = (f32[64,1024]{1,0:T(8,128)S(1)}, f32[64,1024]{1,0:T(8,128)S(1)}, u32[]{:S(2)}, u32[]{:S(2)}) collective-permute-start(f32[64,1024]{1,0:T(8,128)S(1)} %pad_maximum_fusion.3), channel_id=1, source_target_pairs={{0,0},{1,2},{2,1},{3,4},{4,3},{5,6},{6,5},{7,8},{8,7},{9,10},{10,9... | collective-permute-start | bytes 786440 | tf_op jit(solution)/shard_map/ppermute | solution.py:470
  76.6 6.0 %collective-permute-start.8 = (f32[64,512]{1,0:T(8,128)S(1)}, f32[64,512]{1,0:T(8,128)S(1)}, u32[]{:S(2)}, u32[]{:S(2)}) collective-permute-start(f32[64,512]{1,0:T(8,128)S(1)} %get-tuple-element.46), channel_id=1, source_target_pairs={{0,32},{32,0},{64,96},{96,64},{1,33},{33,1},{65,97},{97,65},{2,34}... | collective-permute-start | bytes 393224 | tf_op jit(solution)/shard_map/ppermute | solution.py:462
  80.2 2.4 %collective-permute-start.9 = (f32[64,512]{1,0:T(8,128)S(1)}, f32[64,512]{1,0:T(8,128)S(1)}, u32[]{:S(2)}, u32[]{:S(2)}) collective-permute-start(f32[64,512]{1,0:T(8,128)S(1)} %get-tuple-element.47), channel_id=1, source_target_pairs={{0,0},{32,64},{64,32},{96,96},{1,1},{33,65},{65,33},{97,97},{2,2},... | collective-permute-start | bytes 393224 | tf_op jit(solution)/shard_map/ppermute | solution.py:463
  82.6 5.6 %collective-permute-start.10 = (f32[64,1024]{1,0:T(8,128)S(1)}, f32[64,1024]{1,0:T(8,128)S(1)}, u32[]{:S(2)}, u32[]{:S(2)}) collective-permute-start(f32[64,1024]{1,0:T(8,128)S(1)} %pad_maximum_fusion.4), channel_id=1, source_target_pairs={{0,1},{1,0},{2,3},{3,2},{4,5},{5,4},{6,7},{7,6},{8,9},{9,8},{10,11... | collective-permute-start | bytes 786440 | tf_op jit(solution)/shard_map/ppermute | solution.py:471
  82.7 9.6 %collective-permute-start.11 = (f32[64,1024]{1,0:T(8,128)S(1)}, f32[64,1024]{1,0:T(8,128)S(1)}, u32[]{:S(2)}, u32[]{:S(2)}) collective-permute-start(f32[64,1024]{1,0:T(8,128)S(1)} %pad_maximum_fusion.5), channel_id=1, source_target_pairs={{0,0},{1,2},{2,1},{3,4},{4,3},{5,6},{6,5},{7,8},{8,7},{9,10},{10,9... | collective-permute-start | bytes 786440 | tf_op jit(solution)/shard_map/ppermute | solution.py:470

commit v3 on v2

--- a/solution.py
+++ b/solution.py
@@ -308,40 +308,41 @@
     )(place, vmem(recv), vmem(mask), vmem(rowabs))
 
 
-def apply_kernel(order, place_ref, v_ref, diag_ref, mask_ref, maskc_ref, ra_ref, rb_ref, ga_ref, gb_ref, w_ref, *rest):
-    rest = list(rest)
-    mom_ref = rest.pop(0) if order else None
-    o_ref, mom_out = rest[:2]
-    edges = rest[2:-2]
-    high, low = rest[-2:]
+def spread(part):
+    lanes = lane_iota((NODES, BZ))
+    before = jnp.where(lanes == 0, 0.0, pltpu.roll(part[:NODES], 1, 1))
+    after = jnp.where(lanes == BZ - 1, 0.0, pltpu.roll(part[2 * NODES :], BZ - 1, 1))
+    return part[NODES : 2 * NODES] + before + after
+
+
+def split(src):
+    top = src.astype(BF16)
+    return top, (src - top.astype(F32)).astype(BF16)
+
+
+def sides_kernel(place_ref, v_ref, mask_ref, ra_ref, rb_ref, ya_ref, yb_ref, w_ref, o_ref, high, low):
     (x_low, x_high), (y_low, y_high) = parity_weights(place_ref)
-    last = len(edges) == 0
 
     def put(px, py, src):
-        top = src.astype(BF16)
         rows = pl.ds((px * 4 + py) * NODES, NODES)
-        high[rows, :] = top
-        low[rows, :] = (src - top.astype(F32)).astype(BF16)
+        high[rows, :], low[rows, :] = split(src)
 
     for x in range(2):
         for y in range(2):
             put(x + 1, y + 1, v_ref[:, column(x, y)] * mask_ref[0:1, column(x, y)])
-    for y in range(2):
-        at = pl.ds(y * BZ, BZ)
-        put(0, y + 1, blend(x_low, ra_ref[:, at], rb_ref[:, at]))
-        put(3, y + 1, blend(x_high, ra_ref[:, at], rb_ref[:, at]))
-    for py, pair in ((0, y_low), (3, y_high)):
-        line = [blend(pair, ga_ref[:, pl.ds(k * BZ, BZ)], gb_ref[:, pl.ds(k * BZ, BZ)]) for k in range(4)]
-        put(1, py, line[1])
-        put(2, py, line[2])
-        put(0, py, blend(x_low, line[0], line[3]))
-        put(3, py, blend(x_high, line[0], line[3]))
-    lanes = lane_iota((NODES, BZ))
-    sq = jnp.zeros((NODES, BZ), F32)
-    cross = jnp.zeros((NODES, BZ), F32)
-    masked = []
+    for k in range(2):
+        at = pl.ds(k * BZ, BZ)
+        put(0, k + 1, blend(x_low, ra_ref[:, at], rb_ref[:, at]))
+        put(3, k + 1, blend(x_high, ra_ref[:, at], rb_ref[:, at]))
+        put(k + 1, 0, blend(y_low, ya_ref[:, at], yb_ref[:, at]))
+        put(k + 1, 3, blend(y_high, ya_ref[:, at], yb_ref[:, at]))
+    nothing = jnp.zeros((NODES, BZ), BF16)
+    for px in (0, 3):
+        for py in (0, 3):
+            rows = pl.ds((px * 4 + py) * NODES, NODES)
+            high[rows, :] = nothing
+            low[rows, :] = nothing
     for x in range(2):
-        masked.append([])
         for y in range(2):
             full = jnp.zeros((6 * NODES, BZ), F32)
             half = jnp.zeros((3 * NODES, BZ), F32)
@@ -349,18 +350,48 @@
                 rows = pl.ds(((x + dx) * 4 + y) * NODES, 3 * NODES)
                 full = full + jnp.dot(w_ref[dx], high[rows, :], preferred_element_type=F32)
                 half = half + jnp.dot(w_ref[dx, 0 : 3 * NODES, :], low[rows, :], preferred_element_type=F32)
-            part = full[: 3 * NODES] + full[3 * NODES :] + half
-            before = jnp.where(lanes == 0, 0.0, pltpu.roll(part[:NODES], 1, 1))
-            after = jnp.where(lanes == BZ - 1, 0.0, pltpu.roll(part[2 * NODES :], BZ - 1, 1))
-            total = part[NODES : 2 * NODES] + before + after
+            o_ref[:, column(x, y)] = spread(full[: 3 * NODES] + full[3 * NODES :] + half)
+
+
+def sides(place, v, mask, ra, rb, ya, yb, weights):
+    operands = (v, mask, ra, rb, ya, yb, weights)
+    return pl.pallas_call(
+        sides_kernel,
+        name="sides",
+        in_specs=in_specs(len(operands)),
+        out_specs=pl.BlockSpec(memory_space=pltpu.VMEM),
+        out_shape=FIELD,
+        scratch_shapes=[pltpu.VMEM((16 * NODES, BZ), BF16), pltpu.VMEM((16 * NODES, BZ), BF16)],
+        compiler_params=pltpu.CompilerParams(vmem_limit_bytes=16 << 20),
+        cost_estimate=pl.CostEstimate(flops=15 * 10**8, transcendentals=0, bytes_accessed=2 * 10**6),
+    )(place, *[vmem(x) for x in operands])
+
+
+def corners_kernel(order, place_ref, sum_ref, v_ref, diag_ref, mask_ref, maskc_ref, ca_ref, cb_ref, w_ref, *rest):
+    rest = list(rest)
+    mom_ref = rest.pop(0) if order else None
+    o_ref, mom_out = rest[:2]
+    edges = rest[2:]
+    x_pairs, y_pairs = parity_weights(place_ref)
+    sq = jnp.zeros((NODES, BZ), F32)
+    cross = jnp.zeros((NODES, BZ), F32)
+    masked = [[], []]
+    for y in range(2):
+        line = [blend(y_pairs[y], ca_ref[:, pl.ds(k * BZ, BZ)], cb_ref[:, pl.ds(k * BZ, BZ)]) for k in range(2)]
+        for x in range(2):
+            high, low = split(blend(x_pairs[x], line[0], line[1]))
+            cols = pl.ds(2 * y * NODES, NODES)
+            full = jnp.dot(w_ref[2 * x, :, cols], high, preferred_element_type=F32)
+            half = jnp.dot(w_ref[2 * x, 0 : 3 * NODES, cols], low, preferred_element_type=F32)
             at = column(x, y)
+            total = sum_ref[:, at] + spread(full[: 3 * NODES] + full[3 * NODES :] + half)
             v = v_ref[:, at]
             new = diag_ref[:, at] * v - maskc_ref[0:1, at] * total
             o_ref[:, at] = new
             masked[x].append(new * mask_ref[0:1, at])
             sq = sq + v * v
             cross = cross + v * new
-    if not last:
+    if edges:
         store_edges(place_ref, masked, *edges)
     sq = jnp.sum(sq, keepdims=True)
     cross = jnp.sum(cross, keepdims=True)
@@ -370,19 +401,20 @@
     mom_out[...] = jnp.broadcast_to(mom, mom_out.shape)
 
 
-def apply_stiffness(order, place, v, diag, mask, maskc, halos, weights, moments):
+def apply_stiffness(order, place, v, diag, mask, maskc, edges, weights, moments):
+    ra, rb, ya, yb, ca, cb = exchange(place[1], *edges)
+    part = sides(place, v, mask, ra, rb, ya, yb, weights)
     more = [] if moments is None else [moments]
     last = order == 2
     moment = jax.ShapeDtypeStruct((SENDERS, 128), F32) if last else pltpu.VMEM((8, 128), F32)
     shapes = [FIELD, moment] + ([] if last else [EDGE] * 4)
-    operands = [v, diag, mask, maskc, *halos, weights] + more
+    operands = [part, v, diag, mask, maskc, ca, cb, weights] + more
     return pl.pallas_call(
-        functools.partial(apply_kernel, order),
-        name="stiffness",
+        functools.partial(corners_kernel, order),
+        name="corners",
         in_specs=in_specs(len(operands)),
         out_specs=[pl.BlockSpec(memory_space=pltpu.VMEM)] * len(shapes),
         out_shape=shapes,
-        scratch_shapes=[pltpu.VMEM((16 * NODES, BZ), BF16), pltpu.VMEM((16 * NODES, BZ), BF16)],
         compiler_params=pltpu.CompilerParams(vmem_limit_bytes=16 << 20),
     )(place, *[vmem(x) for x in operands])
 
@@ -459,17 +491,18 @@
 
 
 def exchange(grp, ea, eb, oa, ob):
+    yb = lax.ppermute(ob, "grp", swap("grp", 1))
     ra = lax.ppermute(ea, "slab", swap("slab", 0))
     rb = lax.ppermute(eb, "slab", swap("slab", 1))
+    ya = lax.ppermute(oa, "grp", swap("grp", 0))
     up = grp % 2 == 0
 
-    def line(own, upper):
-        take = [jnp.where(upper, r[:, BZ:], r[:, :BZ]) for r in (ra, rb)]
-        return jnp.concatenate([take[0], own, take[1]], axis=1)
-
-    gb = lax.ppermute(line(ob, jnp.logical_not(up)), "grp", swap("grp", 1))
-    ga = lax.ppermute(line(oa, up), "grp", swap("grp", 0))
-    return ra, rb, ga, gb
+    def line(upper):
+        return jnp.concatenate([jnp.where(upper, r[:, BZ:], r[:, :BZ]) for r in (ra, rb)], axis=1)
+
+    cb = lax.ppermute(line(jnp.logical_not(up)), "grp", swap("grp", 1))
+    ca = lax.ppermute(line(up), "grp", swap("grp", 0))
+    return ra, rb, ya, yb, ca, cb
 
 
 def on_device(samples, block_ids, tile_counts, occupied, coupling):
@@ -483,7 +516,7 @@
     moments = None
     for order in range(3):
         v, moments, *edges = apply_stiffness(
-            order, place, v, diag, mask, maskc, exchange(grp, *edges), weights, moments
+            order, place, v, diag, mask, maskc, edges, weights, moments
         )
         fields.append(v)
     shared = lax.all_to_all(moments.reshape(SENDERS, 1, 128), AXES, split_axis=0, concat_axis=0, tiled=True)

time: 117 us -> 112 us (0.957)
  waiting for transfers between devices: 33.9 us -> 18.9 us
  starting transfers between devices: 35 us -> 41 us
  Pallas kernels: 25.4 us -> 28.7 us
  blocking collectives: 20.7 us -> 22.1 us
    ppermute x6 -> x12, waiting for transfers between devices: 13.6 us -> 5.16 us  [the longest x3 4.57 us: exchange(): cb = lax.ppermute(line(jnp.logical_not(up)), 'grp', swap('grp', 1))]
    ppermute x6 -> x12, starting transfers between devices: 13.9 us -> 20.8 us  [the longest x3 8.6 us: exchange(): yb = lax.ppermute(ob, 'grp', swap('grp', 1))]
    ppermute x3, waiting for transfers between devices: 6.5 us -> 0.01 us  [exchange(): ra = lax.ppermute(ea, 'slab', swap('slab', 0))]
    pallas_call x3 -> x6, Pallas kernels: 5.56 us -> 8.9 us  [the longest x3 5.12 us: sides(): pl.pallas_call(sides_kernel, name='sides', in_specs=in_specs(len(operands...]
    all_to_all x1, blocking collectives: 20.7 us -> 22.1 us  [on_device(): lax.all_to_all(moments.reshape(SENDERS, 1, 128), AXES, split_axis=0, conc...]
  transfers between devices with their start and end apart: 13 -> 19, of which waited for: 7 -> 6; matrix products, arithmetic and copies ran while one was open for 0% -> 0% of each run, Pallas kernels for 0% -> 5%
where the time goes in v3:
time: 112 us
  starting transfers between devices  41 us (37%)
  Pallas kernels  28.7 us (26%)
  blocking collectives  22.1 us (20%)
  waiting for transfers between devices  18.9 us (17%)
    all_to_all x1, blocking collectives, on_device(): lax.all_to_all(moments.reshape(SENDERS, 1, 128), AXES, split_axis=0, conc...  22.1 us
    pallas_call x1, Pallas kernels, splat(): pl.pallas_call(splat_kernel, name='splat', grid=(groups,), in_specs=[pl.B...  16.5 us
    all_to_all x1, waiting for transfers between devices, on_device(): lax.all_to_all(payload.reshape(SENDERS, 1, ROWS * 128), AXES, split_axis=...  13.8 us
    all_to_all x1, starting transfers between devices, on_device(): lax.all_to_all(payload.reshape(SENDERS, 1, ROWS * 128), AXES, split_axis=...  11.5 us
    ppermute x3, starting transfers between devices, exchange(): yb = lax.ppermute(ob, 'grp', swap('grp', 1))  8.6 us
    ppermute x3, starting transfers between devices, exchange(): cb = lax.ppermute(line(jnp.logical_not(up)), 'grp', swap('grp', 1))  8.48 us
    ppermute x3, starting transfers between devices, exchange(): ra = lax.ppermute(ea, 'slab', swap('slab', 0))  6.72 us
    pallas_call x3, Pallas kernels, sides(): pl.pallas_call(sides_kernel, name='sides', in_specs=in_specs(len(operands...  5.12 us
  transfers between devices with their start and end apart: 19, of which 6 were waited for; matrix products, arithmetic and copies ran while one was open for 0% of the time, Pallas kernels for 5%

profile of v3, /device:TPU:1, one launch (start us, length us, event | category | flops | bytes accessed | tf_op | source)
XLA Modules:
  0.0 112.1 jit_solution(17855062946376855705)
XLA Ops:
  0.7 16.5 %splat.1 = f32[8,144,128]{2,1,0:T(8,128)} custom-call(f32[6,1024,128]{2,1,0:T(8,128)} %bitcast.24, s32[8,128]{1,0:T(8,128)} %bitcast.26, s32[8,128]{1,0:T(8,128)} %bitcast.27), custom_call_target="tpu_custom_call" | custom-call | tf_op jit(solution)/shard_map/splat/pallas_call | solution.py:153
  17.2 11.5 %all-to-all-start = ((f32[128,1,1152]{2,1,0:T(1,128)}), f32[128,1,1152]{2,1,0:T(1,128)S(1)}, u32[]{:S(2)}, u32[]{:S(2)}) async-start(f32[128,1,1152]{2,1,0:T(1,128)} %bitcast.25), calls=%async_computation | async-start | bytes 1179648 | tf_op jit(solution)/shard_map/all_to_all | solution.py:512
  29.2 13.8 %all-to-all-done = f32[128,1,1152]{2,1,0:T(1,128)S(1)} async-done(((f32[128,1,1152]{2,1,0:T(1,128)}), f32[128,1,1152]{2,1,0:T(1,128)S(1)}, u32[]{:S(2)}, u32[]{:S(2)}) %all-to-all-start) | async-done | bytes 589856 | tf_op jit(solution)/shard_map/all_to_all | solution.py:512
  43.0 1.5 %assemble.1 = (f32[64,1024]{1,0:T(8,128)S(1)}, f32[64,1024]{1,0:T(8,128)S(1)}, f32[8,1024]{1,0:T(8,128)S(1)}, f32[8,128]{1,0:T(8,128)S(1)}, f32[64,512]{1,0:T(8,...) custom-call(s32[4]{0:T(128)S(1)} %pad_add_fusion.place_ref, ...), custom_call_target="tpu_custom_call" | custom-call | tf_op jit(solution)/shard_map/assemble/pallas_call | solution.py:300
  45.2 1.5 %collective-permute-start.2 = (f32[64,512]{1,0:T(8,128)S(1)}, f32[64,512]{1,0:T(8,128)S(1)}, u32[]{:S(2)}, u32[]{:S(2)}) collective-permute-start(f32[64,512]{1,0:T(8,128)S(1)} %get-tuple-element.34), channel_id=1, source_target_pairs={{0,1},{1,0},{2,3},{3,2},{4,5},{5,4},{6,7},{7,6},{8,9},{9,8},{10,11... | collective-permute-start | bytes 393224 | tf_op jit(solution)/shard_map/ppermute | solution.py:497
  46.7 1.9 %collective-permute-start.3 = (f32[64,512]{1,0:T(8,128)S(1)}, f32[64,512]{1,0:T(8,128)S(1)}, u32[]{:S(2)}, u32[]{:S(2)}) collective-permute-start(f32[64,512]{1,0:T(8,128)S(1)} %get-tuple-element.35), channel_id=1, source_target_pairs={{0,0},{1,2},{2,1},{3,4},{4,3},{5,6},{6,5},{7,8},{8,7},{9,10},{10,9... | collective-permute-start | bytes 393224 | tf_op jit(solution)/shard_map/ppermute | solution.py:494
  48.7 1.9 %collective-permute-start.4 = (f32[64,512]{1,0:T(8,128)S(1)}, f32[64,512]{1,0:T(8,128)S(1)}, u32[]{:S(2)}, u32[]{:S(2)}) collective-permute-start(f32[64,512]{1,0:T(8,128)S(1)} %pad_maximum_fusion), channel_id=1, source_target_pairs={{0,1},{1,0},{2,3},{3,2},{4,5},{5,4},{6,7},{7,6},{8,9},{9,8},{10,11... | collective-permute-start | bytes 393224 | tf_op jit(solution)/shard_map/ppermute | solution.py:504
  50.6 2.1 %collective-permute-start.5 = (f32[64,512]{1,0:T(8,128)S(1)}, f32[64,512]{1,0:T(8,128)S(1)}, u32[]{:S(2)}, u32[]{:S(2)}) collective-permute-start(f32[64,512]{1,0:T(8,128)S(1)} %pad_maximum_fusion.1), channel_id=1, source_target_pairs={{0,0},{1,2},{2,1},{3,4},{4,3},{5,6},{6,5},{7,8},{8,7},{9,10},{10,9... | collective-permute-start | bytes 393224 | tf_op jit(solution)/shard_map/ppermute | solution.py:503
  53.0 1.7 %sides.3.sum_ref = f32[64,1024]{1,0:T(8,128)S(1)} custom-call(s32[4]{0:T(128)S(1)} %pad_add_fusion.place_ref, f32[64,1024]{1,0:T(8,128)S(1)} %get-tuple-element.31.v_ref.v0_ref, f32[8,1024]{1,0:T(8,128)S(1)} %get-tuple-element.29.mask_ref, f32[64,512]{1,0:T(8,128)S(1)} %collective-permute-done.ra_ref, f32[64,512]{1,0:T(8,128)S(1)} %collective-permute-done.1.rb_ref, ...), custom_call_target="tpu_custom_call" | custom-call | flops 1500000000 | bytes 2000000 | tf_op jit(solution)/shard_map/sides/pallas_call | solution.py:358
  54.7 2.2 %collective-permute-done.5.cb_ref = f32[64,512]{1,0:T(8,128)S(1)} collective-permute-done((f32[64,512]{1,0:T(8,128)S(1)}, f32[64,512]{1,0:T(8,128)S(1)}, u32[]{:S(2)}, u32[]{:S(2)}) %collective-permute-start.5) | collective-permute-done | bytes 131104 | tf_op jit(solution)/shard_map/ppermute | solution.py:503
  56.9 1.3 %corners.3 = (f32[64,1024]{1,0:T(8,128)S(1)}, f32[8,128]{1,0:T(8,128)S(1)}, f32[64,512]{1,0:T(8,128)S(1)}, f32[64,512]{1,0:T(8,128)S(1)}, f32[64,512]{1,0:T(8,128)S(1)}, /*index=5*/f32[64,512]{1,0:T(8,128)S(1)}) custom-call(s32[4]{0:T(128)S(1)} %pad_add_fusion.place_ref, f32[64,1024]{1,0:T(8,128)S(1)} %sides.3.sum_ref, ...), custom_call_target="tpu_custom_call" | custom-call | tf_op jit(solution)/shard_map/corners/pallas_call | solution.py:412
  58.2 3.7 %collective-permute-start.6 = (f32[64,512]{1,0:T(8,128)S(1)}, f32[64,512]{1,0:T(8,128)S(1)}, u32[]{:S(2)}, u32[]{:S(2)}) collective-permute-start(f32[64,512]{1,0:T(8,128)S(1)} %get-tuple-element.40), channel_id=1, source_target_pairs={{0,32},{32,0},{64,96},{96,64},{1,33},{33,1},{65,97},{97,65},{2,34}... | collective-permute-start | bytes 393224 | tf_op jit(solution)/shard_map/ppermute | solution.py:495
  62.6 2.6 %collective-permute-start.9 = (f32[64,512]{1,0:T(8,128)S(1)}, f32[64,512]{1,0:T(8,128)S(1)}, u32[]{:S(2)}, u32[]{:S(2)}) collective-permute-start(f32[64,512]{1,0:T(8,128)S(1)} %get-tuple-element.43), channel_id=1, source_target_pairs={{0,0},{1,2},{2,1},{3,4},{4,3},{5,6},{6,5},{7,8},{8,7},{9,10},{10,9... | collective-permute-start | bytes 393224 | tf_op jit(solution)/shard_map/ppermute | solution.py:494
  65.4 3.2 %collective-permute-start.11 = (f32[64,512]{1,0:T(8,128)S(1)}, f32[64,512]{1,0:T(8,128)S(1)}, u32[]{:S(2)}, u32[]{:S(2)}) collective-permute-start(f32[64,512]{1,0:T(8,128)S(1)} %pad_maximum_fusion.3), channel_id=1, source_target_pairs={{0,0},{1,2},{2,1},{3,4},{4,3},{5,6},{6,5},{7,8},{8,7},{9,10},{10,9... | collective-permute-start | bytes 393224 | tf_op jit(solution)/shard_map/ppermute | solution.py:503
  68.9 1.7 %sides.4.sum_ref = f32[64,1024]{1,0:T(8,128)S(1)} custom-call(s32[4]{0:T(128)S(1)} %pad_add_fusion.place_ref, f32[64,1024]{1,0:T(8,128)S(1)} %get-tuple-element.39.v_ref.v1_ref, f32[8,1024]{1,0:T(8,128)S(1)} %get-tuple-element.29.mask_ref, f32[64,512]{1,0:T(8,128)S(1)} %collective-permute-done.6.ra_ref, f32[64,512]{1,0:T(8,128)S(1)} %collective-permute-done.7.rb_ref, ...), custom_call_target="tpu_custom_call" | custom-call | flops 1500000000 | bytes 2000000 | tf_op jit(solution)/shard_map/sides/pallas_call | solution.py:358
  71.7 1.3 %corners.4 = (f32[64,1024]{1,0:T(8,128)S(1)}, f32[8,128]{1,0:T(8,128)S(1)}, f32[64,512]{1,0:T(8,128)S(1)}, f32[64,512]{1,0:T(8,128)S(1)}, f32[64,512]{1,0:T(8,128)S(1)}, /*index=5*/f32[64,512]{1,0:T(8,128)S(1)}) custom-call(s32[4]{0:T(128)S(1)} %pad_add_fusion.place_ref, f32[64,1024]{1,0:T(8,128)S(1)} %sides.4.sum_ref, ...), custom_call_target="tpu_custom_call" | custom-call | tf_op jit(solution)/shard_map/corners/pallas_call | solution.py:412
  73.0 3.0 %collective-permute-start.12 = (f32[64,512]{1,0:T(8,128)S(1)}, f32[64,512]{1,0:T(8,128)S(1)}, u32[]{:S(2)}, u32[]{:S(2)}) collective-permute-start(f32[64,512]{1,0:T(8,128)S(1)} %get-tuple-element.46), channel_id=1, source_target_pairs={{0,32},{32,0},{64,96},{96,64},{1,33},{33,1},{65,97},{97,65},{2,34}... | collective-permute-start | bytes 393224 | tf_op jit(solution)/shard_map/ppermute | solution.py:495
  76.7 4.1 %collective-permute-start.15 = (f32[64,512]{1,0:T(8,128)S(1)}, f32[64,512]{1,0:T(8,128)S(1)}, u32[]{:S(2)}, u32[]{:S(2)}) collective-permute-start(f32[64,512]{1,0:T(8,128)S(1)} %get-tuple-element.49), channel_id=1, source_target_pairs={{0,0},{1,2},{2,1},{3,4},{4,3},{5,6},{6,5},{7,8},{8,7},{9,10},{10,9... | collective-permute-start | bytes 393224 | tf_op jit(solution)/shard_map/ppermute | solution.py:494
  81.0 3.2 %collective-permute-start.17 = (f32[64,512]{1,0:T(8,128)S(1)}, f32[64,512]{1,0:T(8,128)S(1)}, u32[]{:S(2)}, u32[]{:S(2)}) collective-permute-start(f32[64,512]{1,0:T(8,128)S(1)} %pad_maximum_fusion.5), channel_id=1, source_target_pairs={{0,0},{1,2},{2,1},{3,4},{4,3},{5,6},{6,5},{7,8},{8,7},{9,10},{10,9... | collective-permute-start | bytes 393224 | tf_op jit(solution)/shard_map/ppermute | solution.py:503
  84.2 1.7 %sides.5.sum_ref = f32[64,1024]{1,0:T(8,128)S(1)} custom-call(s32[4]{0:T(128)S(1)} %pad_add_fusion.place_ref, f32[64,1024]{1,0:T(8,128)S(1)} %get-tuple-element.45.v_ref.v2_ref, f32[8,1024]{1,0:T(8,128)S(1)} %get-tuple-element.29.mask_ref, f32[64,512]{1,0:T(8,128)S(1)} %collective-permute-done.12.ra_ref, f32[64,512]{1,0:T(8,128)S(1)} %collective-permute-done.13.rb_ref, ...), custom_call_target="tpu_custom_call" | custom-call | flops 1500000000 | bytes 2000000 | tf_op jit(solution)/shard_map/sides/pallas_call | solution.py:358
  85.9 1.3 %collective-permute-done.17.cb_ref = f32[64,512]{1,0:T(8,128)S(1)} collective-permute-done((f32[64,512]{1,0:T(8,128)S(1)}, f32[64,512]{1,0:T(8,128)S(1)}, u32[]{:S(2)}, u32[]{:S(2)}) %collective-permute-start.17) | collective-permute-done | bytes 131104 | tf_op jit(solution)/shard_map/ppermute | solution.py:503
  87.3 1.2 %corners.5 = (f32[64,1024]{1,0:T(8,128)S(1)}, f32[128,128]{1,0:T(8,128)S(1)}) custom-call(s32[4]{0:T(128)S(1)} %pad_add_fusion.place_ref, f32[64,1024]{1,0:T(8,128)S(1)} %sides.5.sum_ref, f32[64,1024]{1,0:T(8,128)S(1)} %get-tuple-element.45.v_ref.v2_ref, f32[64,1024]{1,0:T(8,128)S(1)} %get-tuple-element.37.diag_ref, ...), custom_call_target="tpu_custom_call" | custom-call | tf_op jit(solution)/shard_map/corners/pallas_call | solution.py:412
  88.5 22.1 %all_to_all.10 = f32[128,1,128]{2,1,0:T(1,128)S(1)} all-to-all(f32[128,1,128]{2,1,0:T(1,128)S(1)} %bitcast.23), channel_id=1, replica_groups=mesh['slab'=4,'grp'=32] {'slab','grp'}, dimensions={0} | all-to-all | bytes 131072 | tf_op jit(solution)/shard_map/all_to_all | solution.py:522
  110.7 1.4 %finish.1 = (f32[64,8,128]{2,1,0:T(8,128)}, f32[64,8,128]{2,1,0:T(8,128)}) custom-call(f32[128,128]{1,0:T(8,128)S(1)} %bitcast.22, f32[8,128]{1,0:T(8,128)S(1)} %get-tuple-element.52.c_ref, f32[64,1024]{1,0:T(8,128)S(1)} %get-tuple-element.31.v_ref.v0_ref, f32[64,1024]{1,0:T(8,128)S(1)} %get-tuple-element.39.v_ref.v1_ref, ...), custom_call_target="tpu_custom_call" | custom-call | tf_op jit(solution)/shard_map/finish/pallas_call | solution.py:474
  (42 shorter events, 4.7 us)
Async XLA Ops:
  0.6 28.1 %copy-start = (f32[27,64,64]{2,1,0:T(8,128)S(1)}, f32[27,64,64]{2,1,0:T(8,128)}, u32[]{:S(2)}) copy-start(f32[27,64,64]{2,1,0:T(8,128)} %coupling_ref.1) | copy-start | bytes 1327108
  0.6 28.1 %copy-start.1 = (s32[2,2,256]{2,1,0:T(2,128)S(1)}, s32[2,2,256]{2,1,0:T(2,128)}, u32[]{:S(2)}) copy-start(s32[2,2,256]{2,1,0:T(2,128)} %occ_ref.1) | copy-start | bytes 12292
  17.2 25.8 %all-to-all-start = ((f32[128,1,1152]{2,1,0:T(1,128)}), f32[128,1,1152]{2,1,0:T(1,128)S(1)}, u32[]{:S(2)}, u32[]{:S(2)}) async-start(f32[128,1,1152]{2,1,0:T(1,128)} %bitcast.25), calls=%async_computation | async-start | bytes 1179648 | tf_op jit(solution)/shard_map/all_to_all | solution.py:512
  44.5 4.2 %collective-permute-start = (f32[64,512]{1,0:T(8,128)S(1)}, f32[64,512]{1,0:T(8,128)S(1)}, u32[]{:S(2)}, u32[]{:S(2)}) collective-permute-start(f32[64,512]{1,0:T(8,128)S(1)} %get-tuple-element.32), channel_id=1, source_target_pairs={{0,32},{32,0},{64,96},{96,64},{1,33},{33,1},{65,97},{97,65},{2,34}... | collective-permute-start | bytes 393224 | tf_op jit(solution)/shard_map/ppermute | solution.py:495
  44.6 4.1 %collective-permute-start.1 = (f32[64,512]{1,0:T(8,128)S(1)}, f32[64,512]{1,0:T(8,128)S(1)}, u32[]{:S(2)}, u32[]{:S(2)}) collective-permute-start(f32[64,512]{1,0:T(8,128)S(1)} %get-tuple-element.33), channel_id=1, source_target_pairs={{0,0},{32,64},{64,32},{96,96},{1,1},{33,65},{65,33},{97,97},{2,2},... | collective-permute-start | bytes 393224 | tf_op jit(solution)/shard_map/ppermute | solution.py:496
  45.2 7.5 %collective-permute-start.2 = (f32[64,512]{1,0:T(8,128)S(1)}, f32[64,512]{1,0:T(8,128)S(1)}, u32[]{:S(2)}, u32[]{:S(2)}) collective-permute-start(f32[64,512]{1,0:T(8,128)S(1)} %get-tuple-element.34), channel_id=1, source_target_pairs={{0,1},{1,0},{2,3},{3,2},{4,5},{5,4},{6,7},{7,6},{8,9},{9,8},{10,11... | collective-permute-start | bytes 393224 | tf_op jit(solution)/shard_map/ppermute | solution.py:497
  46.7 6.3 %collective-permute-start.3 = (f32[64,512]{1,0:T(8,128)S(1)}, f32[64,512]{1,0:T(8,128)S(1)}, u32[]{:S(2)}, u32[]{:S(2)}) collective-permute-start(f32[64,512]{1,0:T(8,128)S(1)} %get-tuple-element.35), channel_id=1, source_target_pairs={{0,0},{1,2},{2,1},{3,4},{4,3},{5,6},{6,5},{7,8},{8,7},{9,10},{10,9... | collective-permute-start | bytes 393224 | tf_op jit(solution)/shard_map/ppermute | solution.py:494
  48.7 6.0 %collective-permute-start.4 = (f32[64,512]{1,0:T(8,128)S(1)}, f32[64,512]{1,0:T(8,128)S(1)}, u32[]{:S(2)}, u32[]{:S(2)}) collective-permute-start(f32[64,512]{1,0:T(8,128)S(1)} %pad_maximum_fusion), channel_id=1, source_target_pairs={{0,1},{1,0},{2,3},{3,2},{4,5},{5,4},{6,7},{7,6},{8,9},{9,8},{10,11... | collective-permute-start | bytes 393224 | tf_op jit(solution)/shard_map/ppermute | solution.py:504
  50.6 6.3 %collective-permute-start.5 = (f32[64,512]{1,0:T(8,128)S(1)}, f32[64,512]{1,0:T(8,128)S(1)}, u32[]{:S(2)}, u32[]{:S(2)}) collective-permute-start(f32[64,512]{1,0:T(8,128)S(1)} %pad_maximum_fusion.1), channel_id=1, source_target_pairs={{0,0},{1,2},{2,1},{3,4},{4,3},{5,6},{6,5},{7,8},{8,7},{9,10},{10,9... | collective-permute-start | bytes 393224 | tf_op jit(solution)/shard_map/ppermute | solution.py:503
  58.2 7.0 %collective-permute-start.6 = (f32[64,512]{1,0:T(8,128)S(1)}, f32[64,512]{1,0:T(8,128)S(1)}, u32[]{:S(2)}, u32[]{:S(2)}) collective-permute-start(f32[64,512]{1,0:T(8,128)S(1)} %get-tuple-element.40), channel_id=1, source_target_pairs={{0,32},{32,0},{64,96},{96,64},{1,33},{33,1},{65,97},{97,65},{2,34}... | collective-permute-start | bytes 393224 | tf_op jit(solution)/shard_map/ppermute | solution.py:495
  61.9 3.4 %collective-permute-start.7 = (f32[64,512]{1,0:T(8,128)S(1)}, f32[64,512]{1,0:T(8,128)S(1)}, u32[]{:S(2)}, u32[]{:S(2)}) collective-permute-start(f32[64,512]{1,0:T(8,128)S(1)} %get-tuple-element.41), channel_id=1, source_target_pairs={{0,0},{32,64},{64,32},{96,96},{1,1},{33,65},{65,33},{97,97},{2,2},... | collective-permute-start | bytes 393224 | tf_op jit(solution)/shard_map/ppermute | solution.py:496
  62.5 6.1 %collective-permute-start.8 = (f32[64,512]{1,0:T(8,128)S(1)}, f32[64,512]{1,0:T(8,128)S(1)}, u32[]{:S(2)}, u32[]{:S(2)}) collective-permute-start(f32[64,512]{1,0:T(8,128)S(1)} %get-tuple-element.42), channel_id=1, source_target_pairs={{0,1},{1,0},{2,3},{3,2},{4,5},{5,4},{6,7},{7,6},{8,9},{9,8},{10,11... | collective-permute-start | bytes 393224 | tf_op jit(solution)/shard_map/ppermute | solution.py:497
  62.6 6.3 %collective-permute-start.9 = (f32[64,512]{1,0:T(8,128)S(1)}, f32[64,512]{1,0:T(8,128)S(1)}, u32[]{:S(2)}, u32[]{:S(2)}) collective-permute-start(f32[64,512]{1,0:T(8,128)S(1)} %get-tuple-element.43), channel_id=1, source_target_pairs={{0,0},{1,2},{2,1},{3,4},{4,3},{5,6},{6,5},{7,8},{8,7},{9,10},{10,9... | collective-permute-start | bytes 393224 | tf_op jit(solution)/shard_map/ppermute | solution.py:494
  65.3 5.3 %collective-permute-start.10 = (f32[64,512]{1,0:T(8,128)S(1)}, f32[64,512]{1,0:T(8,128)S(1)}, u32[]{:S(2)}, u32[]{:S(2)}) collective-permute-start(f32[64,512]{1,0:T(8,128)S(1)} %pad_maximum_fusion.2), channel_id=1, source_target_pairs={{0,1},{1,0},{2,3},{3,2},{4,5},{5,4},{6,7},{7,6},{8,9},{9,8},{10,11... | collective-permute-start | bytes 393224 | tf_op jit(solution)/shard_map/ppermute | solution.py:504
  65.4 6.3 %collective-permute-start.11 = (f32[64,512]{1,0:T(8,128)S(1)}, f32[64,512]{1,0:T(8,128)S(1)}, u32[]{:S(2)}, u32[]{:S(2)}) collective-permute-start(f32[64,512]{1,0:T(8,128)S(1)} %pad_maximum_fusion.3), channel_id=1, source_target_pairs={{0,0},{1,2},{2,1},{3,4},{4,3},{5,6},{6,5},{7,8},{8,7},{9,10},{10,9... | collective-permute-start | bytes 393224 | tf_op jit(solution)/shard_map/ppermute | solution.py:503
  73.0 7.8 %collective-permute-start.12 = (f32[64,512]{1,0:T(8,128)S(1)}, f32[64,512]{1,0:T(8,128)S(1)}, u32[]{:S(2)}, u32[]{:S(2)}) collective-permute-start(f32[64,512]{1,0:T(8,128)S(1)} %get-tuple-element.46), channel_id=1, source_target_pairs={{0,32},{32,0},{64,96},{96,64},{1,33},{33,1},{65,97},{97,65},{2,34}... | collective-permute-start | bytes 393224 | tf_op jit(solution)/shard_map/ppermute | solution.py:495
  75.9 4.9 %collective-permute-start.13 = (f32[64,512]{1,0:T(8,128)S(1)}, f32[64,512]{1,0:T(8,128)S(1)}, u32[]{:S(2)}, u32[]{:S(2)}) collective-permute-start(f32[64,512]{1,0:T(8,128)S(1)} %get-tuple-element.47), channel_id=1, source_target_pairs={{0,0},{32,64},{64,32},{96,96},{1,1},{33,65},{65,33},{97,97},{2,2},... | collective-permute-start | bytes 393224 | tf_op jit(solution)/shard_map/ppermute | solution.py:496
  76.6 7.6 %collective-permute-start.14 = (f32[64,512]{1,0:T(8,128)S(1)}, f32[64,512]{1,0:T(8,128)S(1)}, u32[]{:S(2)}, u32[]{:S(2)}) collective-permute-start(f32[64,512]{1,0:T(8,128)S(1)} %get-tuple-element.48), channel_id=1, source_target_pairs={{0,1},{1,0},{2,3},{3,2},{4,5},{5,4},{6,7},{7,6},{8,9},{9,8},{10,11... | collective-permute-start | bytes 393224 | tf_op jit(solution)/shard_map/ppermute | solution.py:497
  76.7 7.5 %collective-permute-start.15 = (f32[64,512]{1,0:T(8,128)S(1)}, f32[64,512]{1,0:T(8,128)S(1)}, u32[]{:S(2)}, u32[]{:S(2)}) collective-permute-start(f32[64,512]{1,0:T(8,128)S(1)} %get-tuple-element.49), channel_id=1, source_target_pairs={{0,0},{1,2},{2,1},{3,4},{4,3},{5,6},{6,5},{7,8},{8,7},{9,10},{10,9... | collective-permute-start | bytes 393224 | tf_op jit(solution)/shard_map/ppermute | solution.py:494
  80.9 5.0 %collective-permute-start.16 = (f32[64,512]{1,0:T(8,128)S(1)}, f32[64,512]{1,0:T(8,128)S(1)}, u32[]{:S(2)}, u32[]{:S(2)}) collective-permute-start(f32[64,512]{1,0:T(8,128)S(1)} %pad_maximum_fusion.4), channel_id=1, source_target_pairs={{0,1},{1,0},{2,3},{3,2},{4,5},{5,4},{6,7},{7,6},{8,9},{9,8},{10,11... | collective-permute-start | bytes 393224 | tf_op jit(solution)/shard_map/ppermute | solution.py:504
  81.0 6.3 %collective-permute-start.17 = (f32[64,512]{1,0:T(8,128)S(1)}, f32[64,512]{1,0:T(8,128)S(1)}, u32[]{:S(2)}, u32[]{:S(2)}) collective-permute-start(f32[64,512]{1,0:T(8,128)S(1)} %pad_maximum_fusion.5), channel_id=1, source_target_pairs={{0,0},{1,2},{2,1},{3,4},{4,3},{5,6},{6,5},{7,8},{8,7},{9,10},{10,9... | collective-permute-start | bytes 393224 | tf_op jit(solution)/shard_map/ppermute | solution.py:503

commit v4 on v3

--- a/solution.py
+++ b/solution.py
@@ -28,67 +28,61 @@
 
 def basis_of(pos):
     u = 4.0 * pos
-    cell = jnp.floor(u)
-    w = u - cell
-    rest = 1.0 - w
-    low = 0.5 * (rest * rest)
-    high = 0.5 * (w * w)
-    off = w - 0.5
-    mid = 0.75 - off * off
-    slow = -4.0 * rest
-    shigh = 4.0 * w
-    smid = -8.0 * off
-    at = [cell == float(i) for i in range(4)]
+    w = u - jnp.floor(u)
+    back = w - 1.0
+    low = back * back
+    high = w * w
+    turn = w * back
+    mid = 1.0 - (turn + turn)
+    smid = -(w + back)
+    in0, in1, in2 = u < 1.0, u < 2.0, u < 3.0
     zero = jnp.zeros_like(u)
-    values, slopes = [], []
-    for i in range(4):
-        val, slo = zero, zero
-        if i + 1 < 4:
-            val = jnp.where(at[i + 1], low, val)
-            slo = jnp.where(at[i + 1], slow, slo)
-        if i - 1 >= 0:
-            val = jnp.where(at[i - 1], high, val)
-            slo = jnp.where(at[i - 1], shigh, slo)
-        values.append(jnp.where(at[i], mid, val))
-        slopes.append(jnp.where(at[i], smid, slo))
-    return values, slopes
-
-
-def splat_kernel(samp_ref, cnt_ref, ids_ref, out_ref, flip, basis, acc, stats):
-    step = pl.program_id(0)
-    last = pl.num_programs(0) - 1
-
-    @pl.when(step == 0)
-    def _():
-        stats[...] = jnp.zeros_like(stats)
-
-    for k in range(6):
-        flip[k] = samp_ref[k].T
-    counts = cnt_ref[pl.ds(step, 1), :]
-
-    def evaluate(group, carry):
-        rows = pl.ds(pl.multiple_of(group * 8, 8), 8)
-        valid = (row_iota((8, 128)) + group * 8 < counts).astype(F32)
-        n0 = flip[3, rows, :] * valid
-        n1 = flip[4, rows, :] * valid
-        n2 = flip[5, rows, :] * valid
-        val, slo = basis_of(flip[0, rows, :])
-        for i in range(4):
-            basis[i, rows, :] = slo[i] * n0
-            basis[4 + i, rows, :] = val[i] * n1
-            basis[8 + i, rows, :] = val[i] * n2
-            basis[12 + i, rows, :] = val[i] * valid
-        for d in (1, 2):
-            val, slo = basis_of(flip[d, rows, :])
+
+    def nodes(below, at, above):
+        return [
+            jnp.where(in0, at, jnp.where(in1, below, zero)),
+            jnp.where(in0, above, jnp.where(in1, at, jnp.where(in2, below, zero))),
+            jnp.where(in0, zero, jnp.where(in1, above, jnp.where(in2, at, below))),
+            jnp.where(in1, zero, jnp.where(in2, above, at)),
+        ]
+
+    return nodes(low, mid, high), nodes(back, smid, w)
+
+
+def splat_kernel(samp_ref, cnt_ref, ids_ref, out_ref, held, sems, flip, basis, acc, stats):
+    groups = out_ref.shape[0]
+
+    def fetch(g):
+        return pltpu.make_async_copy(samp_ref.at[:, pl.ds(g * 128, 128), :], held.at[g], sems.at[g])
+
+    def turn(g):
+        for k in range(6):
+            flip[k] = held[g, k].T
+
+    def evaluate(g):
+        counts = cnt_ref[pl.ds(g, 1), :]
+        for group in range(16):
+            rows = pl.ds(group * 8, 8)
+            live = row_iota((8, 128)) + group * 8 < counts
+            n0 = jnp.where(live, flip[3, rows, :], 0.0)
+            n1 = jnp.where(live, flip[4, rows, :], 0.0)
+            n2 = jnp.where(live, flip[5, rows, :], 0.0)
+            eighth = jnp.where(live, 0.125, 0.0)
+            val, slo = basis_of(flip[0, rows, :])
             for i in range(4):
-                basis[8 + 8 * d + i, rows, :] = val[i]
-                basis[12 + 8 * d + i, rows, :] = slo[i]
-        return carry
-
-    lax.fori_loop(0, 16, evaluate, 0, unroll=2)
-
-    for i in range(4):
-        def add_group(group, sums, i=i):
+                basis[i, rows, :] = slo[i] * n0
+                basis[4 + i, rows, :] = val[i] * n1
+                basis[8 + i, rows, :] = val[i] * n2
+                basis[12 + i, rows, :] = val[i] * eighth
+            for d in (1, 2):
+                val, slo = basis_of(flip[d, rows, :])
+                for i in range(4):
+                    basis[8 + 8 * d + i, rows, :] = val[i]
+                    basis[12 + 8 * d + i, rows, :] = slo[i]
+
+    def accumulate(i, js):
+        rhs_sums, dens_sums = {}, {}
+        for group in range(16):
             rows = pl.ds(group * 8, 8)
             a = basis[i, rows, :]
             b = basis[4 + i, rows, :]
@@ -96,8 +90,7 @@
             d = basis[12 + i, rows, :]
             v2 = [basis[24 + l, rows, :] for l in range(4)]
             s2 = [basis[28 + l, rows, :] for l in range(4)]
-            out = list(sums)
-            for j in range(4):
+            for j in js:
                 v1 = basis[16 + j, rows, :]
                 s1 = basis[20 + j, rows, :]
                 first = a * v1 + b * s1
@@ -105,46 +98,65 @@
                 dens = d * v1
                 for l in range(4):
                     at = j * 4 + l
-                    out[at] = out[at] + (first * v2[l] + second * s2[l])
-                    out[16 + at] = out[16 + at] + dens * v2[l]
-            return tuple(out)
-
-        zero = jnp.zeros((8, 128), F32)
-        sums = (zero,) * 32
-        for group in range(16):
-            sums = add_group(group, sums)
-        for at in range(16):
-            acc[pl.ds((i * 16 + at) * 8, 8), :] = sums[at]
-            acc[pl.ds((64 + i * 16 + at) * 8, 8), :] = sums[16 + at]
-
-    total = acc[pl.ds(0, 128, stride=8), :]
-    for s in range(1, 8):
-        total = total + acc[pl.ds(s, 128, stride=8), :]
-    square = total[:64] * total[:64]
-    weighted = total[64:] * square
-    part, wpart = square[:8], weighted[:8]
-    for k in range(1, 8):
-        part = part + square[8 * k : 8 * k + 8]
-        wpart = wpart + weighted[8 * k : 8 * k + 8]
-    stats[0] = stats[0] + part
-    stats[1] = stats[1] + wpart
-    by_tile = total.T
-    for d in range(16):
-        out_ref[step, pl.ds(ROWS * d, 8), :] = by_tile[8 * d : 8 * d + 8]
-
-    @pl.when(step == last)
-    def _():
-        ids = ids_ref[...]
-        local = ((ids >> 14) & 1) * 512 + ((ids >> 8) & 1) * 256 + (ids & 255)
-        local = local.astype(F32)
-        sum0 = jnp.sum(stats[0], keepdims=True)
-        sum1 = jnp.sum(stats[1], keepdims=True)
-        lanes = lane_iota((1, 128))
-        both = jnp.where(lanes % 2 == 0, sum0, sum1)
-        for g in range(8):
-            for d in range(16):
-                row = jnp.where(lanes // 8 == d, local[g : g + 1], both)
-                out_ref[g, pl.ds(ROWS * d + CAP, 1), :] = row
+                    rhs = first * v2[l] + second * s2[l]
+                    den = dens * v2[l]
+                    rhs_sums[at] = rhs if group == 0 else rhs_sums[at] + rhs
+                    dens_sums[at] = den if group == 0 else dens_sums[at] + den
+        for at in rhs_sums:
+            acc[pl.ds((i * 16 + at) * 8, 8), :] = rhs_sums[at]
+            acc[pl.ds((64 + i * 16 + at) * 8, 8), :] = dens_sums[at]
+
+    def settle(g, real):
+        total = acc[pl.ds(0, 128, stride=8), :]
+        for s in range(1, 8):
+            total = total + acc[pl.ds(s, 128, stride=8), :]
+        square = total[:64] * total[:64]
+        weighted = total[64:] * square
+        part, wpart = square[:8], weighted[:8]
+        for k in range(1, 8):
+            part = part + square[8 * k : 8 * k + 8]
+            wpart = wpart + weighted[8 * k : 8 * k + 8]
+        stats[0] = stats[0] + jnp.where(real, part, 0.0)
+        stats[1] = stats[1] + jnp.where(real, wpart, 0.0)
+        by_tile = total.T
+        for d in range(16):
+            out_ref[g, pl.ds(ROWS * d, 8), :] = by_tile[8 * d : 8 * d + 8]
+
+    for g in range(groups):
+        fetch(g).start()
+    stats[...] = jnp.zeros_like(stats)
+    acc[...] = jnp.zeros_like(acc)
+    fetch(0).wait()
+    turn(0)
+
+    def advance(g, carry):
+        following = jnp.minimum(g + 1, groups - 1)
+
+        @pl.when(g + 1 < groups)
+        def _():
+            fetch(following).wait()
+
+        settle(jnp.maximum(g - 1, 0), g > 0)
+        evaluate(g)
+        turn(following)
+        for i in range(4):
+            for js in ((0, 1), (2, 3)):
+                accumulate(i, js)
+        return carry
+
+    lax.fori_loop(0, groups, advance, 0)
+    settle(groups - 1, True)
+    ids = ids_ref[...]
+    local = ((ids >> 14) & 1) * 512 + ((ids >> 8) & 1) * 256 + (ids & 255)
+    local = local.astype(F32)
+    sum0 = jnp.sum(stats[0], keepdims=True)
+    sum1 = jnp.sum(stats[1], keepdims=True)
+    lanes = lane_iota((1, 128))
+    both = jnp.where(lanes % 2 == 0, sum0, sum1)
+    for g in range(groups):
+        for d in range(16):
+            row = jnp.where(lanes // 8 == d, local[g : g + 1], both)
+            out_ref[g, pl.ds(ROWS * d + CAP, 1), :] = row
 
 
 def splat(samples, counts, ids):
@@ -153,21 +165,19 @@
     return pl.pallas_call(
         splat_kernel,
         name="splat",
-        grid=(groups,),
-        in_specs=[
-            pl.BlockSpec((6, 128, 128), lambda g: (0, g, 0)),
-            pl.BlockSpec((groups, 128), lambda g: (0, 0)),
-            pl.BlockSpec((groups, 128), lambda g: (0, 0)),
-        ],
-        out_specs=pl.BlockSpec((groups, 16 * ROWS, 128), lambda g: (0, 0, 0)),
-        out_shape=jax.ShapeDtypeStruct((groups, 16 * ROWS, 128), F32),
+        in_specs=[pl.BlockSpec(memory_space=pltpu.HBM)] + [pl.BlockSpec(memory_space=pltpu.VMEM)] * 2,
+        out_specs=pl.BlockSpec(memory_space=pltpu.VMEM),
+        out_shape=pltpu.VMEM((groups, 16 * ROWS, 128), F32),
         scratch_shapes=[
+            pltpu.VMEM((groups, 6, 128, 128), F32),
+            pltpu.SemaphoreType.DMA((groups,)),
             pltpu.VMEM((6, 128, 128), F32),
             pltpu.VMEM((32, 128, 128), F32),
             pltpu.VMEM((1024, 128), F32),
             pltpu.VMEM((2, 8, 128), F32),
         ],
-    )(jnp.transpose(samples, (1, 0, 2)), counts.reshape(groups, 128), ids.reshape(groups, 128))
+        compiler_params=pltpu.CompilerParams(vmem_limit_bytes=24 << 20),
+    )(pltpu.with_memory_space_constraint(jnp.transpose(samples, (1, 0, 2)), pltpu.HBM), counts.reshape(groups, 128), ids.reshape(groups, 128))
 
 
 def vmem(x):

time: 112 us -> 112 us (level)
  Pallas kernels: 28.7 us -> 26.8 us
  local copies, waits for them, and re-layouts: 0.01 us -> 1.45 us
    pallas_call x1, Pallas kernels: 16.5 us -> 14.6 us  [splat(): pl.pallas_call(splat_kernel, name='splat', in_specs=[pl.BlockSpec(memory_...]
    unnamed x4 -> x8, local copies, waits for them, and re-layouts: 0.01 us -> 1.45 us
where the time goes in v4:
time: 112 us
  starting transfers between devices  41 us (37%)
  Pallas kernels  26.8 us (24%)
  blocking collectives  22.1 us (20%)
  waiting for transfers between devices  18.9 us (17%)
  local copies, waits for them, and re-layouts  1.45 us (1%)
    all_to_all x1, blocking collectives, on_device(): lax.all_to_all(moments.reshape(SENDERS, 1, 128), AXES, split_axis=0, conc...  22.1 us
    pallas_call x1, Pallas kernels, splat(): pl.pallas_call(splat_kernel, name='splat', in_specs=[pl.BlockSpec(memory_...  14.6 us
    all_to_all x1, waiting for transfers between devices, on_device(): lax.all_to_all(payload.reshape(SENDERS, 1, ROWS * 128), AXES, split_axis=...  13.8 us
    all_to_all x1, starting transfers between devices, on_device(): lax.all_to_all(payload.reshape(SENDERS, 1, ROWS * 128), AXES, split_axis=...  11.5 us
    ppermute x3, starting transfers between devices, exchange(): yb = lax.ppermute(ob, 'grp', swap('grp', 1))  8.6 us
    ppermute x3, starting transfers between devices, exchange(): cb = lax.ppermute(line(jnp.logical_not(up)), 'grp', swap('grp', 1))  8.48 us
    ppermute x3, starting transfers between devices, exchange(): ra = lax.ppermute(ea, 'slab', swap('slab', 0))  6.72 us
    pallas_call x3, Pallas kernels, sides(): pl.pallas_call(sides_kernel, name='sides', in_specs=in_specs(len(operands...  5.12 us
  transfers between devices with their start and end apart: 19, of which 6 were waited for; matrix products, arithmetic and copies ran while one was open for 0% of the time, Pallas kernels for 5%

profile of v4, /device:TPU:1, one launch (start us, length us, event | category | flops | bytes accessed | tf_op | source)
XLA Modules:
  0.0 111.6 jit_solution(1299886949758017557)
XLA Ops:
  2.1 14.6 %splat.1 = f32[8,144,128]{2,1,0:T(8,128)} custom-call(f32[6,1024,128]{2,1,0:T(8,128)} %bitcast.26, s32[8,128]{1,0:T(8,128)S(1)} %bitcast.24, s32[8,128]{1,0:T(8,128)S(1)} %bitcast.25), custom_call_target="tpu_custom_call" | custom-call | tf_op jit(solution)/shard_map/splat/pallas_call | solution.py:165
  16.7 11.5 %all-to-all-start = ((f32[128,1,1152]{2,1,0:T(1,128)}), f32[128,1,1152]{2,1,0:T(1,128)S(1)}, u32[]{:S(2)}, u32[]{:S(2)}) async-start(f32[128,1,1152]{2,1,0:T(1,128)} %bitcast.5), calls=%async_computation | async-start | bytes 1179648 | tf_op jit(solution)/shard_map/all_to_all | solution.py:522
  28.8 13.8 %all-to-all-done = f32[128,1,1152]{2,1,0:T(1,128)S(1)} async-done(((f32[128,1,1152]{2,1,0:T(1,128)}), f32[128,1,1152]{2,1,0:T(1,128)S(1)}, u32[]{:S(2)}, u32[]{:S(2)}) %all-to-all-start) | async-done | bytes 589856 | tf_op jit(solution)/shard_map/all_to_all | solution.py:522
  42.5 1.5 %assemble.1 = (f32[64,1024]{1,0:T(8,128)S(1)}, f32[64,1024]{1,0:T(8,128)S(1)}, f32[8,1024]{1,0:T(8,128)S(1)}, f32[8,128]{1,0:T(8,128)S(1)}, f32[64,512]{1,0:T(8,...) custom-call(s32[4]{0:T(128)S(1)} %pad_add_fusion.place_ref, ...), custom_call_target="tpu_custom_call" | custom-call | tf_op jit(solution)/shard_map/assemble/pallas_call | solution.py:310
  44.8 1.5 %collective-permute-start.2 = (f32[64,512]{1,0:T(8,128)S(1)}, f32[64,512]{1,0:T(8,128)S(1)}, u32[]{:S(2)}, u32[]{:S(2)}) collective-permute-start(f32[64,512]{1,0:T(8,128)S(1)} %get-tuple-element.34), channel_id=1, source_target_pairs={{0,1},{1,0},{2,3},{3,2},{4,5},{5,4},{6,7},{7,6},{8,9},{9,8},{10,11... | collective-permute-start | bytes 393224 | tf_op jit(solution)/shard_map/ppermute | solution.py:507
  46.3 1.9 %collective-permute-start.3 = (f32[64,512]{1,0:T(8,128)S(1)}, f32[64,512]{1,0:T(8,128)S(1)}, u32[]{:S(2)}, u32[]{:S(2)}) collective-permute-start(f32[64,512]{1,0:T(8,128)S(1)} %get-tuple-element.35), channel_id=1, source_target_pairs={{0,0},{1,2},{2,1},{3,4},{4,3},{5,6},{6,5},{7,8},{8,7},{9,10},{10,9... | collective-permute-start | bytes 393224 | tf_op jit(solution)/shard_map/ppermute | solution.py:504
  48.3 1.9 %collective-permute-start.4 = (f32[64,512]{1,0:T(8,128)S(1)}, f32[64,512]{1,0:T(8,128)S(1)}, u32[]{:S(2)}, u32[]{:S(2)}) collective-permute-start(f32[64,512]{1,0:T(8,128)S(1)} %pad_maximum_fusion), channel_id=1, source_target_pairs={{0,1},{1,0},{2,3},{3,2},{4,5},{5,4},{6,7},{7,6},{8,9},{9,8},{10,11... | collective-permute-start | bytes 393224 | tf_op jit(solution)/shard_map/ppermute | solution.py:514
  50.1 2.1 %collective-permute-start.5 = (f32[64,512]{1,0:T(8,128)S(1)}, f32[64,512]{1,0:T(8,128)S(1)}, u32[]{:S(2)}, u32[]{:S(2)}) collective-permute-start(f32[64,512]{1,0:T(8,128)S(1)} %pad_maximum_fusion.1), channel_id=1, source_target_pairs={{0,0},{1,2},{2,1},{3,4},{4,3},{5,6},{6,5},{7,8},{8,7},{9,10},{10,9... | collective-permute-start | bytes 393224 | tf_op jit(solution)/shard_map/ppermute | solution.py:513
  52.5 1.7 %sides.3.sum_ref = f32[64,1024]{1,0:T(8,128)S(1)} custom-call(s32[4]{0:T(128)S(1)} %pad_add_fusion.place_ref, f32[64,1024]{1,0:T(8,128)S(1)} %get-tuple-element.31.v_ref.v0_ref, f32[8,1024]{1,0:T(8,128)S(1)} %get-tuple-element.29.mask_ref, f32[64,512]{1,0:T(8,128)S(1)} %collective-permute-done.ra_ref, f32[64,512]{1,0:T(8,128)S(1)} %collective-permute-done.1.rb_ref, ...), custom_call_target="tpu_custom_call" | custom-call | flops 1500000000 | bytes 2000000 | tf_op jit(solution)/shard_map/sides/pallas_call | solution.py:368
  54.3 2.2 %collective-permute-done.5.cb_ref = f32[64,512]{1,0:T(8,128)S(1)} collective-permute-done((f32[64,512]{1,0:T(8,128)S(1)}, f32[64,512]{1,0:T(8,128)S(1)}, u32[]{:S(2)}, u32[]{:S(2)}) %collective-permute-start.5) | collective-permute-done | bytes 131104 | tf_op jit(solution)/shard_map/ppermute | solution.py:513
  56.4 1.3 %corners.3 = (f32[64,1024]{1,0:T(8,128)S(1)}, f32[8,128]{1,0:T(8,128)S(1)}, f32[64,512]{1,0:T(8,128)S(1)}, f32[64,512]{1,0:T(8,128)S(1)}, f32[64,512]{1,0:T(8,128)S(1)}, /*index=5*/f32[64,512]{1,0:T(8,128)S(1)}) custom-call(s32[4]{0:T(128)S(1)} %pad_add_fusion.place_ref, f32[64,1024]{1,0:T(8,128)S(1)} %sides.3.sum_ref, ...), custom_call_target="tpu_custom_call" | custom-call | tf_op jit(solution)/shard_map/corners/pallas_call | solution.py:422
  57.7 3.7 %collective-permute-start.6 = (f32[64,512]{1,0:T(8,128)S(1)}, f32[64,512]{1,0:T(8,128)S(1)}, u32[]{:S(2)}, u32[]{:S(2)}) collective-permute-start(f32[64,512]{1,0:T(8,128)S(1)} %get-tuple-element.40), channel_id=1, source_target_pairs={{0,32},{32,0},{64,96},{96,64},{1,33},{33,1},{65,97},{97,65},{2,34}... | collective-permute-start | bytes 393224 | tf_op jit(solution)/shard_map/ppermute | solution.py:505
  62.1 2.6 %collective-permute-start.9 = (f32[64,512]{1,0:T(8,128)S(1)}, f32[64,512]{1,0:T(8,128)S(1)}, u32[]{:S(2)}, u32[]{:S(2)}) collective-permute-start(f32[64,512]{1,0:T(8,128)S(1)} %get-tuple-element.43), channel_id=1, source_target_pairs={{0,0},{1,2},{2,1},{3,4},{4,3},{5,6},{6,5},{7,8},{8,7},{9,10},{10,9... | collective-permute-start | bytes 393224 | tf_op jit(solution)/shard_map/ppermute | solution.py:504
  64.9 3.2 %collective-permute-start.11 = (f32[64,512]{1,0:T(8,128)S(1)}, f32[64,512]{1,0:T(8,128)S(1)}, u32[]{:S(2)}, u32[]{:S(2)}) collective-permute-start(f32[64,512]{1,0:T(8,128)S(1)} %pad_maximum_fusion.3), channel_id=1, source_target_pairs={{0,0},{1,2},{2,1},{3,4},{4,3},{5,6},{6,5},{7,8},{8,7},{9,10},{10,9... | collective-permute-start | bytes 393224 | tf_op jit(solution)/shard_map/ppermute | solution.py:513
  68.4 1.7 %sides.4.sum_ref = f32[64,1024]{1,0:T(8,128)S(1)} custom-call(s32[4]{0:T(128)S(1)} %pad_add_fusion.place_ref, f32[64,1024]{1,0:T(8,128)S(1)} %get-tuple-element.39.v_ref.v1_ref, f32[8,1024]{1,0:T(8,128)S(1)} %get-tuple-element.29.mask_ref, f32[64,512]{1,0:T(8,128)S(1)} %collective-permute-done.6.ra_ref, f32[64,512]{1,0:T(8,128)S(1)} %collective-permute-done.7.rb_ref, ...), custom_call_target="tpu_custom_call" | custom-call | flops 1500000000 | bytes 2000000 | tf_op jit(solution)/shard_map/sides/pallas_call | solution.py:368
  71.2 1.3 %corners.4 = (f32[64,1024]{1,0:T(8,128)S(1)}, f32[8,128]{1,0:T(8,128)S(1)}, f32[64,512]{1,0:T(8,128)S(1)}, f32[64,512]{1,0:T(8,128)S(1)}, f32[64,512]{1,0:T(8,128)S(1)}, /*index=5*/f32[64,512]{1,0:T(8,128)S(1)}) custom-call(s32[4]{0:T(128)S(1)} %pad_add_fusion.place_ref, f32[64,1024]{1,0:T(8,128)S(1)} %sides.4.sum_ref, ...), custom_call_target="tpu_custom_call" | custom-call | tf_op jit(solution)/shard_map/corners/pallas_call | solution.py:422
  72.5 3.0 %collective-permute-start.12 = (f32[64,512]{1,0:T(8,128)S(1)}, f32[64,512]{1,0:T(8,128)S(1)}, u32[]{:S(2)}, u32[]{:S(2)}) collective-permute-start(f32[64,512]{1,0:T(8,128)S(1)} %get-tuple-element.46), channel_id=1, source_target_pairs={{0,32},{32,0},{64,96},{96,64},{1,33},{33,1},{65,97},{97,65},{2,34}... | collective-permute-start | bytes 393224 | tf_op jit(solution)/shard_map/ppermute | solution.py:505
  76.2 4.1 %collective-permute-start.15 = (f32[64,512]{1,0:T(8,128)S(1)}, f32[64,512]{1,0:T(8,128)S(1)}, u32[]{:S(2)}, u32[]{:S(2)}) collective-permute-start(f32[64,512]{1,0:T(8,128)S(1)} %get-tuple-element.49), channel_id=1, source_target_pairs={{0,0},{1,2},{2,1},{3,4},{4,3},{5,6},{6,5},{7,8},{8,7},{9,10},{10,9... | collective-permute-start | bytes 393224 | tf_op jit(solution)/shard_map/ppermute | solution.py:504
  80.5 3.2 %collective-permute-start.17 = (f32[64,512]{1,0:T(8,128)S(1)}, f32[64,512]{1,0:T(8,128)S(1)}, u32[]{:S(2)}, u32[]{:S(2)}) collective-permute-start(f32[64,512]{1,0:T(8,128)S(1)} %pad_maximum_fusion.5), channel_id=1, source_target_pairs={{0,0},{1,2},{2,1},{3,4},{4,3},{5,6},{6,5},{7,8},{8,7},{9,10},{10,9... | collective-permute-start | bytes 393224 | tf_op jit(solution)/shard_map/ppermute | solution.py:513
  83.7 1.7 %sides.5.sum_ref = f32[64,1024]{1,0:T(8,128)S(1)} custom-call(s32[4]{0:T(128)S(1)} %pad_add_fusion.place_ref, f32[64,1024]{1,0:T(8,128)S(1)} %get-tuple-element.45.v_ref.v2_ref, f32[8,1024]{1,0:T(8,128)S(1)} %get-tuple-element.29.mask_ref, f32[64,512]{1,0:T(8,128)S(1)} %collective-permute-done.12.ra_ref, f32[64,512]{1,0:T(8,128)S(1)} %collective-permute-done.13.rb_ref, ...), custom_call_target="tpu_custom_call" | custom-call | flops 1500000000 | bytes 2000000 | tf_op jit(solution)/shard_map/sides/pallas_call | solution.py:368
  85.5 1.3 %collective-permute-done.17.cb_ref = f32[64,512]{1,0:T(8,128)S(1)} collective-permute-done((f32[64,512]{1,0:T(8,128)S(1)}, f32[64,512]{1,0:T(8,128)S(1)}, u32[]{:S(2)}, u32[]{:S(2)}) %collective-permute-start.17) | collective-permute-done | bytes 131104 | tf_op jit(solution)/shard_map/ppermute | solution.py:513
  86.8 1.3 %corners.5 = (f32[64,1024]{1,0:T(8,128)S(1)}, f32[128,128]{1,0:T(8,128)S(1)}) custom-call(s32[4]{0:T(128)S(1)} %pad_add_fusion.place_ref, f32[64,1024]{1,0:T(8,128)S(1)} %sides.5.sum_ref, f32[64,1024]{1,0:T(8,128)S(1)} %get-tuple-element.45.v_ref.v2_ref, f32[64,1024]{1,0:T(8,128)S(1)} %get-tuple-element.37.diag_ref, ...), custom_call_target="tpu_custom_call" | custom-call | tf_op jit(solution)/shard_map/corners/pallas_call | solution.py:422
  88.1 22.1 %all_to_all.10 = f32[128,1,128]{2,1,0:T(1,128)S(1)} all-to-all(f32[128,1,128]{2,1,0:T(1,128)S(1)} %bitcast.23), channel_id=1, replica_groups=mesh['slab'=4,'grp'=32] {'slab','grp'}, dimensions={0} | all-to-all | bytes 131072 | tf_op jit(solution)/shard_map/all_to_all | solution.py:532
  110.2 1.4 %finish.1 = (f32[64,8,128]{2,1,0:T(8,128)}, f32[64,8,128]{2,1,0:T(8,128)}) custom-call(f32[128,128]{1,0:T(8,128)S(1)} %bitcast.22, f32[8,128]{1,0:T(8,128)S(1)} %get-tuple-element.52.c_ref, f32[64,1024]{1,0:T(8,128)S(1)} %get-tuple-element.31.v_ref.v0_ref, f32[64,1024]{1,0:T(8,128)S(1)} %get-tuple-element.39.v_ref.v1_ref, ...), custom_call_target="tpu_custom_call" | custom-call | tf_op jit(solution)/shard_map/finish/pallas_call | solution.py:484
  (46 shorter events, 6.2 us)
Async XLA Ops:
  0.6 27.6 %copy-start = (f32[27,64,64]{2,1,0:T(8,128)S(1)}, f32[27,64,64]{2,1,0:T(8,128)}, u32[]{:S(2)}) copy-start(f32[27,64,64]{2,1,0:T(8,128)} %coupling_ref.1) | copy-start | bytes 1327108
  0.6 0.8 copy-start.1
  1.4 0.7 copy-start.2
  2.1 26.1 %copy-start.3 = (s32[2,2,256]{2,1,0:T(2,128)S(1)}, s32[2,2,256]{2,1,0:T(2,128)}, u32[]{:S(2)}) copy-start(s32[2,2,256]{2,1,0:T(2,128)} %occ_ref.1) | copy-start | bytes 12292
  16.7 25.8 %all-to-all-start = ((f32[128,1,1152]{2,1,0:T(1,128)}), f32[128,1,1152]{2,1,0:T(1,128)S(1)}, u32[]{:S(2)}, u32[]{:S(2)}) async-start(f32[128,1,1152]{2,1,0:T(1,128)} %bitcast.5), calls=%async_computation | async-start | bytes 1179648 | tf_op jit(solution)/shard_map/all_to_all | solution.py:522
  44.0 4.2 %collective-permute-start = (f32[64,512]{1,0:T(8,128)S(1)}, f32[64,512]{1,0:T(8,128)S(1)}, u32[]{:S(2)}, u32[]{:S(2)}) collective-permute-start(f32[64,512]{1,0:T(8,128)S(1)} %get-tuple-element.32), channel_id=1, source_target_pairs={{0,32},{32,0},{64,96},{96,64},{1,33},{33,1},{65,97},{97,65},{2,34}... | collective-permute-start | bytes 393224 | tf_op jit(solution)/shard_map/ppermute | solution.py:505
  44.1 4.1 %collective-permute-start.1 = (f32[64,512]{1,0:T(8,128)S(1)}, f32[64,512]{1,0:T(8,128)S(1)}, u32[]{:S(2)}, u32[]{:S(2)}) collective-permute-start(f32[64,512]{1,0:T(8,128)S(1)} %get-tuple-element.33), channel_id=1, source_target_pairs={{0,0},{32,64},{64,32},{96,96},{1,1},{33,65},{65,33},{97,97},{2,2},... | collective-permute-start | bytes 393224 | tf_op jit(solution)/shard_map/ppermute | solution.py:506
  44.8 7.5 %collective-permute-start.2 = (f32[64,512]{1,0:T(8,128)S(1)}, f32[64,512]{1,0:T(8,128)S(1)}, u32[]{:S(2)}, u32[]{:S(2)}) collective-permute-start(f32[64,512]{1,0:T(8,128)S(1)} %get-tuple-element.34), channel_id=1, source_target_pairs={{0,1},{1,0},{2,3},{3,2},{4,5},{5,4},{6,7},{7,6},{8,9},{9,8},{10,11... | collective-permute-start | bytes 393224 | tf_op jit(solution)/shard_map/ppermute | solution.py:507
  46.3 6.3 %collective-permute-start.3 = (f32[64,512]{1,0:T(8,128)S(1)}, f32[64,512]{1,0:T(8,128)S(1)}, u32[]{:S(2)}, u32[]{:S(2)}) collective-permute-start(f32[64,512]{1,0:T(8,128)S(1)} %get-tuple-element.35), channel_id=1, source_target_pairs={{0,0},{1,2},{2,1},{3,4},{4,3},{5,6},{6,5},{7,8},{8,7},{9,10},{10,9... | collective-permute-start | bytes 393224 | tf_op jit(solution)/shard_map/ppermute | solution.py:504
  48.3 6.0 %collective-permute-start.4 = (f32[64,512]{1,0:T(8,128)S(1)}, f32[64,512]{1,0:T(8,128)S(1)}, u32[]{:S(2)}, u32[]{:S(2)}) collective-permute-start(f32[64,512]{1,0:T(8,128)S(1)} %pad_maximum_fusion), channel_id=1, source_target_pairs={{0,1},{1,0},{2,3},{3,2},{4,5},{5,4},{6,7},{7,6},{8,9},{9,8},{10,11... | collective-permute-start | bytes 393224 | tf_op jit(solution)/shard_map/ppermute | solution.py:514
  50.1 6.3 %collective-permute-start.5 = (f32[64,512]{1,0:T(8,128)S(1)}, f32[64,512]{1,0:T(8,128)S(1)}, u32[]{:S(2)}, u32[]{:S(2)}) collective-permute-start(f32[64,512]{1,0:T(8,128)S(1)} %pad_maximum_fusion.1), channel_id=1, source_target_pairs={{0,0},{1,2},{2,1},{3,4},{4,3},{5,6},{6,5},{7,8},{8,7},{9,10},{10,9... | collective-permute-start | bytes 393224 | tf_op jit(solution)/shard_map/ppermute | solution.py:513
  57.7 7.0 %collective-permute-start.6 = (f32[64,512]{1,0:T(8,128)S(1)}, f32[64,512]{1,0:T(8,128)S(1)}, u32[]{:S(2)}, u32[]{:S(2)}) collective-permute-start(f32[64,512]{1,0:T(8,128)S(1)} %get-tuple-element.40), channel_id=1, source_target_pairs={{0,32},{32,0},{64,96},{96,64},{1,33},{33,1},{65,97},{97,65},{2,34}... | collective-permute-start | bytes 393224 | tf_op jit(solution)/shard_map/ppermute | solution.py:505
  61.4 3.4 %collective-permute-start.7 = (f32[64,512]{1,0:T(8,128)S(1)}, f32[64,512]{1,0:T(8,128)S(1)}, u32[]{:S(2)}, u32[]{:S(2)}) collective-permute-start(f32[64,512]{1,0:T(8,128)S(1)} %get-tuple-element.41), channel_id=1, source_target_pairs={{0,0},{32,64},{64,32},{96,96},{1,1},{33,65},{65,33},{97,97},{2,2},... | collective-permute-start | bytes 393224 | tf_op jit(solution)/shard_map/ppermute | solution.py:506
  62.0 6.1 %collective-permute-start.8 = (f32[64,512]{1,0:T(8,128)S(1)}, f32[64,512]{1,0:T(8,128)S(1)}, u32[]{:S(2)}, u32[]{:S(2)}) collective-permute-start(f32[64,512]{1,0:T(8,128)S(1)} %get-tuple-element.42), channel_id=1, source_target_pairs={{0,1},{1,0},{2,3},{3,2},{4,5},{5,4},{6,7},{7,6},{8,9},{9,8},{10,11... | collective-permute-start | bytes 393224 | tf_op jit(solution)/shard_map/ppermute | solution.py:507
  62.1 6.3 %collective-permute-start.9 = (f32[64,512]{1,0:T(8,128)S(1)}, f32[64,512]{1,0:T(8,128)S(1)}, u32[]{:S(2)}, u32[]{:S(2)}) collective-permute-start(f32[64,512]{1,0:T(8,128)S(1)} %get-tuple-element.43), channel_id=1, source_target_pairs={{0,0},{1,2},{2,1},{3,4},{4,3},{5,6},{6,5},{7,8},{8,7},{9,10},{10,9... | collective-permute-start | bytes 393224 | tf_op jit(solution)/shard_map/ppermute | solution.py:504
  64.8 5.3 %collective-permute-start.10 = (f32[64,512]{1,0:T(8,128)S(1)}, f32[64,512]{1,0:T(8,128)S(1)}, u32[]{:S(2)}, u32[]{:S(2)}) collective-permute-start(f32[64,512]{1,0:T(8,128)S(1)} %pad_maximum_fusion.2), channel_id=1, source_target_pairs={{0,1},{1,0},{2,3},{3,2},{4,5},{5,4},{6,7},{7,6},{8,9},{9,8},{10,11... | collective-permute-start | bytes 393224 | tf_op jit(solution)/shard_map/ppermute | solution.py:514
  64.9 6.3 %collective-permute-start.11 = (f32[64,512]{1,0:T(8,128)S(1)}, f32[64,512]{1,0:T(8,128)S(1)}, u32[]{:S(2)}, u32[]{:S(2)}) collective-permute-start(f32[64,512]{1,0:T(8,128)S(1)} %pad_maximum_fusion.3), channel_id=1, source_target_pairs={{0,0},{1,2},{2,1},{3,4},{4,3},{5,6},{6,5},{7,8},{8,7},{9,10},{10,9... | collective-permute-start | bytes 393224 | tf_op jit(solution)/shard_map/ppermute | solution.py:513
  72.5 7.8 %collective-permute-start.12 = (f32[64,512]{1,0:T(8,128)S(1)}, f32[64,512]{1,0:T(8,128)S(1)}, u32[]{:S(2)}, u32[]{:S(2)}) collective-permute-start(f32[64,512]{1,0:T(8,128)S(1)} %get-tuple-element.46), channel_id=1, source_target_pairs={{0,32},{32,0},{64,96},{96,64},{1,33},{33,1},{65,97},{97,65},{2,34}... | collective-permute-start | bytes 393224 | tf_op jit(solution)/shard_map/ppermute | solution.py:505
  75.4 4.9 %collective-permute-start.13 = (f32[64,512]{1,0:T(8,128)S(1)}, f32[64,512]{1,0:T(8,128)S(1)}, u32[]{:S(2)}, u32[]{:S(2)}) collective-permute-start(f32[64,512]{1,0:T(8,128)S(1)} %get-tuple-element.47), channel_id=1, source_target_pairs={{0,0},{32,64},{64,32},{96,96},{1,1},{33,65},{65,33},{97,97},{2,2},... | collective-permute-start | bytes 393224 | tf_op jit(solution)/shard_map/ppermute | solution.py:506
  76.1 7.6 %collective-permute-start.14 = (f32[64,512]{1,0:T(8,128)S(1)}, f32[64,512]{1,0:T(8,128)S(1)}, u32[]{:S(2)}, u32[]{:S(2)}) collective-permute-start(f32[64,512]{1,0:T(8,128)S(1)} %get-tuple-element.48), channel_id=1, source_target_pairs={{0,1},{1,0},{2,3},{3,2},{4,5},{5,4},{6,7},{7,6},{8,9},{9,8},{10,11... | collective-permute-start | bytes 393224 | tf_op jit(solution)/shard_map/ppermute | solution.py:507
  76.2 7.5 %collective-permute-start.15 = (f32[64,512]{1,0:T(8,128)S(1)}, f32[64,512]{1,0:T(8,128)S(1)}, u32[]{:S(2)}, u32[]{:S(2)}) collective-permute-start(f32[64,512]{1,0:T(8,128)S(1)} %get-tuple-element.49), channel_id=1, source_target_pairs={{0,0},{1,2},{2,1},{3,4},{4,3},{5,6},{6,5},{7,8},{8,7},{9,10},{10,9... | collective-permute-start | bytes 393224 | tf_op jit(solution)/shard_map/ppermute | solution.py:504
  80.4 5.0 %collective-permute-start.16 = (f32[64,512]{1,0:T(8,128)S(1)}, f32[64,512]{1,0:T(8,128)S(1)}, u32[]{:S(2)}, u32[]{:S(2)}) collective-permute-start(f32[64,512]{1,0:T(8,128)S(1)} %pad_maximum_fusion.4), channel_id=1, source_target_pairs={{0,1},{1,0},{2,3},{3,2},{4,5},{5,4},{6,7},{7,6},{8,9},{9,8},{10,11... | collective-permute-start | bytes 393224 | tf_op jit(solution)/shard_map/ppermute | solution.py:514
  80.5 6.3 %collective-permute-start.17 = (f32[64,512]{1,0:T(8,128)S(1)}, f32[64,512]{1,0:T(8,128)S(1)}, u32[]{:S(2)}, u32[]{:S(2)}) collective-permute-start(f32[64,512]{1,0:T(8,128)S(1)} %pad_maximum_fusion.5), channel_id=1, source_target_pairs={{0,0},{1,2},{2,1},{3,4},{4,3},{5,6},{6,5},{7,8},{8,7},{9,10},{10,9... | collective-permute-start | bytes 393224 | tf_op jit(solution)/shard_map/ppermute | solution.py:513

commit v5 on v4

--- a/solution.py
+++ b/solution.py
@@ -330,28 +330,52 @@
     return top, (src - top.astype(F32)).astype(BF16)
 
 
-def sides_kernel(place_ref, v_ref, mask_ref, ra_ref, rb_ref, ya_ref, yb_ref, w_ref, o_ref, high, low):
+def product(w_ref, dx, cols, high, low):
+    full = jnp.dot(w_ref[dx, :, cols], high, preferred_element_type=F32)
+    half = jnp.dot(w_ref[dx, 0 : 3 * NODES, cols], low, preferred_element_type=F32)
+    return spread(full[: 3 * NODES] + full[3 * NODES :] + half)
+
+
+def put_moments(order, mom_ref, mom_out, sq, cross):
+    sq = jnp.sum(sq, keepdims=True)
+    cross = jnp.sum(cross, keepdims=True)
+    spot = lane_iota((1, 128))
+    before = jnp.zeros((1, 128), F32) if mom_ref is None else mom_ref[0:1, :]
+    mom = jnp.where(spot == 2 * order, sq, jnp.where(spot == 2 * order + 1, cross, before))
+    mom_out[...] = jnp.broadcast_to(mom, mom_out.shape)
+
+
+def sides_kernel(last, place_ref, v_ref, mask_ref, ra_ref, rb_ref, ya_ref, yb_ref, w_ref, *rest):
+    if last:
+        diag_ref, maskc_ref, c_ref, mom_ref, o_ref, mom_out, high, low = rest
+    else:
+        o_ref, high, low = rest
     (x_low, x_high), (y_low, y_high) = parity_weights(place_ref)
+    halo = {}
+
+    def at_rows(px, py):
+        return pl.ds((px * 4 + py) * NODES, NODES)
 
     def put(px, py, src):
-        rows = pl.ds((px * 4 + py) * NODES, NODES)
-        high[rows, :], low[rows, :] = split(src)
+        high[at_rows(px, py), :], low[at_rows(px, py), :] = split(src)
 
     for x in range(2):
         for y in range(2):
             put(x + 1, y + 1, v_ref[:, column(x, y)] * mask_ref[0:1, column(x, y)])
     for k in range(2):
         at = pl.ds(k * BZ, BZ)
-        put(0, k + 1, blend(x_low, ra_ref[:, at], rb_ref[:, at]))
-        put(3, k + 1, blend(x_high, ra_ref[:, at], rb_ref[:, at]))
+        halo[k] = (blend(x_low, ra_ref[:, at], rb_ref[:, at]), blend(x_high, ra_ref[:, at], rb_ref[:, at]))
+        put(0, k + 1, halo[k][0])
+        put(3, k + 1, halo[k][1])
         put(k + 1, 0, blend(y_low, ya_ref[:, at], yb_ref[:, at]))
         put(k + 1, 3, blend(y_high, ya_ref[:, at], yb_ref[:, at]))
     nothing = jnp.zeros((NODES, BZ), BF16)
     for px in (0, 3):
         for py in (0, 3):
-            rows = pl.ds((px * 4 + py) * NODES, NODES)
-            high[rows, :] = nothing
-            low[rows, :] = nothing
+            high[at_rows(px, py), :] = nothing
+            low[at_rows(px, py), :] = nothing
+    sq = jnp.zeros((NODES, BZ), F32)
+    cross = jnp.zeros((NODES, BZ), F32)
     for x in range(2):
         for y in range(2):
             full = jnp.zeros((6 * NODES, BZ), F32)
@@ -360,28 +384,43 @@
                 rows = pl.ds(((x + dx) * 4 + y) * NODES, 3 * NODES)
                 full = full + jnp.dot(w_ref[dx], high[rows, :], preferred_element_type=F32)
                 half = half + jnp.dot(w_ref[dx, 0 : 3 * NODES, :], low[rows, :], preferred_element_type=F32)
-            o_ref[:, column(x, y)] = spread(full[: 3 * NODES] + full[3 * NODES :] + half)
-
-
-def sides(place, v, mask, ra, rb, ya, yb, weights):
-    operands = (v, mask, ra, rb, ya, yb, weights)
+            at = column(x, y)
+            total = spread(full[: 3 * NODES] + full[3 * NODES :] + half)
+            o_ref[:, at] = total
+            if last:
+                v = v_ref[:, at]
+                sq = sq + v * v
+                cross = cross + v * (diag_ref[:, at] * v - maskc_ref[0:1, at] * total)
+    if not last:
+        return
+    energy = jnp.zeros((NODES, BZ), F32)
+    for x in range(2):
+        for y in range(2):
+            near = at_rows(x + 1, 3 * y)
+            cols = pl.ds(2 * y * NODES, NODES)
+            energy = energy + halo[y][x] * product(w_ref, 2 - 2 * x, cols, high[near, :], low[near, :])
+    cross = cross - energy * (1.0 / c_ref[0:1, 0:1])
+    put_moments(2, mom_ref, mom_out, sq, cross)
+
+
+def sides(place, operands, last):
+    shapes = [FIELD] + ([pltpu.VMEM((SENDERS, 128), F32)] if last else [])
     return pl.pallas_call(
-        sides_kernel,
+        functools.partial(sides_kernel, last),
         name="sides",
         in_specs=in_specs(len(operands)),
-        out_specs=pl.BlockSpec(memory_space=pltpu.VMEM),
-        out_shape=FIELD,
+        out_specs=[pl.BlockSpec(memory_space=pltpu.VMEM)] * len(shapes),
+        out_shape=shapes,
         scratch_shapes=[pltpu.VMEM((16 * NODES, BZ), BF16), pltpu.VMEM((16 * NODES, BZ), BF16)],
         compiler_params=pltpu.CompilerParams(vmem_limit_bytes=16 << 20),
         cost_estimate=pl.CostEstimate(flops=15 * 10**8, transcendentals=0, bytes_accessed=2 * 10**6),
     )(place, *[vmem(x) for x in operands])
 
 
-def corners_kernel(order, place_ref, sum_ref, v_ref, diag_ref, mask_ref, maskc_ref, ca_ref, cb_ref, w_ref, *rest):
+def corners_kernel(order, last, place_ref, sum_ref, v_ref, diag_ref, mask_ref, maskc_ref, ca_ref, cb_ref, w_ref, *rest):
     rest = list(rest)
-    mom_ref = rest.pop(0) if order else None
-    o_ref, mom_out = rest[:2]
-    edges = rest[2:]
+    mom_ref = rest.pop(0) if order and not last else None
+    o_ref = rest.pop(0)
     x_pairs, y_pairs = parity_weights(place_ref)
     sq = jnp.zeros((NODES, BZ), F32)
     cross = jnp.zeros((NODES, BZ), F32)
@@ -390,43 +429,43 @@
         line = [blend(y_pairs[y], ca_ref[:, pl.ds(k * BZ, BZ)], cb_ref[:, pl.ds(k * BZ, BZ)]) for k in range(2)]
         for x in range(2):
             high, low = split(blend(x_pairs[x], line[0], line[1]))
-            cols = pl.ds(2 * y * NODES, NODES)
-            full = jnp.dot(w_ref[2 * x, :, cols], high, preferred_element_type=F32)
-            half = jnp.dot(w_ref[2 * x, 0 : 3 * NODES, cols], low, preferred_element_type=F32)
             at = column(x, y)
-            total = sum_ref[:, at] + spread(full[: 3 * NODES] + full[3 * NODES :] + half)
+            total = sum_ref[:, at] + product(w_ref, 2 * x, pl.ds(2 * y * NODES, NODES), high, low)
             v = v_ref[:, at]
             new = diag_ref[:, at] * v - maskc_ref[0:1, at] * total
             o_ref[:, at] = new
-            masked[x].append(new * mask_ref[0:1, at])
-            sq = sq + v * v
-            cross = cross + v * new
-    if edges:
-        store_edges(place_ref, masked, *edges)
-    sq = jnp.sum(sq, keepdims=True)
-    cross = jnp.sum(cross, keepdims=True)
-    spot = lane_iota((1, 128))
-    before = mom_ref[0:1, :] if order else jnp.zeros((1, 128), F32)
-    mom = jnp.where(spot == 2 * order, sq, jnp.where(spot == 2 * order + 1, cross, before))
-    mom_out[...] = jnp.broadcast_to(mom, mom_out.shape)
-
-
-def apply_stiffness(order, place, v, diag, mask, maskc, edges, weights, moments):
-    ra, rb, ya, yb, ca, cb = exchange(place[1], *edges)
-    part = sides(place, v, mask, ra, rb, ya, yb, weights)
-    more = [] if moments is None else [moments]
-    last = order == 2
-    moment = jax.ShapeDtypeStruct((SENDERS, 128), F32) if last else pltpu.VMEM((8, 128), F32)
-    shapes = [FIELD, moment] + ([] if last else [EDGE] * 4)
-    operands = [part, v, diag, mask, maskc, ca, cb, weights] + more
+            if not last:
+                masked[x].append(new * mask_ref[0:1, at])
+                sq = sq + v * v
+                cross = cross + v * new
+    if not last:
+        store_edges(place_ref, masked, *rest[1:])
+        put_moments(order, mom_ref, rest[0], sq, cross)
+
+
+def corners(order, place, operands, last):
+    shapes = [FIELD] + ([] if last else [pltpu.VMEM((8, 128), F32)] + [EDGE] * 4)
     return pl.pallas_call(
-        functools.partial(corners_kernel, order),
+        functools.partial(corners_kernel, order, last),
         name="corners",
         in_specs=in_specs(len(operands)),
         out_specs=[pl.BlockSpec(memory_space=pltpu.VMEM)] * len(shapes),
         out_shape=shapes,
         compiler_params=pltpu.CompilerParams(vmem_limit_bytes=16 << 20),
+        cost_estimate=pl.CostEstimate(flops=5 * 10**8, transcendentals=0, bytes_accessed=2 * 10**6),
     )(place, *[vmem(x) for x in operands])
+
+
+def apply_stiffness(order, place, v, diag, mask, maskc, centre, edges, weights, moments):
+    last = order == 2
+    ra, rb, ya, yb, ca, cb = exchange(place[1], *edges)
+    operands = [v, mask, ra, rb, ya, yb, weights] + ([diag, maskc, centre, moments] if last else [])
+    part, *shared = sides(place, operands, last)
+    operands = [part, v, diag, mask, maskc, ca, cb, weights]
+    if last:
+        return corners(order, place, operands, last)[0], shared[0], []
+    new, moments, *edges = corners(order, place, operands + ([] if moments is None else [moments]), last)
+    return new, moments, edges
 
 
 def finish_kernel(mom_ref, c_ref, v0_ref, v1_ref, v2_ref, v3_ref, x_ref, r_ref):
@@ -525,8 +564,8 @@
     fields = [v]
     moments = None
     for order in range(3):
-        v, moments, *edges = apply_stiffness(
-            order, place, v, diag, mask, maskc, edges, weights, moments
+        v, moments, edges = apply_stiffness(
+            order, place, v, diag, mask, maskc, centre, edges, weights, moments
         )
         fields.append(v)
     shared = lax.all_to_all(moments.reshape(SENDERS, 1, 128), AXES, split_axis=0, concat_axis=0, tiled=True)

time: 112 us -> 111 us (level)
  blocking collectives: 22.1 us -> 0 us
  starting transfers between devices: 41 us -> 53.6 us
  waiting for transfers between devices: 18.9 us -> 26.1 us
    all_to_all x1 -> x0, blocking collectives: 22.1 us -> none  [on_device(): lax.all_to_all(moments.reshape(SENDERS, 1, 128), AXES, split_axis=0, conc...]
    all_to_all x0 -> x1, starting transfers between devices: none -> 10.7 us  [on_device(): lax.all_to_all(moments.reshape(SENDERS, 1, 128), AXES, split_axis=0, conc...]
    all_to_all x0 -> x1, waiting for transfers between devices: none -> 8.42 us  [on_device(): lax.all_to_all(moments.reshape(SENDERS, 1, 128), AXES, split_axis=0, conc...]
    ppermute x3, starting transfers between devices: 6.72 us -> 9.06 us  [exchange(): ra = lax.ppermute(ea, 'slab', swap('slab', 0))]
    ppermute x3, waiting for transfers between devices: 4.57 us -> 2.86 us  [exchange(): cb = lax.ppermute(line(jnp.logical_not(up)), 'grp', swap('grp', 1))]
  transfers between devices with their start and end apart: 19 -> 20, of which waited for: 6 -> 7; matrix products, arithmetic and copies ran while one was open for 0% -> 0% of each run, Pallas kernels for 5% -> 7%
where the time goes in v5:
time: 111 us; the launch traced here: 110 us
  starting transfers between devices  53.6 us (48%)
  Pallas kernels  27.7 us (25%)
  waiting for transfers between devices  26.1 us (24%)
  local copies, waits for them, and re-layouts  1.45 us (1%)
    pallas_call x1, Pallas kernels, splat(): pl.pallas_call(splat_kernel, name='splat', in_specs=[pl.BlockSpec(memory_...  14.6 us
    all_to_all x1, waiting for transfers between devices, on_device(): lax.all_to_all(payload.reshape(SENDERS, 1, ROWS * 128), AXES, split_axis=...  13.8 us
    all_to_all x1, starting transfers between devices, on_device(): lax.all_to_all(payload.reshape(SENDERS, 1, ROWS * 128), AXES, split_axis=...  11.5 us
    all_to_all x1, starting transfers between devices, on_device(): lax.all_to_all(moments.reshape(SENDERS, 1, 128), AXES, split_axis=0, conc...  10.7 us
    ppermute x3, starting transfers between devices, exchange(): cb = lax.ppermute(line(jnp.logical_not(up)), 'grp', swap('grp', 1))  9.12 us
    ppermute x3, starting transfers between devices, exchange(): ra = lax.ppermute(ea, 'slab', swap('slab', 0))  9.06 us
    ppermute x3, starting transfers between devices, exchange(): yb = lax.ppermute(ob, 'grp', swap('grp', 1))  8.63 us
    all_to_all x1, waiting for transfers between devices, on_device(): lax.all_to_all(moments.reshape(SENDERS, 1, 128), AXES, split_axis=0, conc...  8.42 us
  transfers between devices with their start and end apart: 20, of which 7 were waited for; matrix products, arithmetic and copies ran while one was open for 0% of the time, Pallas kernels for 7%

profile of v5, /device:TPU:1, one launch (start us, length us, event | category | flops | bytes accessed | tf_op | source)
XLA Modules:
  0.0 110.2 jit_solution(18328450491347691702)
XLA Ops:
  2.1 14.6 %splat.1 = f32[8,144,128]{2,1,0:T(8,128)} custom-call(f32[6,1024,128]{2,1,0:T(8,128)} %bitcast.25, s32[8,128]{1,0:T(8,128)S(1)} %bitcast.23, s32[8,128]{1,0:T(8,128)S(1)} %bitcast.24), custom_call_target="tpu_custom_call" | custom-call | tf_op jit(solution)/shard_map/splat/pallas_call | solution.py:165
  16.7 11.5 %all-to-all-start = ((f32[128,1,1152]{2,1,0:T(1,128)}), f32[128,1,1152]{2,1,0:T(1,128)S(1)}, u32[]{:S(2)}, u32[]{:S(2)}) async-start(f32[128,1,1152]{2,1,0:T(1,128)} %bitcast.5), calls=%async_computation | async-start | bytes 1179648 | tf_op jit(solution)/shard_map/all_to_all | solution.py:561
  28.8 13.8 %all-to-all-done = f32[128,1,1152]{2,1,0:T(1,128)S(1)} async-done(((f32[128,1,1152]{2,1,0:T(1,128)}), f32[128,1,1152]{2,1,0:T(1,128)S(1)}, u32[]{:S(2)}, u32[]{:S(2)}) %all-to-all-start) | async-done | bytes 589856 | tf_op jit(solution)/shard_map/all_to_all | solution.py:561
  42.5 1.5 %assemble.1 = (f32[64,1024]{1,0:T(8,128)S(1)}, f32[64,1024]{1,0:T(8,128)S(1)}, f32[8,1024]{1,0:T(8,128)S(1)}, f32[8,128]{1,0:T(8,128)S(1)}, f32[64,512]{1,0:T(8,...) custom-call(s32[4]{0:T(128)S(1)} %pad_add_fusion.place_ref, ...), custom_call_target="tpu_custom_call" | custom-call | tf_op jit(solution)/shard_map/assemble/pallas_call | solution.py:310
  44.7 2.0 %collective-permute-start = (f32[64,512]{1,0:T(8,128)S(1)}, f32[64,512]{1,0:T(8,128)S(1)}, u32[]{:S(2)}, u32[]{:S(2)}) collective-permute-start(f32[64,512]{1,0:T(8,128)S(1)} %get-tuple-element.32), channel_id=1, source_target_pairs={{0,32},{32,0},{64,96},{96,64},{1,33},{33,1},{65,97},{97,65},{2,34}... | collective-permute-start | bytes 393224 | tf_op jit(solution)/shard_map/ppermute | solution.py:544
  47.6 2.0 %collective-permute-start.3 = (f32[64,512]{1,0:T(8,128)S(1)}, f32[64,512]{1,0:T(8,128)S(1)}, u32[]{:S(2)}, u32[]{:S(2)}) collective-permute-start(f32[64,512]{1,0:T(8,128)S(1)} %get-tuple-element.35), channel_id=1, source_target_pairs={{0,0},{1,2},{2,1},{3,4},{4,3},{5,6},{6,5},{7,8},{8,7},{9,10},{10,9... | collective-permute-start | bytes 393224 | tf_op jit(solution)/shard_map/ppermute | solution.py:543
  49.8 1.5 %collective-permute-start.4 = (f32[64,512]{1,0:T(8,128)S(1)}, f32[64,512]{1,0:T(8,128)S(1)}, u32[]{:S(2)}, u32[]{:S(2)}) collective-permute-start(f32[64,512]{1,0:T(8,128)S(1)} %pad_maximum_fusion), channel_id=1, source_target_pairs={{0,1},{1,0},{2,3},{3,2},{4,5},{5,4},{6,7},{7,6},{8,9},{9,8},{10,11... | collective-permute-start | bytes 393224 | tf_op jit(solution)/shard_map/ppermute | solution.py:553
  51.2 2.1 %collective-permute-start.5 = (f32[64,512]{1,0:T(8,128)S(1)}, f32[64,512]{1,0:T(8,128)S(1)}, u32[]{:S(2)}, u32[]{:S(2)}) collective-permute-start(f32[64,512]{1,0:T(8,128)S(1)} %pad_maximum_fusion.1), channel_id=1, source_target_pairs={{0,0},{1,2},{2,1},{3,4},{4,3},{5,6},{6,5},{7,8},{8,7},{9,10},{10,9... | collective-permute-start | bytes 393224 | tf_op jit(solution)/shard_map/ppermute | solution.py:552
  53.9 1.7 %sides.3.sum_ref = f32[64,1024]{1,0:T(8,128)S(1)} custom-call(s32[4]{0:T(128)S(1)} %pad_add_fusion.place_ref, f32[64,1024]{1,0:T(8,128)S(1)} %get-tuple-element.31.v_ref.v0_ref, f32[8,1024]{1,0:T(8,128)S(1)} %get-tuple-element.29.mask_ref, f32[64,512]{1,0:T(8,128)S(1)} %collective-permute-done.ra_ref, f32[64,512]{1,0:T(8,128)S(1)} %collective-permute-done.1.rb_ref, ...), custom_call_target="tpu_custom_call" | custom-call | flops 1500000000 | bytes 2000000 | tf_op jit(solution)/shard_map/sides/pallas_call | solution.py:408
  55.6 1.9 %collective-permute-done.5.cb_ref = f32[64,512]{1,0:T(8,128)S(1)} collective-permute-done((f32[64,512]{1,0:T(8,128)S(1)}, f32[64,512]{1,0:T(8,128)S(1)}, u32[]{:S(2)}, u32[]{:S(2)}) %collective-permute-start.5) | collective-permute-done | bytes 131104 | tf_op jit(solution)/shard_map/ppermute | solution.py:552
  57.5 1.3 %corners.3 = (f32[64,1024]{1,0:T(8,128)S(1)}, f32[8,128]{1,0:T(8,128)S(1)}, f32[64,512]{1,0:T(8,128)S(1)}, f32[64,512]{1,0:T(8,128)S(1)}, f32[64,512]{1,0:T(8,128)S(1)}, /*index=5*/f32[64,512]{1,0:T(8,128)S(1)}) custom-call(s32[4]{0:T(128)S(1)} %pad_add_fusion.place_ref, f32[64,1024]{1,0:T(8,128)S(1)} %sides.3.sum_ref, ...), custom_call_target="tpu_custom_call" | custom-call | flops 500000000 | bytes 2000000 | tf_op jit(solution)/shard_map/corners/pallas_call | solution.py:448
  59.5 4.1 %collective-permute-start.6 = (f32[64,512]{1,0:T(8,128)S(1)}, f32[64,512]{1,0:T(8,128)S(1)}, u32[]{:S(2)}, u32[]{:S(2)}) collective-permute-start(f32[64,512]{1,0:T(8,128)S(1)} %get-tuple-element.40), channel_id=1, source_target_pairs={{0,32},{32,0},{64,96},{96,64},{1,33},{33,1},{65,97},{97,65},{2,34}... | collective-permute-start | bytes 393224 | tf_op jit(solution)/shard_map/ppermute | solution.py:544
  63.6 2.5 %collective-permute-start.9 = (f32[64,512]{1,0:T(8,128)S(1)}, f32[64,512]{1,0:T(8,128)S(1)}, u32[]{:S(2)}, u32[]{:S(2)}) collective-permute-start(f32[64,512]{1,0:T(8,128)S(1)} %get-tuple-element.43), channel_id=1, source_target_pairs={{0,0},{1,2},{2,1},{3,4},{4,3},{5,6},{6,5},{7,8},{8,7},{9,10},{10,9... | collective-permute-start | bytes 393224 | tf_op jit(solution)/shard_map/ppermute | solution.py:543
  66.2 3.1 %collective-permute-start.11 = (f32[64,512]{1,0:T(8,128)S(1)}, f32[64,512]{1,0:T(8,128)S(1)}, u32[]{:S(2)}, u32[]{:S(2)}) collective-permute-start(f32[64,512]{1,0:T(8,128)S(1)} %pad_maximum_fusion.3), channel_id=1, source_target_pairs={{0,0},{1,2},{2,1},{3,4},{4,3},{5,6},{6,5},{7,8},{8,7},{9,10},{10,9... | collective-permute-start | bytes 393224 | tf_op jit(solution)/shard_map/ppermute | solution.py:552
  69.8 1.7 %sides.4.sum_ref = f32[64,1024]{1,0:T(8,128)S(1)} custom-call(s32[4]{0:T(128)S(1)} %pad_add_fusion.place_ref, f32[64,1024]{1,0:T(8,128)S(1)} %get-tuple-element.39.v_ref.v1_ref, f32[8,1024]{1,0:T(8,128)S(1)} %get-tuple-element.29.mask_ref, f32[64,512]{1,0:T(8,128)S(1)} %collective-permute-done.6.ra_ref, f32[64,512]{1,0:T(8,128)S(1)} %collective-permute-done.7.rb_ref, ...), custom_call_target="tpu_custom_call" | custom-call | flops 1500000000 | bytes 2000000 | tf_op jit(solution)/shard_map/sides/pallas_call | solution.py:408
  72.5 1.3 %corners.4 = (f32[64,1024]{1,0:T(8,128)S(1)}, f32[8,128]{1,0:T(8,128)S(1)}, f32[64,512]{1,0:T(8,128)S(1)}, f32[64,512]{1,0:T(8,128)S(1)}, f32[64,512]{1,0:T(8,128)S(1)}, /*index=5*/f32[64,512]{1,0:T(8,128)S(1)}) custom-call(s32[4]{0:T(128)S(1)} %pad_add_fusion.place_ref, f32[64,1024]{1,0:T(8,128)S(1)} %sides.4.sum_ref, ...), custom_call_target="tpu_custom_call" | custom-call | flops 500000000 | bytes 2000000 | tf_op jit(solution)/shard_map/corners/pallas_call | solution.py:448
  74.5 3.0 %collective-permute-start.12 = (f32[64,512]{1,0:T(8,128)S(1)}, f32[64,512]{1,0:T(8,128)S(1)}, u32[]{:S(2)}, u32[]{:S(2)}) collective-permute-start(f32[64,512]{1,0:T(8,128)S(1)} %get-tuple-element.46), channel_id=1, source_target_pairs={{0,32},{32,0},{64,96},{96,64},{1,33},{33,1},{65,97},{97,65},{2,34}... | collective-permute-start | bytes 393224 | tf_op jit(solution)/shard_map/ppermute | solution.py:544
  77.5 4.2 %collective-permute-start.15 = (f32[64,512]{1,0:T(8,128)S(1)}, f32[64,512]{1,0:T(8,128)S(1)}, u32[]{:S(2)}, u32[]{:S(2)}) collective-permute-start(f32[64,512]{1,0:T(8,128)S(1)} %get-tuple-element.49), channel_id=1, source_target_pairs={{0,0},{1,2},{2,1},{3,4},{4,3},{5,6},{6,5},{7,8},{8,7},{9,10},{10,9... | collective-permute-start | bytes 393224 | tf_op jit(solution)/shard_map/ppermute | solution.py:543
  81.9 3.8 %collective-permute-start.17 = (f32[64,512]{1,0:T(8,128)S(1)}, f32[64,512]{1,0:T(8,128)S(1)}, u32[]{:S(2)}, u32[]{:S(2)}) collective-permute-start(f32[64,512]{1,0:T(8,128)S(1)} %pad_maximum_fusion.5), channel_id=1, source_target_pairs={{0,0},{1,2},{2,1},{3,4},{4,3},{5,6},{6,5},{7,8},{8,7},{9,10},{10,9... | collective-permute-start | bytes 393224 | tf_op jit(solution)/shard_map/ppermute | solution.py:552
  85.7 2.8 %sides.5 = (f32[64,1024]{1,0:T(8,128)S(1)}, f32[128,128]{1,0:T(8,128)}) custom-call(s32[4]{0:T(128)S(1)} %pad_add_fusion.place_ref, f32[64,1024]{1,0:T(8,128)S(1)} %get-tuple-element.45.v_ref.v2_ref, f32[8,1024]{1,0:T(8,128)S(1)} %get-tuple-element.29.mask_ref, f32[64,512]{1,0:T(8,128)S(1)} %collective-permute-done.12.ra_ref, ...), custom_call_target="tpu_custom_call" | custom-call | flops 1500000000 | bytes 2000000 | tf_op jit(solution)/shard_map/sides/pallas_call | solution.py:408
  88.5 10.7 %all-to-all-start.1 = ((f32[128,1,128]{2,1,0:T(1,128)}), f32[128,1,128]{2,1,0:T(1,128)S(1)}, u32[]{:S(2)}, u32[]{:S(2)}) async-start(f32[128,1,128]{2,1,0:T(1,128)} %bitcast.8), calls=%async_computation.1 | async-start | bytes 131072 | tf_op jit(solution)/shard_map/all_to_all | solution.py:571
  99.2 1.1 %corners.5.v3_ref = f32[64,1024]{1,0:T(8,128)S(1)} custom-call(s32[4]{0:T(128)S(1)} %pad_add_fusion.place_ref, f32[64,1024]{1,0:T(8,128)S(1)} %get-tuple-element.53.sum_ref, f32[64,1024]{1,0:T(8,128)S(1)} %get-tuple-element.45.v_ref.v2_ref, f32[64,1024]{1,0:T(8,128)S(1)} %get-tuple-element.37.diag_ref.rest_0_, f32[8,1024]{1,0:T(8,128)S(1)} %get-tuple-element.29.mask_ref, ...), custom_call_target="tpu_custom_call" | custom-call | flops 500000000 | bytes 2000000 | tf_op jit(solution)/shard_map/corners/pallas_call | solution.py:448
  100.3 8.4 %all-to-all-done.1 = f32[128,1,128]{2,1,0:T(1,128)S(1)} async-done(((f32[128,1,128]{2,1,0:T(1,128)}), f32[128,1,128]{2,1,0:T(1,128)S(1)}, u32[]{:S(2)}, u32[]{:S(2)}) %all-to-all-start.1) | async-done | bytes 65568 | tf_op jit(solution)/shard_map/all_to_all | solution.py:571
  108.7 1.4 %finish.1 = (f32[64,8,128]{2,1,0:T(8,128)}, f32[64,8,128]{2,1,0:T(8,128)}) custom-call(f32[128,128]{1,0:T(8,128)S(1)} %bitcast.22, f32[8,128]{1,0:T(8,128)S(1)} %get-tuple-element.50.rest_2_.c_ref, f32[64,1024]{1,0:T(8,128)S(1)} %get-tuple-element.31.v_ref.v0_ref, f32[64,1024]{1,0:T(8,128)S(1)} %get-tuple-element.39.v_ref.v1_ref, ...), custom_call_target="tpu_custom_call" | custom-call | tf_op jit(solution)/shard_map/finish/pallas_call | solution.py:523
  (47 shorter events, 7.3 us)
Async XLA Ops:
  0.6 27.6 %copy-start = (f32[27,64,64]{2,1,0:T(8,128)S(1)}, f32[27,64,64]{2,1,0:T(8,128)}, u32[]{:S(2)}) copy-start(f32[27,64,64]{2,1,0:T(8,128)} %coupling_ref.1) | copy-start | bytes 1327108
  0.6 0.8 copy-start.1
  1.4 0.7 copy-start.2
  2.1 26.1 %copy-start.3 = (s32[2,2,256]{2,1,0:T(2,128)S(1)}, s32[2,2,256]{2,1,0:T(2,128)}, u32[]{:S(2)}) copy-start(s32[2,2,256]{2,1,0:T(2,128)} %occ_ref.1) | copy-start | bytes 12292
  16.7 25.8 %all-to-all-start = ((f32[128,1,1152]{2,1,0:T(1,128)}), f32[128,1,1152]{2,1,0:T(1,128)S(1)}, u32[]{:S(2)}, u32[]{:S(2)}) async-start(f32[128,1,1152]{2,1,0:T(1,128)} %bitcast.5), calls=%async_computation | async-start | bytes 1179648 | tf_op jit(solution)/shard_map/all_to_all | solution.py:561
  44.0 5.6 %collective-permute-start.1 = (f32[64,512]{1,0:T(8,128)S(1)}, f32[64,512]{1,0:T(8,128)S(1)}, u32[]{:S(2)}, u32[]{:S(2)}) collective-permute-start(f32[64,512]{1,0:T(8,128)S(1)} %get-tuple-element.33), channel_id=1, source_target_pairs={{0,0},{32,64},{64,32},{96,96},{1,1},{33,65},{65,33},{97,97},{2,2},... | collective-permute-start | bytes 393224 | tf_op jit(solution)/shard_map/ppermute | solution.py:545
  44.7 5.1 %collective-permute-start = (f32[64,512]{1,0:T(8,128)S(1)}, f32[64,512]{1,0:T(8,128)S(1)}, u32[]{:S(2)}, u32[]{:S(2)}) collective-permute-start(f32[64,512]{1,0:T(8,128)S(1)} %get-tuple-element.32), channel_id=1, source_target_pairs={{0,32},{32,0},{64,96},{96,64},{1,33},{33,1},{65,97},{97,65},{2,34}... | collective-permute-start | bytes 393224 | tf_op jit(solution)/shard_map/ppermute | solution.py:544
  46.7 6.7 %collective-permute-start.2 = (f32[64,512]{1,0:T(8,128)S(1)}, f32[64,512]{1,0:T(8,128)S(1)}, u32[]{:S(2)}, u32[]{:S(2)}) collective-permute-start(f32[64,512]{1,0:T(8,128)S(1)} %get-tuple-element.34), channel_id=1, source_target_pairs={{0,1},{1,0},{2,3},{3,2},{4,5},{5,4},{6,7},{7,6},{8,9},{9,8},{10,11... | collective-permute-start | bytes 393224 | tf_op jit(solution)/shard_map/ppermute | solution.py:546
  47.6 6.3 %collective-permute-start.3 = (f32[64,512]{1,0:T(8,128)S(1)}, f32[64,512]{1,0:T(8,128)S(1)}, u32[]{:S(2)}, u32[]{:S(2)}) collective-permute-start(f32[64,512]{1,0:T(8,128)S(1)} %get-tuple-element.35), channel_id=1, source_target_pairs={{0,0},{1,2},{2,1},{3,4},{4,3},{5,6},{6,5},{7,8},{8,7},{9,10},{10,9... | collective-permute-start | bytes 393224 | tf_op jit(solution)/shard_map/ppermute | solution.py:543
  49.8 5.9 %collective-permute-start.4 = (f32[64,512]{1,0:T(8,128)S(1)}, f32[64,512]{1,0:T(8,128)S(1)}, u32[]{:S(2)}, u32[]{:S(2)}) collective-permute-start(f32[64,512]{1,0:T(8,128)S(1)} %pad_maximum_fusion), channel_id=1, source_target_pairs={{0,1},{1,0},{2,3},{3,2},{4,5},{5,4},{6,7},{7,6},{8,9},{9,8},{10,11... | collective-permute-start | bytes 393224 | tf_op jit(solution)/shard_map/ppermute | solution.py:553
  51.2 6.3 %collective-permute-start.5 = (f32[64,512]{1,0:T(8,128)S(1)}, f32[64,512]{1,0:T(8,128)S(1)}, u32[]{:S(2)}, u32[]{:S(2)}) collective-permute-start(f32[64,512]{1,0:T(8,128)S(1)} %pad_maximum_fusion.1), channel_id=1, source_target_pairs={{0,0},{1,2},{2,1},{3,4},{4,3},{5,6},{6,5},{7,8},{8,7},{9,10},{10,9... | collective-permute-start | bytes 393224 | tf_op jit(solution)/shard_map/ppermute | solution.py:552
  58.8 7.3 %collective-permute-start.7 = (f32[64,512]{1,0:T(8,128)S(1)}, f32[64,512]{1,0:T(8,128)S(1)}, u32[]{:S(2)}, u32[]{:S(2)}) collective-permute-start(f32[64,512]{1,0:T(8,128)S(1)} %get-tuple-element.41), channel_id=1, source_target_pairs={{0,0},{32,64},{64,32},{96,96},{1,1},{33,65},{65,33},{97,97},{2,2},... | collective-permute-start | bytes 393224 | tf_op jit(solution)/shard_map/ppermute | solution.py:545
  59.5 6.6 %collective-permute-start.6 = (f32[64,512]{1,0:T(8,128)S(1)}, f32[64,512]{1,0:T(8,128)S(1)}, u32[]{:S(2)}, u32[]{:S(2)}) collective-permute-start(f32[64,512]{1,0:T(8,128)S(1)} %get-tuple-element.40), channel_id=1, source_target_pairs={{0,32},{32,0},{64,96},{96,64},{1,33},{33,1},{65,97},{97,65},{2,34}... | collective-permute-start | bytes 393224 | tf_op jit(solution)/shard_map/ppermute | solution.py:544
  63.6 5.8 %collective-permute-start.8 = (f32[64,512]{1,0:T(8,128)S(1)}, f32[64,512]{1,0:T(8,128)S(1)}, u32[]{:S(2)}, u32[]{:S(2)}) collective-permute-start(f32[64,512]{1,0:T(8,128)S(1)} %get-tuple-element.42), channel_id=1, source_target_pairs={{0,1},{1,0},{2,3},{3,2},{4,5},{5,4},{6,7},{7,6},{8,9},{9,8},{10,11... | collective-permute-start | bytes 393224 | tf_op jit(solution)/shard_map/ppermute | solution.py:546
  63.6 6.3 %collective-permute-start.9 = (f32[64,512]{1,0:T(8,128)S(1)}, f32[64,512]{1,0:T(8,128)S(1)}, u32[]{:S(2)}, u32[]{:S(2)}) collective-permute-start(f32[64,512]{1,0:T(8,128)S(1)} %get-tuple-element.43), channel_id=1, source_target_pairs={{0,0},{1,2},{2,1},{3,4},{4,3},{5,6},{6,5},{7,8},{8,7},{9,10},{10,9... | collective-permute-start | bytes 393224 | tf_op jit(solution)/shard_map/ppermute | solution.py:543
  66.1 5.4 %collective-permute-start.10 = (f32[64,512]{1,0:T(8,128)S(1)}, f32[64,512]{1,0:T(8,128)S(1)}, u32[]{:S(2)}, u32[]{:S(2)}) collective-permute-start(f32[64,512]{1,0:T(8,128)S(1)} %pad_maximum_fusion.2), channel_id=1, source_target_pairs={{0,1},{1,0},{2,3},{3,2},{4,5},{5,4},{6,7},{7,6},{8,9},{9,8},{10,11... | collective-permute-start | bytes 393224 | tf_op jit(solution)/shard_map/ppermute | solution.py:553
  66.2 6.3 %collective-permute-start.11 = (f32[64,512]{1,0:T(8,128)S(1)}, f32[64,512]{1,0:T(8,128)S(1)}, u32[]{:S(2)}, u32[]{:S(2)}) collective-permute-start(f32[64,512]{1,0:T(8,128)S(1)} %pad_maximum_fusion.3), channel_id=1, source_target_pairs={{0,0},{1,2},{2,1},{3,4},{4,3},{5,6},{6,5},{7,8},{8,7},{9,10},{10,9... | collective-permute-start | bytes 393224 | tf_op jit(solution)/shard_map/ppermute | solution.py:552
  73.8 7.9 %collective-permute-start.13 = (f32[64,512]{1,0:T(8,128)S(1)}, f32[64,512]{1,0:T(8,128)S(1)}, u32[]{:S(2)}, u32[]{:S(2)}) collective-permute-start(f32[64,512]{1,0:T(8,128)S(1)} %get-tuple-element.47), channel_id=1, source_target_pairs={{0,0},{32,64},{64,32},{96,96},{1,1},{33,65},{65,33},{97,97},{2,2},... | collective-permute-start | bytes 393224 | tf_op jit(solution)/shard_map/ppermute | solution.py:545
  74.5 7.2 %collective-permute-start.12 = (f32[64,512]{1,0:T(8,128)S(1)}, f32[64,512]{1,0:T(8,128)S(1)}, u32[]{:S(2)}, u32[]{:S(2)}) collective-permute-start(f32[64,512]{1,0:T(8,128)S(1)} %get-tuple-element.46), channel_id=1, source_target_pairs={{0,32},{32,0},{64,96},{96,64},{1,33},{33,1},{65,97},{97,65},{2,34}... | collective-permute-start | bytes 393224 | tf_op jit(solution)/shard_map/ppermute | solution.py:544
  77.5 8.2 %collective-permute-start.14 = (f32[64,512]{1,0:T(8,128)S(1)}, f32[64,512]{1,0:T(8,128)S(1)}, u32[]{:S(2)}, u32[]{:S(2)}) collective-permute-start(f32[64,512]{1,0:T(8,128)S(1)} %get-tuple-element.48), channel_id=1, source_target_pairs={{0,1},{1,0},{2,3},{3,2},{4,5},{5,4},{6,7},{7,6},{8,9},{9,8},{10,11... | collective-permute-start | bytes 393224 | tf_op jit(solution)/shard_map/ppermute | solution.py:546
  77.5 8.2 %collective-permute-start.15 = (f32[64,512]{1,0:T(8,128)S(1)}, f32[64,512]{1,0:T(8,128)S(1)}, u32[]{:S(2)}, u32[]{:S(2)}) collective-permute-start(f32[64,512]{1,0:T(8,128)S(1)} %get-tuple-element.49), channel_id=1, source_target_pairs={{0,0},{1,2},{2,1},{3,4},{4,3},{5,6},{6,5},{7,8},{8,7},{9,10},{10,9... | collective-permute-start | bytes 393224 | tf_op jit(solution)/shard_map/ppermute | solution.py:543
  81.7 17.4 %collective-permute-start.16 = (f32[64,512]{1,0:T(8,128)S(1)}, f32[64,512]{1,0:T(8,128)S(1)}, u32[]{:S(2)}, u32[]{:S(2)}) collective-permute-start(f32[64,512]{1,0:T(8,128)S(1)} %pad_maximum_fusion.4), channel_id=1, source_target_pairs={{0,1},{1,0},{2,3},{3,2},{4,5},{5,4},{6,7},{7,6},{8,9},{9,8},{10,11... | collective-permute-start | bytes 393224 | tf_op jit(solution)/shard_map/ppermute | solution.py:553
  81.9 17.3 %collective-permute-start.17 = (f32[64,512]{1,0:T(8,128)S(1)}, f32[64,512]{1,0:T(8,128)S(1)}, u32[]{:S(2)}, u32[]{:S(2)}) collective-permute-start(f32[64,512]{1,0:T(8,128)S(1)} %pad_maximum_fusion.5), channel_id=1, source_target_pairs={{0,0},{1,2},{2,1},{3,4},{4,3},{5,6},{6,5},{7,8},{8,7},{9,10},{10,9... | collective-permute-start | bytes 393224 | tf_op jit(solution)/shard_map/ppermute | solution.py:552
  88.5 20.3 %all-to-all-start.1 = ((f32[128,1,128]{2,1,0:T(1,128)}), f32[128,1,128]{2,1,0:T(1,128)S(1)}, u32[]{:S(2)}, u32[]{:S(2)}) async-start(f32[128,1,128]{2,1,0:T(1,128)} %bitcast.8), calls=%async_computation.1 | async-start | bytes 131072 | tf_op jit(solution)/shard_map/all_to_all | solution.py:571

commit v6 on v5

--- a/solution.py
+++ b/solution.py
@@ -532,11 +532,7 @@
 
 def swap(axis, first):
     count = lax.axis_size(axis)
-    pairs = []
-    for i in range(count):
-        j = i + 1 if (i - first) % 2 == 0 else i - 1
-        pairs.append((i, j if 0 <= j < count else i))
-    return pairs
+    return [(i, (i + 1 if (i - first) % 2 == 0 else i - 1) % count) for i in range(count)]
 
 
 def exchange(grp, ea, eb, oa, ob):

time: 111 us -> 105 us (0.946)
  starting transfers between devices: 53.6 us -> 43 us
  waiting for transfers between devices: 26.1 us -> 31.2 us
    ppermute x3, starting transfers between devices: 1.63 us -> 11.6 us  [exchange(): ca = lax.ppermute(line(up), 'grp', swap('grp', 0))]
    ppermute x3, starting transfers between devices: 9.06 us -> 0.36 us  [exchange(): ra = lax.ppermute(ea, 'slab', swap('slab', 0))]
    ppermute x3, starting transfers between devices: 8.63 us -> 0.11 us  [exchange(): yb = lax.ppermute(ob, 'grp', swap('grp', 1))]
    ppermute x3, starting transfers between devices: 9.12 us -> 0.63 us  [exchange(): cb = lax.ppermute(line(jnp.logical_not(up)), 'grp', swap('grp', 1))]
    ppermute x3, starting transfers between devices: 0.98 us -> 8.21 us  [exchange(): ya = lax.ppermute(oa, 'grp', swap('grp', 0))]
    ppermute x3, waiting for transfers between devices: 0.01 us -> 3.72 us  [exchange(): rb = lax.ppermute(eb, 'slab', swap('slab', 1))]
    all_to_all x1, starting transfers between devices: 10.7 us -> 7.35 us  [on_device(): lax.all_to_all(moments.reshape(SENDERS, 1, 128), AXES, split_axis=0, conc...]
    ppermute x3, waiting for transfers between devices: 2.86 us -> 5.1 us  [exchange(): cb = lax.ppermute(line(jnp.logical_not(up)), 'grp', swap('grp', 1))]
where the time goes in v6:
time: 105 us
  starting transfers between devices  43 us (41%)
  waiting for transfers between devices  31.2 us (30%)
  Pallas kernels  27.7 us (26%)
  local copies, waits for them, and re-layouts  1.45 us (1%)
    pallas_call x1, Pallas kernels, splat(): pl.pallas_call(splat_kernel, name='splat', in_specs=[pl.BlockSpec(memory_...  14.6 us
    all_to_all x1, waiting for transfers between devices, on_device(): lax.all_to_all(payload.reshape(SENDERS, 1, ROWS * 128), AXES, split_axis=...  13.8 us
    ppermute x3, starting transfers between devices, exchange(): ca = lax.ppermute(line(up), 'grp', swap('grp', 0))  11.6 us
    all_to_all x1, starting transfers between devices, on_device(): lax.all_to_all(payload.reshape(SENDERS, 1, ROWS * 128), AXES, split_axis=...  11.5 us
    all_to_all x1, waiting for transfers between devices, on_device(): lax.all_to_all(moments.reshape(SENDERS, 1, 128), AXES, split_axis=0, conc...  8.42 us
    ppermute x3, starting transfers between devices, exchange(): ya = lax.ppermute(oa, 'grp', swap('grp', 0))  8.21 us
    all_to_all x1, starting transfers between devices, on_device(): lax.all_to_all(moments.reshape(SENDERS, 1, 128), AXES, split_axis=0, conc...  7.35 us
    pallas_call x3, Pallas kernels, sides(): pl.pallas_call(functools.partial(sides_kernel, last), name='sides', in_sp...  6.19 us
  transfers between devices with their start and end apart: 20, of which 7 were waited for; matrix products, arithmetic and copies ran while one was open for 0% of the time, Pallas kernels for 7%

profile of v6, /device:TPU:1, one launch (start us, length us, event | category | flops | bytes accessed | tf_op | source)
XLA Modules:
  0.0 104.5 jit_solution(3954237221229475034)
XLA Ops:
  2.1 14.6 %splat.1 = f32[8,144,128]{2,1,0:T(8,128)} custom-call(f32[6,1024,128]{2,1,0:T(8,128)} %bitcast.25, s32[8,128]{1,0:T(8,128)S(1)} %bitcast.23, s32[8,128]{1,0:T(8,128)S(1)} %bitcast.24), custom_call_target="tpu_custom_call" | custom-call | tf_op jit(solution)/shard_map/splat/pallas_call | solution.py:165
  16.7 11.5 %all-to-all-start = ((f32[128,1,1152]{2,1,0:T(1,128)}), f32[128,1,1152]{2,1,0:T(1,128)S(1)}, u32[]{:S(2)}, u32[]{:S(2)}) async-start(f32[128,1,1152]{2,1,0:T(1,128)} %bitcast.5), calls=%async_computation | async-start | bytes 1179648 | tf_op jit(solution)/shard_map/all_to_all | solution.py:557
  28.8 13.8 %all-to-all-done = f32[128,1,1152]{2,1,0:T(1,128)S(1)} async-done(((f32[128,1,1152]{2,1,0:T(1,128)}), f32[128,1,1152]{2,1,0:T(1,128)S(1)}, u32[]{:S(2)}, u32[]{:S(2)}) %all-to-all-start) | async-done | bytes 589856 | tf_op jit(solution)/shard_map/all_to_all | solution.py:557
  42.5 1.5 %assemble.1 = (f32[64,1024]{1,0:T(8,128)S(1)}, f32[64,1024]{1,0:T(8,128)S(1)}, f32[8,1024]{1,0:T(8,128)S(1)}, f32[8,128]{1,0:T(8,128)S(1)}, f32[64,512]{1,0:T(8,...) custom-call(s32[4]{0:T(128)S(1)} %pad_add_fusion.place_ref, ...), custom_call_target="tpu_custom_call" | custom-call | tf_op jit(solution)/shard_map/assemble/pallas_call | solution.py:310
  44.7 1.0 collective-permute-start.2
  45.8 3.3 %collective-permute-done.1.rb_ref = f32[64,512]{1,0:T(8,128)S(1)} collective-permute-done((f32[64,512]{1,0:T(8,128)S(1)}, f32[64,512]{1,0:T(8,128)S(1)}, u32[]{:S(2)}, u32[]{:S(2)}) %collective-permute-start.1) | collective-permute-done | bytes 131104 | tf_op jit(solution)/shard_map/ppermute | solution.py:541
  49.2 2.2 %collective-permute-start.4 = (f32[64,512]{1,0:T(8,128)S(1)}, f32[64,512]{1,0:T(8,128)S(1)}, u32[]{:S(2)}, u32[]{:S(2)}) collective-permute-start(f32[64,512]{1,0:T(8,128)S(1)} %pad_maximum_fusion), channel_id=1, source_target_pairs={{0,1},{1,0},{2,3},{3,2},{4,5},{5,4},{6,7},{7,6},{8,9},{9,8},{10,11... | collective-permute-start | bytes 393224 | tf_op jit(solution)/shard_map/ppermute | solution.py:549
  51.7 1.7 %sides.3.sum_ref = f32[64,1024]{1,0:T(8,128)S(1)} custom-call(s32[4]{0:T(128)S(1)} %pad_add_fusion.place_ref, f32[64,1024]{1,0:T(8,128)S(1)} %get-tuple-element.31.v_ref.v0_ref, f32[8,1024]{1,0:T(8,128)S(1)} %get-tuple-element.29.mask_ref, f32[64,512]{1,0:T(8,128)S(1)} %collective-permute-done.ra_ref, f32[64,512]{1,0:T(8,128)S(1)} %collective-permute-done.1.rb_ref, ...), custom_call_target="tpu_custom_call" | custom-call | flops 1500000000 | bytes 2000000 | tf_op jit(solution)/shard_map/sides/pallas_call | solution.py:408
  53.4 2.5 %collective-permute-done.5.cb_ref = f32[64,512]{1,0:T(8,128)S(1)} collective-permute-done((f32[64,512]{1,0:T(8,128)S(1)}, f32[64,512]{1,0:T(8,128)S(1)}, u32[]{:S(2)}, u32[]{:S(2)}) %collective-permute-start.5) | collective-permute-done | bytes 131104 | tf_op jit(solution)/shard_map/ppermute | solution.py:548
  55.8 1.3 %corners.3 = (f32[64,1024]{1,0:T(8,128)S(1)}, f32[8,128]{1,0:T(8,128)S(1)}, f32[64,512]{1,0:T(8,128)S(1)}, f32[64,512]{1,0:T(8,128)S(1)}, f32[64,512]{1,0:T(8,128)S(1)}, /*index=5*/f32[64,512]{1,0:T(8,128)S(1)}) custom-call(s32[4]{0:T(128)S(1)} %pad_add_fusion.place_ref, f32[64,1024]{1,0:T(8,128)S(1)} %sides.3.sum_ref, ...), custom_call_target="tpu_custom_call" | custom-call | flops 500000000 | bytes 2000000 | tf_op jit(solution)/shard_map/corners/pallas_call | solution.py:448
  57.1 1.8 %collective-permute-start.7 = (f32[64,512]{1,0:T(8,128)S(1)}, f32[64,512]{1,0:T(8,128)S(1)}, u32[]{:S(2)}, u32[]{:S(2)}) collective-permute-start(f32[64,512]{1,0:T(8,128)S(1)} %get-tuple-element.41), channel_id=1, source_target_pairs={{0,96},{32,64},{64,32},{96,0},{1,97},{33,65},{65,33},{97,1},{2,98}... | collective-permute-start | bytes 393224 | tf_op jit(solution)/shard_map/ppermute | solution.py:541
  58.9 3.6 %collective-permute-start.8 = (f32[64,512]{1,0:T(8,128)S(1)}, f32[64,512]{1,0:T(8,128)S(1)}, u32[]{:S(2)}, u32[]{:S(2)}) collective-permute-start(f32[64,512]{1,0:T(8,128)S(1)} %get-tuple-element.42), channel_id=1, source_target_pairs={{0,1},{1,0},{2,3},{3,2},{4,5},{5,4},{6,7},{7,6},{8,9},{9,8},{10,11... | collective-permute-start | bytes 393224 | tf_op jit(solution)/shard_map/ppermute | solution.py:542
  62.8 4.8 %collective-permute-start.10 = (f32[64,512]{1,0:T(8,128)S(1)}, f32[64,512]{1,0:T(8,128)S(1)}, u32[]{:S(2)}, u32[]{:S(2)}) collective-permute-start(f32[64,512]{1,0:T(8,128)S(1)} %pad_maximum_fusion.2), channel_id=1, source_target_pairs={{0,1},{1,0},{2,3},{3,2},{4,5},{5,4},{6,7},{7,6},{8,9},{9,8},{10,11... | collective-permute-start | bytes 393224 | tf_op jit(solution)/shard_map/ppermute | solution.py:549
  67.7 1.7 %sides.4.sum_ref = f32[64,1024]{1,0:T(8,128)S(1)} custom-call(s32[4]{0:T(128)S(1)} %pad_add_fusion.place_ref, f32[64,1024]{1,0:T(8,128)S(1)} %get-tuple-element.39.v_ref.v1_ref, f32[8,1024]{1,0:T(8,128)S(1)} %get-tuple-element.29.mask_ref, f32[64,512]{1,0:T(8,128)S(1)} %collective-permute-done.6.ra_ref, f32[64,512]{1,0:T(8,128)S(1)} %collective-permute-done.7.rb_ref, ...), custom_call_target="tpu_custom_call" | custom-call | flops 1500000000 | bytes 2000000 | tf_op jit(solution)/shard_map/sides/pallas_call | solution.py:408
  69.5 2.6 %collective-permute-done.11.cb_ref = f32[64,512]{1,0:T(8,128)S(1)} collective-permute-done((f32[64,512]{1,0:T(8,128)S(1)}, f32[64,512]{1,0:T(8,128)S(1)}, u32[]{:S(2)}, u32[]{:S(2)}) %collective-permute-start.11) | collective-permute-done | bytes 131104 | tf_op jit(solution)/shard_map/ppermute | solution.py:548
  72.1 1.3 %corners.4 = (f32[64,1024]{1,0:T(8,128)S(1)}, f32[8,128]{1,0:T(8,128)S(1)}, f32[64,512]{1,0:T(8,128)S(1)}, f32[64,512]{1,0:T(8,128)S(1)}, f32[64,512]{1,0:T(8,128)S(1)}, /*index=5*/f32[64,512]{1,0:T(8,128)S(1)}) custom-call(s32[4]{0:T(128)S(1)} %pad_add_fusion.place_ref, f32[64,1024]{1,0:T(8,128)S(1)} %sides.4.sum_ref, ...), custom_call_target="tpu_custom_call" | custom-call | flops 500000000 | bytes 2000000 | tf_op jit(solution)/shard_map/corners/pallas_call | solution.py:448
  73.4 1.0 %collective-permute-start.13 = (f32[64,512]{1,0:T(8,128)S(1)}, f32[64,512]{1,0:T(8,128)S(1)}, u32[]{:S(2)}, u32[]{:S(2)}) collective-permute-start(f32[64,512]{1,0:T(8,128)S(1)} %get-tuple-element.47), channel_id=1, source_target_pairs={{0,96},{32,64},{64,32},{96,0},{1,97},{33,65},{65,33},{97,1},{2,98}... | collective-permute-start | bytes 393224 | tf_op jit(solution)/shard_map/ppermute | solution.py:541
  74.4 3.6 %collective-permute-start.14 = (f32[64,512]{1,0:T(8,128)S(1)}, f32[64,512]{1,0:T(8,128)S(1)}, u32[]{:S(2)}, u32[]{:S(2)}) collective-permute-start(f32[64,512]{1,0:T(8,128)S(1)} %get-tuple-element.48), channel_id=1, source_target_pairs={{0,1},{1,0},{2,3},{3,2},{4,5},{5,4},{6,7},{7,6},{8,9},{9,8},{10,11... | collective-permute-start | bytes 393224 | tf_op jit(solution)/shard_map/ppermute | solution.py:542
  78.5 4.6 %collective-permute-start.16 = (f32[64,512]{1,0:T(8,128)S(1)}, f32[64,512]{1,0:T(8,128)S(1)}, u32[]{:S(2)}, u32[]{:S(2)}) collective-permute-start(f32[64,512]{1,0:T(8,128)S(1)} %pad_maximum_fusion.4), channel_id=1, source_target_pairs={{0,1},{1,0},{2,3},{3,2},{4,5},{5,4},{6,7},{7,6},{8,9},{9,8},{10,11... | collective-permute-start | bytes 393224 | tf_op jit(solution)/shard_map/ppermute | solution.py:549
  83.4 2.8 %sides.5 = (f32[64,1024]{1,0:T(8,128)S(1)}, f32[128,128]{1,0:T(8,128)}) custom-call(s32[4]{0:T(128)S(1)} %pad_add_fusion.place_ref, f32[64,1024]{1,0:T(8,128)S(1)} %get-tuple-element.45.v_ref.v2_ref, f32[8,1024]{1,0:T(8,128)S(1)} %get-tuple-element.29.mask_ref, f32[64,512]{1,0:T(8,128)S(1)} %collective-permute-done.12.ra_ref, ...), custom_call_target="tpu_custom_call" | custom-call | flops 1500000000 | bytes 2000000 | tf_op jit(solution)/shard_map/sides/pallas_call | solution.py:408
  86.2 7.3 %all-to-all-start.1 = ((f32[128,1,128]{2,1,0:T(1,128)}), f32[128,1,128]{2,1,0:T(1,128)S(1)}, u32[]{:S(2)}, u32[]{:S(2)}) async-start(f32[128,1,128]{2,1,0:T(1,128)} %bitcast.8), calls=%async_computation.1 | async-start | bytes 131072 | tf_op jit(solution)/shard_map/all_to_all | solution.py:567
  93.6 1.1 %corners.5.v3_ref = f32[64,1024]{1,0:T(8,128)S(1)} custom-call(s32[4]{0:T(128)S(1)} %pad_add_fusion.place_ref, f32[64,1024]{1,0:T(8,128)S(1)} %get-tuple-element.53.sum_ref, f32[64,1024]{1,0:T(8,128)S(1)} %get-tuple-element.45.v_ref.v2_ref, f32[64,1024]{1,0:T(8,128)S(1)} %get-tuple-element.37.diag_ref.rest_0_, f32[8,1024]{1,0:T(8,128)S(1)} %get-tuple-element.29.mask_ref, ...), custom_call_target="tpu_custom_call" | custom-call | flops 500000000 | bytes 2000000 | tf_op jit(solution)/shard_map/corners/pallas_call | solution.py:448
  94.7 8.4 %all-to-all-done.1 = f32[128,1,128]{2,1,0:T(1,128)S(1)} async-done(((f32[128,1,128]{2,1,0:T(1,128)}), f32[128,1,128]{2,1,0:T(1,128)S(1)}, u32[]{:S(2)}, u32[]{:S(2)}) %all-to-all-start.1) | async-done | bytes 65568 | tf_op jit(solution)/shard_map/all_to_all | solution.py:567
  103.1 1.4 %finish.1 = (f32[64,8,128]{2,1,0:T(8,128)}, f32[64,8,128]{2,1,0:T(8,128)}) custom-call(f32[128,128]{1,0:T(8,128)S(1)} %bitcast.22, f32[8,128]{1,0:T(8,128)S(1)} %get-tuple-element.50.rest_2_.c_ref, f32[64,1024]{1,0:T(8,128)S(1)} %get-tuple-element.31.v_ref.v0_ref, f32[64,1024]{1,0:T(8,128)S(1)} %get-tuple-element.39.v_ref.v1_ref, ...), custom_call_target="tpu_custom_call" | custom-call | tf_op jit(solution)/shard_map/finish/pallas_call | solution.py:523
  (47 shorter events, 4.2 us)
Async XLA Ops:
  0.6 27.6 %copy-start = (f32[27,64,64]{2,1,0:T(8,128)S(1)}, f32[27,64,64]{2,1,0:T(8,128)}, u32[]{:S(2)}) copy-start(f32[27,64,64]{2,1,0:T(8,128)} %coupling_ref.1) | copy-start | bytes 1327108
  0.6 0.8 copy-start.1
  1.4 0.7 copy-start.2
  2.1 26.1 %copy-start.3 = (s32[2,2,256]{2,1,0:T(2,128)S(1)}, s32[2,2,256]{2,1,0:T(2,128)}, u32[]{:S(2)}) copy-start(s32[2,2,256]{2,1,0:T(2,128)} %occ_ref.1) | copy-start | bytes 12292
  16.7 25.8 %all-to-all-start = ((f32[128,1,1152]{2,1,0:T(1,128)}), f32[128,1,1152]{2,1,0:T(1,128)S(1)}, u32[]{:S(2)}, u32[]{:S(2)}) async-start(f32[128,1,1152]{2,1,0:T(1,128)} %bitcast.5), calls=%async_computation | async-start | bytes 1179648 | tf_op jit(solution)/shard_map/all_to_all | solution.py:557
  44.0 5.1 %collective-permute-start.1 = (f32[64,512]{1,0:T(8,128)S(1)}, f32[64,512]{1,0:T(8,128)S(1)}, u32[]{:S(2)}, u32[]{:S(2)}) collective-permute-start(f32[64,512]{1,0:T(8,128)S(1)} %get-tuple-element.33), channel_id=1, source_target_pairs={{0,96},{32,64},{64,32},{96,0},{1,97},{33,65},{65,33},{97,1},{2,98}... | collective-permute-start | bytes 393224 | tf_op jit(solution)/shard_map/ppermute | solution.py:541
  44.4 4.7 %collective-permute-start = (f32[64,512]{1,0:T(8,128)S(1)}, f32[64,512]{1,0:T(8,128)S(1)}, u32[]{:S(2)}, u32[]{:S(2)}) collective-permute-start(f32[64,512]{1,0:T(8,128)S(1)} %get-tuple-element.32), channel_id=1, source_target_pairs={{0,32},{32,0},{64,96},{96,64},{1,33},{33,1},{65,97},{97,65},{2,34}... | collective-permute-start | bytes 393224 | tf_op jit(solution)/shard_map/ppermute | solution.py:540
  44.7 6.9 %collective-permute-start.2 = (f32[64,512]{1,0:T(8,128)S(1)}, f32[64,512]{1,0:T(8,128)S(1)}, u32[]{:S(2)}, u32[]{:S(2)}) collective-permute-start(f32[64,512]{1,0:T(8,128)S(1)} %get-tuple-element.34), channel_id=1, source_target_pairs={{0,1},{1,0},{2,3},{3,2},{4,5},{5,4},{6,7},{7,6},{8,9},{9,8},{10,11... | collective-permute-start | bytes 393224 | tf_op jit(solution)/shard_map/ppermute | solution.py:542
  45.7 6.0 %collective-permute-start.3 = (f32[64,512]{1,0:T(8,128)S(1)}, f32[64,512]{1,0:T(8,128)S(1)}, u32[]{:S(2)}, u32[]{:S(2)}) collective-permute-start(f32[64,512]{1,0:T(8,128)S(1)} %get-tuple-element.35), channel_id=1, source_target_pairs={{0,31},{1,2},{2,1},{3,4},{4,3},{5,6},{6,5},{7,8},{8,7},{9,10},{10,... | collective-permute-start | bytes 393224 | tf_op jit(solution)/shard_map/ppermute | solution.py:539
  49.2 4.2 %collective-permute-start.4 = (f32[64,512]{1,0:T(8,128)S(1)}, f32[64,512]{1,0:T(8,128)S(1)}, u32[]{:S(2)}, u32[]{:S(2)}) collective-permute-start(f32[64,512]{1,0:T(8,128)S(1)} %pad_maximum_fusion), channel_id=1, source_target_pairs={{0,1},{1,0},{2,3},{3,2},{4,5},{5,4},{6,7},{7,6},{8,9},{9,8},{10,11... | collective-permute-start | bytes 393224 | tf_op jit(solution)/shard_map/ppermute | solution.py:549
  51.4 4.5 %collective-permute-start.5 = (f32[64,512]{1,0:T(8,128)S(1)}, f32[64,512]{1,0:T(8,128)S(1)}, u32[]{:S(2)}, u32[]{:S(2)}) collective-permute-start(f32[64,512]{1,0:T(8,128)S(1)} %pad_maximum_fusion.1), channel_id=1, source_target_pairs={{0,31},{1,2},{2,1},{3,4},{4,3},{5,6},{6,5},{7,8},{8,7},{9,10},{10,... | collective-permute-start | bytes 393224 | tf_op jit(solution)/shard_map/ppermute | solution.py:548
  57.1 5.4 %collective-permute-start.7 = (f32[64,512]{1,0:T(8,128)S(1)}, f32[64,512]{1,0:T(8,128)S(1)}, u32[]{:S(2)}, u32[]{:S(2)}) collective-permute-start(f32[64,512]{1,0:T(8,128)S(1)} %get-tuple-element.41), channel_id=1, source_target_pairs={{0,96},{32,64},{64,32},{96,0},{1,97},{33,65},{65,33},{97,1},{2,98}... | collective-permute-start | bytes 393224 | tf_op jit(solution)/shard_map/ppermute | solution.py:541
  58.9 3.8 %collective-permute-start.6 = (f32[64,512]{1,0:T(8,128)S(1)}, f32[64,512]{1,0:T(8,128)S(1)}, u32[]{:S(2)}, u32[]{:S(2)}) collective-permute-start(f32[64,512]{1,0:T(8,128)S(1)} %get-tuple-element.40), channel_id=1, source_target_pairs={{0,32},{32,0},{64,96},{96,64},{1,33},{33,1},{65,97},{97,65},{2,34}... | collective-permute-start | bytes 393224 | tf_op jit(solution)/shard_map/ppermute | solution.py:540
  58.9 8.8 %collective-permute-start.8 = (f32[64,512]{1,0:T(8,128)S(1)}, f32[64,512]{1,0:T(8,128)S(1)}, u32[]{:S(2)}, u32[]{:S(2)}) collective-permute-start(f32[64,512]{1,0:T(8,128)S(1)} %get-tuple-element.42), channel_id=1, source_target_pairs={{0,1},{1,0},{2,3},{3,2},{4,5},{5,4},{6,7},{7,6},{8,9},{9,8},{10,11... | collective-permute-start | bytes 393224 | tf_op jit(solution)/shard_map/ppermute | solution.py:542
  62.5 5.2 %collective-permute-start.9 = (f32[64,512]{1,0:T(8,128)S(1)}, f32[64,512]{1,0:T(8,128)S(1)}, u32[]{:S(2)}, u32[]{:S(2)}) collective-permute-start(f32[64,512]{1,0:T(8,128)S(1)} %get-tuple-element.43), channel_id=1, source_target_pairs={{0,31},{1,2},{2,1},{3,4},{4,3},{5,6},{6,5},{7,8},{8,7},{9,10},{10,... | collective-permute-start | bytes 393224 | tf_op jit(solution)/shard_map/ppermute | solution.py:539
  62.8 6.7 %collective-permute-start.10 = (f32[64,512]{1,0:T(8,128)S(1)}, f32[64,512]{1,0:T(8,128)S(1)}, u32[]{:S(2)}, u32[]{:S(2)}) collective-permute-start(f32[64,512]{1,0:T(8,128)S(1)} %pad_maximum_fusion.2), channel_id=1, source_target_pairs={{0,1},{1,0},{2,3},{3,2},{4,5},{5,4},{6,7},{7,6},{8,9},{9,8},{10,11... | collective-permute-start | bytes 393224 | tf_op jit(solution)/shard_map/ppermute | solution.py:549
  67.6 4.5 %collective-permute-start.11 = (f32[64,512]{1,0:T(8,128)S(1)}, f32[64,512]{1,0:T(8,128)S(1)}, u32[]{:S(2)}, u32[]{:S(2)}) collective-permute-start(f32[64,512]{1,0:T(8,128)S(1)} %pad_maximum_fusion.3), channel_id=1, source_target_pairs={{0,31},{1,2},{2,1},{3,4},{4,3},{5,6},{6,5},{7,8},{8,7},{9,10},{10,... | collective-permute-start | bytes 393224 | tf_op jit(solution)/shard_map/ppermute | solution.py:548
  73.4 5.1 %collective-permute-start.13 = (f32[64,512]{1,0:T(8,128)S(1)}, f32[64,512]{1,0:T(8,128)S(1)}, u32[]{:S(2)}, u32[]{:S(2)}) collective-permute-start(f32[64,512]{1,0:T(8,128)S(1)} %get-tuple-element.47), channel_id=1, source_target_pairs={{0,96},{32,64},{64,32},{96,0},{1,97},{33,65},{65,33},{97,1},{2,98}... | collective-permute-start | bytes 393224 | tf_op jit(solution)/shard_map/ppermute | solution.py:541
  74.4 4.1 %collective-permute-start.12 = (f32[64,512]{1,0:T(8,128)S(1)}, f32[64,512]{1,0:T(8,128)S(1)}, u32[]{:S(2)}, u32[]{:S(2)}) collective-permute-start(f32[64,512]{1,0:T(8,128)S(1)} %get-tuple-element.46), channel_id=1, source_target_pairs={{0,32},{32,0},{64,96},{96,64},{1,33},{33,1},{65,97},{97,65},{2,34}... | collective-permute-start | bytes 393224 | tf_op jit(solution)/shard_map/ppermute | solution.py:540
  74.4 9.0 %collective-permute-start.14 = (f32[64,512]{1,0:T(8,128)S(1)}, f32[64,512]{1,0:T(8,128)S(1)}, u32[]{:S(2)}, u32[]{:S(2)}) collective-permute-start(f32[64,512]{1,0:T(8,128)S(1)} %get-tuple-element.48), channel_id=1, source_target_pairs={{0,1},{1,0},{2,3},{3,2},{4,5},{5,4},{6,7},{7,6},{8,9},{9,8},{10,11... | collective-permute-start | bytes 393224 | tf_op jit(solution)/shard_map/ppermute | solution.py:542
  78.0 5.4 %collective-permute-start.15 = (f32[64,512]{1,0:T(8,128)S(1)}, f32[64,512]{1,0:T(8,128)S(1)}, u32[]{:S(2)}, u32[]{:S(2)}) collective-permute-start(f32[64,512]{1,0:T(8,128)S(1)} %get-tuple-element.49), channel_id=1, source_target_pairs={{0,31},{1,2},{2,1},{3,4},{4,3},{5,6},{6,5},{7,8},{8,7},{9,10},{10,... | collective-permute-start | bytes 393224 | tf_op jit(solution)/shard_map/ppermute | solution.py:539
  78.5 15.0 %collective-permute-start.16 = (f32[64,512]{1,0:T(8,128)S(1)}, f32[64,512]{1,0:T(8,128)S(1)}, u32[]{:S(2)}, u32[]{:S(2)}) collective-permute-start(f32[64,512]{1,0:T(8,128)S(1)} %pad_maximum_fusion.4), channel_id=1, source_target_pairs={{0,1},{1,0},{2,3},{3,2},{4,5},{5,4},{6,7},{7,6},{8,9},{9,8},{10,11... | collective-permute-start | bytes 393224 | tf_op jit(solution)/shard_map/ppermute | solution.py:549
  83.1 10.4 %collective-permute-start.17 = (f32[64,512]{1,0:T(8,128)S(1)}, f32[64,512]{1,0:T(8,128)S(1)}, u32[]{:S(2)}, u32[]{:S(2)}) collective-permute-start(f32[64,512]{1,0:T(8,128)S(1)} %pad_maximum_fusion.5), channel_id=1, source_target_pairs={{0,31},{1,2},{2,1},{3,4},{4,3},{5,6},{6,5},{7,8},{8,7},{9,10},{10,... | collective-permute-start | bytes 393224 | tf_op jit(solution)/shard_map/ppermute | solution.py:548
  86.2 16.9 %all-to-all-start.1 = ((f32[128,1,128]{2,1,0:T(1,128)}), f32[128,1,128]{2,1,0:T(1,128)S(1)}, u32[]{:S(2)}, u32[]{:S(2)}) async-start(f32[128,1,128]{2,1,0:T(1,128)} %bitcast.8), calls=%async_computation.1 | async-start | bytes 131072 | tf_op jit(solution)/shard_map/all_to_all | solution.py:567

commit v7 on v6

--- a/solution.py
+++ b/solution.py
@@ -535,8 +535,20 @@
     return [(i, (i + 1 if (i - first) % 2 == 0 else i - 1) % count) for i in range(count)]
 
 
+def odd_swap():
+    slabs, grps = lax.axis_size("slab"), lax.axis_size("grp")
+    pairs = []
+    for s in range(slabs):
+        for g in range(grps):
+            if g in (0, grps - 1):
+                pairs.append((s * grps + g, (s ^ 1) * grps + g))
+            else:
+                pairs.append((s * grps + g, s * grps + (g + 1 if g % 2 else g - 1)))
+    return pairs
+
+
 def exchange(grp, ea, eb, oa, ob):
-    yb = lax.ppermute(ob, "grp", swap("grp", 1))
+    yb = lax.ppermute(ob, AXES, odd_swap())
     ra = lax.ppermute(ea, "slab", swap("slab", 0))
     rb = lax.ppermute(eb, "slab", swap("slab", 1))
     ya = lax.ppermute(oa, "grp", swap("grp", 0))
@@ -545,7 +557,7 @@
     def line(upper):
         return jnp.concatenate([jnp.where(upper, r[:, BZ:], r[:, :BZ]) for r in (ra, rb)], axis=1)
 
-    cb = lax.ppermute(line(jnp.logical_not(up)), "grp", swap("grp", 1))
+    cb = lax.ppermute(line(jnp.logical_not(up)), AXES, odd_swap())
     ca = lax.ppermute(line(up), "grp", swap("grp", 0))
     return ra, rb, ya, yb, ca, cb
 

time: 105 us -> 101 us (0.962)
  starting transfers between devices: 43 us -> 32.1 us
  waiting for transfers between devices: 31.2 us -> 38.6 us
    ppermute x3, waiting for transfers between devices: 3.72 us -> 10.7 us  [exchange(): rb = lax.ppermute(eb, 'slab', swap('slab', 1))]
    ppermute x3, starting transfers between devices: 11.6 us -> 5.14 us  [exchange(): ca = lax.ppermute(line(up), 'grp', swap('grp', 0))]
    ppermute x3, starting transfers between devices: 8.21 us -> 2.32 us  [exchange(): ya = lax.ppermute(oa, 'grp', swap('grp', 0))]
    all_to_all x1, starting transfers between devices: 7.35 us -> 8.57 us  [on_device(): lax.all_to_all(moments.reshape(SENDERS, 1, 128), AXES, split_axis=0, conc...]
  transfers between devices with their start and end apart: 20 -> 20, of which waited for: 7 -> 8; matrix products, arithmetic and copies ran while one was open for 0% -> 0% of each run, Pallas kernels for 7% -> 8%
where the time goes in v7:
time: 101 us
  waiting for transfers between devices  38.6 us (38%)
  starting transfers between devices  32.1 us (32%)
  Pallas kernels  27.7 us (27%)
  local copies, waits for them, and re-layouts  1.45 us (1%)
    pallas_call x1, Pallas kernels, splat(): pl.pallas_call(splat_kernel, name='splat', in_specs=[pl.BlockSpec(memory_...  14.6 us
    all_to_all x1, waiting for transfers between devices, on_device(): lax.all_to_all(payload.reshape(SENDERS, 1, ROWS * 128), AXES, split_axis=...  13.8 us
    all_to_all x1, starting transfers between devices, on_device(): lax.all_to_all(payload.reshape(SENDERS, 1, ROWS * 128), AXES, split_axis=...  11.5 us
    ppermute x3, waiting for transfers between devices, exchange(): rb = lax.ppermute(eb, 'slab', swap('slab', 1))  10.7 us
    all_to_all x1, starting transfers between devices, on_device(): lax.all_to_all(moments.reshape(SENDERS, 1, 128), AXES, split_axis=0, conc...  8.57 us
    all_to_all x1, waiting for transfers between devices, on_device(): lax.all_to_all(moments.reshape(SENDERS, 1, 128), AXES, split_axis=0, conc...  8.42 us
    pallas_call x3, Pallas kernels, sides(): pl.pallas_call(functools.partial(sides_kernel, last), name='sides', in_sp...  6.19 us
    ppermute x3, waiting for transfers between devices, exchange(): cb = lax.ppermute(line(jnp.logical_not(up)), AXES, odd_swap())  5.5 us
  transfers between devices with their start and end apart: 20, of which 8 were waited for; matrix products, arithmetic and copies ran while one was open for 0% of the time, Pallas kernels for 8%

profile of v7, /device:TPU:1, one launch (start us, length us, event | category | flops | bytes accessed | tf_op | source)
XLA Modules:
  0.0 101.1 jit_solution(3255710538940395746)
XLA Ops:
  2.1 14.6 %splat.1 = f32[8,144,128]{2,1,0:T(8,128)} custom-call(f32[6,1024,128]{2,1,0:T(8,128)} %bitcast.25, s32[8,128]{1,0:T(8,128)S(1)} %bitcast.23, s32[8,128]{1,0:T(8,128)S(1)} %bitcast.24), custom_call_target="tpu_custom_call" | custom-call | tf_op jit(solution)/shard_map/splat/pallas_call | solution.py:165
  16.7 11.5 %all-to-all-start = ((f32[128,1,1152]{2,1,0:T(1,128)}), f32[128,1,1152]{2,1,0:T(1,128)S(1)}, u32[]{:S(2)}, u32[]{:S(2)}) async-start(f32[128,1,1152]{2,1,0:T(1,128)} %bitcast.5), calls=%async_computation | async-start | bytes 1179648 | tf_op jit(solution)/shard_map/all_to_all | solution.py:569
  28.8 13.8 %all-to-all-done = f32[128,1,1152]{2,1,0:T(1,128)S(1)} async-done(((f32[128,1,1152]{2,1,0:T(1,128)}), f32[128,1,1152]{2,1,0:T(1,128)S(1)}, u32[]{:S(2)}, u32[]{:S(2)}) %all-to-all-start) | async-done | bytes 589856 | tf_op jit(solution)/shard_map/all_to_all | solution.py:569
  42.5 1.5 %assemble.1 = (f32[64,1024]{1,0:T(8,128)S(1)}, f32[64,1024]{1,0:T(8,128)S(1)}, f32[8,1024]{1,0:T(8,128)S(1)}, f32[8,128]{1,0:T(8,128)S(1)}, f32[64,512]{1,0:T(8,...) custom-call(s32[4]{0:T(128)S(1)} %pad_add_fusion.place_ref, ...), custom_call_target="tpu_custom_call" | custom-call | tf_op jit(solution)/shard_map/assemble/pallas_call | solution.py:310
  44.7 1.0 collective-permute-start.2
  45.8 3.3 %collective-permute-done.1.rb_ref = f32[64,512]{1,0:T(8,128)S(1)} collective-permute-done((f32[64,512]{1,0:T(8,128)S(1)}, f32[64,512]{1,0:T(8,128)S(1)}, u32[]{:S(2)}, u32[]{:S(2)}) %collective-permute-start.1) | collective-permute-done | bytes 131104 | tf_op jit(solution)/shard_map/ppermute | solution.py:553
  49.2 2.2 %collective-permute-start.4 = (f32[64,512]{1,0:T(8,128)S(1)}, f32[64,512]{1,0:T(8,128)S(1)}, u32[]{:S(2)}, u32[]{:S(2)}) collective-permute-start(f32[64,512]{1,0:T(8,128)S(1)} %pad_maximum_fusion), channel_id=1, source_target_pairs={{0,1},{1,0},{2,3},{3,2},{4,5},{5,4},{6,7},{7,6},{8,9},{9,8},{10,11... | collective-permute-start | bytes 393224 | tf_op jit(solution)/shard_map/ppermute | solution.py:561
  51.7 1.7 %sides.3.sum_ref = f32[64,1024]{1,0:T(8,128)S(1)} custom-call(s32[4]{0:T(128)S(1)} %pad_add_fusion.place_ref, f32[64,1024]{1,0:T(8,128)S(1)} %get-tuple-element.31.v_ref.v0_ref, f32[8,1024]{1,0:T(8,128)S(1)} %get-tuple-element.29.mask_ref, f32[64,512]{1,0:T(8,128)S(1)} %collective-permute-done.ra_ref, f32[64,512]{1,0:T(8,128)S(1)} %collective-permute-done.1.rb_ref, ...), custom_call_target="tpu_custom_call" | custom-call | flops 1500000000 | bytes 2000000 | tf_op jit(solution)/shard_map/sides/pallas_call | solution.py:408
  53.4 2.7 %collective-permute-done.5.cb_ref = f32[64,512]{1,0:T(8,128)S(1)} collective-permute-done((f32[64,512]{1,0:T(8,128)S(1)}, f32[64,512]{1,0:T(8,128)S(1)}, u32[]{:S(2)}, u32[]{:S(2)}) %collective-permute-start.5) | collective-permute-done | bytes 131104 | tf_op jit(solution)/shard_map/ppermute | solution.py:560
  56.0 1.3 %corners.3 = (f32[64,1024]{1,0:T(8,128)S(1)}, f32[8,128]{1,0:T(8,128)S(1)}, f32[64,512]{1,0:T(8,128)S(1)}, f32[64,512]{1,0:T(8,128)S(1)}, f32[64,512]{1,0:T(8,128)S(1)}, /*index=5*/f32[64,512]{1,0:T(8,128)S(1)}) custom-call(s32[4]{0:T(128)S(1)} %pad_add_fusion.place_ref, f32[64,1024]{1,0:T(8,128)S(1)} %sides.3.sum_ref, ...), custom_call_target="tpu_custom_call" | custom-call | flops 500000000 | bytes 2000000 | tf_op jit(solution)/shard_map/corners/pallas_call | solution.py:448
  57.3 1.8 %collective-permute-start.7 = (f32[64,512]{1,0:T(8,128)S(1)}, f32[64,512]{1,0:T(8,128)S(1)}, u32[]{:S(2)}, u32[]{:S(2)}) collective-permute-start(f32[64,512]{1,0:T(8,128)S(1)} %get-tuple-element.41), channel_id=1, source_target_pairs={{0,96},{32,64},{64,32},{96,0},{1,97},{33,65},{65,33},{97,1},{2,98}... | collective-permute-start | bytes 393224 | tf_op jit(solution)/shard_map/ppermute | solution.py:553
  59.8 3.5 %collective-permute-done.7.rb_ref = f32[64,512]{1,0:T(8,128)S(1)} collective-permute-done((f32[64,512]{1,0:T(8,128)S(1)}, f32[64,512]{1,0:T(8,128)S(1)}, u32[]{:S(2)}, u32[]{:S(2)}) %collective-permute-start.7) | collective-permute-done | bytes 131104 | tf_op jit(solution)/shard_map/ppermute | solution.py:553
  63.5 1.6 %collective-permute-start.10 = (f32[64,512]{1,0:T(8,128)S(1)}, f32[64,512]{1,0:T(8,128)S(1)}, u32[]{:S(2)}, u32[]{:S(2)}) collective-permute-start(f32[64,512]{1,0:T(8,128)S(1)} %pad_maximum_fusion.2), channel_id=1, source_target_pairs={{0,1},{1,0},{2,3},{3,2},{4,5},{5,4},{6,7},{7,6},{8,9},{9,8},{10,11... | collective-permute-start | bytes 393224 | tf_op jit(solution)/shard_map/ppermute | solution.py:561
  65.3 1.7 %sides.4.sum_ref = f32[64,1024]{1,0:T(8,128)S(1)} custom-call(s32[4]{0:T(128)S(1)} %pad_add_fusion.place_ref, f32[64,1024]{1,0:T(8,128)S(1)} %get-tuple-element.39.v_ref.v1_ref, f32[8,1024]{1,0:T(8,128)S(1)} %get-tuple-element.29.mask_ref, f32[64,512]{1,0:T(8,128)S(1)} %collective-permute-done.6.ra_ref, f32[64,512]{1,0:T(8,128)S(1)} %collective-permute-done.7.rb_ref, ...), custom_call_target="tpu_custom_call" | custom-call | flops 1500000000 | bytes 2000000 | tf_op jit(solution)/shard_map/sides/pallas_call | solution.py:408
  67.0 2.8 %collective-permute-done.11.cb_ref = f32[64,512]{1,0:T(8,128)S(1)} collective-permute-done((f32[64,512]{1,0:T(8,128)S(1)}, f32[64,512]{1,0:T(8,128)S(1)}, u32[]{:S(2)}, u32[]{:S(2)}) %collective-permute-start.11) | collective-permute-done | bytes 131104 | tf_op jit(solution)/shard_map/ppermute | solution.py:560
  69.8 1.3 %corners.4 = (f32[64,1024]{1,0:T(8,128)S(1)}, f32[8,128]{1,0:T(8,128)S(1)}, f32[64,512]{1,0:T(8,128)S(1)}, f32[64,512]{1,0:T(8,128)S(1)}, f32[64,512]{1,0:T(8,128)S(1)}, /*index=5*/f32[64,512]{1,0:T(8,128)S(1)}) custom-call(s32[4]{0:T(128)S(1)} %pad_add_fusion.place_ref, f32[64,1024]{1,0:T(8,128)S(1)} %sides.4.sum_ref, ...), custom_call_target="tpu_custom_call" | custom-call | flops 500000000 | bytes 2000000 | tf_op jit(solution)/shard_map/corners/pallas_call | solution.py:448
  71.1 1.3 %collective-permute-start.13 = (f32[64,512]{1,0:T(8,128)S(1)}, f32[64,512]{1,0:T(8,128)S(1)}, u32[]{:S(2)}, u32[]{:S(2)}) collective-permute-start(f32[64,512]{1,0:T(8,128)S(1)} %get-tuple-element.47), channel_id=1, source_target_pairs={{0,96},{32,64},{64,32},{96,0},{1,97},{33,65},{65,33},{97,1},{2,98}... | collective-permute-start | bytes 393224 | tf_op jit(solution)/shard_map/ppermute | solution.py:553
  73.1 3.9 %collective-permute-done.13.rb_ref = f32[64,512]{1,0:T(8,128)S(1)} collective-permute-done((f32[64,512]{1,0:T(8,128)S(1)}, f32[64,512]{1,0:T(8,128)S(1)}, u32[]{:S(2)}, u32[]{:S(2)}) %collective-permute-start.13) | collective-permute-done | bytes 131104 | tf_op jit(solution)/shard_map/ppermute | solution.py:553
  77.1 1.3 %collective-permute-start.16 = (f32[64,512]{1,0:T(8,128)S(1)}, f32[64,512]{1,0:T(8,128)S(1)}, u32[]{:S(2)}, u32[]{:S(2)}) collective-permute-start(f32[64,512]{1,0:T(8,128)S(1)} %pad_maximum_fusion.4), channel_id=1, source_target_pairs={{0,1},{1,0},{2,3},{3,2},{4,5},{5,4},{6,7},{7,6},{8,9},{9,8},{10,11... | collective-permute-start | bytes 393224 | tf_op jit(solution)/shard_map/ppermute | solution.py:561
  78.7 2.8 %sides.5 = (f32[64,1024]{1,0:T(8,128)S(1)}, f32[128,128]{1,0:T(8,128)}) custom-call(s32[4]{0:T(128)S(1)} %pad_add_fusion.place_ref, f32[64,1024]{1,0:T(8,128)S(1)} %get-tuple-element.45.v_ref.v2_ref, f32[8,1024]{1,0:T(8,128)S(1)} %get-tuple-element.29.mask_ref, f32[64,512]{1,0:T(8,128)S(1)} %collective-permute-done.12.ra_ref, ...), custom_call_target="tpu_custom_call" | custom-call | flops 1500000000 | bytes 2000000 | tf_op jit(solution)/shard_map/sides/pallas_call | solution.py:408
  81.5 8.6 %all-to-all-start.1 = ((f32[128,1,128]{2,1,0:T(1,128)}), f32[128,1,128]{2,1,0:T(1,128)S(1)}, u32[]{:S(2)}, u32[]{:S(2)}) async-start(f32[128,1,128]{2,1,0:T(1,128)} %bitcast.8), calls=%async_computation.1 | async-start | bytes 131072 | tf_op jit(solution)/shard_map/all_to_all | solution.py:579
  90.1 1.1 %corners.5.v3_ref = f32[64,1024]{1,0:T(8,128)S(1)} custom-call(s32[4]{0:T(128)S(1)} %pad_add_fusion.place_ref, f32[64,1024]{1,0:T(8,128)S(1)} %get-tuple-element.53.sum_ref, f32[64,1024]{1,0:T(8,128)S(1)} %get-tuple-element.45.v_ref.v2_ref, f32[64,1024]{1,0:T(8,128)S(1)} %get-tuple-element.37.diag_ref.rest_0_, f32[8,1024]{1,0:T(8,128)S(1)} %get-tuple-element.29.mask_ref, ...), custom_call_target="tpu_custom_call" | custom-call | flops 500000000 | bytes 2000000 | tf_op jit(solution)/shard_map/corners/pallas_call | solution.py:448
  91.2 8.4 %all-to-all-done.1 = f32[128,1,128]{2,1,0:T(1,128)S(1)} async-done(((f32[128,1,128]{2,1,0:T(1,128)}), f32[128,1,128]{2,1,0:T(1,128)S(1)}, u32[]{:S(2)}, u32[]{:S(2)}) %all-to-all-start.1) | async-done | bytes 65568 | tf_op jit(solution)/shard_map/all_to_all | solution.py:579
  99.7 1.4 %finish.1 = (f32[64,8,128]{2,1,0:T(8,128)}, f32[64,8,128]{2,1,0:T(8,128)}) custom-call(f32[128,128]{1,0:T(8,128)S(1)} %bitcast.22, f32[8,128]{1,0:T(8,128)S(1)} %get-tuple-element.50.rest_2_.c_ref, f32[64,1024]{1,0:T(8,128)S(1)} %get-tuple-element.31.v_ref.v0_ref, f32[64,1024]{1,0:T(8,128)S(1)} %get-tuple-element.39.v_ref.v1_ref, ...), custom_call_target="tpu_custom_call" | custom-call | tf_op jit(solution)/shard_map/finish/pallas_call | solution.py:523
  (47 shorter events, 5.2 us)
Async XLA Ops:
  0.6 27.6 %copy-start = (f32[27,64,64]{2,1,0:T(8,128)S(1)}, f32[27,64,64]{2,1,0:T(8,128)}, u32[]{:S(2)}) copy-start(f32[27,64,64]{2,1,0:T(8,128)} %coupling_ref.1) | copy-start | bytes 1327108
  0.6 0.8 copy-start.1
  1.4 0.7 copy-start.2
  2.1 26.1 %copy-start.3 = (s32[2,2,256]{2,1,0:T(2,128)S(1)}, s32[2,2,256]{2,1,0:T(2,128)}, u32[]{:S(2)}) copy-start(s32[2,2,256]{2,1,0:T(2,128)} %occ_ref.1) | copy-start | bytes 12292
  16.7 25.8 %all-to-all-start = ((f32[128,1,1152]{2,1,0:T(1,128)}), f32[128,1,1152]{2,1,0:T(1,128)S(1)}, u32[]{:S(2)}, u32[]{:S(2)}) async-start(f32[128,1,1152]{2,1,0:T(1,128)} %bitcast.5), calls=%async_computation | async-start | bytes 1179648 | tf_op jit(solution)/shard_map/all_to_all | solution.py:569
  44.0 5.1 %collective-permute-start.1 = (f32[64,512]{1,0:T(8,128)S(1)}, f32[64,512]{1,0:T(8,128)S(1)}, u32[]{:S(2)}, u32[]{:S(2)}) collective-permute-start(f32[64,512]{1,0:T(8,128)S(1)} %get-tuple-element.33), channel_id=1, source_target_pairs={{0,96},{32,64},{64,32},{96,0},{1,97},{33,65},{65,33},{97,1},{2,98}... | collective-permute-start | bytes 393224 | tf_op jit(solution)/shard_map/ppermute | solution.py:553
  44.4 4.7 %collective-permute-start = (f32[64,512]{1,0:T(8,128)S(1)}, f32[64,512]{1,0:T(8,128)S(1)}, u32[]{:S(2)}, u32[]{:S(2)}) collective-permute-start(f32[64,512]{1,0:T(8,128)S(1)} %get-tuple-element.32), channel_id=1, source_target_pairs={{0,32},{32,0},{64,96},{96,64},{1,33},{33,1},{65,97},{97,65},{2,34}... | collective-permute-start | bytes 393224 | tf_op jit(solution)/shard_map/ppermute | solution.py:552
  44.7 6.9 %collective-permute-start.2 = (f32[64,512]{1,0:T(8,128)S(1)}, f32[64,512]{1,0:T(8,128)S(1)}, u32[]{:S(2)}, u32[]{:S(2)}) collective-permute-start(f32[64,512]{1,0:T(8,128)S(1)} %get-tuple-element.34), channel_id=1, source_target_pairs={{0,1},{1,0},{2,3},{3,2},{4,5},{5,4},{6,7},{7,6},{8,9},{9,8},{10,11... | collective-permute-start | bytes 393224 | tf_op jit(solution)/shard_map/ppermute | solution.py:554
  45.7 6.0 %collective-permute-start.3 = (f32[64,512]{1,0:T(8,128)S(1)}, f32[64,512]{1,0:T(8,128)S(1)}, u32[]{:S(2)}, u32[]{:S(2)}) collective-permute-start(f32[64,512]{1,0:T(8,128)S(1)} %get-tuple-element.35), channel_id=1, source_target_pairs={{0,32},{1,2},{2,1},{3,4},{4,3},{5,6},{6,5},{7,8},{8,7},{9,10},{10,... | collective-permute-start | bytes 393224 | tf_op jit(solution)/shard_map/ppermute | solution.py:551
  49.2 4.2 %collective-permute-start.4 = (f32[64,512]{1,0:T(8,128)S(1)}, f32[64,512]{1,0:T(8,128)S(1)}, u32[]{:S(2)}, u32[]{:S(2)}) collective-permute-start(f32[64,512]{1,0:T(8,128)S(1)} %pad_maximum_fusion), channel_id=1, source_target_pairs={{0,1},{1,0},{2,3},{3,2},{4,5},{5,4},{6,7},{7,6},{8,9},{9,8},{10,11... | collective-permute-start | bytes 393224 | tf_op jit(solution)/shard_map/ppermute | solution.py:561
  51.4 4.7 %collective-permute-start.5 = (f32[64,512]{1,0:T(8,128)S(1)}, f32[64,512]{1,0:T(8,128)S(1)}, u32[]{:S(2)}, u32[]{:S(2)}) collective-permute-start(f32[64,512]{1,0:T(8,128)S(1)} %pad_maximum_fusion.1), channel_id=1, source_target_pairs={{0,32},{1,2},{2,1},{3,4},{4,3},{5,6},{6,5},{7,8},{8,7},{9,10},{10,... | collective-permute-start | bytes 393224 | tf_op jit(solution)/shard_map/ppermute | solution.py:560
  57.3 6.0 %collective-permute-start.7 = (f32[64,512]{1,0:T(8,128)S(1)}, f32[64,512]{1,0:T(8,128)S(1)}, u32[]{:S(2)}, u32[]{:S(2)}) collective-permute-start(f32[64,512]{1,0:T(8,128)S(1)} %get-tuple-element.41), channel_id=1, source_target_pairs={{0,96},{32,64},{64,32},{96,0},{1,97},{33,65},{65,33},{97,1},{2,98}... | collective-permute-start | bytes 393224 | tf_op jit(solution)/shard_map/ppermute | solution.py:553
  59.1 4.4 %collective-permute-start.6 = (f32[64,512]{1,0:T(8,128)S(1)}, f32[64,512]{1,0:T(8,128)S(1)}, u32[]{:S(2)}, u32[]{:S(2)}) collective-permute-start(f32[64,512]{1,0:T(8,128)S(1)} %get-tuple-element.40), channel_id=1, source_target_pairs={{0,32},{32,0},{64,96},{96,64},{1,33},{33,1},{65,97},{97,65},{2,34}... | collective-permute-start | bytes 393224 | tf_op jit(solution)/shard_map/ppermute | solution.py:552
  59.1 6.1 %collective-permute-start.8 = (f32[64,512]{1,0:T(8,128)S(1)}, f32[64,512]{1,0:T(8,128)S(1)}, u32[]{:S(2)}, u32[]{:S(2)}) collective-permute-start(f32[64,512]{1,0:T(8,128)S(1)} %get-tuple-element.42), channel_id=1, source_target_pairs={{0,1},{1,0},{2,3},{3,2},{4,5},{5,4},{6,7},{7,6},{8,9},{9,8},{10,11... | collective-permute-start | bytes 393224 | tf_op jit(solution)/shard_map/ppermute | solution.py:554
  59.8 5.5 %collective-permute-start.9 = (f32[64,512]{1,0:T(8,128)S(1)}, f32[64,512]{1,0:T(8,128)S(1)}, u32[]{:S(2)}, u32[]{:S(2)}) collective-permute-start(f32[64,512]{1,0:T(8,128)S(1)} %get-tuple-element.43), channel_id=1, source_target_pairs={{0,32},{1,2},{2,1},{3,4},{4,3},{5,6},{6,5},{7,8},{8,7},{9,10},{10,... | collective-permute-start | bytes 393224 | tf_op jit(solution)/shard_map/ppermute | solution.py:551
  63.5 3.5 %collective-permute-start.10 = (f32[64,512]{1,0:T(8,128)S(1)}, f32[64,512]{1,0:T(8,128)S(1)}, u32[]{:S(2)}, u32[]{:S(2)}) collective-permute-start(f32[64,512]{1,0:T(8,128)S(1)} %pad_maximum_fusion.2), channel_id=1, source_target_pairs={{0,1},{1,0},{2,3},{3,2},{4,5},{5,4},{6,7},{7,6},{8,9},{9,8},{10,11... | collective-permute-start | bytes 393224 | tf_op jit(solution)/shard_map/ppermute | solution.py:561
  65.1 4.7 %collective-permute-start.11 = (f32[64,512]{1,0:T(8,128)S(1)}, f32[64,512]{1,0:T(8,128)S(1)}, u32[]{:S(2)}, u32[]{:S(2)}) collective-permute-start(f32[64,512]{1,0:T(8,128)S(1)} %pad_maximum_fusion.3), channel_id=1, source_target_pairs={{0,32},{1,2},{2,1},{3,4},{4,3},{5,6},{6,5},{7,8},{8,7},{9,10},{10,... | collective-permute-start | bytes 393224 | tf_op jit(solution)/shard_map/ppermute | solution.py:560
  71.1 6.0 %collective-permute-start.13 = (f32[64,512]{1,0:T(8,128)S(1)}, f32[64,512]{1,0:T(8,128)S(1)}, u32[]{:S(2)}, u32[]{:S(2)}) collective-permute-start(f32[64,512]{1,0:T(8,128)S(1)} %get-tuple-element.47), channel_id=1, source_target_pairs={{0,96},{32,64},{64,32},{96,0},{1,97},{33,65},{65,33},{97,1},{2,98}... | collective-permute-start | bytes 393224 | tf_op jit(solution)/shard_map/ppermute | solution.py:553
  72.4 4.6 %collective-permute-start.12 = (f32[64,512]{1,0:T(8,128)S(1)}, f32[64,512]{1,0:T(8,128)S(1)}, u32[]{:S(2)}, u32[]{:S(2)}) collective-permute-start(f32[64,512]{1,0:T(8,128)S(1)} %get-tuple-element.46), channel_id=1, source_target_pairs={{0,32},{32,0},{64,96},{96,64},{1,33},{33,1},{65,97},{97,65},{2,34}... | collective-permute-start | bytes 393224 | tf_op jit(solution)/shard_map/ppermute | solution.py:552
  72.4 6.3 %collective-permute-start.14 = (f32[64,512]{1,0:T(8,128)S(1)}, f32[64,512]{1,0:T(8,128)S(1)}, u32[]{:S(2)}, u32[]{:S(2)}) collective-permute-start(f32[64,512]{1,0:T(8,128)S(1)} %get-tuple-element.48), channel_id=1, source_target_pairs={{0,1},{1,0},{2,3},{3,2},{4,5},{5,4},{6,7},{7,6},{8,9},{9,8},{10,11... | collective-permute-start | bytes 393224 | tf_op jit(solution)/shard_map/ppermute | solution.py:554
  73.1 5.6 %collective-permute-start.15 = (f32[64,512]{1,0:T(8,128)S(1)}, f32[64,512]{1,0:T(8,128)S(1)}, u32[]{:S(2)}, u32[]{:S(2)}) collective-permute-start(f32[64,512]{1,0:T(8,128)S(1)} %get-tuple-element.49), channel_id=1, source_target_pairs={{0,32},{1,2},{2,1},{3,4},{4,3},{5,6},{6,5},{7,8},{8,7},{9,10},{10,... | collective-permute-start | bytes 393224 | tf_op jit(solution)/shard_map/ppermute | solution.py:551
  77.1 13.0 %collective-permute-start.16 = (f32[64,512]{1,0:T(8,128)S(1)}, f32[64,512]{1,0:T(8,128)S(1)}, u32[]{:S(2)}, u32[]{:S(2)}) collective-permute-start(f32[64,512]{1,0:T(8,128)S(1)} %pad_maximum_fusion.4), channel_id=1, source_target_pairs={{0,1},{1,0},{2,3},{3,2},{4,5},{5,4},{6,7},{7,6},{8,9},{9,8},{10,11... | collective-permute-start | bytes 393224 | tf_op jit(solution)/shard_map/ppermute | solution.py:561
  78.4 11.7 %collective-permute-start.17 = (f32[64,512]{1,0:T(8,128)S(1)}, f32[64,512]{1,0:T(8,128)S(1)}, u32[]{:S(2)}, u32[]{:S(2)}) collective-permute-start(f32[64,512]{1,0:T(8,128)S(1)} %pad_maximum_fusion.5), channel_id=1, source_target_pairs={{0,32},{1,2},{2,1},{3,4},{4,3},{5,6},{6,5},{7,8},{8,7},{9,10},{10,... | collective-permute-start | bytes 393224 | tf_op jit(solution)/shard_map/ppermute | solution.py:560
  81.5 18.1 %all-to-all-start.1 = ((f32[128,1,128]{2,1,0:T(1,128)}), f32[128,1,128]{2,1,0:T(1,128)S(1)}, u32[]{:S(2)}, u32[]{:S(2)}) async-start(f32[128,1,128]{2,1,0:T(1,128)} %bitcast.8), calls=%async_computation.1 | async-start | bytes 131072 | tf_op jit(solution)/shard_map/all_to_all | solution.py:579

commit v8 on v7

--- a/solution.py
+++ b/solution.py
@@ -219,20 +219,41 @@
         ob_ref[:, at] = jnp.where(up_grp, masked[k][0], masked[k][1])
 
 
-def prepare_kernel(coupling_ref, occ_ref, w_ref, rowabs_ref, mask_ref):
+def spread(part):
+    lanes = lane_iota((NODES, BZ))
+    before = jnp.where(lanes == 0, 0.0, pltpu.roll(part[:NODES], 1, 1))
+    after = jnp.where(lanes == BZ - 1, 0.0, pltpu.roll(part[2 * NODES :], BZ - 1, 1))
+    return part[NODES : 2 * NODES] + before + after
+
+
+def split(src):
+    top = src.astype(BF16)
+    return top, (src - top.astype(F32)).astype(BF16)
+
+
+def others(x, y):
+    return [(dx, dy) for dx in range(3) for dy in range(3) if (dx, dy) != (2 * x, 2 * y)]
+
+
+def prepare_kernel(coupling_ref, occ_ref, w_ref, corner_ref, rowabs_ref, mask_ref):
     total = jnp.zeros((NODES, NODES), F32)
-    for dx in range(3):
-        for dz in range(3):
-            parts = []
+    high, low = {}, {}
+    for dz in range(3):
+        for dx in range(3):
             for dy in range(3):
                 k = (dx * 3 + dy) * 3 + dz
                 coupled = 0.5 * (coupling_ref[k] + coupling_ref[26 - k].T)
                 total = total + jnp.abs(coupled)
-                parts.append(coupled)
-            wide = jnp.concatenate(parts, axis=1)
-            high = wide.astype(BF16)
-            w_ref[dx, pl.ds(dz * NODES, NODES), :] = high
-            w_ref[dx, pl.ds((3 + dz) * NODES, NODES), :] = (wide - high.astype(F32)).astype(BF16)
+                high[dx, dy], low[dx, dy] = split(coupled)
+        rows = pl.ds(dz * NODES, NODES)
+        for x in range(2):
+            for y in range(2):
+                w_ref[x * 2 + y, rows, :] = jnp.concatenate([high[at] for at in others(x, y)], axis=1)
+                w_ref[x * 2 + y, pl.ds((3 + dz) * NODES, NODES), :] = jnp.concatenate(
+                    [low[at] for at in others(x, y)], axis=1
+                )
+                at = (2 * x, 2 * y)
+                corner_ref[x * 2 + y, rows, :] = jnp.concatenate([high[at], low[at], high[at]], axis=1)
     rowabs_ref[...] = jnp.broadcast_to(jnp.sum(total, axis=1, keepdims=True), (NODES, 128))
     for x in range(2):
         for y in range(2):
@@ -244,13 +265,14 @@
         prepare_kernel,
         name="prepare",
         in_specs=[pl.BlockSpec(memory_space=pltpu.VMEM)] * 2,
-        out_specs=[pl.BlockSpec(memory_space=pltpu.VMEM)] * 3,
+        out_specs=[pl.BlockSpec(memory_space=pltpu.VMEM)] * 4,
         out_shape=[
-            pltpu.VMEM((3, 6 * NODES, 3 * NODES), BF16),
+            pltpu.VMEM((4, 6 * NODES, 8 * NODES), BF16),
+            pltpu.VMEM((4, 3 * NODES, 3 * NODES), BF16),
             pltpu.VMEM((NODES, 128), F32),
             pltpu.VMEM((8, N_COLS * BZ), F32),
         ],
-        compiler_params=pltpu.CompilerParams(vmem_limit_bytes=8 << 20),
+        compiler_params=pltpu.CompilerParams(vmem_limit_bytes=12 << 20),
         cost_estimate=pl.CostEstimate(flops=10**7, transcendentals=0, bytes_accessed=4 * 10**6),
     )(coupling, occupied)
 
@@ -318,22 +340,10 @@
     )(place, vmem(recv), vmem(mask), vmem(rowabs))
 
 
-def spread(part):
-    lanes = lane_iota((NODES, BZ))
-    before = jnp.where(lanes == 0, 0.0, pltpu.roll(part[:NODES], 1, 1))
-    after = jnp.where(lanes == BZ - 1, 0.0, pltpu.roll(part[2 * NODES :], BZ - 1, 1))
-    return part[NODES : 2 * NODES] + before + after
-
-
-def split(src):
-    top = src.astype(BF16)
-    return top, (src - top.astype(F32)).astype(BF16)
-
-
-def product(w_ref, dx, cols, high, low):
-    full = jnp.dot(w_ref[dx, :, cols], high, preferred_element_type=F32)
-    half = jnp.dot(w_ref[dx, 0 : 3 * NODES, cols], low, preferred_element_type=F32)
-    return spread(full[: 3 * NODES] + full[3 * NODES :] + half)
+def product(weights, source):
+    high, low = split(source)
+    stacked = jnp.concatenate([high, high, low], axis=0)
+    return spread(jnp.dot(weights, stacked, preferred_element_type=F32))
 
 
 def put_moments(order, mom_ref, mom_out, sq, cross):
@@ -347,11 +357,11 @@
 
 def sides_kernel(last, place_ref, v_ref, mask_ref, ra_ref, rb_ref, ya_ref, yb_ref, w_ref, *rest):
     if last:
-        diag_ref, maskc_ref, c_ref, mom_ref, o_ref, mom_out, high, low = rest
+        corner_ref, diag_ref, maskc_ref, c_ref, mom_ref, o_ref, mom_out, high, low = rest
     else:
         o_ref, high, low = rest
     (x_low, x_high), (y_low, y_high) = parity_weights(place_ref)
-    halo = {}
+    halo, rise = {}, {}
 
     def at_rows(px, py):
         return pl.ds((px * 4 + py) * NODES, NODES)
@@ -367,23 +377,18 @@
         halo[k] = (blend(x_low, ra_ref[:, at], rb_ref[:, at]), blend(x_high, ra_ref[:, at], rb_ref[:, at]))
         put(0, k + 1, halo[k][0])
         put(3, k + 1, halo[k][1])
-        put(k + 1, 0, blend(y_low, ya_ref[:, at], yb_ref[:, at]))
-        put(k + 1, 3, blend(y_high, ya_ref[:, at], yb_ref[:, at]))
-    nothing = jnp.zeros((NODES, BZ), BF16)
-    for px in (0, 3):
-        for py in (0, 3):
-            high[at_rows(px, py), :] = nothing
-            low[at_rows(px, py), :] = nothing
+        rise[k] = (blend(y_low, ya_ref[:, at], yb_ref[:, at]), blend(y_high, ya_ref[:, at], yb_ref[:, at]))
+        put(k + 1, 0, rise[k][0])
+        put(k + 1, 3, rise[k][1])
     sq = jnp.zeros((NODES, BZ), F32)
     cross = jnp.zeros((NODES, BZ), F32)
     for x in range(2):
         for y in range(2):
-            full = jnp.zeros((6 * NODES, BZ), F32)
-            half = jnp.zeros((3 * NODES, BZ), F32)
-            for dx in range(3):
-                rows = pl.ds(((x + dx) * 4 + y) * NODES, 3 * NODES)
-                full = full + jnp.dot(w_ref[dx], high[rows, :], preferred_element_type=F32)
-                half = half + jnp.dot(w_ref[dx, 0 : 3 * NODES, :], low[rows, :], preferred_element_type=F32)
+            spots = [at_rows(x + dx, y + dy) for dx, dy in others(x, y)]
+            tops = jnp.concatenate([high[rows, :] for rows in spots], axis=0)
+            rests = jnp.concatenate([low[rows, :] for rows in spots], axis=0)
+            full = jnp.dot(w_ref[x * 2 + y], tops, preferred_element_type=F32)
+            half = jnp.dot(w_ref[x * 2 + y, 0 : 3 * NODES, :], rests, preferred_element_type=F32)
             at = column(x, y)
             total = spread(full[: 3 * NODES] + full[3 * NODES :] + half)
             o_ref[:, at] = total
@@ -396,9 +401,7 @@
     energy = jnp.zeros((NODES, BZ), F32)
     for x in range(2):
         for y in range(2):
-            near = at_rows(x + 1, 3 * y)
-            cols = pl.ds(2 * y * NODES, NODES)
-            energy = energy + halo[y][x] * product(w_ref, 2 - 2 * x, cols, high[near, :], low[near, :])
+            energy = energy + halo[y][x] * product(corner_ref[(1 - x) * 2 + y], rise[x][y])
     cross = cross - energy * (1.0 / c_ref[0:1, 0:1])
     put_moments(2, mom_ref, mom_out, sq, cross)
 
@@ -417,7 +420,7 @@
     )(place, *[vmem(x) for x in operands])
 
 
-def corners_kernel(order, last, place_ref, sum_ref, v_ref, diag_ref, mask_ref, maskc_ref, ca_ref, cb_ref, w_ref, *rest):
+def corners_kernel(order, last, place_ref, sum_ref, v_ref, diag_ref, mask_ref, maskc_ref, ca_ref, cb_ref, corner_ref, *rest):
     rest = list(rest)
     mom_ref = rest.pop(0) if order and not last else None
     o_ref = rest.pop(0)
@@ -428,9 +431,8 @@
     for y in range(2):
         line = [blend(y_pairs[y], ca_ref[:, pl.ds(k * BZ, BZ)], cb_ref[:, pl.ds(k * BZ, BZ)]) for k in range(2)]
         for x in range(2):
-            high, low = split(blend(x_pairs[x], line[0], line[1]))
             at = column(x, y)
-            total = sum_ref[:, at] + product(w_ref, 2 * x, pl.ds(2 * y * NODES, NODES), high, low)
+            total = sum_ref[:, at] + product(corner_ref[x * 2 + y], blend(x_pairs[x], line[0], line[1]))
             v = v_ref[:, at]
             new = diag_ref[:, at] * v - maskc_ref[0:1, at] * total
             o_ref[:, at] = new
@@ -456,12 +458,12 @@
     )(place, *[vmem(x) for x in operands])
 
 
-def apply_stiffness(order, place, v, diag, mask, maskc, centre, edges, weights, moments):
+def apply_stiffness(order, place, v, diag, mask, maskc, centre, edges, weights, corner, moments):
     last = order == 2
     ra, rb, ya, yb, ca, cb = exchange(place[1], *edges)
-    operands = [v, mask, ra, rb, ya, yb, weights] + ([diag, maskc, centre, moments] if last else [])
+    operands = [v, mask, ra, rb, ya, yb, weights] + ([corner, diag, maskc, centre, moments] if last else [])
     part, *shared = sides(place, operands, last)
-    operands = [part, v, diag, mask, maskc, ca, cb, weights]
+    operands = [part, v, diag, mask, maskc, ca, cb, corner]
     if last:
         return corners(order, place, operands, last)[0], shared[0], []
     new, moments, *edges = corners(order, place, operands + ([] if moments is None else [moments]), last)
@@ -567,13 +569,13 @@
     place = jnp.stack([slab, grp, lax.axis_size("slab"), lax.axis_size("grp")]).astype(jnp.int32)
     payload = splat(samples, tile_counts, block_ids)
     recv = lax.all_to_all(payload.reshape(SENDERS, 1, ROWS * 128), AXES, split_axis=0, concat_axis=0, tiled=True)
-    weights, rowabs, mask = prepare(coupling, occupied)
+    weights, corner, rowabs, mask = prepare(coupling, occupied)
     v, diag, maskc, centre, *edges = assemble(place, recv.reshape(SENDERS * ROWS, 128), mask, rowabs)
     fields = [v]
     moments = None
     for order in range(3):
         v, moments, edges = apply_stiffness(
-            order, place, v, diag, mask, maskc, centre, edges, weights, moments
+            order, place, v, diag, mask, maskc, centre, edges, weights, corner, moments
         )
         fields.append(v)
     shared = lax.all_to_all(moments.reshape(SENDERS, 1, 128), AXES, split_axis=0, concat_axis=0, tiled=True)

time: 101 us -> 104 us (1.030)
  local copies, waits for them, and re-layouts: 1.45 us -> 6.87 us
  waiting for transfers between devices: 38.6 us -> 35.3 us
  other arithmetic: 0.22 us -> 1.52 us
    unnamed x8 -> x22, local copies, waits for them, and re-layouts: 1.45 us -> 6.87 us
    all_to_all x1, waiting for transfers between devices: 8.42 us -> 4.59 us  [on_device(): lax.all_to_all(moments.reshape(SENDERS, 1, 128), AXES, split_axis=0, conc...]
    concatenate x6, other arithmetic: 0.06 us -> 1.37 us  [line(): jnp.concatenate([jnp.where(upper, r[:, BZ:], r[:, :BZ]) for r in (ra, rb)...]
  transfers between devices with their start and end apart: 20 -> 20, of which waited for: 8 -> 8; matrix products, arithmetic and copies ran while one was open for 0% -> 1% of each run, Pallas kernels for 8% -> 7%
where the time goes in v8:
time: 104 us
  waiting for transfers between devices  35.3 us (34%)
  starting transfers between devices  31.7 us (30%)
  Pallas kernels  27.2 us (26%)
  local copies, waits for them, and re-layouts  6.87 us (7%)
  other arithmetic  1.52 us (1%)
    pallas_call x1, Pallas kernels, splat(): pl.pallas_call(splat_kernel, name='splat', in_specs=[pl.BlockSpec(memory_...  14.6 us
    all_to_all x1, waiting for transfers between devices, on_device(): lax.all_to_all(payload.reshape(SENDERS, 1, ROWS * 128), AXES, split_axis=...  13.6 us
    all_to_all x1, starting transfers between devices, on_device(): lax.all_to_all(payload.reshape(SENDERS, 1, ROWS * 128), AXES, split_axis=...  11.5 us
    ppermute x3, waiting for transfers between devices, exchange(): rb = lax.ppermute(eb, 'slab', swap('slab', 1))  10.9 us
    all_to_all x1, starting transfers between devices, on_device(): lax.all_to_all(moments.reshape(SENDERS, 1, 128), AXES, split_axis=0, conc...  8.58 us
    unnamed x22, local copies, waits for them, and re-layouts  6.87 us
    ppermute x3, waiting for transfers between devices, exchange(): cb = lax.ppermute(line(jnp.logical_not(up)), AXES, odd_swap())  5.97 us
    pallas_call x3, Pallas kernels, sides(): pl.pallas_call(functools.partial(sides_kernel, last), name='sides', in_sp...  5.34 us
  transfers between devices with their start and end apart: 20, of which 8 were waited for; matrix products, arithmetic and copies ran while one was open for 1% of the time, Pallas kernels for 7%

profile of v8, /device:TPU:1, one launch (start us, length us, event | category | flops | bytes accessed | tf_op | source)
XLA Modules:
  0.0 103.5 jit_solution(14802755023938069724)
XLA Ops:
  2.1 14.6 %splat.1 = f32[8,144,128]{2,1,0:T(8,128)} custom-call(f32[6,1024,128]{2,1,0:T(8,128)} %bitcast.25, s32[8,128]{1,0:T(8,128)S(1)} %bitcast.23, s32[8,128]{1,0:T(8,128)S(1)} %bitcast.24), custom_call_target="tpu_custom_call" | custom-call | tf_op jit(solution)/shard_map/splat/pallas_call | solution.py:165
  16.7 11.5 %all-to-all-start = ((f32[128,1,1152]{2,1,0:T(1,128)}), f32[128,1,1152]{2,1,0:T(1,128)S(1)}, u32[]{:S(2)}, u32[]{:S(2)}) async-start(f32[128,1,1152]{2,1,0:T(1,128)} %bitcast.5), calls=%async_computation | async-start | bytes 1179648 | tf_op jit(solution)/shard_map/all_to_all | solution.py:571
  28.9 13.6 %all-to-all-done = f32[128,1,1152]{2,1,0:T(1,128)S(1)} async-done(((f32[128,1,1152]{2,1,0:T(1,128)}), f32[128,1,1152]{2,1,0:T(1,128)S(1)}, u32[]{:S(2)}, u32[]{:S(2)}) %all-to-all-start) | async-done | bytes 589856 | tf_op jit(solution)/shard_map/all_to_all | solution.py:571
  42.5 2.1 %assemble.1 = (f32[64,1024]{1,0:T(8,128)S(1)}, f32[64,1024]{1,0:T(8,128)S(1)}, f32[8,1024]{1,0:T(8,128)S(1)}, f32[8,128]{1,0:T(8,128)S(1)}, f32[64,512]{1,0:T(8,...) custom-call(s32[4]{0:T(128)S(1)} %pad_add_fusion.place_ref, f32[1152,128]{1,0:T(8,128)S(1)} %bitcast.21, ...), custom_call_target="tpu_custom_call" | custom-call | tf_op jit(solution)/shard_map/assemble/pallas_call | solution.py:332
  45.9 1.0 collective-permute-start.2
  47.0 3.5 %collective-permute-done.1.rb_ref = f32[64,512]{1,0:T(8,128)S(1)} collective-permute-done((f32[64,512]{1,0:T(8,128)}, f32[64,512]{1,0:T(8,128)S(1)}, u32[]{:S(2)}, u32[]{:S(2)}) %collective-permute-start.1) | collective-permute-done | bytes 131104 | tf_op jit(solution)/shard_map/ppermute | solution.py:555
  50.6 2.2 %collective-permute-start.4 = (f32[64,512]{1,0:T(8,128)S(1)}, f32[64,512]{1,0:T(8,128)S(1)}, u32[]{:S(2)}, u32[]{:S(2)}) collective-permute-start(f32[64,512]{1,0:T(8,128)S(1)} %pad_maximum_fusion), channel_id=1, source_target_pairs={{0,1},{1,0},{2,3},{3,2},{4,5},{5,4},{6,7},{7,6},{8,9},{9,8},{10,11... | collective-permute-start | bytes 393224 | tf_op jit(solution)/shard_map/ppermute | solution.py:563
  53.1 1.5 %sides.3.sum_ref = f32[64,1024]{1,0:T(8,128)S(1)} custom-call(s32[4]{0:T(128)S(1)} %pad_add_fusion.place_ref, f32[64,1024]{1,0:T(8,128)S(1)} %get-tuple-element.32.v_ref.v0_ref, f32[8,1024]{1,0:T(8,128)S(1)} %get-tuple-element.30.mask_ref, f32[64,512]{1,0:T(8,128)S(1)} %collective-permute-done.ra_ref, f32[64,512]{1,0:T(8,128)S(1)} %collective-permute-done.1.rb_ref, ...), custom_call_target="tpu_custom_call" | custom-call | flops 1500000000 | bytes 2000000 | tf_op jit(solution)/shard_map/sides/pallas_call | solution.py:411
  54.6 2.9 %collective-permute-done.5.cb_ref = f32[64,512]{1,0:T(8,128)S(1)} collective-permute-done((f32[64,512]{1,0:T(8,128)S(1)}, f32[64,512]{1,0:T(8,128)S(1)}, u32[]{:S(2)}, u32[]{:S(2)}) %collective-permute-start.5) | collective-permute-done | bytes 131104 | tf_op jit(solution)/shard_map/ppermute | solution.py:562
  57.5 1.1 %corners.3 = (f32[64,1024]{1,0:T(8,128)S(1)}, f32[8,128]{1,0:T(8,128)S(1)}, f32[64,512]{1,0:T(8,128)S(1)}, f32[64,512]{1,0:T(8,128)S(1)}, f32[64,512]{1,0:T(8,128)S(1)}, /*index=5*/f32[64,512]{1,0:T(8,128)S(1)}) custom-call(s32[4]{0:T(128)S(1)} %pad_add_fusion.place_ref, f32[64,1024]{1,0:T(8,128)S(1)} %sides.3.sum_ref, ...), custom_call_target="tpu_custom_call" | custom-call | flops 500000000 | bytes 2000000 | tf_op jit(solution)/shard_map/corners/pallas_call | solution.py:450
  58.6 1.8 %collective-permute-start.7 = (f32[64,512]{1,0:T(8,128)S(1)}, f32[64,512]{1,0:T(8,128)S(1)}, u32[]{:S(2)}, u32[]{:S(2)}) collective-permute-start(f32[64,512]{1,0:T(8,128)S(1)} %get-tuple-element.43), channel_id=1, source_target_pairs={{0,96},{32,64},{64,32},{96,0},{1,97},{33,65},{65,33},{97,1},{2,98}... | collective-permute-start | bytes 393224 | tf_op jit(solution)/shard_map/ppermute | solution.py:555
  61.1 3.5 %collective-permute-done.7.rb_ref = f32[64,512]{1,0:T(8,128)S(1)} collective-permute-done((f32[64,512]{1,0:T(8,128)S(1)}, f32[64,512]{1,0:T(8,128)S(1)}, u32[]{:S(2)}, u32[]{:S(2)}) %collective-permute-start.7) | collective-permute-done | bytes 131104 | tf_op jit(solution)/shard_map/ppermute | solution.py:555
  64.8 1.6 %collective-permute-start.10 = (f32[64,512]{1,0:T(8,128)S(1)}, f32[64,512]{1,0:T(8,128)S(1)}, u32[]{:S(2)}, u32[]{:S(2)}) collective-permute-start(f32[64,512]{1,0:T(8,128)S(1)} %pad_maximum_fusion.2), channel_id=1, source_target_pairs={{0,1},{1,0},{2,3},{3,2},{4,5},{5,4},{6,7},{7,6},{8,9},{9,8},{10,11... | collective-permute-start | bytes 393224 | tf_op jit(solution)/shard_map/ppermute | solution.py:563
  66.5 1.5 %sides.4.sum_ref = f32[64,1024]{1,0:T(8,128)S(1)} custom-call(s32[4]{0:T(128)S(1)} %pad_add_fusion.place_ref, f32[64,1024]{1,0:T(8,128)S(1)} %get-tuple-element.41.v_ref.v1_ref, f32[8,1024]{1,0:T(8,128)S(1)} %get-tuple-element.30.mask_ref, f32[64,512]{1,0:T(8,128)S(1)} %collective-permute-done.6.ra_ref, f32[64,512]{1,0:T(8,128)S(1)} %collective-permute-done.7.rb_ref, ...), custom_call_target="tpu_custom_call" | custom-call | flops 1500000000 | bytes 2000000 | tf_op jit(solution)/shard_map/sides/pallas_call | solution.py:411
  68.0 3.1 %collective-permute-done.11.cb_ref = f32[64,512]{1,0:T(8,128)S(1)} collective-permute-done((f32[64,512]{1,0:T(8,128)S(1)}, f32[64,512]{1,0:T(8,128)S(1)}, u32[]{:S(2)}, u32[]{:S(2)}) %collective-permute-start.11) | collective-permute-done | bytes 131104 | tf_op jit(solution)/shard_map/ppermute | solution.py:562
  71.1 1.1 %corners.4 = (f32[64,1024]{1,0:T(8,128)S(1)}, f32[8,128]{1,0:T(8,128)S(1)}, f32[64,512]{1,0:T(8,128)S(1)}, f32[64,512]{1,0:T(8,128)S(1)}, f32[64,512]{1,0:T(8,128)S(1)}, /*index=5*/f32[64,512]{1,0:T(8,128)S(1)}) custom-call(s32[4]{0:T(128)S(1)} %pad_add_fusion.place_ref, f32[64,1024]{1,0:T(8,128)S(1)} %sides.4.sum_ref, ...), custom_call_target="tpu_custom_call" | custom-call | flops 500000000 | bytes 2000000 | tf_op jit(solution)/shard_map/corners/pallas_call | solution.py:450
  72.2 1.3 %collective-permute-start.13 = (f32[64,512]{1,0:T(8,128)S(1)}, f32[64,512]{1,0:T(8,128)S(1)}, u32[]{:S(2)}, u32[]{:S(2)}) collective-permute-start(f32[64,512]{1,0:T(8,128)S(1)} %get-tuple-element.49), channel_id=1, source_target_pairs={{0,96},{32,64},{64,32},{96,0},{1,97},{33,65},{65,33},{97,1},{2,98}... | collective-permute-start | bytes 393224 | tf_op jit(solution)/shard_map/ppermute | solution.py:555
  74.2 4.0 %collective-permute-done.13.rb_ref = f32[64,512]{1,0:T(8,128)S(1)} collective-permute-done((f32[64,512]{1,0:T(8,128)S(1)}, f32[64,512]{1,0:T(8,128)S(1)}, u32[]{:S(2)}, u32[]{:S(2)}) %collective-permute-start.13) | collective-permute-done | bytes 131104 | tf_op jit(solution)/shard_map/ppermute | solution.py:555
  78.9 1.3 %collective-permute-start.16 = (f32[64,512]{1,0:T(8,128)}, f32[64,512]{1,0:T(8,128)S(1)}, u32[]{:S(2)}, u32[]{:S(2)}) collective-permute-start(f32[64,512]{1,0:T(8,128)} %pad_maximum_fusion.4), channel_id=1, source_target_pairs={{0,1},{1,0},{2,3},{3,2},{4,5},{5,4},{6,7},{7,6},{8,9},{9,8},{10,11... | collective-permute-start | bytes 393224 | tf_op jit(solution)/shard_map/ppermute | solution.py:563
  80.8 2.4 %sides.5 = (f32[64,1024]{1,0:T(8,128)S(1)}, f32[128,128]{1,0:T(8,128)}) custom-call(s32[4]{0:T(128)S(1)} %pad_add_fusion.place_ref, f32[64,1024]{1,0:T(8,128)S(1)} %get-tuple-element.47.v_ref.v2_ref, f32[8,1024]{1,0:T(8,128)S(1)} %get-tuple-element.30.mask_ref, f32[64,512]{1,0:T(8,128)S(1)} %collective-permute-done.12.ra_ref, ...), custom_call_target="tpu_custom_call" | custom-call | flops 1500000000 | bytes 2000000 | tf_op jit(solution)/shard_map/sides/pallas_call | solution.py:411
  83.9 8.6 %all-to-all-start.1 = ((f32[128,1,128]{2,1,0:T(1,128)}), f32[128,1,128]{2,1,0:T(1,128)S(1)}, u32[]{:S(2)}, u32[]{:S(2)}) async-start(f32[128,1,128]{2,1,0:T(1,128)} %bitcast.8), calls=%async_computation.1 | async-start | bytes 131072 | tf_op jit(solution)/shard_map/all_to_all | solution.py:581
  96.6 1.0 corners.5.v3_ref
  97.5 4.6 %all-to-all-done.1 = f32[128,1,128]{2,1,0:T(1,128)S(1)} async-done(((f32[128,1,128]{2,1,0:T(1,128)}), f32[128,1,128]{2,1,0:T(1,128)S(1)}, u32[]{:S(2)}, u32[]{:S(2)}) %all-to-all-start.1) | async-done | bytes 65568 | tf_op jit(solution)/shard_map/all_to_all | solution.py:581
  102.1 1.4 %finish.1 = (f32[64,8,128]{2,1,0:T(8,128)}, f32[64,8,128]{2,1,0:T(8,128)}) custom-call(f32[128,128]{1,0:T(8,128)S(1)} %bitcast.22, f32[8,128]{1,0:T(8,128)S(1)} %get-tuple-element.52.rest_3_.c_ref, f32[64,1024]{1,0:T(8,128)S(1)} %get-tuple-element.32.v_ref.v0_ref, f32[64,1024]{1,0:T(8,128)S(1)} %get-tuple-element.41.v_ref.v1_ref, ...), custom_call_target="tpu_custom_call" | custom-call | tf_op jit(solution)/shard_map/finish/pallas_call | solution.py:525
  (61 shorter events, 11.7 us)
Async XLA Ops:
  0.6 27.6 %copy-start = (f32[27,64,64]{2,1,0:T(8,128)S(1)}, f32[27,64,64]{2,1,0:T(8,128)}, u32[]{:S(2)}) copy-start(f32[27,64,64]{2,1,0:T(8,128)} %coupling_ref.1) | copy-start | bytes 1327108
  2.1 26.1 %copy-start.3 = (s32[2,2,256]{2,1,0:T(2,128)S(1)}, s32[2,2,256]{2,1,0:T(2,128)}, u32[]{:S(2)}) copy-start(s32[2,2,256]{2,1,0:T(2,128)} %occ_ref.1) | copy-start | bytes 12292
  16.7 25.8 %all-to-all-start = ((f32[128,1,1152]{2,1,0:T(1,128)}), f32[128,1,1152]{2,1,0:T(1,128)S(1)}, u32[]{:S(2)}, u32[]{:S(2)}) async-start(f32[128,1,1152]{2,1,0:T(1,128)} %bitcast.5), calls=%async_computation | async-start | bytes 1179648 | tf_op jit(solution)/shard_map/all_to_all | solution.py:571
  45.3 5.2 %collective-permute-start.1 = (f32[64,512]{1,0:T(8,128)}, f32[64,512]{1,0:T(8,128)S(1)}, u32[]{:S(2)}, u32[]{:S(2)}) collective-permute-start(f32[64,512]{1,0:T(8,128)} %get-tuple-element.34), channel_id=1, source_target_pairs={{0,96},{32,64},{64,32},{96,0},{1,97},{33,65},{65,33},{97,1},{2,98}... | collective-permute-start | bytes 393224 | tf_op jit(solution)/shard_map/ppermute | solution.py:555
  45.6 4.9 %collective-permute-start = (f32[64,512]{1,0:T(8,128)}, f32[64,512]{1,0:T(8,128)S(1)}, u32[]{:S(2)}, u32[]{:S(2)}) collective-permute-start(f32[64,512]{1,0:T(8,128)} %copy-done.4), channel_id=1, source_target_pairs={{0,32},{32,0},{64,96},{96,64},{1,33},{33,1},{65,97},{97,65},{2,34}... | collective-permute-start | bytes 393224 | tf_op jit(solution)/shard_map/ppermute | solution.py:554
  45.9 7.1 %collective-permute-start.2 = (f32[64,512]{1,0:T(8,128)S(1)}, f32[64,512]{1,0:T(8,128)S(1)}, u32[]{:S(2)}, u32[]{:S(2)}) collective-permute-start(f32[64,512]{1,0:T(8,128)S(1)} %get-tuple-element.35), channel_id=1, source_target_pairs={{0,1},{1,0},{2,3},{3,2},{4,5},{5,4},{6,7},{7,6},{8,9},{9,8},{10,11... | collective-permute-start | bytes 393224 | tf_op jit(solution)/shard_map/ppermute | solution.py:556
  46.9 6.2 %collective-permute-start.3 = (f32[64,512]{1,0:T(8,128)S(1)}, f32[64,512]{1,0:T(8,128)S(1)}, u32[]{:S(2)}, u32[]{:S(2)}) collective-permute-start(f32[64,512]{1,0:T(8,128)S(1)} %get-tuple-element.36), channel_id=1, source_target_pairs={{0,32},{1,2},{2,1},{3,4},{4,3},{5,6},{6,5},{7,8},{8,7},{9,10},{10,... | collective-permute-start | bytes 393224 | tf_op jit(solution)/shard_map/ppermute | solution.py:553
  50.6 4.0 %collective-permute-start.4 = (f32[64,512]{1,0:T(8,128)S(1)}, f32[64,512]{1,0:T(8,128)S(1)}, u32[]{:S(2)}, u32[]{:S(2)}) collective-permute-start(f32[64,512]{1,0:T(8,128)S(1)} %pad_maximum_fusion), channel_id=1, source_target_pairs={{0,1},{1,0},{2,3},{3,2},{4,5},{5,4},{6,7},{7,6},{8,9},{9,8},{10,11... | collective-permute-start | bytes 393224 | tf_op jit(solution)/shard_map/ppermute | solution.py:563
  52.8 4.7 %collective-permute-start.5 = (f32[64,512]{1,0:T(8,128)S(1)}, f32[64,512]{1,0:T(8,128)S(1)}, u32[]{:S(2)}, u32[]{:S(2)}) collective-permute-start(f32[64,512]{1,0:T(8,128)S(1)} %pad_maximum_fusion.1), channel_id=1, source_target_pairs={{0,32},{1,2},{2,1},{3,4},{4,3},{5,6},{6,5},{7,8},{8,7},{9,10},{10,... | collective-permute-start | bytes 393224 | tf_op jit(solution)/shard_map/ppermute | solution.py:562
  58.6 6.0 %collective-permute-start.7 = (f32[64,512]{1,0:T(8,128)S(1)}, f32[64,512]{1,0:T(8,128)S(1)}, u32[]{:S(2)}, u32[]{:S(2)}) collective-permute-start(f32[64,512]{1,0:T(8,128)S(1)} %get-tuple-element.43), channel_id=1, source_target_pairs={{0,96},{32,64},{64,32},{96,0},{1,97},{33,65},{65,33},{97,1},{2,98}... | collective-permute-start | bytes 393224 | tf_op jit(solution)/shard_map/ppermute | solution.py:555
  60.4 4.4 %collective-permute-start.6 = (f32[64,512]{1,0:T(8,128)S(1)}, f32[64,512]{1,0:T(8,128)S(1)}, u32[]{:S(2)}, u32[]{:S(2)}) collective-permute-start(f32[64,512]{1,0:T(8,128)S(1)} %get-tuple-element.42), channel_id=1, source_target_pairs={{0,32},{32,0},{64,96},{96,64},{1,33},{33,1},{65,97},{97,65},{2,34}... | collective-permute-start | bytes 393224 | tf_op jit(solution)/shard_map/ppermute | solution.py:554
  60.4 6.1 %collective-permute-start.8 = (f32[64,512]{1,0:T(8,128)S(1)}, f32[64,512]{1,0:T(8,128)S(1)}, u32[]{:S(2)}, u32[]{:S(2)}) collective-permute-start(f32[64,512]{1,0:T(8,128)S(1)} %get-tuple-element.44), channel_id=1, source_target_pairs={{0,1},{1,0},{2,3},{3,2},{4,5},{5,4},{6,7},{7,6},{8,9},{9,8},{10,11... | collective-permute-start | bytes 393224 | tf_op jit(solution)/shard_map/ppermute | solution.py:556
  61.1 5.5 %collective-permute-start.9 = (f32[64,512]{1,0:T(8,128)S(1)}, f32[64,512]{1,0:T(8,128)S(1)}, u32[]{:S(2)}, u32[]{:S(2)}) collective-permute-start(f32[64,512]{1,0:T(8,128)S(1)} %get-tuple-element.45), channel_id=1, source_target_pairs={{0,32},{1,2},{2,1},{3,4},{4,3},{5,6},{6,5},{7,8},{8,7},{9,10},{10,... | collective-permute-start | bytes 393224 | tf_op jit(solution)/shard_map/ppermute | solution.py:553
  64.8 3.2 %collective-permute-start.10 = (f32[64,512]{1,0:T(8,128)S(1)}, f32[64,512]{1,0:T(8,128)S(1)}, u32[]{:S(2)}, u32[]{:S(2)}) collective-permute-start(f32[64,512]{1,0:T(8,128)S(1)} %pad_maximum_fusion.2), channel_id=1, source_target_pairs={{0,1},{1,0},{2,3},{3,2},{4,5},{5,4},{6,7},{7,6},{8,9},{9,8},{10,11... | collective-permute-start | bytes 393224 | tf_op jit(solution)/shard_map/ppermute | solution.py:563
  66.4 4.7 %collective-permute-start.11 = (f32[64,512]{1,0:T(8,128)S(1)}, f32[64,512]{1,0:T(8,128)S(1)}, u32[]{:S(2)}, u32[]{:S(2)}) collective-permute-start(f32[64,512]{1,0:T(8,128)S(1)} %pad_maximum_fusion.3), channel_id=1, source_target_pairs={{0,32},{1,2},{2,1},{3,4},{4,3},{5,6},{6,5},{7,8},{8,7},{9,10},{10,... | collective-permute-start | bytes 393224 | tf_op jit(solution)/shard_map/ppermute | solution.py:562
  72.2 6.0 %collective-permute-start.13 = (f32[64,512]{1,0:T(8,128)S(1)}, f32[64,512]{1,0:T(8,128)S(1)}, u32[]{:S(2)}, u32[]{:S(2)}) collective-permute-start(f32[64,512]{1,0:T(8,128)S(1)} %get-tuple-element.49), channel_id=1, source_target_pairs={{0,96},{32,64},{64,32},{96,0},{1,97},{33,65},{65,33},{97,1},{2,98}... | collective-permute-start | bytes 393224 | tf_op jit(solution)/shard_map/ppermute | solution.py:555
  73.5 4.6 %collective-permute-start.12 = (f32[64,512]{1,0:T(8,128)S(1)}, f32[64,512]{1,0:T(8,128)S(1)}, u32[]{:S(2)}, u32[]{:S(2)}) collective-permute-start(f32[64,512]{1,0:T(8,128)S(1)} %get-tuple-element.48), channel_id=1, source_target_pairs={{0,32},{32,0},{64,96},{96,64},{1,33},{33,1},{65,97},{97,65},{2,34}... | collective-permute-start | bytes 393224 | tf_op jit(solution)/shard_map/ppermute | solution.py:554
  73.5 7.3 %collective-permute-start.14 = (f32[64,512]{1,0:T(8,128)S(1)}, f32[64,512]{1,0:T(8,128)S(1)}, u32[]{:S(2)}, u32[]{:S(2)}) collective-permute-start(f32[64,512]{1,0:T(8,128)S(1)} %get-tuple-element.50), channel_id=1, source_target_pairs={{0,1},{1,0},{2,3},{3,2},{4,5},{5,4},{6,7},{7,6},{8,9},{9,8},{10,11... | collective-permute-start | bytes 393224 | tf_op jit(solution)/shard_map/ppermute | solution.py:556
  74.2 6.6 %collective-permute-start.15 = (f32[64,512]{1,0:T(8,128)S(1)}, f32[64,512]{1,0:T(8,128)S(1)}, u32[]{:S(2)}, u32[]{:S(2)}) collective-permute-start(f32[64,512]{1,0:T(8,128)S(1)} %get-tuple-element.51), channel_id=1, source_target_pairs={{0,32},{1,2},{2,1},{3,4},{4,3},{5,6},{6,5},{7,8},{8,7},{9,10},{10,... | collective-permute-start | bytes 393224 | tf_op jit(solution)/shard_map/ppermute | solution.py:553
  78.9 13.6 %collective-permute-start.16 = (f32[64,512]{1,0:T(8,128)}, f32[64,512]{1,0:T(8,128)S(1)}, u32[]{:S(2)}, u32[]{:S(2)}) collective-permute-start(f32[64,512]{1,0:T(8,128)} %pad_maximum_fusion.4), channel_id=1, source_target_pairs={{0,1},{1,0},{2,3},{3,2},{4,5},{5,4},{6,7},{7,6},{8,9},{9,8},{10,11... | collective-permute-start | bytes 393224 | tf_op jit(solution)/shard_map/ppermute | solution.py:563
  80.8 12.4 %collective-permute-start.17 = (f32[64,512]{1,0:T(8,128)}, f32[64,512]{1,0:T(8,128)S(1)}, u32[]{:S(2)}, u32[]{:S(2)}) collective-permute-start(f32[64,512]{1,0:T(8,128)} %pad_maximum_fusion.5), channel_id=1, source_target_pairs={{0,32},{1,2},{2,1},{3,4},{4,3},{5,6},{6,5},{7,8},{8,7},{9,10},{10,... | collective-permute-start | bytes 393224 | tf_op jit(solution)/shard_map/ppermute | solution.py:562
  83.9 18.2 %all-to-all-start.1 = ((f32[128,1,128]{2,1,0:T(1,128)}), f32[128,1,128]{2,1,0:T(1,128)S(1)}, u32[]{:S(2)}, u32[]{:S(2)}) async-start(f32[128,1,128]{2,1,0:T(1,128)} %bitcast.8), calls=%async_computation.1 | async-start | bytes 131072 | tf_op jit(solution)/shard_map/all_to_all | solution.py:581
  93.8 0.9 copy-start.6
  95.6 0.9 copy-start.10
  (7 other events, 5.0 us)

commit v9 on v8

--- a/solution.py
+++ b/solution.py
@@ -49,7 +49,7 @@
     return nodes(low, mid, high), nodes(back, smid, w)
 
 
-def splat_kernel(samp_ref, cnt_ref, ids_ref, out_ref, held, sems, flip, basis, acc, stats):
+def splat_kernel(samp_ref, cnt_hbm, ids_hbm, out_ref, held, sems, cnt_ref, ids_ref, small_sems, flip, basis, acc, stats):
     groups = out_ref.shape[0]
 
     def fetch(g):
@@ -122,10 +122,15 @@
         for d in range(16):
             out_ref[g, pl.ds(ROWS * d, 8), :] = by_tile[8 * d : 8 * d + 8]
 
+    counts_copy = pltpu.make_async_copy(cnt_hbm, cnt_ref, small_sems.at[0])
+    ids_copy = pltpu.make_async_copy(ids_hbm, ids_ref, small_sems.at[1])
+    counts_copy.start()
     for g in range(groups):
         fetch(g).start()
+    ids_copy.start()
     stats[...] = jnp.zeros_like(stats)
     acc[...] = jnp.zeros_like(acc)
+    counts_copy.wait()
     fetch(0).wait()
     turn(0)
 
@@ -146,6 +151,7 @@
 
     lax.fori_loop(0, groups, advance, 0)
     settle(groups - 1, True)
+    ids_copy.wait()
     ids = ids_ref[...]
     local = ((ids >> 14) & 1) * 512 + ((ids >> 8) & 1) * 256 + (ids & 255)
     local = local.astype(F32)
@@ -165,19 +171,26 @@
     return pl.pallas_call(
         splat_kernel,
         name="splat",
-        in_specs=[pl.BlockSpec(memory_space=pltpu.HBM)] + [pl.BlockSpec(memory_space=pltpu.VMEM)] * 2,
+        in_specs=[pl.BlockSpec(memory_space=pltpu.HBM)] * 3,
         out_specs=pl.BlockSpec(memory_space=pltpu.VMEM),
         out_shape=pltpu.VMEM((groups, 16 * ROWS, 128), F32),
         scratch_shapes=[
             pltpu.VMEM((groups, 6, 128, 128), F32),
             pltpu.SemaphoreType.DMA((groups,)),
+            pltpu.VMEM((groups, 128), jnp.int32),
+            pltpu.VMEM((groups, 128), jnp.int32),
+            pltpu.SemaphoreType.DMA((2,)),
             pltpu.VMEM((6, 128, 128), F32),
             pltpu.VMEM((32, 128, 128), F32),
             pltpu.VMEM((1024, 128), F32),
             pltpu.VMEM((2, 8, 128), F32),
         ],
         compiler_params=pltpu.CompilerParams(vmem_limit_bytes=24 << 20),
-    )(pltpu.with_memory_space_constraint(jnp.transpose(samples, (1, 0, 2)), pltpu.HBM), counts.reshape(groups, 128), ids.reshape(groups, 128))
+    )(hbm(jnp.transpose(samples, (1, 0, 2))), hbm(counts.reshape(groups, 128)), hbm(ids.reshape(groups, 128)))
+
+
+def hbm(x):
+    return pltpu.with_memory_space_constraint(x, pltpu.HBM)
 
 
 def vmem(x):
@@ -231,27 +244,21 @@
     return top, (src - top.astype(F32)).astype(BF16)
 
 
-def others(x, y):
-    return [(dx, dy) for dx in range(3) for dy in range(3) if (dx, dy) != (2 * x, 2 * y)]
-
-
 def prepare_kernel(coupling_ref, occ_ref, w_ref, corner_ref, rowabs_ref, mask_ref):
     total = jnp.zeros((NODES, NODES), F32)
     high, low = {}, {}
     for dz in range(3):
+        rows = pl.ds(dz * NODES, NODES)
         for dx in range(3):
             for dy in range(3):
                 k = (dx * 3 + dy) * 3 + dz
                 coupled = 0.5 * (coupling_ref[k] + coupling_ref[26 - k].T)
                 total = total + jnp.abs(coupled)
                 high[dx, dy], low[dx, dy] = split(coupled)
-        rows = pl.ds(dz * NODES, NODES)
+            w_ref[dx, rows, :] = jnp.concatenate([high[dx, dy] for dy in range(3)], axis=1)
+            w_ref[dx, pl.ds((3 + dz) * NODES, NODES), :] = jnp.concatenate([low[dx, dy] for dy in range(3)], axis=1)
         for x in range(2):
             for y in range(2):
-                w_ref[x * 2 + y, rows, :] = jnp.concatenate([high[at] for at in others(x, y)], axis=1)
-                w_ref[x * 2 + y, pl.ds((3 + dz) * NODES, NODES), :] = jnp.concatenate(
-                    [low[at] for at in others(x, y)], axis=1
-                )
                 at = (2 * x, 2 * y)
                 corner_ref[x * 2 + y, rows, :] = jnp.concatenate([high[at], low[at], high[at]], axis=1)
     rowabs_ref[...] = jnp.broadcast_to(jnp.sum(total, axis=1, keepdims=True), (NODES, 128))
@@ -267,7 +274,7 @@
         in_specs=[pl.BlockSpec(memory_space=pltpu.VMEM)] * 2,
         out_specs=[pl.BlockSpec(memory_space=pltpu.VMEM)] * 4,
         out_shape=[
-            pltpu.VMEM((4, 6 * NODES, 8 * NODES), BF16),
+            pltpu.VMEM((3, 6 * NODES, 3 * NODES), BF16),
             pltpu.VMEM((4, 3 * NODES, 3 * NODES), BF16),
             pltpu.VMEM((NODES, 128), F32),
             pltpu.VMEM((8, N_COLS * BZ), F32),
@@ -380,15 +387,21 @@
         rise[k] = (blend(y_low, ya_ref[:, at], yb_ref[:, at]), blend(y_high, ya_ref[:, at], yb_ref[:, at]))
         put(k + 1, 0, rise[k][0])
         put(k + 1, 3, rise[k][1])
+    nothing = jnp.zeros((NODES, BZ), BF16)
+    for px in (0, 3):
+        for py in (0, 3):
+            high[at_rows(px, py), :] = nothing
+            low[at_rows(px, py), :] = nothing
     sq = jnp.zeros((NODES, BZ), F32)
     cross = jnp.zeros((NODES, BZ), F32)
     for x in range(2):
         for y in range(2):
-            spots = [at_rows(x + dx, y + dy) for dx, dy in others(x, y)]
-            tops = jnp.concatenate([high[rows, :] for rows in spots], axis=0)
-            rests = jnp.concatenate([low[rows, :] for rows in spots], axis=0)
-            full = jnp.dot(w_ref[x * 2 + y], tops, preferred_element_type=F32)
-            half = jnp.dot(w_ref[x * 2 + y, 0 : 3 * NODES, :], rests, preferred_element_type=F32)
+            full = jnp.zeros((6 * NODES, BZ), F32)
+            half = jnp.zeros((3 * NODES, BZ), F32)
+            for dx in range(3):
+                rows = pl.ds(((x + dx) * 4 + y) * NODES, 3 * NODES)
+                full = full + jnp.dot(w_ref[dx], high[rows, :], preferred_element_type=F32)
+                half = half + jnp.dot(w_ref[dx, 0 : 3 * NODES, :], low[rows, :], preferred_element_type=F32)
             at = column(x, y)
             total = spread(full[: 3 * NODES] + full[3 * NODES :] + half)
             o_ref[:, at] = total

time: 104 us -> 99.9 us (0.961)
  local copies, waits for them, and re-layouts: 6.87 us -> 0.01 us
  waiting for transfers between devices: 35.3 us -> 38.7 us
  other arithmetic: 1.52 us -> 0.22 us
    unnamed x22 -> x4, local copies, waits for them, and re-layouts: 6.87 us -> 0.01 us
    all_to_all x1, waiting for transfers between devices: 4.59 us -> 8.57 us  [on_device(): lax.all_to_all(moments.reshape(SENDERS, 1, 128), AXES, split_axis=0, conc...]
    concatenate x6, other arithmetic: 1.37 us -> 0.06 us  [line(): jnp.concatenate([jnp.where(upper, r[:, BZ:], r[:, :BZ]) for r in (ra, rb)...]
  transfers between devices with their start and end apart: 20 -> 20, of which waited for: 8 -> 8; matrix products, arithmetic and copies ran while one was open for 1% -> 0% of each run, Pallas kernels for 7% -> 8%
where the time goes in v9:
time: 99.9 us; the launch traced here: 99.7 us
  waiting for transfers between devices  38.7 us (39%)
  starting transfers between devices  32.1 us (32%)
  Pallas kernels  27.7 us (28%)
    pallas_call x1, Pallas kernels, splat(): pl.pallas_call(splat_kernel, name='splat', in_specs=[pl.BlockSpec(memory_...  15.2 us
    all_to_all x1, waiting for transfers between devices, on_device(): lax.all_to_all(payload.reshape(SENDERS, 1, ROWS * 128), AXES, split_axis=...  13.7 us
    all_to_all x1, starting transfers between devices, on_device(): lax.all_to_all(payload.reshape(SENDERS, 1, ROWS * 128), AXES, split_axis=...  11.5 us
    ppermute x3, waiting for transfers between devices, exchange(): rb = lax.ppermute(eb, 'slab', swap('slab', 1))  10.7 us
    all_to_all x1, waiting for transfers between devices, on_device(): lax.all_to_all(moments.reshape(SENDERS, 1, 128), AXES, split_axis=0, conc...  8.57 us
    all_to_all x1, starting transfers between devices, on_device(): lax.all_to_all(moments.reshape(SENDERS, 1, 128), AXES, split_axis=0, conc...  8.56 us
    pallas_call x3, Pallas kernels, sides(): pl.pallas_call(functools.partial(sides_kernel, last), name='sides', in_sp...  6.05 us
    ppermute x3, waiting for transfers between devices, exchange(): cb = lax.ppermute(line(jnp.logical_not(up)), AXES, odd_swap())  5.48 us
  transfers between devices with their start and end apart: 20, of which 8 were waited for; matrix products, arithmetic and copies ran while one was open for 0% of the time, Pallas kernels for 8%

profile of v9, /device:TPU:1, one launch (start us, length us, event | category | flops | bytes accessed | tf_op | source)
XLA Modules:
  0.0 99.7 jit_solution(6949235529681044078)
XLA Ops:
  0.7 15.2 %splat.1 = f32[8,144,128]{2,1,0:T(8,128)} custom-call(f32[6,1024,128]{2,1,0:T(8,128)} %bitcast.23, s32[8,128]{1,0:T(8,128)} %bitcast.24, s32[8,128]{1,0:T(8,128)} %bitcast.25), custom_call_target="tpu_custom_call" | custom-call | tf_op jit(solution)/shard_map/splat/pallas_call | solution.py:171
  15.8 11.5 %all-to-all-start = ((f32[128,1,1152]{2,1,0:T(1,128)}), f32[128,1,1152]{2,1,0:T(1,128)S(1)}, u32[]{:S(2)}, u32[]{:S(2)}) async-start(f32[128,1,1152]{2,1,0:T(1,128)} %bitcast.5), calls=%async_computation | async-start | bytes 1179648 | tf_op jit(solution)/shard_map/all_to_all | solution.py:584
  27.9 13.7 %all-to-all-done = f32[128,1,1152]{2,1,0:T(1,128)S(1)} async-done(((f32[128,1,1152]{2,1,0:T(1,128)}), f32[128,1,1152]{2,1,0:T(1,128)S(1)}, u32[]{:S(2)}, u32[]{:S(2)}) %all-to-all-start) | async-done | bytes 589856 | tf_op jit(solution)/shard_map/all_to_all | solution.py:584
  41.6 1.5 %assemble.1 = (f32[64,1024]{1,0:T(8,128)S(1)}, f32[64,1024]{1,0:T(8,128)S(1)}, f32[8,1024]{1,0:T(8,128)S(1)}, f32[8,128]{1,0:T(8,128)S(1)}, f32[64,512]{1,0:T(8,...) custom-call(s32[4]{0:T(128)S(1)} %pad_add_fusion.place_ref, ...), custom_call_target="tpu_custom_call" | custom-call | tf_op jit(solution)/shard_map/assemble/pallas_call | solution.py:339
  43.8 1.0 collective-permute-start.2
  44.9 3.3 %collective-permute-done.1.rb_ref = f32[64,512]{1,0:T(8,128)S(1)} collective-permute-done((f32[64,512]{1,0:T(8,128)S(1)}, f32[64,512]{1,0:T(8,128)S(1)}, u32[]{:S(2)}, u32[]{:S(2)}) %collective-permute-start.1) | collective-permute-done | bytes 131104 | tf_op jit(solution)/shard_map/ppermute | solution.py:568
  48.3 2.2 %collective-permute-start.4 = (f32[64,512]{1,0:T(8,128)S(1)}, f32[64,512]{1,0:T(8,128)S(1)}, u32[]{:S(2)}, u32[]{:S(2)}) collective-permute-start(f32[64,512]{1,0:T(8,128)S(1)} %pad_maximum_fusion), channel_id=1, source_target_pairs={{0,1},{1,0},{2,3},{3,2},{4,5},{5,4},{6,7},{7,6},{8,9},{9,8},{10,11... | collective-permute-start | bytes 393224 | tf_op jit(solution)/shard_map/ppermute | solution.py:576
  50.8 1.7 %sides.3.sum_ref = f32[64,1024]{1,0:T(8,128)S(1)} custom-call(s32[4]{0:T(128)S(1)} %pad_add_fusion.place_ref, f32[64,1024]{1,0:T(8,128)S(1)} %get-tuple-element.32.v_ref.v0_ref, f32[8,1024]{1,0:T(8,128)S(1)} %get-tuple-element.30.mask_ref, f32[64,512]{1,0:T(8,128)S(1)} %collective-permute-done.ra_ref, f32[64,512]{1,0:T(8,128)S(1)} %collective-permute-done.1.rb_ref, ...), custom_call_target="tpu_custom_call" | custom-call | flops 1500000000 | bytes 2000000 | tf_op jit(solution)/shard_map/sides/pallas_call | solution.py:424
  52.5 2.7 %collective-permute-done.5.cb_ref = f32[64,512]{1,0:T(8,128)S(1)} collective-permute-done((f32[64,512]{1,0:T(8,128)S(1)}, f32[64,512]{1,0:T(8,128)S(1)}, u32[]{:S(2)}, u32[]{:S(2)}) %collective-permute-start.5) | collective-permute-done | bytes 131104 | tf_op jit(solution)/shard_map/ppermute | solution.py:575
  55.1 1.1 %corners.3 = (f32[64,1024]{1,0:T(8,128)S(1)}, f32[8,128]{1,0:T(8,128)S(1)}, f32[64,512]{1,0:T(8,128)S(1)}, f32[64,512]{1,0:T(8,128)S(1)}, f32[64,512]{1,0:T(8,128)S(1)}, /*index=5*/f32[64,512]{1,0:T(8,128)S(1)}) custom-call(s32[4]{0:T(128)S(1)} %pad_add_fusion.place_ref, f32[64,1024]{1,0:T(8,128)S(1)} %sides.3.sum_ref, ...), custom_call_target="tpu_custom_call" | custom-call | flops 500000000 | bytes 2000000 | tf_op jit(solution)/shard_map/corners/pallas_call | solution.py:463
  56.3 1.8 %collective-permute-start.7 = (f32[64,512]{1,0:T(8,128)S(1)}, f32[64,512]{1,0:T(8,128)S(1)}, u32[]{:S(2)}, u32[]{:S(2)}) collective-permute-start(f32[64,512]{1,0:T(8,128)S(1)} %get-tuple-element.43), channel_id=1, source_target_pairs={{0,96},{32,64},{64,32},{96,0},{1,97},{33,65},{65,33},{97,1},{2,98}... | collective-permute-start | bytes 393224 | tf_op jit(solution)/shard_map/ppermute | solution.py:568
  58.7 3.5 %collective-permute-done.7.rb_ref = f32[64,512]{1,0:T(8,128)S(1)} collective-permute-done((f32[64,512]{1,0:T(8,128)S(1)}, f32[64,512]{1,0:T(8,128)S(1)}, u32[]{:S(2)}, u32[]{:S(2)}) %collective-permute-start.7) | collective-permute-done | bytes 131104 | tf_op jit(solution)/shard_map/ppermute | solution.py:568
  62.5 1.6 %collective-permute-start.10 = (f32[64,512]{1,0:T(8,128)S(1)}, f32[64,512]{1,0:T(8,128)S(1)}, u32[]{:S(2)}, u32[]{:S(2)}) collective-permute-start(f32[64,512]{1,0:T(8,128)S(1)} %pad_maximum_fusion.2), channel_id=1, source_target_pairs={{0,1},{1,0},{2,3},{3,2},{4,5},{5,4},{6,7},{7,6},{8,9},{9,8},{10,11... | collective-permute-start | bytes 393224 | tf_op jit(solution)/shard_map/ppermute | solution.py:576
  64.2 1.7 %sides.4.sum_ref = f32[64,1024]{1,0:T(8,128)S(1)} custom-call(s32[4]{0:T(128)S(1)} %pad_add_fusion.place_ref, f32[64,1024]{1,0:T(8,128)S(1)} %get-tuple-element.41.v_ref.v1_ref, f32[8,1024]{1,0:T(8,128)S(1)} %get-tuple-element.30.mask_ref, f32[64,512]{1,0:T(8,128)S(1)} %collective-permute-done.6.ra_ref, f32[64,512]{1,0:T(8,128)S(1)} %collective-permute-done.7.rb_ref, ...), custom_call_target="tpu_custom_call" | custom-call | flops 1500000000 | bytes 2000000 | tf_op jit(solution)/shard_map/sides/pallas_call | solution.py:424
  65.9 2.8 %collective-permute-done.11.cb_ref = f32[64,512]{1,0:T(8,128)S(1)} collective-permute-done((f32[64,512]{1,0:T(8,128)S(1)}, f32[64,512]{1,0:T(8,128)S(1)}, u32[]{:S(2)}, u32[]{:S(2)}) %collective-permute-start.11) | collective-permute-done | bytes 131104 | tf_op jit(solution)/shard_map/ppermute | solution.py:575
  68.8 1.1 %corners.4 = (f32[64,1024]{1,0:T(8,128)S(1)}, f32[8,128]{1,0:T(8,128)S(1)}, f32[64,512]{1,0:T(8,128)S(1)}, f32[64,512]{1,0:T(8,128)S(1)}, f32[64,512]{1,0:T(8,128)S(1)}, /*index=5*/f32[64,512]{1,0:T(8,128)S(1)}) custom-call(s32[4]{0:T(128)S(1)} %pad_add_fusion.place_ref, f32[64,1024]{1,0:T(8,128)S(1)} %sides.4.sum_ref, ...), custom_call_target="tpu_custom_call" | custom-call | flops 500000000 | bytes 2000000 | tf_op jit(solution)/shard_map/corners/pallas_call | solution.py:463
  69.9 1.3 %collective-permute-start.13 = (f32[64,512]{1,0:T(8,128)S(1)}, f32[64,512]{1,0:T(8,128)S(1)}, u32[]{:S(2)}, u32[]{:S(2)}) collective-permute-start(f32[64,512]{1,0:T(8,128)S(1)} %get-tuple-element.49), channel_id=1, source_target_pairs={{0,96},{32,64},{64,32},{96,0},{1,97},{33,65},{65,33},{97,1},{2,98}... | collective-permute-start | bytes 393224 | tf_op jit(solution)/shard_map/ppermute | solution.py:568
  71.9 4.0 %collective-permute-done.13.rb_ref = f32[64,512]{1,0:T(8,128)S(1)} collective-permute-done((f32[64,512]{1,0:T(8,128)S(1)}, f32[64,512]{1,0:T(8,128)S(1)}, u32[]{:S(2)}, u32[]{:S(2)}) %collective-permute-start.13) | collective-permute-done | bytes 131104 | tf_op jit(solution)/shard_map/ppermute | solution.py:568
  75.9 1.3 %collective-permute-start.16 = (f32[64,512]{1,0:T(8,128)S(1)}, f32[64,512]{1,0:T(8,128)S(1)}, u32[]{:S(2)}, u32[]{:S(2)}) collective-permute-start(f32[64,512]{1,0:T(8,128)S(1)} %pad_maximum_fusion.4), channel_id=1, source_target_pairs={{0,1},{1,0},{2,3},{3,2},{4,5},{5,4},{6,7},{7,6},{8,9},{9,8},{10,11... | collective-permute-start | bytes 393224 | tf_op jit(solution)/shard_map/ppermute | solution.py:576
  77.5 2.6 %sides.5 = (f32[64,1024]{1,0:T(8,128)S(1)}, f32[128,128]{1,0:T(8,128)}) custom-call(s32[4]{0:T(128)S(1)} %pad_add_fusion.place_ref, f32[64,1024]{1,0:T(8,128)S(1)} %get-tuple-element.47.v_ref.v2_ref, f32[8,1024]{1,0:T(8,128)S(1)} %get-tuple-element.30.mask_ref, f32[64,512]{1,0:T(8,128)S(1)} %collective-permute-done.12.ra_ref, ...), custom_call_target="tpu_custom_call" | custom-call | flops 1500000000 | bytes 2000000 | tf_op jit(solution)/shard_map/sides/pallas_call | solution.py:424
  80.2 8.6 %all-to-all-start.1 = ((f32[128,1,128]{2,1,0:T(1,128)}), f32[128,1,128]{2,1,0:T(1,128)S(1)}, u32[]{:S(2)}, u32[]{:S(2)}) async-start(f32[128,1,128]{2,1,0:T(1,128)} %bitcast.8), calls=%async_computation.1 | async-start | bytes 131072 | tf_op jit(solution)/shard_map/all_to_all | solution.py:594
  88.8 1.0 corners.5.v3_ref
  89.7 8.6 %all-to-all-done.1 = f32[128,1,128]{2,1,0:T(1,128)S(1)} async-done(((f32[128,1,128]{2,1,0:T(1,128)}), f32[128,1,128]{2,1,0:T(1,128)S(1)}, u32[]{:S(2)}, u32[]{:S(2)}) %all-to-all-start.1) | async-done | bytes 65568 | tf_op jit(solution)/shard_map/all_to_all | solution.py:594
  98.3 1.4 %finish.1 = (f32[64,8,128]{2,1,0:T(8,128)}, f32[64,8,128]{2,1,0:T(8,128)}) custom-call(f32[128,128]{1,0:T(8,128)S(1)} %bitcast.22, f32[8,128]{1,0:T(8,128)S(1)} %get-tuple-element.52.rest_3_.c_ref, f32[64,1024]{1,0:T(8,128)S(1)} %get-tuple-element.32.v_ref.v0_ref, f32[64,1024]{1,0:T(8,128)S(1)} %get-tuple-element.41.v_ref.v1_ref, ...), custom_call_target="tpu_custom_call" | custom-call | tf_op jit(solution)/shard_map/finish/pallas_call | solution.py:538
  (43 shorter events, 3.8 us)
Async XLA Ops:
  0.6 26.7 %copy-start = (f32[27,64,64]{2,1,0:T(8,128)S(1)}, f32[27,64,64]{2,1,0:T(8,128)}, u32[]{:S(2)}) copy-start(f32[27,64,64]{2,1,0:T(8,128)} %coupling_ref.1) | copy-start | bytes 1327108
  0.6 26.7 %copy-start.1 = (s32[2,2,256]{2,1,0:T(2,128)S(1)}, s32[2,2,256]{2,1,0:T(2,128)}, u32[]{:S(2)}) copy-start(s32[2,2,256]{2,1,0:T(2,128)} %occ_ref.1) | copy-start | bytes 12292
  15.8 25.8 %all-to-all-start = ((f32[128,1,1152]{2,1,0:T(1,128)}), f32[128,1,1152]{2,1,0:T(1,128)S(1)}, u32[]{:S(2)}, u32[]{:S(2)}) async-start(f32[128,1,1152]{2,1,0:T(1,128)} %bitcast.5), calls=%async_computation | async-start | bytes 1179648 | tf_op jit(solution)/shard_map/all_to_all | solution.py:584
  43.1 5.1 %collective-permute-start.1 = (f32[64,512]{1,0:T(8,128)S(1)}, f32[64,512]{1,0:T(8,128)S(1)}, u32[]{:S(2)}, u32[]{:S(2)}) collective-permute-start(f32[64,512]{1,0:T(8,128)S(1)} %get-tuple-element.34), channel_id=1, source_target_pairs={{0,96},{32,64},{64,32},{96,0},{1,97},{33,65},{65,33},{97,1},{2,98}... | collective-permute-start | bytes 393224 | tf_op jit(solution)/shard_map/ppermute | solution.py:568
  43.5 4.7 %collective-permute-start = (f32[64,512]{1,0:T(8,128)S(1)}, f32[64,512]{1,0:T(8,128)S(1)}, u32[]{:S(2)}, u32[]{:S(2)}) collective-permute-start(f32[64,512]{1,0:T(8,128)S(1)} %get-tuple-element.33), channel_id=1, source_target_pairs={{0,32},{32,0},{64,96},{96,64},{1,33},{33,1},{65,97},{97,65},{2,34}... | collective-permute-start | bytes 393224 | tf_op jit(solution)/shard_map/ppermute | solution.py:567
  43.8 6.9 %collective-permute-start.2 = (f32[64,512]{1,0:T(8,128)S(1)}, f32[64,512]{1,0:T(8,128)S(1)}, u32[]{:S(2)}, u32[]{:S(2)}) collective-permute-start(f32[64,512]{1,0:T(8,128)S(1)} %get-tuple-element.35), channel_id=1, source_target_pairs={{0,1},{1,0},{2,3},{3,2},{4,5},{5,4},{6,7},{7,6},{8,9},{9,8},{10,11... | collective-permute-start | bytes 393224 | tf_op jit(solution)/shard_map/ppermute | solution.py:569
  44.8 6.0 %collective-permute-start.3 = (f32[64,512]{1,0:T(8,128)S(1)}, f32[64,512]{1,0:T(8,128)S(1)}, u32[]{:S(2)}, u32[]{:S(2)}) collective-permute-start(f32[64,512]{1,0:T(8,128)S(1)} %get-tuple-element.36), channel_id=1, source_target_pairs={{0,32},{1,2},{2,1},{3,4},{4,3},{5,6},{6,5},{7,8},{8,7},{9,10},{10,... | collective-permute-start | bytes 393224 | tf_op jit(solution)/shard_map/ppermute | solution.py:566
  48.3 4.2 %collective-permute-start.4 = (f32[64,512]{1,0:T(8,128)S(1)}, f32[64,512]{1,0:T(8,128)S(1)}, u32[]{:S(2)}, u32[]{:S(2)}) collective-permute-start(f32[64,512]{1,0:T(8,128)S(1)} %pad_maximum_fusion), channel_id=1, source_target_pairs={{0,1},{1,0},{2,3},{3,2},{4,5},{5,4},{6,7},{7,6},{8,9},{9,8},{10,11... | collective-permute-start | bytes 393224 | tf_op jit(solution)/shard_map/ppermute | solution.py:576
  50.5 4.7 %collective-permute-start.5 = (f32[64,512]{1,0:T(8,128)S(1)}, f32[64,512]{1,0:T(8,128)S(1)}, u32[]{:S(2)}, u32[]{:S(2)}) collective-permute-start(f32[64,512]{1,0:T(8,128)S(1)} %pad_maximum_fusion.1), channel_id=1, source_target_pairs={{0,32},{1,2},{2,1},{3,4},{4,3},{5,6},{6,5},{7,8},{8,7},{9,10},{10,... | collective-permute-start | bytes 393224 | tf_op jit(solution)/shard_map/ppermute | solution.py:575
  56.3 6.0 %collective-permute-start.7 = (f32[64,512]{1,0:T(8,128)S(1)}, f32[64,512]{1,0:T(8,128)S(1)}, u32[]{:S(2)}, u32[]{:S(2)}) collective-permute-start(f32[64,512]{1,0:T(8,128)S(1)} %get-tuple-element.43), channel_id=1, source_target_pairs={{0,96},{32,64},{64,32},{96,0},{1,97},{33,65},{65,33},{97,1},{2,98}... | collective-permute-start | bytes 393224 | tf_op jit(solution)/shard_map/ppermute | solution.py:568
  58.0 4.4 %collective-permute-start.6 = (f32[64,512]{1,0:T(8,128)S(1)}, f32[64,512]{1,0:T(8,128)S(1)}, u32[]{:S(2)}, u32[]{:S(2)}) collective-permute-start(f32[64,512]{1,0:T(8,128)S(1)} %get-tuple-element.42), channel_id=1, source_target_pairs={{0,32},{32,0},{64,96},{96,64},{1,33},{33,1},{65,97},{97,65},{2,34}... | collective-permute-start | bytes 393224 | tf_op jit(solution)/shard_map/ppermute | solution.py:567
  58.0 6.1 %collective-permute-start.8 = (f32[64,512]{1,0:T(8,128)S(1)}, f32[64,512]{1,0:T(8,128)S(1)}, u32[]{:S(2)}, u32[]{:S(2)}) collective-permute-start(f32[64,512]{1,0:T(8,128)S(1)} %get-tuple-element.44), channel_id=1, source_target_pairs={{0,1},{1,0},{2,3},{3,2},{4,5},{5,4},{6,7},{7,6},{8,9},{9,8},{10,11... | collective-permute-start | bytes 393224 | tf_op jit(solution)/shard_map/ppermute | solution.py:569
  58.7 5.5 %collective-permute-start.9 = (f32[64,512]{1,0:T(8,128)S(1)}, f32[64,512]{1,0:T(8,128)S(1)}, u32[]{:S(2)}, u32[]{:S(2)}) collective-permute-start(f32[64,512]{1,0:T(8,128)S(1)} %get-tuple-element.45), channel_id=1, source_target_pairs={{0,32},{1,2},{2,1},{3,4},{4,3},{5,6},{6,5},{7,8},{8,7},{9,10},{10,... | collective-permute-start | bytes 393224 | tf_op jit(solution)/shard_map/ppermute | solution.py:566
  62.5 3.5 %collective-permute-start.10 = (f32[64,512]{1,0:T(8,128)S(1)}, f32[64,512]{1,0:T(8,128)S(1)}, u32[]{:S(2)}, u32[]{:S(2)}) collective-permute-start(f32[64,512]{1,0:T(8,128)S(1)} %pad_maximum_fusion.2), channel_id=1, source_target_pairs={{0,1},{1,0},{2,3},{3,2},{4,5},{5,4},{6,7},{7,6},{8,9},{9,8},{10,11... | collective-permute-start | bytes 393224 | tf_op jit(solution)/shard_map/ppermute | solution.py:576
  64.1 4.7 %collective-permute-start.11 = (f32[64,512]{1,0:T(8,128)S(1)}, f32[64,512]{1,0:T(8,128)S(1)}, u32[]{:S(2)}, u32[]{:S(2)}) collective-permute-start(f32[64,512]{1,0:T(8,128)S(1)} %pad_maximum_fusion.3), channel_id=1, source_target_pairs={{0,32},{1,2},{2,1},{3,4},{4,3},{5,6},{6,5},{7,8},{8,7},{9,10},{10,... | collective-permute-start | bytes 393224 | tf_op jit(solution)/shard_map/ppermute | solution.py:575
  69.9 6.0 %collective-permute-start.13 = (f32[64,512]{1,0:T(8,128)S(1)}, f32[64,512]{1,0:T(8,128)S(1)}, u32[]{:S(2)}, u32[]{:S(2)}) collective-permute-start(f32[64,512]{1,0:T(8,128)S(1)} %get-tuple-element.49), channel_id=1, source_target_pairs={{0,96},{32,64},{64,32},{96,0},{1,97},{33,65},{65,33},{97,1},{2,98}... | collective-permute-start | bytes 393224 | tf_op jit(solution)/shard_map/ppermute | solution.py:568
  71.2 4.7 %collective-permute-start.12 = (f32[64,512]{1,0:T(8,128)S(1)}, f32[64,512]{1,0:T(8,128)S(1)}, u32[]{:S(2)}, u32[]{:S(2)}) collective-permute-start(f32[64,512]{1,0:T(8,128)S(1)} %get-tuple-element.48), channel_id=1, source_target_pairs={{0,32},{32,0},{64,96},{96,64},{1,33},{33,1},{65,97},{97,65},{2,34}... | collective-permute-start | bytes 393224 | tf_op jit(solution)/shard_map/ppermute | solution.py:567
  71.2 6.3 %collective-permute-start.14 = (f32[64,512]{1,0:T(8,128)S(1)}, f32[64,512]{1,0:T(8,128)S(1)}, u32[]{:S(2)}, u32[]{:S(2)}) collective-permute-start(f32[64,512]{1,0:T(8,128)S(1)} %get-tuple-element.50), channel_id=1, source_target_pairs={{0,1},{1,0},{2,3},{3,2},{4,5},{5,4},{6,7},{7,6},{8,9},{9,8},{10,11... | collective-permute-start | bytes 393224 | tf_op jit(solution)/shard_map/ppermute | solution.py:569
  71.9 5.7 %collective-permute-start.15 = (f32[64,512]{1,0:T(8,128)S(1)}, f32[64,512]{1,0:T(8,128)S(1)}, u32[]{:S(2)}, u32[]{:S(2)}) collective-permute-start(f32[64,512]{1,0:T(8,128)S(1)} %get-tuple-element.51), channel_id=1, source_target_pairs={{0,32},{1,2},{2,1},{3,4},{4,3},{5,6},{6,5},{7,8},{8,7},{9,10},{10,... | collective-permute-start | bytes 393224 | tf_op jit(solution)/shard_map/ppermute | solution.py:566
  75.9 12.8 %collective-permute-start.16 = (f32[64,512]{1,0:T(8,128)S(1)}, f32[64,512]{1,0:T(8,128)S(1)}, u32[]{:S(2)}, u32[]{:S(2)}) collective-permute-start(f32[64,512]{1,0:T(8,128)S(1)} %pad_maximum_fusion.4), channel_id=1, source_target_pairs={{0,1},{1,0},{2,3},{3,2},{4,5},{5,4},{6,7},{7,6},{8,9},{9,8},{10,11... | collective-permute-start | bytes 393224 | tf_op jit(solution)/shard_map/ppermute | solution.py:576
  77.2 11.5 %collective-permute-start.17 = (f32[64,512]{1,0:T(8,128)S(1)}, f32[64,512]{1,0:T(8,128)S(1)}, u32[]{:S(2)}, u32[]{:S(2)}) collective-permute-start(f32[64,512]{1,0:T(8,128)S(1)} %pad_maximum_fusion.5), channel_id=1, source_target_pairs={{0,32},{1,2},{2,1},{3,4},{4,3},{5,6},{6,5},{7,8},{8,7},{9,10},{10,... | collective-permute-start | bytes 393224 | tf_op jit(solution)/shard_map/ppermute | solution.py:575
  80.2 18.1 %all-to-all-start.1 = ((f32[128,1,128]{2,1,0:T(1,128)}), f32[128,1,128]{2,1,0:T(1,128)S(1)}, u32[]{:S(2)}, u32[]{:S(2)}) async-start(f32[128,1,128]{2,1,0:T(1,128)} %bitcast.8), calls=%async_computation.1 | async-start | bytes 131072 | tf_op jit(solution)/shard_map/all_to_all | solution.py:594

commit v10 on v9

--- a/solution.py
+++ b/solution.py
@@ -55,9 +55,8 @@
     def fetch(g):
         return pltpu.make_async_copy(samp_ref.at[:, pl.ds(g * 128, 128), :], held.at[g], sems.at[g])
 
-    def turn(g):
-        for k in range(6):
-            flip[k] = held[g, k].T
+    def turn(g, k):
+        flip[k] = held[g, k].T
 
     def evaluate(g):
         counts = cnt_ref[pl.ds(g, 1), :]
@@ -80,7 +79,8 @@
                     basis[8 + 8 * d + i, rows, :] = val[i]
                     basis[12 + 8 * d + i, rows, :] = slo[i]
 
-    def accumulate(i, js):
+    def accumulate(block):
+        i = block
         rhs_sums, dens_sums = {}, {}
         for group in range(16):
             rows = pl.ds(group * 8, 8)
@@ -90,7 +90,7 @@
             d = basis[12 + i, rows, :]
             v2 = [basis[24 + l, rows, :] for l in range(4)]
             s2 = [basis[28 + l, rows, :] for l in range(4)]
-            for j in js:
+            for j in range(4):
                 v1 = basis[16 + j, rows, :]
                 s1 = basis[20 + j, rows, :]
                 first = a * v1 + b * s1
@@ -102,9 +102,9 @@
                     den = dens * v2[l]
                     rhs_sums[at] = rhs if group == 0 else rhs_sums[at] + rhs
                     dens_sums[at] = den if group == 0 else dens_sums[at] + den
-        for at in rhs_sums:
-            acc[pl.ds((i * 16 + at) * 8, 8), :] = rhs_sums[at]
-            acc[pl.ds((64 + i * 16 + at) * 8, 8), :] = dens_sums[at]
+        for at in range(16):
+            acc[pl.ds(pl.multiple_of(block * 128, 128) + at * 8, 8), :] = rhs_sums[at]
+            acc[pl.ds(pl.multiple_of(block * 128, 128) + 512 + at * 8, 8), :] = dens_sums[at]
 
     def settle(g, real):
         total = acc[pl.ds(0, 128, stride=8), :]
@@ -132,7 +132,8 @@
     acc[...] = jnp.zeros_like(acc)
     counts_copy.wait()
     fetch(0).wait()
-    turn(0)
+    for k in range(6):
+        turn(0, k)
 
     def advance(g, carry):
         following = jnp.minimum(g + 1, groups - 1)
@@ -143,10 +144,14 @@
 
         settle(jnp.maximum(g - 1, 0), g > 0)
         evaluate(g)
-        turn(following)
-        for i in range(4):
-            for js in ((0, 1), (2, 3)):
-                accumulate(i, js)
+
+        def block_sums(block, kept):
+            turn(following, block)
+            turn(following, 4 + block % 2)
+            accumulate(block)
+            return kept
+
+        lax.fori_loop(0, 4, block_sums, 0)
         return carry
 
     lax.fori_loop(0, groups, advance, 0)

time: 99.9 us -> 100 us (level)
  no operation moved by 1% of the time
where the time goes in v10:
time: 100 us
  waiting for transfers between devices  38.7 us (39%)
  starting transfers between devices  31.9 us (32%)
  Pallas kernels  28.2 us (28%)
    pallas_call x1, Pallas kernels, splat(): pl.pallas_call(splat_kernel, name='splat', in_specs=[pl.BlockSpec(memory_...  15.6 us
    all_to_all x1, waiting for transfers between devices, on_device(): lax.all_to_all(payload.reshape(SENDERS, 1, ROWS * 128), AXES, split_axis=...  13.7 us
    all_to_all x1, starting transfers between devices, on_device(): lax.all_to_all(payload.reshape(SENDERS, 1, ROWS * 128), AXES, split_axis=...  11.5 us
    ppermute x3, waiting for transfers between devices, exchange(): rb = lax.ppermute(eb, 'slab', swap('slab', 1))  10.7 us
    all_to_all x1, waiting for transfers between devices, on_device(): lax.all_to_all(moments.reshape(SENDERS, 1, 128), AXES, split_axis=0, conc...  8.57 us
    all_to_all x1, starting transfers between devices, on_device(): lax.all_to_all(moments.reshape(SENDERS, 1, 128), AXES, split_axis=0, conc...  8.56 us
    pallas_call x3, Pallas kernels, sides(): pl.pallas_call(functools.partial(sides_kernel, last), name='sides', in_sp...  6.05 us
    ppermute x3, waiting for transfers between devices, exchange(): cb = lax.ppermute(line(jnp.logical_not(up)), AXES, odd_swap())  5.48 us
  transfers between devices with their start and end apart: 20, of which 8 were waited for; matrix products, arithmetic and copies ran while one was open for 0% of the time, Pallas kernels for 8%

profile of v10, /device:TPU:1, one launch (start us, length us, event | category | flops | bytes accessed | tf_op | source)
XLA Modules:
  0.0 100.0 jit_solution(1195953727651503048)
XLA Ops:
  0.7 15.6 %splat.1 = f32[8,144,128]{2,1,0:T(8,128)} custom-call(f32[6,1024,128]{2,1,0:T(8,128)} %bitcast.23, s32[8,128]{1,0:T(8,128)} %bitcast.24, s32[8,128]{1,0:T(8,128)} %bitcast.25), custom_call_target="tpu_custom_call" | custom-call | tf_op jit(solution)/shard_map/splat/pallas_call | solution.py:176
  16.3 11.5 %all-to-all-start = ((f32[128,1,1152]{2,1,0:T(1,128)}), f32[128,1,1152]{2,1,0:T(1,128)S(1)}, u32[]{:S(2)}, u32[]{:S(2)}) async-start(f32[128,1,1152]{2,1,0:T(1,128)} %bitcast.5), calls=%async_computation | async-start | bytes 1179648 | tf_op jit(solution)/shard_map/all_to_all | solution.py:589
  28.4 13.7 %all-to-all-done = f32[128,1,1152]{2,1,0:T(1,128)S(1)} async-done(((f32[128,1,1152]{2,1,0:T(1,128)}), f32[128,1,1152]{2,1,0:T(1,128)S(1)}, u32[]{:S(2)}, u32[]{:S(2)}) %all-to-all-start) | async-done | bytes 589856 | tf_op jit(solution)/shard_map/all_to_all | solution.py:589
  42.1 1.5 %assemble.1 = (f32[64,1024]{1,0:T(8,128)S(1)}, f32[64,1024]{1,0:T(8,128)S(1)}, f32[8,1024]{1,0:T(8,128)S(1)}, f32[8,128]{1,0:T(8,128)S(1)}, f32[64,512]{1,0:T(8,...) custom-call(s32[4]{0:T(128)S(1)} %pad_add_fusion.place_ref, ...), custom_call_target="tpu_custom_call" | custom-call | tf_op jit(solution)/shard_map/assemble/pallas_call | solution.py:344
  44.3 1.0 collective-permute-start.2
  45.4 3.3 %collective-permute-done.1.rb_ref = f32[64,512]{1,0:T(8,128)S(1)} collective-permute-done((f32[64,512]{1,0:T(8,128)S(1)}, f32[64,512]{1,0:T(8,128)S(1)}, u32[]{:S(2)}, u32[]{:S(2)}) %collective-permute-start.1) | collective-permute-done | bytes 131104 | tf_op jit(solution)/shard_map/ppermute | solution.py:573
  48.7 2.2 %collective-permute-start.4 = (f32[64,512]{1,0:T(8,128)S(1)}, f32[64,512]{1,0:T(8,128)S(1)}, u32[]{:S(2)}, u32[]{:S(2)}) collective-permute-start(f32[64,512]{1,0:T(8,128)S(1)} %pad_maximum_fusion), channel_id=1, source_target_pairs={{0,1},{1,0},{2,3},{3,2},{4,5},{5,4},{6,7},{7,6},{8,9},{9,8},{10,11... | collective-permute-start | bytes 393224 | tf_op jit(solution)/shard_map/ppermute | solution.py:581
  51.2 1.7 %sides.3.sum_ref = f32[64,1024]{1,0:T(8,128)S(1)} custom-call(s32[4]{0:T(128)S(1)} %pad_add_fusion.place_ref, f32[64,1024]{1,0:T(8,128)S(1)} %get-tuple-element.32.v_ref.v0_ref, f32[8,1024]{1,0:T(8,128)S(1)} %get-tuple-element.30.mask_ref, f32[64,512]{1,0:T(8,128)S(1)} %collective-permute-done.ra_ref, f32[64,512]{1,0:T(8,128)S(1)} %collective-permute-done.1.rb_ref, ...), custom_call_target="tpu_custom_call" | custom-call | flops 1500000000 | bytes 2000000 | tf_op jit(solution)/shard_map/sides/pallas_call | solution.py:429
  53.0 2.7 %collective-permute-done.5.cb_ref = f32[64,512]{1,0:T(8,128)S(1)} collective-permute-done((f32[64,512]{1,0:T(8,128)S(1)}, f32[64,512]{1,0:T(8,128)S(1)}, u32[]{:S(2)}, u32[]{:S(2)}) %collective-permute-start.5) | collective-permute-done | bytes 131104 | tf_op jit(solution)/shard_map/ppermute | solution.py:580
  55.6 1.1 %corners.3 = (f32[64,1024]{1,0:T(8,128)S(1)}, f32[8,128]{1,0:T(8,128)S(1)}, f32[64,512]{1,0:T(8,128)S(1)}, f32[64,512]{1,0:T(8,128)S(1)}, f32[64,512]{1,0:T(8,128)S(1)}, /*index=5*/f32[64,512]{1,0:T(8,128)S(1)}) custom-call(s32[4]{0:T(128)S(1)} %pad_add_fusion.place_ref, f32[64,1024]{1,0:T(8,128)S(1)} %sides.3.sum_ref, ...), custom_call_target="tpu_custom_call" | custom-call | flops 500000000 | bytes 2000000 | tf_op jit(solution)/shard_map/corners/pallas_call | solution.py:468
  56.7 1.8 %collective-permute-start.7 = (f32[64,512]{1,0:T(8,128)S(1)}, f32[64,512]{1,0:T(8,128)S(1)}, u32[]{:S(2)}, u32[]{:S(2)}) collective-permute-start(f32[64,512]{1,0:T(8,128)S(1)} %get-tuple-element.43), channel_id=1, source_target_pairs={{0,96},{32,64},{64,32},{96,0},{1,97},{33,65},{65,33},{97,1},{2,98}... | collective-permute-start | bytes 393224 | tf_op jit(solution)/shard_map/ppermute | solution.py:573
  59.2 3.5 %collective-permute-done.7.rb_ref = f32[64,512]{1,0:T(8,128)S(1)} collective-permute-done((f32[64,512]{1,0:T(8,128)S(1)}, f32[64,512]{1,0:T(8,128)S(1)}, u32[]{:S(2)}, u32[]{:S(2)}) %collective-permute-start.7) | collective-permute-done | bytes 131104 | tf_op jit(solution)/shard_map/ppermute | solution.py:573
  62.9 1.6 %collective-permute-start.10 = (f32[64,512]{1,0:T(8,128)S(1)}, f32[64,512]{1,0:T(8,128)S(1)}, u32[]{:S(2)}, u32[]{:S(2)}) collective-permute-start(f32[64,512]{1,0:T(8,128)S(1)} %pad_maximum_fusion.2), channel_id=1, source_target_pairs={{0,1},{1,0},{2,3},{3,2},{4,5},{5,4},{6,7},{7,6},{8,9},{9,8},{10,11... | collective-permute-start | bytes 393224 | tf_op jit(solution)/shard_map/ppermute | solution.py:581
  64.7 1.7 %sides.4.sum_ref = f32[64,1024]{1,0:T(8,128)S(1)} custom-call(s32[4]{0:T(128)S(1)} %pad_add_fusion.place_ref, f32[64,1024]{1,0:T(8,128)S(1)} %get-tuple-element.41.v_ref.v1_ref, f32[8,1024]{1,0:T(8,128)S(1)} %get-tuple-element.30.mask_ref, f32[64,512]{1,0:T(8,128)S(1)} %collective-permute-done.6.ra_ref, f32[64,512]{1,0:T(8,128)S(1)} %collective-permute-done.7.rb_ref, ...), custom_call_target="tpu_custom_call" | custom-call | flops 1500000000 | bytes 2000000 | tf_op jit(solution)/shard_map/sides/pallas_call | solution.py:429
  66.4 2.8 %collective-permute-done.11.cb_ref = f32[64,512]{1,0:T(8,128)S(1)} collective-permute-done((f32[64,512]{1,0:T(8,128)S(1)}, f32[64,512]{1,0:T(8,128)S(1)}, u32[]{:S(2)}, u32[]{:S(2)}) %collective-permute-start.11) | collective-permute-done | bytes 131104 | tf_op jit(solution)/shard_map/ppermute | solution.py:580
  69.2 1.1 %corners.4 = (f32[64,1024]{1,0:T(8,128)S(1)}, f32[8,128]{1,0:T(8,128)S(1)}, f32[64,512]{1,0:T(8,128)S(1)}, f32[64,512]{1,0:T(8,128)S(1)}, f32[64,512]{1,0:T(8,128)S(1)}, /*index=5*/f32[64,512]{1,0:T(8,128)S(1)}) custom-call(s32[4]{0:T(128)S(1)} %pad_add_fusion.place_ref, f32[64,1024]{1,0:T(8,128)S(1)} %sides.4.sum_ref, ...), custom_call_target="tpu_custom_call" | custom-call | flops 500000000 | bytes 2000000 | tf_op jit(solution)/shard_map/corners/pallas_call | solution.py:468
  70.4 1.3 %collective-permute-start.13 = (f32[64,512]{1,0:T(8,128)S(1)}, f32[64,512]{1,0:T(8,128)S(1)}, u32[]{:S(2)}, u32[]{:S(2)}) collective-permute-start(f32[64,512]{1,0:T(8,128)S(1)} %get-tuple-element.49), channel_id=1, source_target_pairs={{0,96},{32,64},{64,32},{96,0},{1,97},{33,65},{65,33},{97,1},{2,98}... | collective-permute-start | bytes 393224 | tf_op jit(solution)/shard_map/ppermute | solution.py:573
  72.4 4.0 %collective-permute-done.13.rb_ref = f32[64,512]{1,0:T(8,128)S(1)} collective-permute-done((f32[64,512]{1,0:T(8,128)S(1)}, f32[64,512]{1,0:T(8,128)S(1)}, u32[]{:S(2)}, u32[]{:S(2)}) %collective-permute-start.13) | collective-permute-done | bytes 131104 | tf_op jit(solution)/shard_map/ppermute | solution.py:573
  76.4 1.3 %collective-permute-start.16 = (f32[64,512]{1,0:T(8,128)S(1)}, f32[64,512]{1,0:T(8,128)S(1)}, u32[]{:S(2)}, u32[]{:S(2)}) collective-permute-start(f32[64,512]{1,0:T(8,128)S(1)} %pad_maximum_fusion.4), channel_id=1, source_target_pairs={{0,1},{1,0},{2,3},{3,2},{4,5},{5,4},{6,7},{7,6},{8,9},{9,8},{10,11... | collective-permute-start | bytes 393224 | tf_op jit(solution)/shard_map/ppermute | solution.py:581
  77.8 2.6 %sides.5 = (f32[64,1024]{1,0:T(8,128)S(1)}, f32[128,128]{1,0:T(8,128)}) custom-call(s32[4]{0:T(128)S(1)} %pad_add_fusion.place_ref, f32[64,1024]{1,0:T(8,128)S(1)} %get-tuple-element.47.v_ref.v2_ref, f32[8,1024]{1,0:T(8,128)S(1)} %get-tuple-element.30.mask_ref, f32[64,512]{1,0:T(8,128)S(1)} %collective-permute-done.12.ra_ref, ...), custom_call_target="tpu_custom_call" | custom-call | flops 1500000000 | bytes 2000000 | tf_op jit(solution)/shard_map/sides/pallas_call | solution.py:429
  80.5 8.6 %all-to-all-start.1 = ((f32[128,1,128]{2,1,0:T(1,128)}), f32[128,1,128]{2,1,0:T(1,128)S(1)}, u32[]{:S(2)}, u32[]{:S(2)}) async-start(f32[128,1,128]{2,1,0:T(1,128)} %bitcast.8), calls=%async_computation.1 | async-start | bytes 131072 | tf_op jit(solution)/shard_map/all_to_all | solution.py:599
  89.1 1.0 corners.5.v3_ref
  90.0 8.6 %all-to-all-done.1 = f32[128,1,128]{2,1,0:T(1,128)S(1)} async-done(((f32[128,1,128]{2,1,0:T(1,128)}), f32[128,1,128]{2,1,0:T(1,128)S(1)}, u32[]{:S(2)}, u32[]{:S(2)}) %all-to-all-start.1) | async-done | bytes 65568 | tf_op jit(solution)/shard_map/all_to_all | solution.py:599
  98.6 1.4 %finish.1 = (f32[64,8,128]{2,1,0:T(8,128)}, f32[64,8,128]{2,1,0:T(8,128)}) custom-call(f32[128,128]{1,0:T(8,128)S(1)} %bitcast.22, f32[8,128]{1,0:T(8,128)S(1)} %get-tuple-element.52.rest_3_.c_ref, f32[64,1024]{1,0:T(8,128)S(1)} %get-tuple-element.32.v_ref.v0_ref, f32[64,1024]{1,0:T(8,128)S(1)} %get-tuple-element.41.v_ref.v1_ref, ...), custom_call_target="tpu_custom_call" | custom-call | tf_op jit(solution)/shard_map/finish/pallas_call | solution.py:543
  (43 shorter events, 3.6 us)
Async XLA Ops:
  0.6 27.2 %copy-start = (f32[27,64,64]{2,1,0:T(8,128)S(1)}, f32[27,64,64]{2,1,0:T(8,128)}, u32[]{:S(2)}) copy-start(f32[27,64,64]{2,1,0:T(8,128)} %coupling_ref.1) | copy-start | bytes 1327108
  0.6 27.2 %copy-start.1 = (s32[2,2,256]{2,1,0:T(2,128)S(1)}, s32[2,2,256]{2,1,0:T(2,128)}, u32[]{:S(2)}) copy-start(s32[2,2,256]{2,1,0:T(2,128)} %occ_ref.1) | copy-start | bytes 12292
  16.3 25.8 %all-to-all-start = ((f32[128,1,1152]{2,1,0:T(1,128)}), f32[128,1,1152]{2,1,0:T(1,128)S(1)}, u32[]{:S(2)}, u32[]{:S(2)}) async-start(f32[128,1,1152]{2,1,0:T(1,128)} %bitcast.5), calls=%async_computation | async-start | bytes 1179648 | tf_op jit(solution)/shard_map/all_to_all | solution.py:589
  43.6 5.1 %collective-permute-start.1 = (f32[64,512]{1,0:T(8,128)S(1)}, f32[64,512]{1,0:T(8,128)S(1)}, u32[]{:S(2)}, u32[]{:S(2)}) collective-permute-start(f32[64,512]{1,0:T(8,128)S(1)} %get-tuple-element.34), channel_id=1, source_target_pairs={{0,96},{32,64},{64,32},{96,0},{1,97},{33,65},{65,33},{97,1},{2,98}... | collective-permute-start | bytes 393224 | tf_op jit(solution)/shard_map/ppermute | solution.py:573
  44.0 4.7 %collective-permute-start = (f32[64,512]{1,0:T(8,128)S(1)}, f32[64,512]{1,0:T(8,128)S(1)}, u32[]{:S(2)}, u32[]{:S(2)}) collective-permute-start(f32[64,512]{1,0:T(8,128)S(1)} %get-tuple-element.33), channel_id=1, source_target_pairs={{0,32},{32,0},{64,96},{96,64},{1,33},{33,1},{65,97},{97,65},{2,34}... | collective-permute-start | bytes 393224 | tf_op jit(solution)/shard_map/ppermute | solution.py:572
  44.3 6.9 %collective-permute-start.2 = (f32[64,512]{1,0:T(8,128)S(1)}, f32[64,512]{1,0:T(8,128)S(1)}, u32[]{:S(2)}, u32[]{:S(2)}) collective-permute-start(f32[64,512]{1,0:T(8,128)S(1)} %get-tuple-element.35), channel_id=1, source_target_pairs={{0,1},{1,0},{2,3},{3,2},{4,5},{5,4},{6,7},{7,6},{8,9},{9,8},{10,11... | collective-permute-start | bytes 393224 | tf_op jit(solution)/shard_map/ppermute | solution.py:574
  45.3 6.0 %collective-permute-start.3 = (f32[64,512]{1,0:T(8,128)S(1)}, f32[64,512]{1,0:T(8,128)S(1)}, u32[]{:S(2)}, u32[]{:S(2)}) collective-permute-start(f32[64,512]{1,0:T(8,128)S(1)} %get-tuple-element.36), channel_id=1, source_target_pairs={{0,32},{1,2},{2,1},{3,4},{4,3},{5,6},{6,5},{7,8},{8,7},{9,10},{10,... | collective-permute-start | bytes 393224 | tf_op jit(solution)/shard_map/ppermute | solution.py:571
  48.7 4.2 %collective-permute-start.4 = (f32[64,512]{1,0:T(8,128)S(1)}, f32[64,512]{1,0:T(8,128)S(1)}, u32[]{:S(2)}, u32[]{:S(2)}) collective-permute-start(f32[64,512]{1,0:T(8,128)S(1)} %pad_maximum_fusion), channel_id=1, source_target_pairs={{0,1},{1,0},{2,3},{3,2},{4,5},{5,4},{6,7},{7,6},{8,9},{9,8},{10,11... | collective-permute-start | bytes 393224 | tf_op jit(solution)/shard_map/ppermute | solution.py:581
  50.9 4.7 %collective-permute-start.5 = (f32[64,512]{1,0:T(8,128)S(1)}, f32[64,512]{1,0:T(8,128)S(1)}, u32[]{:S(2)}, u32[]{:S(2)}) collective-permute-start(f32[64,512]{1,0:T(8,128)S(1)} %pad_maximum_fusion.1), channel_id=1, source_target_pairs={{0,32},{1,2},{2,1},{3,4},{4,3},{5,6},{6,5},{7,8},{8,7},{9,10},{10,... | collective-permute-start | bytes 393224 | tf_op jit(solution)/shard_map/ppermute | solution.py:580
  56.7 6.0 %collective-permute-start.7 = (f32[64,512]{1,0:T(8,128)S(1)}, f32[64,512]{1,0:T(8,128)S(1)}, u32[]{:S(2)}, u32[]{:S(2)}) collective-permute-start(f32[64,512]{1,0:T(8,128)S(1)} %get-tuple-element.43), channel_id=1, source_target_pairs={{0,96},{32,64},{64,32},{96,0},{1,97},{33,65},{65,33},{97,1},{2,98}... | collective-permute-start | bytes 393224 | tf_op jit(solution)/shard_map/ppermute | solution.py:573
  58.5 4.4 %collective-permute-start.6 = (f32[64,512]{1,0:T(8,128)S(1)}, f32[64,512]{1,0:T(8,128)S(1)}, u32[]{:S(2)}, u32[]{:S(2)}) collective-permute-start(f32[64,512]{1,0:T(8,128)S(1)} %get-tuple-element.42), channel_id=1, source_target_pairs={{0,32},{32,0},{64,96},{96,64},{1,33},{33,1},{65,97},{97,65},{2,34}... | collective-permute-start | bytes 393224 | tf_op jit(solution)/shard_map/ppermute | solution.py:572
  58.5 6.1 %collective-permute-start.8 = (f32[64,512]{1,0:T(8,128)S(1)}, f32[64,512]{1,0:T(8,128)S(1)}, u32[]{:S(2)}, u32[]{:S(2)}) collective-permute-start(f32[64,512]{1,0:T(8,128)S(1)} %get-tuple-element.44), channel_id=1, source_target_pairs={{0,1},{1,0},{2,3},{3,2},{4,5},{5,4},{6,7},{7,6},{8,9},{9,8},{10,11... | collective-permute-start | bytes 393224 | tf_op jit(solution)/shard_map/ppermute | solution.py:574
  59.2 5.5 %collective-permute-start.9 = (f32[64,512]{1,0:T(8,128)S(1)}, f32[64,512]{1,0:T(8,128)S(1)}, u32[]{:S(2)}, u32[]{:S(2)}) collective-permute-start(f32[64,512]{1,0:T(8,128)S(1)} %get-tuple-element.45), channel_id=1, source_target_pairs={{0,32},{1,2},{2,1},{3,4},{4,3},{5,6},{6,5},{7,8},{8,7},{9,10},{10,... | collective-permute-start | bytes 393224 | tf_op jit(solution)/shard_map/ppermute | solution.py:571
  62.9 3.5 %collective-permute-start.10 = (f32[64,512]{1,0:T(8,128)S(1)}, f32[64,512]{1,0:T(8,128)S(1)}, u32[]{:S(2)}, u32[]{:S(2)}) collective-permute-start(f32[64,512]{1,0:T(8,128)S(1)} %pad_maximum_fusion.2), channel_id=1, source_target_pairs={{0,1},{1,0},{2,3},{3,2},{4,5},{5,4},{6,7},{7,6},{8,9},{9,8},{10,11... | collective-permute-start | bytes 393224 | tf_op jit(solution)/shard_map/ppermute | solution.py:581
  64.6 4.7 %collective-permute-start.11 = (f32[64,512]{1,0:T(8,128)S(1)}, f32[64,512]{1,0:T(8,128)S(1)}, u32[]{:S(2)}, u32[]{:S(2)}) collective-permute-start(f32[64,512]{1,0:T(8,128)S(1)} %pad_maximum_fusion.3), channel_id=1, source_target_pairs={{0,32},{1,2},{2,1},{3,4},{4,3},{5,6},{6,5},{7,8},{8,7},{9,10},{10,... | collective-permute-start | bytes 393224 | tf_op jit(solution)/shard_map/ppermute | solution.py:580
  70.4 6.0 %collective-permute-start.13 = (f32[64,512]{1,0:T(8,128)S(1)}, f32[64,512]{1,0:T(8,128)S(1)}, u32[]{:S(2)}, u32[]{:S(2)}) collective-permute-start(f32[64,512]{1,0:T(8,128)S(1)} %get-tuple-element.49), channel_id=1, source_target_pairs={{0,96},{32,64},{64,32},{96,0},{1,97},{33,65},{65,33},{97,1},{2,98}... | collective-permute-start | bytes 393224 | tf_op jit(solution)/shard_map/ppermute | solution.py:573
  71.7 4.7 %collective-permute-start.12 = (f32[64,512]{1,0:T(8,128)S(1)}, f32[64,512]{1,0:T(8,128)S(1)}, u32[]{:S(2)}, u32[]{:S(2)}) collective-permute-start(f32[64,512]{1,0:T(8,128)S(1)} %get-tuple-element.48), channel_id=1, source_target_pairs={{0,32},{32,0},{64,96},{96,64},{1,33},{33,1},{65,97},{97,65},{2,34}... | collective-permute-start | bytes 393224 | tf_op jit(solution)/shard_map/ppermute | solution.py:572
  71.7 6.1 %collective-permute-start.14 = (f32[64,512]{1,0:T(8,128)S(1)}, f32[64,512]{1,0:T(8,128)S(1)}, u32[]{:S(2)}, u32[]{:S(2)}) collective-permute-start(f32[64,512]{1,0:T(8,128)S(1)} %get-tuple-element.50), channel_id=1, source_target_pairs={{0,1},{1,0},{2,3},{3,2},{4,5},{5,4},{6,7},{7,6},{8,9},{9,8},{10,11... | collective-permute-start | bytes 393224 | tf_op jit(solution)/shard_map/ppermute | solution.py:574
  72.4 5.5 %collective-permute-start.15 = (f32[64,512]{1,0:T(8,128)S(1)}, f32[64,512]{1,0:T(8,128)S(1)}, u32[]{:S(2)}, u32[]{:S(2)}) collective-permute-start(f32[64,512]{1,0:T(8,128)S(1)} %get-tuple-element.51), channel_id=1, source_target_pairs={{0,32},{1,2},{2,1},{3,4},{4,3},{5,6},{6,5},{7,8},{8,7},{9,10},{10,... | collective-permute-start | bytes 393224 | tf_op jit(solution)/shard_map/ppermute | solution.py:571
  76.4 12.7 %collective-permute-start.16 = (f32[64,512]{1,0:T(8,128)S(1)}, f32[64,512]{1,0:T(8,128)S(1)}, u32[]{:S(2)}, u32[]{:S(2)}) collective-permute-start(f32[64,512]{1,0:T(8,128)S(1)} %pad_maximum_fusion.4), channel_id=1, source_target_pairs={{0,1},{1,0},{2,3},{3,2},{4,5},{5,4},{6,7},{7,6},{8,9},{9,8},{10,11... | collective-permute-start | bytes 393224 | tf_op jit(solution)/shard_map/ppermute | solution.py:581
  77.7 11.3 %collective-permute-start.17 = (f32[64,512]{1,0:T(8,128)S(1)}, f32[64,512]{1,0:T(8,128)S(1)}, u32[]{:S(2)}, u32[]{:S(2)}) collective-permute-start(f32[64,512]{1,0:T(8,128)S(1)} %pad_maximum_fusion.5), channel_id=1, source_target_pairs={{0,32},{1,2},{2,1},{3,4},{4,3},{5,6},{6,5},{7,8},{8,7},{9,10},{10,... | collective-permute-start | bytes 393224 | tf_op jit(solution)/shard_map/ppermute | solution.py:580
  80.5 18.1 %all-to-all-start.1 = ((f32[128,1,128]{2,1,0:T(1,128)}), f32[128,1,128]{2,1,0:T(1,128)S(1)}, u32[]{:S(2)}, u32[]{:S(2)}) async-start(f32[128,1,128]{2,1,0:T(1,128)} %bitcast.8), calls=%async_computation.1 | async-start | bytes 131072 | tf_op jit(solution)/shard_map/all_to_all | solution.py:599

commit v11 on v9

--- a/solution.py
+++ b/solution.py
@@ -197,9 +197,9 @@
     return pltpu.with_memory_space_constraint(x, pltpu.VMEM)
 
 
-def parity_weights(place_ref):
-    slab, grp = place_ref[0], place_ref[1]
-    slabs, grps = place_ref[2], place_ref[3]
+def parity_weights():
+    slab, grp = lax.axis_index("slab"), lax.axis_index("grp")
+    slabs, grps = lax.axis_size("slab"), lax.axis_size("grp")
 
     def pick(cond):
         return jnp.where(cond, 1.0, 0.0).astype(F32)
@@ -221,9 +221,9 @@
     return pl.ds((x * 2 + y) * BZ, BZ)
 
 
-def store_edges(place_ref, masked, ea_ref, eb_ref, oa_ref, ob_ref):
-    up_slab = place_ref[0] % 2 == 0
-    up_grp = place_ref[1] % 2 == 0
+def store_edges(masked, ea_ref, eb_ref, oa_ref, ob_ref):
+    up_slab = lax.axis_index("slab") % 2 == 0
+    up_grp = lax.axis_index("grp") % 2 == 0
     for k in range(2):
         at = pl.ds(k * BZ, BZ)
         ea_ref[:, at] = jnp.where(up_slab, masked[1][k], masked[0][k])
@@ -284,9 +284,9 @@
     )(coupling, occupied)
 
 
-def assemble_kernel(place_ref, recv_ref, mask_ref, rowabs_ref, v_ref, diag_ref, maskc_ref, c_ref,
+def assemble_kernel(recv_ref, mask_ref, rowabs_ref, v_ref, diag_ref, maskc_ref, c_ref,
                     ea_ref, eb_ref, oa_ref, ob_ref, turned):
-    seat = place_ref[1] % 16
+    seat = lax.axis_index("grp") % 16
     turned[...] = recv_ref[pl.ds(CAP, SENDERS, stride=ROWS), :].T
     where = turned[pl.ds(pl.multiple_of(seat * 8, 8), 8), :].astype(jnp.int32)
     other = lax.rem(seat + 1, 16)
@@ -324,7 +324,7 @@
             diag_ref[:, column(x, y)] = (diag - centre) * inverse
             maskc_ref[:, column(x, y)] = jnp.broadcast_to(mask * inverse, (8, BZ))
             masked[x].append(rhs * mask)
-    store_edges(place_ref, masked, ea_ref, eb_ref, oa_ref, ob_ref)
+    store_edges(masked, ea_ref, eb_ref, oa_ref, ob_ref)
 
 
 FIELD = pltpu.VMEM((NODES, N_COLS * BZ), F32)
@@ -332,10 +332,10 @@
 
 
 def in_specs(count):
-    return [pl.BlockSpec(memory_space=pltpu.SMEM)] + [pl.BlockSpec(memory_space=pltpu.VMEM)] * count
-
-
-def assemble(place, recv, mask, rowabs):
+    return [pl.BlockSpec(memory_space=pltpu.VMEM)] * count
+
+
+def assemble(recv, mask, rowabs):
     return pl.pallas_call(
         assemble_kernel,
         name="assemble",
@@ -344,7 +344,7 @@
         out_shape=[FIELD, FIELD, pltpu.VMEM((8, N_COLS * BZ), F32), pltpu.VMEM((8, 128), F32), EDGE, EDGE, EDGE, EDGE],
         scratch_shapes=[pltpu.VMEM((128, 128), F32)],
         compiler_params=pltpu.CompilerParams(vmem_limit_bytes=16 << 20),
-    )(place, vmem(recv), vmem(mask), vmem(rowabs))
+    )(vmem(recv), vmem(mask), vmem(rowabs))
 
 
 def product(weights, source):
@@ -362,12 +362,12 @@
     mom_out[...] = jnp.broadcast_to(mom, mom_out.shape)
 
 
-def sides_kernel(last, place_ref, v_ref, mask_ref, ra_ref, rb_ref, ya_ref, yb_ref, w_ref, *rest):
+def sides_kernel(last, v_ref, mask_ref, ra_ref, rb_ref, ya_ref, yb_ref, w_ref, *rest):
     if last:
         corner_ref, diag_ref, maskc_ref, c_ref, mom_ref, o_ref, mom_out, high, low = rest
     else:
         o_ref, high, low = rest
-    (x_low, x_high), (y_low, y_high) = parity_weights(place_ref)
+    (x_low, x_high), (y_low, y_high) = parity_weights()
     halo, rise = {}, {}
 
     def at_rows(px, py):
@@ -419,7 +419,7 @@
     put_moments(2, mom_ref, mom_out, sq, cross)
 
 
-def sides(place, operands, last):
+def sides(operands, last):
     shapes = [FIELD] + ([pltpu.VMEM((SENDERS, 128), F32)] if last else [])
     return pl.pallas_call(
         functools.partial(sides_kernel, last),
@@ -430,14 +430,14 @@
         scratch_shapes=[pltpu.VMEM((16 * NODES, BZ), BF16), pltpu.VMEM((16 * NODES, BZ), BF16)],
         compiler_params=pltpu.CompilerParams(vmem_limit_bytes=16 << 20),
         cost_estimate=pl.CostEstimate(flops=15 * 10**8, transcendentals=0, bytes_accessed=2 * 10**6),
-    )(place, *[vmem(x) for x in operands])
-
-
-def corners_kernel(order, last, place_ref, sum_ref, v_ref, diag_ref, mask_ref, maskc_ref, ca_ref, cb_ref, corner_ref, *rest):
+    )(*[vmem(x) for x in operands])
+
+
+def corners_kernel(order, last, sum_ref, v_ref, diag_ref, mask_ref, maskc_ref, ca_ref, cb_ref, corner_ref, *rest):
     rest = list(rest)
     mom_ref = rest.pop(0) if order and not last else None
     o_ref = rest.pop(0)
-    x_pairs, y_pairs = parity_weights(place_ref)
+    x_pairs, y_pairs = parity_weights()
     sq = jnp.zeros((NODES, BZ), F32)
     cross = jnp.zeros((NODES, BZ), F32)
     masked = [[], []]
@@ -454,11 +454,11 @@
                 sq = sq + v * v
                 cross = cross + v * new
     if not last:
-        store_edges(place_ref, masked, *rest[1:])
+        store_edges(masked, *rest[1:])
         put_moments(order, mom_ref, rest[0], sq, cross)
 
 
-def corners(order, place, operands, last):
+def corners(order, operands, last):
     shapes = [FIELD] + ([] if last else [pltpu.VMEM((8, 128), F32)] + [EDGE] * 4)
     return pl.pallas_call(
         functools.partial(corners_kernel, order, last),
@@ -468,18 +468,18 @@
         out_shape=shapes,
         compiler_params=pltpu.CompilerParams(vmem_limit_bytes=16 << 20),
         cost_estimate=pl.CostEstimate(flops=5 * 10**8, transcendentals=0, bytes_accessed=2 * 10**6),
-    )(place, *[vmem(x) for x in operands])
-
-
-def apply_stiffness(order, place, v, diag, mask, maskc, centre, edges, weights, corner, moments):
+    )(*[vmem(x) for x in operands])
+
+
+def apply_stiffness(order, v, diag, mask, maskc, centre, edges, weights, corner, moments):
     last = order == 2
-    ra, rb, ya, yb, ca, cb = exchange(place[1], *edges)
+    ra, rb, ya, yb, ca, cb = exchange(lax.axis_index("grp"), *edges)
     operands = [v, mask, ra, rb, ya, yb, weights] + ([corner, diag, maskc, centre, moments] if last else [])
-    part, *shared = sides(place, operands, last)
+    part, *shared = sides(operands, last)
     operands = [part, v, diag, mask, maskc, ca, cb, corner]
     if last:
-        return corners(order, place, operands, last)[0], shared[0], []
-    new, moments, *edges = corners(order, place, operands + ([] if moments is None else [moments]), last)
+        return corners(order, operands, last)[0], shared[0], []
+    new, moments, *edges = corners(order, operands + ([] if moments is None else [moments]), last)
     return new, moments, edges
 
 
@@ -578,17 +578,15 @@
 
 
 def on_device(samples, block_ids, tile_counts, occupied, coupling):
-    slab, grp = lax.axis_index("slab"), lax.axis_index("grp")
-    place = jnp.stack([slab, grp, lax.axis_size("slab"), lax.axis_size("grp")]).astype(jnp.int32)
     payload = splat(samples, tile_counts, block_ids)
     recv = lax.all_to_all(payload.reshape(SENDERS, 1, ROWS * 128), AXES, split_axis=0, concat_axis=0, tiled=True)
     weights, corner, rowabs, mask = prepare(coupling, occupied)
-    v, diag, maskc, centre, *edges = assemble(place, recv.reshape(SENDERS * ROWS, 128), mask, rowabs)
+    v, diag, maskc, centre, *edges = assemble(recv.reshape(SENDERS * ROWS, 128), mask, rowabs)
     fields = [v]
     moments = None
     for order in range(3):
         v, moments, edges = apply_stiffness(
-            order, place, v, diag, mask, maskc, centre, edges, weights, corner, moments
+            order, v, diag, mask, maskc, centre, edges, weights, corner, moments
         )
         fields.append(v)
     shared = lax.all_to_all(moments.reshape(SENDERS, 1, 128), AXES, split_axis=0, concat_axis=0, tiled=True)

time: 99.9 us -> 97.7 us (0.978)
  Pallas kernels: 27.7 us -> 24 us
  waiting for transfers between devices: 38.7 us -> 40.4 us
    pallas_call x3, Pallas kernels: 6.05 us -> 4.43 us  [sides(): pl.pallas_call(functools.partial(sides_kernel, last), name='sides', in_sp...]
    pallas_call x3, Pallas kernels: 3.18 us -> 1.58 us  [corners(): pl.pallas_call(functools.partial(corners_kernel, order, last), name='corn...]
    ppermute x3, waiting for transfers between devices: 5.48 us -> 6.57 us  [exchange(): cb = lax.ppermute(line(jnp.logical_not(up)), AXES, odd_swap())]
  transfers between devices with their start and end apart: 20 -> 20, of which waited for: 8 -> 8; matrix products, arithmetic and copies ran while one was open for 0% -> 0% of each run, Pallas kernels for 8% -> 5%
where the time goes in v11:
time: 97.7 us; the launch traced here: 97.6 us
  waiting for transfers between devices  40.4 us (41%)
  starting transfers between devices  32.1 us (33%)
  Pallas kernels  24 us (25%)
    pallas_call x1, Pallas kernels, splat(): pl.pallas_call(splat_kernel, name='splat', in_specs=[pl.BlockSpec(memory_...  15.2 us
    all_to_all x1, waiting for transfers between devices, on_device(): lax.all_to_all(payload.reshape(SENDERS, 1, ROWS * 128), AXES, split_axis=...  13.8 us
    all_to_all x1, starting transfers between devices, on_device(): lax.all_to_all(payload.reshape(SENDERS, 1, ROWS * 128), AXES, split_axis=...  11.5 us
    ppermute x3, waiting for transfers between devices, exchange(): rb = lax.ppermute(eb, 'slab', swap('slab', 1))  10.7 us
    all_to_all x1, waiting for transfers between devices, on_device(): lax.all_to_all(moments.reshape(SENDERS, 1, 128), AXES, split_axis=0, conc...  9.11 us
    all_to_all x1, starting transfers between devices, on_device(): lax.all_to_all(moments.reshape(SENDERS, 1, 128), AXES, split_axis=0, conc...  8.56 us
    ppermute x3, waiting for transfers between devices, exchange(): cb = lax.ppermute(line(jnp.logical_not(up)), AXES, odd_swap())  6.57 us
    ppermute x3, starting transfers between devices, exchange(): ca = lax.ppermute(line(up), 'grp', swap('grp', 0))  5.15 us
  transfers between devices with their start and end apart: 20, of which 8 were waited for; matrix products, arithmetic and copies ran while one was open for 0% of the time, Pallas kernels for 5%

profile of v11, /device:TPU:1, one launch (start us, length us, event | category | flops | bytes accessed | tf_op | source)
XLA Modules:
  0.0 97.6 jit_solution(3980023798253796207)
XLA Ops:
  0.7 15.2 %splat.1 = f32[8,144,128]{2,1,0:T(8,128)} custom-call(f32[6,1024,128]{2,1,0:T(8,128)} %bitcast.21, s32[8,128]{1,0:T(8,128)} %bitcast.22, s32[8,128]{1,0:T(8,128)} %bitcast.23), custom_call_target="tpu_custom_call" | custom-call | tf_op jit(solution)/shard_map/splat/pallas_call | solution.py:171
  15.8 11.5 %all-to-all-start = ((f32[128,1,1152]{2,1,0:T(1,128)}), f32[128,1,1152]{2,1,0:T(1,128)S(1)}, u32[]{:S(2)}, u32[]{:S(2)}) async-start(f32[128,1,1152]{2,1,0:T(1,128)} %bitcast.3), calls=%async_computation | async-start | bytes 1179648 | tf_op jit(solution)/shard_map/all_to_all | solution.py:582
  27.8 13.8 %all-to-all-done = f32[128,1,1152]{2,1,0:T(1,128)S(1)} async-done(((f32[128,1,1152]{2,1,0:T(1,128)}), f32[128,1,1152]{2,1,0:T(1,128)S(1)}, u32[]{:S(2)}, u32[]{:S(2)}) %all-to-all-start) | async-done | bytes 589856 | tf_op jit(solution)/shard_map/all_to_all | solution.py:582
  41.6 0.9 assemble.1
  43.3 1.0 collective-permute-start.2
  44.4 3.3 %collective-permute-done.1.rb_ref = f32[64,512]{1,0:T(8,128)S(1)} collective-permute-done((f32[64,512]{1,0:T(8,128)S(1)}, f32[64,512]{1,0:T(8,128)S(1)}, u32[]{:S(2)}, u32[]{:S(2)}) %collective-permute-start.1) | collective-permute-done | bytes 131104 | tf_op jit(solution)/shard_map/ppermute | solution.py:568
  47.7 2.2 %collective-permute-start.4 = (f32[64,512]{1,0:T(8,128)S(1)}, f32[64,512]{1,0:T(8,128)S(1)}, u32[]{:S(2)}, u32[]{:S(2)}) collective-permute-start(f32[64,512]{1,0:T(8,128)S(1)} %pad_maximum_fusion), channel_id=1, source_target_pairs={{0,1},{1,0},{2,3},{3,2},{4,5},{5,4},{6,7},{7,6},{8,9},{9,8},{10,11... | collective-permute-start | bytes 393224 | tf_op jit(solution)/shard_map/ppermute | solution.py:576
  50.2 1.2 %sides.3.sum_ref = f32[64,1024]{1,0:T(8,128)S(1)} custom-call(f32[64,1024]{1,0:T(8,128)S(1)} %get-tuple-element.32.v_ref.v0_ref, f32[8,1024]{1,0:T(8,128)S(1)} %get-tuple-element.30.mask_ref, f32[64,512]{1,0:T(8,128)S(1)} %collective-permute-done.ra_ref, f32[64,512]{1,0:T(8,128)S(1)} %collective-permute-done.1.rb_ref, ...), custom_call_target="tpu_custom_call" | custom-call | flops 1500000000 | bytes 2000000 | tf_op jit(solution)/shard_map/sides/pallas_call | solution.py:424
  51.4 3.2 %collective-permute-done.5.cb_ref = f32[64,512]{1,0:T(8,128)S(1)} collective-permute-done((f32[64,512]{1,0:T(8,128)S(1)}, f32[64,512]{1,0:T(8,128)S(1)}, u32[]{:S(2)}, u32[]{:S(2)}) %collective-permute-start.5) | collective-permute-done | bytes 131104 | tf_op jit(solution)/shard_map/ppermute | solution.py:575
  55.2 1.8 %collective-permute-start.7 = (f32[64,512]{1,0:T(8,128)S(1)}, f32[64,512]{1,0:T(8,128)S(1)}, u32[]{:S(2)}, u32[]{:S(2)}) collective-permute-start(f32[64,512]{1,0:T(8,128)S(1)} %get-tuple-element.43), channel_id=1, source_target_pairs={{0,96},{32,64},{64,32},{96,0},{1,97},{33,65},{65,33},{97,1},{2,98}... | collective-permute-start | bytes 393224 | tf_op jit(solution)/shard_map/ppermute | solution.py:568
  57.0 0.7 collective-permute-start.8
  57.7 3.5 %collective-permute-done.7.rb_ref = f32[64,512]{1,0:T(8,128)S(1)} collective-permute-done((f32[64,512]{1,0:T(8,128)S(1)}, f32[64,512]{1,0:T(8,128)S(1)}, u32[]{:S(2)}, u32[]{:S(2)}) %collective-permute-start.7) | collective-permute-done | bytes 131104 | tf_op jit(solution)/shard_map/ppermute | solution.py:568
  61.4 1.6 %collective-permute-start.10 = (f32[64,512]{1,0:T(8,128)S(1)}, f32[64,512]{1,0:T(8,128)S(1)}, u32[]{:S(2)}, u32[]{:S(2)}) collective-permute-start(f32[64,512]{1,0:T(8,128)S(1)} %pad_maximum_fusion.2), channel_id=1, source_target_pairs={{0,1},{1,0},{2,3},{3,2},{4,5},{5,4},{6,7},{7,6},{8,9},{9,8},{10,11... | collective-permute-start | bytes 393224 | tf_op jit(solution)/shard_map/ppermute | solution.py:576
  63.1 1.2 %sides.4.sum_ref = f32[64,1024]{1,0:T(8,128)S(1)} custom-call(f32[64,1024]{1,0:T(8,128)S(1)} %get-tuple-element.41.v_ref.v1_ref, f32[8,1024]{1,0:T(8,128)S(1)} %get-tuple-element.30.mask_ref, f32[64,512]{1,0:T(8,128)S(1)} %collective-permute-done.6.ra_ref, f32[64,512]{1,0:T(8,128)S(1)} %collective-permute-done.7.rb_ref, ...), custom_call_target="tpu_custom_call" | custom-call | flops 1500000000 | bytes 2000000 | tf_op jit(solution)/shard_map/sides/pallas_call | solution.py:424
  64.3 3.4 %collective-permute-done.11.cb_ref = f32[64,512]{1,0:T(8,128)S(1)} collective-permute-done((f32[64,512]{1,0:T(8,128)S(1)}, f32[64,512]{1,0:T(8,128)S(1)}, u32[]{:S(2)}, u32[]{:S(2)}) %collective-permute-start.11) | collective-permute-done | bytes 131104 | tf_op jit(solution)/shard_map/ppermute | solution.py:575
  67.7 0.6 corners.4
  68.3 1.3 %collective-permute-start.13 = (f32[64,512]{1,0:T(8,128)S(1)}, f32[64,512]{1,0:T(8,128)S(1)}, u32[]{:S(2)}, u32[]{:S(2)}) collective-permute-start(f32[64,512]{1,0:T(8,128)S(1)} %get-tuple-element.49), channel_id=1, source_target_pairs={{0,96},{32,64},{64,32},{96,0},{1,97},{33,65},{65,33},{97,1},{2,98}... | collective-permute-start | bytes 393224 | tf_op jit(solution)/shard_map/ppermute | solution.py:568
  69.6 0.7 collective-permute-start.14
  70.3 3.9 %collective-permute-done.13.rb_ref = f32[64,512]{1,0:T(8,128)S(1)} collective-permute-done((f32[64,512]{1,0:T(8,128)S(1)}, f32[64,512]{1,0:T(8,128)S(1)}, u32[]{:S(2)}, u32[]{:S(2)}) %collective-permute-start.13) | collective-permute-done | bytes 131104 | tf_op jit(solution)/shard_map/ppermute | solution.py:568
  74.3 1.3 %collective-permute-start.16 = (f32[64,512]{1,0:T(8,128)S(1)}, f32[64,512]{1,0:T(8,128)S(1)}, u32[]{:S(2)}, u32[]{:S(2)}) collective-permute-start(f32[64,512]{1,0:T(8,128)S(1)} %pad_maximum_fusion.4), channel_id=1, source_target_pairs={{0,1},{1,0},{2,3},{3,2},{4,5},{5,4},{6,7},{7,6},{8,9},{9,8},{10,11... | collective-permute-start | bytes 393224 | tf_op jit(solution)/shard_map/ppermute | solution.py:576
  75.9 2.1 %sides.5 = (f32[64,1024]{1,0:T(8,128)S(1)}, f32[128,128]{1,0:T(8,128)}) custom-call(f32[64,1024]{1,0:T(8,128)S(1)} %get-tuple-element.47.v_ref.v2_ref, f32[8,1024]{1,0:T(8,128)S(1)} %get-tuple-element.30.mask_ref, f32[64,512]{1,0:T(8,128)S(1)} %collective-permute-done.12.ra_ref, f32[64,512]{1,0:T(8,128)S(1)} %collective-permute-done.13.rb_ref, ...), custom_call_target="tpu_custom_call" | custom-call | flops 1500000000 | bytes 2000000 | tf_op jit(solution)/shard_map/sides/pallas_call | solution.py:424
  78.0 8.6 %all-to-all-start.1 = ((f32[128,1,128]{2,1,0:T(1,128)}), f32[128,1,128]{2,1,0:T(1,128)S(1)}, u32[]{:S(2)}, u32[]{:S(2)}) async-start(f32[128,1,128]{2,1,0:T(1,128)} %bitcast.6), calls=%async_computation.1 | async-start | bytes 131072 | tf_op jit(solution)/shard_map/all_to_all | solution.py:592
  87.0 9.1 %all-to-all-done.1 = f32[128,1,128]{2,1,0:T(1,128)S(1)} async-done(((f32[128,1,128]{2,1,0:T(1,128)}), f32[128,1,128]{2,1,0:T(1,128)S(1)}, u32[]{:S(2)}, u32[]{:S(2)}) %all-to-all-start.1) | async-done | bytes 65568 | tf_op jit(solution)/shard_map/all_to_all | solution.py:592
  96.2 1.4 %finish.1 = (f32[64,8,128]{2,1,0:T(8,128)}, f32[64,8,128]{2,1,0:T(8,128)}) custom-call(f32[128,128]{1,0:T(8,128)S(1)} %bitcast.20, f32[8,128]{1,0:T(8,128)S(1)} %get-tuple-element.52.rest_3_.c_ref, f32[64,1024]{1,0:T(8,128)S(1)} %get-tuple-element.32.v_ref.v0_ref, f32[64,1024]{1,0:T(8,128)S(1)} %get-tuple-element.41.v_ref.v1_ref, ...), custom_call_target="tpu_custom_call" | custom-call | tf_op jit(solution)/shard_map/finish/pallas_call | solution.py:538
  (42 shorter events, 3.4 us)
Async XLA Ops:
  0.6 26.7 %copy-start = (f32[27,64,64]{2,1,0:T(8,128)S(1)}, f32[27,64,64]{2,1,0:T(8,128)}, u32[]{:S(2)}) copy-start(f32[27,64,64]{2,1,0:T(8,128)} %coupling_ref.1) | copy-start | bytes 1327108
  0.6 26.7 %copy-start.1 = (s32[2,2,256]{2,1,0:T(2,128)S(1)}, s32[2,2,256]{2,1,0:T(2,128)}, u32[]{:S(2)}) copy-start(s32[2,2,256]{2,1,0:T(2,128)} %occ_ref.1) | copy-start | bytes 12292
  15.8 25.8 %all-to-all-start = ((f32[128,1,1152]{2,1,0:T(1,128)}), f32[128,1,1152]{2,1,0:T(1,128)S(1)}, u32[]{:S(2)}, u32[]{:S(2)}) async-start(f32[128,1,1152]{2,1,0:T(1,128)} %bitcast.3), calls=%async_computation | async-start | bytes 1179648 | tf_op jit(solution)/shard_map/all_to_all | solution.py:582
  42.5 5.1 %collective-permute-start.1 = (f32[64,512]{1,0:T(8,128)S(1)}, f32[64,512]{1,0:T(8,128)S(1)}, u32[]{:S(2)}, u32[]{:S(2)}) collective-permute-start(f32[64,512]{1,0:T(8,128)S(1)} %get-tuple-element.34), channel_id=1, source_target_pairs={{0,96},{32,64},{64,32},{96,0},{1,97},{33,65},{65,33},{97,1},{2,98}... | collective-permute-start | bytes 393224 | tf_op jit(solution)/shard_map/ppermute | solution.py:568
  42.9 4.7 %collective-permute-start = (f32[64,512]{1,0:T(8,128)S(1)}, f32[64,512]{1,0:T(8,128)S(1)}, u32[]{:S(2)}, u32[]{:S(2)}) collective-permute-start(f32[64,512]{1,0:T(8,128)S(1)} %get-tuple-element.33), channel_id=1, source_target_pairs={{0,32},{32,0},{64,96},{96,64},{1,33},{33,1},{65,97},{97,65},{2,34}... | collective-permute-start | bytes 393224 | tf_op jit(solution)/shard_map/ppermute | solution.py:567
  43.3 6.9 %collective-permute-start.2 = (f32[64,512]{1,0:T(8,128)S(1)}, f32[64,512]{1,0:T(8,128)S(1)}, u32[]{:S(2)}, u32[]{:S(2)}) collective-permute-start(f32[64,512]{1,0:T(8,128)S(1)} %get-tuple-element.35), channel_id=1, source_target_pairs={{0,1},{1,0},{2,3},{3,2},{4,5},{5,4},{6,7},{7,6},{8,9},{9,8},{10,11... | collective-permute-start | bytes 393224 | tf_op jit(solution)/shard_map/ppermute | solution.py:569
  44.3 6.0 %collective-permute-start.3 = (f32[64,512]{1,0:T(8,128)S(1)}, f32[64,512]{1,0:T(8,128)S(1)}, u32[]{:S(2)}, u32[]{:S(2)}) collective-permute-start(f32[64,512]{1,0:T(8,128)S(1)} %get-tuple-element.36), channel_id=1, source_target_pairs={{0,32},{1,2},{2,1},{3,4},{4,3},{5,6},{6,5},{7,8},{8,7},{9,10},{10,... | collective-permute-start | bytes 393224 | tf_op jit(solution)/shard_map/ppermute | solution.py:566
  47.7 3.7 %collective-permute-start.4 = (f32[64,512]{1,0:T(8,128)S(1)}, f32[64,512]{1,0:T(8,128)S(1)}, u32[]{:S(2)}, u32[]{:S(2)}) collective-permute-start(f32[64,512]{1,0:T(8,128)S(1)} %pad_maximum_fusion), channel_id=1, source_target_pairs={{0,1},{1,0},{2,3},{3,2},{4,5},{5,4},{6,7},{7,6},{8,9},{9,8},{10,11... | collective-permute-start | bytes 393224 | tf_op jit(solution)/shard_map/ppermute | solution.py:576
  49.9 4.7 %collective-permute-start.5 = (f32[64,512]{1,0:T(8,128)S(1)}, f32[64,512]{1,0:T(8,128)S(1)}, u32[]{:S(2)}, u32[]{:S(2)}) collective-permute-start(f32[64,512]{1,0:T(8,128)S(1)} %pad_maximum_fusion.1), channel_id=1, source_target_pairs={{0,32},{1,2},{2,1},{3,4},{4,3},{5,6},{6,5},{7,8},{8,7},{9,10},{10,... | collective-permute-start | bytes 393224 | tf_op jit(solution)/shard_map/ppermute | solution.py:575
  55.2 6.0 %collective-permute-start.7 = (f32[64,512]{1,0:T(8,128)S(1)}, f32[64,512]{1,0:T(8,128)S(1)}, u32[]{:S(2)}, u32[]{:S(2)}) collective-permute-start(f32[64,512]{1,0:T(8,128)S(1)} %get-tuple-element.43), channel_id=1, source_target_pairs={{0,96},{32,64},{64,32},{96,0},{1,97},{33,65},{65,33},{97,1},{2,98}... | collective-permute-start | bytes 393224 | tf_op jit(solution)/shard_map/ppermute | solution.py:568
  57.0 4.4 %collective-permute-start.6 = (f32[64,512]{1,0:T(8,128)S(1)}, f32[64,512]{1,0:T(8,128)S(1)}, u32[]{:S(2)}, u32[]{:S(2)}) collective-permute-start(f32[64,512]{1,0:T(8,128)S(1)} %get-tuple-element.42), channel_id=1, source_target_pairs={{0,32},{32,0},{64,96},{96,64},{1,33},{33,1},{65,97},{97,65},{2,34}... | collective-permute-start | bytes 393224 | tf_op jit(solution)/shard_map/ppermute | solution.py:567
  57.0 6.1 %collective-permute-start.8 = (f32[64,512]{1,0:T(8,128)S(1)}, f32[64,512]{1,0:T(8,128)S(1)}, u32[]{:S(2)}, u32[]{:S(2)}) collective-permute-start(f32[64,512]{1,0:T(8,128)S(1)} %get-tuple-element.44), channel_id=1, source_target_pairs={{0,1},{1,0},{2,3},{3,2},{4,5},{5,4},{6,7},{7,6},{8,9},{9,8},{10,11... | collective-permute-start | bytes 393224 | tf_op jit(solution)/shard_map/ppermute | solution.py:569
  57.7 5.5 %collective-permute-start.9 = (f32[64,512]{1,0:T(8,128)S(1)}, f32[64,512]{1,0:T(8,128)S(1)}, u32[]{:S(2)}, u32[]{:S(2)}) collective-permute-start(f32[64,512]{1,0:T(8,128)S(1)} %get-tuple-element.45), channel_id=1, source_target_pairs={{0,32},{1,2},{2,1},{3,4},{4,3},{5,6},{6,5},{7,8},{8,7},{9,10},{10,... | collective-permute-start | bytes 393224 | tf_op jit(solution)/shard_map/ppermute | solution.py:566
  61.4 2.9 %collective-permute-start.10 = (f32[64,512]{1,0:T(8,128)S(1)}, f32[64,512]{1,0:T(8,128)S(1)}, u32[]{:S(2)}, u32[]{:S(2)}) collective-permute-start(f32[64,512]{1,0:T(8,128)S(1)} %pad_maximum_fusion.2), channel_id=1, source_target_pairs={{0,1},{1,0},{2,3},{3,2},{4,5},{5,4},{6,7},{7,6},{8,9},{9,8},{10,11... | collective-permute-start | bytes 393224 | tf_op jit(solution)/shard_map/ppermute | solution.py:576
  63.0 4.7 %collective-permute-start.11 = (f32[64,512]{1,0:T(8,128)S(1)}, f32[64,512]{1,0:T(8,128)S(1)}, u32[]{:S(2)}, u32[]{:S(2)}) collective-permute-start(f32[64,512]{1,0:T(8,128)S(1)} %pad_maximum_fusion.3), channel_id=1, source_target_pairs={{0,32},{1,2},{2,1},{3,4},{4,3},{5,6},{6,5},{7,8},{8,7},{9,10},{10,... | collective-permute-start | bytes 393224 | tf_op jit(solution)/shard_map/ppermute | solution.py:575
  68.3 5.9 %collective-permute-start.13 = (f32[64,512]{1,0:T(8,128)S(1)}, f32[64,512]{1,0:T(8,128)S(1)}, u32[]{:S(2)}, u32[]{:S(2)}) collective-permute-start(f32[64,512]{1,0:T(8,128)S(1)} %get-tuple-element.49), channel_id=1, source_target_pairs={{0,96},{32,64},{64,32},{96,0},{1,97},{33,65},{65,33},{97,1},{2,98}... | collective-permute-start | bytes 393224 | tf_op jit(solution)/shard_map/ppermute | solution.py:568
  69.6 4.6 %collective-permute-start.12 = (f32[64,512]{1,0:T(8,128)S(1)}, f32[64,512]{1,0:T(8,128)S(1)}, u32[]{:S(2)}, u32[]{:S(2)}) collective-permute-start(f32[64,512]{1,0:T(8,128)S(1)} %get-tuple-element.48), channel_id=1, source_target_pairs={{0,32},{32,0},{64,96},{96,64},{1,33},{33,1},{65,97},{97,65},{2,34}... | collective-permute-start | bytes 393224 | tf_op jit(solution)/shard_map/ppermute | solution.py:567
  69.6 6.3 %collective-permute-start.14 = (f32[64,512]{1,0:T(8,128)S(1)}, f32[64,512]{1,0:T(8,128)S(1)}, u32[]{:S(2)}, u32[]{:S(2)}) collective-permute-start(f32[64,512]{1,0:T(8,128)S(1)} %get-tuple-element.50), channel_id=1, source_target_pairs={{0,1},{1,0},{2,3},{3,2},{4,5},{5,4},{6,7},{7,6},{8,9},{9,8},{10,11... | collective-permute-start | bytes 393224 | tf_op jit(solution)/shard_map/ppermute | solution.py:569
  70.3 5.7 %collective-permute-start.15 = (f32[64,512]{1,0:T(8,128)S(1)}, f32[64,512]{1,0:T(8,128)S(1)}, u32[]{:S(2)}, u32[]{:S(2)}) collective-permute-start(f32[64,512]{1,0:T(8,128)S(1)} %get-tuple-element.51), channel_id=1, source_target_pairs={{0,32},{1,2},{2,1},{3,4},{4,3},{5,6},{6,5},{7,8},{8,7},{9,10},{10,... | collective-permute-start | bytes 393224 | tf_op jit(solution)/shard_map/ppermute | solution.py:566
  74.3 12.3 %collective-permute-start.16 = (f32[64,512]{1,0:T(8,128)S(1)}, f32[64,512]{1,0:T(8,128)S(1)}, u32[]{:S(2)}, u32[]{:S(2)}) collective-permute-start(f32[64,512]{1,0:T(8,128)S(1)} %pad_maximum_fusion.4), channel_id=1, source_target_pairs={{0,1},{1,0},{2,3},{3,2},{4,5},{5,4},{6,7},{7,6},{8,9},{9,8},{10,11... | collective-permute-start | bytes 393224 | tf_op jit(solution)/shard_map/ppermute | solution.py:576
  75.6 11.0 %collective-permute-start.17 = (f32[64,512]{1,0:T(8,128)S(1)}, f32[64,512]{1,0:T(8,128)S(1)}, u32[]{:S(2)}, u32[]{:S(2)}) collective-permute-start(f32[64,512]{1,0:T(8,128)S(1)} %pad_maximum_fusion.5), channel_id=1, source_target_pairs={{0,32},{1,2},{2,1},{3,4},{4,3},{5,6},{6,5},{7,8},{8,7},{9,10},{10,... | collective-permute-start | bytes 393224 | tf_op jit(solution)/shard_map/ppermute | solution.py:575
  78.0 18.1 %all-to-all-start.1 = ((f32[128,1,128]{2,1,0:T(1,128)}), f32[128,1,128]{2,1,0:T(1,128)S(1)}, u32[]{:S(2)}, u32[]{:S(2)}) async-start(f32[128,1,128]{2,1,0:T(1,128)} %bitcast.6), calls=%async_computation.1 | async-start | bytes 131072 | tf_op jit(solution)/shard_map/all_to_all | solution.py:592

commit v12 on v11

--- a/solution.py
+++ b/solution.py
@@ -124,15 +124,16 @@
 
     counts_copy = pltpu.make_async_copy(cnt_hbm, cnt_ref, small_sems.at[0])
     ids_copy = pltpu.make_async_copy(ids_hbm, ids_ref, small_sems.at[1])
+    fetch(0).start()
     counts_copy.start()
-    for g in range(groups):
+    for g in range(1, groups):
         fetch(g).start()
     ids_copy.start()
     stats[...] = jnp.zeros_like(stats)
     acc[...] = jnp.zeros_like(acc)
-    counts_copy.wait()
     fetch(0).wait()
     turn(0)
+    counts_copy.wait()
 
     def advance(g, carry):
         following = jnp.minimum(g + 1, groups - 1)
@@ -483,7 +484,7 @@
     return new, moments, edges
 
 
-def finish_kernel(mom_ref, c_ref, v0_ref, v1_ref, v2_ref, v3_ref, x_ref, r_ref):
+def finish_kernel(mom_ref, c_ref, v0_ref, v1_ref, v2_ref, v3_ref, x_hbm, r_hbm, x_ref, r_ref, sems):
     row = jnp.sum(mom_ref[...], axis=0, keepdims=True)
     lanes = lane_iota((1, 128))
     m = [jnp.sum(jnp.where(lanes == k, row, 0.0), keepdims=True) for k in range(6)]
@@ -524,13 +525,22 @@
             norm = new
     inverse = 1.0 / c_ref[0:1, 0:1]
     x = [value * inverse for value in x]
-    for chunk in range(8):
-        bx, by, zt = chunk // 4, chunk // 2 % 2, chunk % 2
-        spot = bx * 4 + zt * 2 + by
-        at = pl.ds(chunk * 128, 128)
-        v0, v1, v2, v3 = v0_ref[:, at], v1_ref[:, at], v2_ref[:, at], v3_ref[:, at]
-        x_ref[:, spot, :] = x[0] * v0 + x[1] * v1 + x[2] * v2
-        r_ref[:, spot, :] = r[0] * v0 + r[1] * v1 + r[2] * v2 + r[3] * v3
+    send_x = pltpu.make_async_copy(x_ref, x_hbm, sems.at[0])
+    send_r = pltpu.make_async_copy(r_ref, r_hbm, sems.at[1])
+
+    def spots():
+        for chunk in range(8):
+            bx, by, zt = chunk // 4, chunk // 2 % 2, chunk % 2
+            yield bx * 4 + zt * 2 + by, pl.ds(chunk * 128, 128)
+
+    for spot, at in spots():
+        x_ref[:, spot, :] = x[0] * v0_ref[:, at] + x[1] * v1_ref[:, at] + x[2] * v2_ref[:, at]
+    send_x.start()
+    for spot, at in spots():
+        r_ref[:, spot, :] = r[0] * v0_ref[:, at] + r[1] * v1_ref[:, at] + r[2] * v2_ref[:, at] + r[3] * v3_ref[:, at]
+    send_r.start()
+    send_x.wait()
+    send_r.wait()
 
 
 def finish(moments, centre, fields):
@@ -539,8 +549,9 @@
         finish_kernel,
         name="finish",
         in_specs=[pl.BlockSpec(memory_space=pltpu.VMEM)] * 6,
-        out_specs=[pl.BlockSpec(memory_space=pltpu.VMEM)] * 2,
+        out_specs=[pl.BlockSpec(memory_space=pltpu.HBM)] * 2,
         out_shape=[out, out],
+        scratch_shapes=[pltpu.VMEM((NODES, 8, 128), F32)] * 2 + [pltpu.SemaphoreType.DMA((2,))],
         compiler_params=pltpu.CompilerParams(vmem_limit_bytes=16 << 20),
     )(moments, *[vmem(x) for x in (centre, *fields)])
 

time: 97.7 us -> 97.8 us (level)
  no operation moved by 1% of the time
where the time goes in v12:
time: 97.8 us; the launch traced here: 97.6 us
  waiting for transfers between devices  40.4 us (41%)
  starting transfers between devices  32.1 us (33%)
  Pallas kernels  23.8 us (24%)
  between operations  1.07 us (1%)
    pallas_call x1, Pallas kernels, splat(): pl.pallas_call(splat_kernel, name='splat', in_specs=[pl.BlockSpec(memory_...  15 us
    all_to_all x1, waiting for transfers between devices, on_device(): lax.all_to_all(payload.reshape(SENDERS, 1, ROWS * 128), AXES, split_axis=...  13.8 us
    all_to_all x1, starting transfers between devices, on_device(): lax.all_to_all(payload.reshape(SENDERS, 1, ROWS * 128), AXES, split_axis=...  11.5 us
    ppermute x3, waiting for transfers between devices, exchange(): rb = lax.ppermute(eb, 'slab', swap('slab', 1))  10.7 us
    all_to_all x1, waiting for transfers between devices, on_device(): lax.all_to_all(moments.reshape(SENDERS, 1, 128), AXES, split_axis=0, conc...  9.11 us
    all_to_all x1, starting transfers between devices, on_device(): lax.all_to_all(moments.reshape(SENDERS, 1, 128), AXES, split_axis=0, conc...  8.56 us
    ppermute x3, waiting for transfers between devices, exchange(): cb = lax.ppermute(line(jnp.logical_not(up)), AXES, odd_swap())  6.57 us
    ppermute x3, starting transfers between devices, exchange(): ca = lax.ppermute(line(up), 'grp', swap('grp', 0))  5.14 us
  transfers between devices with their start and end apart: 20, of which 8 were waited for; matrix products, arithmetic and copies ran while one was open for 0% of the time, Pallas kernels for 5%

profile of v12, /device:TPU:1, one launch (start us, length us, event | category | flops | bytes accessed | tf_op | source)
XLA Modules:
  0.0 97.6 jit_solution(474242679935204469)
XLA Ops:
  0.7 15.0 %splat.1 = f32[8,144,128]{2,1,0:T(8,128)} custom-call(f32[6,1024,128]{2,1,0:T(8,128)} %bitcast.21, s32[8,128]{1,0:T(8,128)} %bitcast.22, s32[8,128]{1,0:T(8,128)} %bitcast.23), custom_call_target="tpu_custom_call" | custom-call | tf_op jit(solution)/shard_map/splat/pallas_call | solution.py:172
  15.6 11.5 %all-to-all-start = ((f32[128,1,1152]{2,1,0:T(1,128)}), f32[128,1,1152]{2,1,0:T(1,128)S(1)}, u32[]{:S(2)}, u32[]{:S(2)}) async-start(f32[128,1,1152]{2,1,0:T(1,128)} %bitcast.3), calls=%async_computation | async-start | bytes 1179648 | tf_op jit(solution)/shard_map/all_to_all | solution.py:593
  27.7 13.8 %all-to-all-done = f32[128,1,1152]{2,1,0:T(1,128)S(1)} async-done(((f32[128,1,1152]{2,1,0:T(1,128)}), f32[128,1,1152]{2,1,0:T(1,128)S(1)}, u32[]{:S(2)}, u32[]{:S(2)}) %all-to-all-start) | async-done | bytes 589856 | tf_op jit(solution)/shard_map/all_to_all | solution.py:593
  41.5 0.9 assemble.1
  43.1 1.0 collective-permute-start.2
  44.2 3.3 %collective-permute-done.1.rb_ref = f32[64,512]{1,0:T(8,128)S(1)} collective-permute-done((f32[64,512]{1,0:T(8,128)S(1)}, f32[64,512]{1,0:T(8,128)S(1)}, u32[]{:S(2)}, u32[]{:S(2)}) %collective-permute-start.1) | collective-permute-done | bytes 131104 | tf_op jit(solution)/shard_map/ppermute | solution.py:579
  47.5 2.2 %collective-permute-start.4 = (f32[64,512]{1,0:T(8,128)S(1)}, f32[64,512]{1,0:T(8,128)S(1)}, u32[]{:S(2)}, u32[]{:S(2)}) collective-permute-start(f32[64,512]{1,0:T(8,128)S(1)} %pad_maximum_fusion), channel_id=1, source_target_pairs={{0,1},{1,0},{2,3},{3,2},{4,5},{5,4},{6,7},{7,6},{8,9},{9,8},{10,11... | collective-permute-start | bytes 393224 | tf_op jit(solution)/shard_map/ppermute | solution.py:587
  50.0 1.2 %sides.3.sum_ref = f32[64,1024]{1,0:T(8,128)S(1)} custom-call(f32[64,1024]{1,0:T(8,128)S(1)} %get-tuple-element.32.v_ref.v0_ref, f32[8,1024]{1,0:T(8,128)S(1)} %get-tuple-element.30.mask_ref, f32[64,512]{1,0:T(8,128)S(1)} %collective-permute-done.ra_ref, f32[64,512]{1,0:T(8,128)S(1)} %collective-permute-done.1.rb_ref, ...), custom_call_target="tpu_custom_call" | custom-call | flops 1500000000 | bytes 2000000 | tf_op jit(solution)/shard_map/sides/pallas_call | solution.py:425
  51.2 3.2 %collective-permute-done.5.cb_ref = f32[64,512]{1,0:T(8,128)S(1)} collective-permute-done((f32[64,512]{1,0:T(8,128)S(1)}, f32[64,512]{1,0:T(8,128)S(1)}, u32[]{:S(2)}, u32[]{:S(2)}) %collective-permute-start.5) | collective-permute-done | bytes 131104 | tf_op jit(solution)/shard_map/ppermute | solution.py:586
  55.0 1.8 %collective-permute-start.7 = (f32[64,512]{1,0:T(8,128)S(1)}, f32[64,512]{1,0:T(8,128)S(1)}, u32[]{:S(2)}, u32[]{:S(2)}) collective-permute-start(f32[64,512]{1,0:T(8,128)S(1)} %get-tuple-element.43), channel_id=1, source_target_pairs={{0,96},{32,64},{64,32},{96,0},{1,97},{33,65},{65,33},{97,1},{2,98}... | collective-permute-start | bytes 393224 | tf_op jit(solution)/shard_map/ppermute | solution.py:579
  56.8 0.7 collective-permute-start.8
  57.5 3.5 %collective-permute-done.7.rb_ref = f32[64,512]{1,0:T(8,128)S(1)} collective-permute-done((f32[64,512]{1,0:T(8,128)S(1)}, f32[64,512]{1,0:T(8,128)S(1)}, u32[]{:S(2)}, u32[]{:S(2)}) %collective-permute-start.7) | collective-permute-done | bytes 131104 | tf_op jit(solution)/shard_map/ppermute | solution.py:579
  61.2 1.6 %collective-permute-start.10 = (f32[64,512]{1,0:T(8,128)S(1)}, f32[64,512]{1,0:T(8,128)S(1)}, u32[]{:S(2)}, u32[]{:S(2)}) collective-permute-start(f32[64,512]{1,0:T(8,128)S(1)} %pad_maximum_fusion.2), channel_id=1, source_target_pairs={{0,1},{1,0},{2,3},{3,2},{4,5},{5,4},{6,7},{7,6},{8,9},{9,8},{10,11... | collective-permute-start | bytes 393224 | tf_op jit(solution)/shard_map/ppermute | solution.py:587
  63.0 1.2 %sides.4.sum_ref = f32[64,1024]{1,0:T(8,128)S(1)} custom-call(f32[64,1024]{1,0:T(8,128)S(1)} %get-tuple-element.41.v_ref.v1_ref, f32[8,1024]{1,0:T(8,128)S(1)} %get-tuple-element.30.mask_ref, f32[64,512]{1,0:T(8,128)S(1)} %collective-permute-done.6.ra_ref, f32[64,512]{1,0:T(8,128)S(1)} %collective-permute-done.7.rb_ref, ...), custom_call_target="tpu_custom_call" | custom-call | flops 1500000000 | bytes 2000000 | tf_op jit(solution)/shard_map/sides/pallas_call | solution.py:425
  64.2 3.4 %collective-permute-done.11.cb_ref = f32[64,512]{1,0:T(8,128)S(1)} collective-permute-done((f32[64,512]{1,0:T(8,128)S(1)}, f32[64,512]{1,0:T(8,128)S(1)}, u32[]{:S(2)}, u32[]{:S(2)}) %collective-permute-start.11) | collective-permute-done | bytes 131104 | tf_op jit(solution)/shard_map/ppermute | solution.py:586
  67.5 0.6 corners.4
  68.1 1.3 %collective-permute-start.13 = (f32[64,512]{1,0:T(8,128)S(1)}, f32[64,512]{1,0:T(8,128)S(1)}, u32[]{:S(2)}, u32[]{:S(2)}) collective-permute-start(f32[64,512]{1,0:T(8,128)S(1)} %get-tuple-element.49), channel_id=1, source_target_pairs={{0,96},{32,64},{64,32},{96,0},{1,97},{33,65},{65,33},{97,1},{2,98}... | collective-permute-start | bytes 393224 | tf_op jit(solution)/shard_map/ppermute | solution.py:579
  69.4 0.7 collective-permute-start.14
  70.1 3.9 %collective-permute-done.13.rb_ref = f32[64,512]{1,0:T(8,128)S(1)} collective-permute-done((f32[64,512]{1,0:T(8,128)S(1)}, f32[64,512]{1,0:T(8,128)S(1)}, u32[]{:S(2)}, u32[]{:S(2)}) %collective-permute-start.13) | collective-permute-done | bytes 131104 | tf_op jit(solution)/shard_map/ppermute | solution.py:579
  74.1 1.3 %collective-permute-start.16 = (f32[64,512]{1,0:T(8,128)S(1)}, f32[64,512]{1,0:T(8,128)S(1)}, u32[]{:S(2)}, u32[]{:S(2)}) collective-permute-start(f32[64,512]{1,0:T(8,128)S(1)} %pad_maximum_fusion.4), channel_id=1, source_target_pairs={{0,1},{1,0},{2,3},{3,2},{4,5},{5,4},{6,7},{7,6},{8,9},{9,8},{10,11... | collective-permute-start | bytes 393224 | tf_op jit(solution)/shard_map/ppermute | solution.py:587
  75.8 2.1 %sides.5 = (f32[64,1024]{1,0:T(8,128)S(1)}, f32[128,128]{1,0:T(8,128)}) custom-call(f32[64,1024]{1,0:T(8,128)S(1)} %get-tuple-element.47.v_ref.v2_ref, f32[8,1024]{1,0:T(8,128)S(1)} %get-tuple-element.30.mask_ref, f32[64,512]{1,0:T(8,128)S(1)} %collective-permute-done.12.ra_ref, f32[64,512]{1,0:T(8,128)S(1)} %collective-permute-done.13.rb_ref, ...), custom_call_target="tpu_custom_call" | custom-call | flops 1500000000 | bytes 2000000 | tf_op jit(solution)/shard_map/sides/pallas_call | solution.py:425
  77.9 8.6 %all-to-all-start.1 = ((f32[128,1,128]{2,1,0:T(1,128)}), f32[128,1,128]{2,1,0:T(1,128)S(1)}, u32[]{:S(2)}, u32[]{:S(2)}) async-start(f32[128,1,128]{2,1,0:T(1,128)} %bitcast.6), calls=%async_computation.1 | async-start | bytes 131072 | tf_op jit(solution)/shard_map/all_to_all | solution.py:603
  86.9 9.1 %all-to-all-done.1 = f32[128,1,128]{2,1,0:T(1,128)S(1)} async-done(((f32[128,1,128]{2,1,0:T(1,128)}), f32[128,1,128]{2,1,0:T(1,128)S(1)}, u32[]{:S(2)}, u32[]{:S(2)}) %all-to-all-start.1) | async-done | bytes 65568 | tf_op jit(solution)/shard_map/all_to_all | solution.py:603
  96.0 1.4 %finish.1 = (f32[64,8,128]{2,1,0:T(8,128)}, f32[64,8,128]{2,1,0:T(8,128)}) custom-call(f32[128,128]{1,0:T(8,128)S(1)} %bitcast.20, f32[8,128]{1,0:T(8,128)S(1)} %get-tuple-element.52.rest_3_.c_ref, f32[64,1024]{1,0:T(8,128)S(1)} %get-tuple-element.32.v_ref.v0_ref, f32[64,1024]{1,0:T(8,128)S(1)} %get-tuple-element.41.v_ref.v1_ref, ...), custom_call_target="tpu_custom_call" | custom-call | tf_op jit(solution)/shard_map/finish/pallas_call | solution.py:548
  (42 shorter events, 3.4 us)
Async XLA Ops:
  0.6 26.5 %copy-start = (f32[27,64,64]{2,1,0:T(8,128)S(1)}, f32[27,64,64]{2,1,0:T(8,128)}, u32[]{:S(2)}) copy-start(f32[27,64,64]{2,1,0:T(8,128)} %coupling_ref.1) | copy-start | bytes 1327108
  0.6 26.5 %copy-start.1 = (s32[2,2,256]{2,1,0:T(2,128)S(1)}, s32[2,2,256]{2,1,0:T(2,128)}, u32[]{:S(2)}) copy-start(s32[2,2,256]{2,1,0:T(2,128)} %occ_ref.1) | copy-start | bytes 12292
  15.6 25.8 %all-to-all-start = ((f32[128,1,1152]{2,1,0:T(1,128)}), f32[128,1,1152]{2,1,0:T(1,128)S(1)}, u32[]{:S(2)}, u32[]{:S(2)}) async-start(f32[128,1,1152]{2,1,0:T(1,128)} %bitcast.3), calls=%async_computation | async-start | bytes 1179648 | tf_op jit(solution)/shard_map/all_to_all | solution.py:593
  42.4 5.1 %collective-permute-start.1 = (f32[64,512]{1,0:T(8,128)S(1)}, f32[64,512]{1,0:T(8,128)S(1)}, u32[]{:S(2)}, u32[]{:S(2)}) collective-permute-start(f32[64,512]{1,0:T(8,128)S(1)} %get-tuple-element.34), channel_id=1, source_target_pairs={{0,96},{32,64},{64,32},{96,0},{1,97},{33,65},{65,33},{97,1},{2,98}... | collective-permute-start | bytes 393224 | tf_op jit(solution)/shard_map/ppermute | solution.py:579
  42.8 4.7 %collective-permute-start = (f32[64,512]{1,0:T(8,128)S(1)}, f32[64,512]{1,0:T(8,128)S(1)}, u32[]{:S(2)}, u32[]{:S(2)}) collective-permute-start(f32[64,512]{1,0:T(8,128)S(1)} %get-tuple-element.33), channel_id=1, source_target_pairs={{0,32},{32,0},{64,96},{96,64},{1,33},{33,1},{65,97},{97,65},{2,34}... | collective-permute-start | bytes 393224 | tf_op jit(solution)/shard_map/ppermute | solution.py:578
  43.1 6.9 %collective-permute-start.2 = (f32[64,512]{1,0:T(8,128)S(1)}, f32[64,512]{1,0:T(8,128)S(1)}, u32[]{:S(2)}, u32[]{:S(2)}) collective-permute-start(f32[64,512]{1,0:T(8,128)S(1)} %get-tuple-element.35), channel_id=1, source_target_pairs={{0,1},{1,0},{2,3},{3,2},{4,5},{5,4},{6,7},{7,6},{8,9},{9,8},{10,11... | collective-permute-start | bytes 393224 | tf_op jit(solution)/shard_map/ppermute | solution.py:580
  44.1 6.0 %collective-permute-start.3 = (f32[64,512]{1,0:T(8,128)S(1)}, f32[64,512]{1,0:T(8,128)S(1)}, u32[]{:S(2)}, u32[]{:S(2)}) collective-permute-start(f32[64,512]{1,0:T(8,128)S(1)} %get-tuple-element.36), channel_id=1, source_target_pairs={{0,32},{1,2},{2,1},{3,4},{4,3},{5,6},{6,5},{7,8},{8,7},{9,10},{10,... | collective-permute-start | bytes 393224 | tf_op jit(solution)/shard_map/ppermute | solution.py:577
  47.5 3.7 %collective-permute-start.4 = (f32[64,512]{1,0:T(8,128)S(1)}, f32[64,512]{1,0:T(8,128)S(1)}, u32[]{:S(2)}, u32[]{:S(2)}) collective-permute-start(f32[64,512]{1,0:T(8,128)S(1)} %pad_maximum_fusion), channel_id=1, source_target_pairs={{0,1},{1,0},{2,3},{3,2},{4,5},{5,4},{6,7},{7,6},{8,9},{9,8},{10,11... | collective-permute-start | bytes 393224 | tf_op jit(solution)/shard_map/ppermute | solution.py:587
  49.8 4.7 %collective-permute-start.5 = (f32[64,512]{1,0:T(8,128)S(1)}, f32[64,512]{1,0:T(8,128)S(1)}, u32[]{:S(2)}, u32[]{:S(2)}) collective-permute-start(f32[64,512]{1,0:T(8,128)S(1)} %pad_maximum_fusion.1), channel_id=1, source_target_pairs={{0,32},{1,2},{2,1},{3,4},{4,3},{5,6},{6,5},{7,8},{8,7},{9,10},{10,... | collective-permute-start | bytes 393224 | tf_op jit(solution)/shard_map/ppermute | solution.py:586
  55.0 5.9 %collective-permute-start.7 = (f32[64,512]{1,0:T(8,128)S(1)}, f32[64,512]{1,0:T(8,128)S(1)}, u32[]{:S(2)}, u32[]{:S(2)}) collective-permute-start(f32[64,512]{1,0:T(8,128)S(1)} %get-tuple-element.43), channel_id=1, source_target_pairs={{0,96},{32,64},{64,32},{96,0},{1,97},{33,65},{65,33},{97,1},{2,98}... | collective-permute-start | bytes 393224 | tf_op jit(solution)/shard_map/ppermute | solution.py:579
  56.8 4.4 %collective-permute-start.6 = (f32[64,512]{1,0:T(8,128)S(1)}, f32[64,512]{1,0:T(8,128)S(1)}, u32[]{:S(2)}, u32[]{:S(2)}) collective-permute-start(f32[64,512]{1,0:T(8,128)S(1)} %get-tuple-element.42), channel_id=1, source_target_pairs={{0,32},{32,0},{64,96},{96,64},{1,33},{33,1},{65,97},{97,65},{2,34}... | collective-permute-start | bytes 393224 | tf_op jit(solution)/shard_map/ppermute | solution.py:578
  56.8 6.1 %collective-permute-start.8 = (f32[64,512]{1,0:T(8,128)S(1)}, f32[64,512]{1,0:T(8,128)S(1)}, u32[]{:S(2)}, u32[]{:S(2)}) collective-permute-start(f32[64,512]{1,0:T(8,128)S(1)} %get-tuple-element.44), channel_id=1, source_target_pairs={{0,1},{1,0},{2,3},{3,2},{4,5},{5,4},{6,7},{7,6},{8,9},{9,8},{10,11... | collective-permute-start | bytes 393224 | tf_op jit(solution)/shard_map/ppermute | solution.py:580
  57.5 5.5 %collective-permute-start.9 = (f32[64,512]{1,0:T(8,128)S(1)}, f32[64,512]{1,0:T(8,128)S(1)}, u32[]{:S(2)}, u32[]{:S(2)}) collective-permute-start(f32[64,512]{1,0:T(8,128)S(1)} %get-tuple-element.45), channel_id=1, source_target_pairs={{0,32},{1,2},{2,1},{3,4},{4,3},{5,6},{6,5},{7,8},{8,7},{9,10},{10,... | collective-permute-start | bytes 393224 | tf_op jit(solution)/shard_map/ppermute | solution.py:577
  61.2 2.9 %collective-permute-start.10 = (f32[64,512]{1,0:T(8,128)S(1)}, f32[64,512]{1,0:T(8,128)S(1)}, u32[]{:S(2)}, u32[]{:S(2)}) collective-permute-start(f32[64,512]{1,0:T(8,128)S(1)} %pad_maximum_fusion.2), channel_id=1, source_target_pairs={{0,1},{1,0},{2,3},{3,2},{4,5},{5,4},{6,7},{7,6},{8,9},{9,8},{10,11... | collective-permute-start | bytes 393224 | tf_op jit(solution)/shard_map/ppermute | solution.py:587
  62.8 4.7 %collective-permute-start.11 = (f32[64,512]{1,0:T(8,128)S(1)}, f32[64,512]{1,0:T(8,128)S(1)}, u32[]{:S(2)}, u32[]{:S(2)}) collective-permute-start(f32[64,512]{1,0:T(8,128)S(1)} %pad_maximum_fusion.3), channel_id=1, source_target_pairs={{0,32},{1,2},{2,1},{3,4},{4,3},{5,6},{6,5},{7,8},{8,7},{9,10},{10,... | collective-permute-start | bytes 393224 | tf_op jit(solution)/shard_map/ppermute | solution.py:586
  68.1 5.9 %collective-permute-start.13 = (f32[64,512]{1,0:T(8,128)S(1)}, f32[64,512]{1,0:T(8,128)S(1)}, u32[]{:S(2)}, u32[]{:S(2)}) collective-permute-start(f32[64,512]{1,0:T(8,128)S(1)} %get-tuple-element.49), channel_id=1, source_target_pairs={{0,96},{32,64},{64,32},{96,0},{1,97},{33,65},{65,33},{97,1},{2,98}... | collective-permute-start | bytes 393224 | tf_op jit(solution)/shard_map/ppermute | solution.py:579
  69.4 4.6 %collective-permute-start.12 = (f32[64,512]{1,0:T(8,128)S(1)}, f32[64,512]{1,0:T(8,128)S(1)}, u32[]{:S(2)}, u32[]{:S(2)}) collective-permute-start(f32[64,512]{1,0:T(8,128)S(1)} %get-tuple-element.48), channel_id=1, source_target_pairs={{0,32},{32,0},{64,96},{96,64},{1,33},{33,1},{65,97},{97,65},{2,34}... | collective-permute-start | bytes 393224 | tf_op jit(solution)/shard_map/ppermute | solution.py:578
  69.4 6.3 %collective-permute-start.14 = (f32[64,512]{1,0:T(8,128)S(1)}, f32[64,512]{1,0:T(8,128)S(1)}, u32[]{:S(2)}, u32[]{:S(2)}) collective-permute-start(f32[64,512]{1,0:T(8,128)S(1)} %get-tuple-element.50), channel_id=1, source_target_pairs={{0,1},{1,0},{2,3},{3,2},{4,5},{5,4},{6,7},{7,6},{8,9},{9,8},{10,11... | collective-permute-start | bytes 393224 | tf_op jit(solution)/shard_map/ppermute | solution.py:580
  70.1 5.7 %collective-permute-start.15 = (f32[64,512]{1,0:T(8,128)S(1)}, f32[64,512]{1,0:T(8,128)S(1)}, u32[]{:S(2)}, u32[]{:S(2)}) collective-permute-start(f32[64,512]{1,0:T(8,128)S(1)} %get-tuple-element.51), channel_id=1, source_target_pairs={{0,32},{1,2},{2,1},{3,4},{4,3},{5,6},{6,5},{7,8},{8,7},{9,10},{10,... | collective-permute-start | bytes 393224 | tf_op jit(solution)/shard_map/ppermute | solution.py:577
  74.1 12.3 %collective-permute-start.16 = (f32[64,512]{1,0:T(8,128)S(1)}, f32[64,512]{1,0:T(8,128)S(1)}, u32[]{:S(2)}, u32[]{:S(2)}) collective-permute-start(f32[64,512]{1,0:T(8,128)S(1)} %pad_maximum_fusion.4), channel_id=1, source_target_pairs={{0,1},{1,0},{2,3},{3,2},{4,5},{5,4},{6,7},{7,6},{8,9},{9,8},{10,11... | collective-permute-start | bytes 393224 | tf_op jit(solution)/shard_map/ppermute | solution.py:587
  75.5 11.0 %collective-permute-start.17 = (f32[64,512]{1,0:T(8,128)S(1)}, f32[64,512]{1,0:T(8,128)S(1)}, u32[]{:S(2)}, u32[]{:S(2)}) collective-permute-start(f32[64,512]{1,0:T(8,128)S(1)} %pad_maximum_fusion.5), channel_id=1, source_target_pairs={{0,32},{1,2},{2,1},{3,4},{4,3},{5,6},{6,5},{7,8},{8,7},{9,10},{10,... | collective-permute-start | bytes 393224 | tf_op jit(solution)/shard_map/ppermute | solution.py:586
  77.9 18.1 %all-to-all-start.1 = ((f32[128,1,128]{2,1,0:T(1,128)}), f32[128,1,128]{2,1,0:T(1,128)S(1)}, u32[]{:S(2)}, u32[]{:S(2)}) async-start(f32[128,1,128]{2,1,0:T(1,128)} %bitcast.6), calls=%async_computation.1 | async-start | bytes 131072 | tf_op jit(solution)/shard_map/all_to_all | solution.py:603

commit v13 on v11

--- a/solution.py
+++ b/solution.py
@@ -124,15 +124,16 @@
 
     counts_copy = pltpu.make_async_copy(cnt_hbm, cnt_ref, small_sems.at[0])
     ids_copy = pltpu.make_async_copy(ids_hbm, ids_ref, small_sems.at[1])
+    fetch(0).start()
     counts_copy.start()
-    for g in range(groups):
+    for g in range(1, groups):
         fetch(g).start()
     ids_copy.start()
     stats[...] = jnp.zeros_like(stats)
     acc[...] = jnp.zeros_like(acc)
-    counts_copy.wait()
     fetch(0).wait()
     turn(0)
+    counts_copy.wait()
 
     def advance(g, carry):
         following = jnp.minimum(g + 1, groups - 1)

time: 97.7 us -> 97.6 us (level)
  no operation moved by 1% of the time
where the time goes in v13:
time: 97.6 us; the launch traced here: 97.4 us
  waiting for transfers between devices  40.4 us (41%)
  starting transfers between devices  32.1 us (33%)
  Pallas kernels  23.8 us (24%)
    pallas_call x1, Pallas kernels, splat(): pl.pallas_call(splat_kernel, name='splat', in_specs=[pl.BlockSpec(memory_...  15 us
    all_to_all x1, waiting for transfers between devices, on_device(): lax.all_to_all(payload.reshape(SENDERS, 1, ROWS * 128), AXES, split_axis=...  13.8 us
    all_to_all x1, starting transfers between devices, on_device(): lax.all_to_all(payload.reshape(SENDERS, 1, ROWS * 128), AXES, split_axis=...  11.5 us
    ppermute x3, waiting for transfers between devices, exchange(): rb = lax.ppermute(eb, 'slab', swap('slab', 1))  10.7 us
    all_to_all x1, waiting for transfers between devices, on_device(): lax.all_to_all(moments.reshape(SENDERS, 1, 128), AXES, split_axis=0, conc...  9.11 us
    all_to_all x1, starting transfers between devices, on_device(): lax.all_to_all(moments.reshape(SENDERS, 1, 128), AXES, split_axis=0, conc...  8.56 us
    ppermute x3, waiting for transfers between devices, exchange(): cb = lax.ppermute(line(jnp.logical_not(up)), AXES, odd_swap())  6.57 us
    ppermute x3, starting transfers between devices, exchange(): ca = lax.ppermute(line(up), 'grp', swap('grp', 0))  5.14 us
  transfers between devices with their start and end apart: 20, of which 8 were waited for; matrix products, arithmetic and copies ran while one was open for 0% of the time, Pallas kernels for 5%

profile of v13, /device:TPU:1, one launch (start us, length us, event | category | flops | bytes accessed | tf_op | source)
XLA Modules:
  0.0 97.4 jit_solution(16694529980945348018)
XLA Ops:
  0.7 15.0 %splat.1 = f32[8,144,128]{2,1,0:T(8,128)} custom-call(f32[6,1024,128]{2,1,0:T(8,128)} %bitcast.21, s32[8,128]{1,0:T(8,128)} %bitcast.22, s32[8,128]{1,0:T(8,128)} %bitcast.23), custom_call_target="tpu_custom_call" | custom-call | tf_op jit(solution)/shard_map/splat/pallas_call | solution.py:172
  15.6 11.5 %all-to-all-start = ((f32[128,1,1152]{2,1,0:T(1,128)}), f32[128,1,1152]{2,1,0:T(1,128)S(1)}, u32[]{:S(2)}, u32[]{:S(2)}) async-start(f32[128,1,1152]{2,1,0:T(1,128)} %bitcast.3), calls=%async_computation | async-start | bytes 1179648 | tf_op jit(solution)/shard_map/all_to_all | solution.py:583
  27.7 13.8 %all-to-all-done = f32[128,1,1152]{2,1,0:T(1,128)S(1)} async-done(((f32[128,1,1152]{2,1,0:T(1,128)}), f32[128,1,1152]{2,1,0:T(1,128)S(1)}, u32[]{:S(2)}, u32[]{:S(2)}) %all-to-all-start) | async-done | bytes 589856 | tf_op jit(solution)/shard_map/all_to_all | solution.py:583
  41.5 0.9 assemble.1
  43.1 1.0 collective-permute-start.2
  44.2 3.3 %collective-permute-done.1.rb_ref = f32[64,512]{1,0:T(8,128)S(1)} collective-permute-done((f32[64,512]{1,0:T(8,128)S(1)}, f32[64,512]{1,0:T(8,128)S(1)}, u32[]{:S(2)}, u32[]{:S(2)}) %collective-permute-start.1) | collective-permute-done | bytes 131104 | tf_op jit(solution)/shard_map/ppermute | solution.py:569
  47.5 2.2 %collective-permute-start.4 = (f32[64,512]{1,0:T(8,128)S(1)}, f32[64,512]{1,0:T(8,128)S(1)}, u32[]{:S(2)}, u32[]{:S(2)}) collective-permute-start(f32[64,512]{1,0:T(8,128)S(1)} %pad_maximum_fusion), channel_id=1, source_target_pairs={{0,1},{1,0},{2,3},{3,2},{4,5},{5,4},{6,7},{7,6},{8,9},{9,8},{10,11... | collective-permute-start | bytes 393224 | tf_op jit(solution)/shard_map/ppermute | solution.py:577
  50.0 1.2 %sides.3.sum_ref = f32[64,1024]{1,0:T(8,128)S(1)} custom-call(f32[64,1024]{1,0:T(8,128)S(1)} %get-tuple-element.32.v_ref.v0_ref, f32[8,1024]{1,0:T(8,128)S(1)} %get-tuple-element.30.mask_ref, f32[64,512]{1,0:T(8,128)S(1)} %collective-permute-done.ra_ref, f32[64,512]{1,0:T(8,128)S(1)} %collective-permute-done.1.rb_ref, ...), custom_call_target="tpu_custom_call" | custom-call | flops 1500000000 | bytes 2000000 | tf_op jit(solution)/shard_map/sides/pallas_call | solution.py:425
  51.2 3.2 %collective-permute-done.5.cb_ref = f32[64,512]{1,0:T(8,128)S(1)} collective-permute-done((f32[64,512]{1,0:T(8,128)S(1)}, f32[64,512]{1,0:T(8,128)S(1)}, u32[]{:S(2)}, u32[]{:S(2)}) %collective-permute-start.5) | collective-permute-done | bytes 131104 | tf_op jit(solution)/shard_map/ppermute | solution.py:576
  55.0 1.8 %collective-permute-start.7 = (f32[64,512]{1,0:T(8,128)S(1)}, f32[64,512]{1,0:T(8,128)S(1)}, u32[]{:S(2)}, u32[]{:S(2)}) collective-permute-start(f32[64,512]{1,0:T(8,128)S(1)} %get-tuple-element.43), channel_id=1, source_target_pairs={{0,96},{32,64},{64,32},{96,0},{1,97},{33,65},{65,33},{97,1},{2,98}... | collective-permute-start | bytes 393224 | tf_op jit(solution)/shard_map/ppermute | solution.py:569
  56.8 0.7 collective-permute-start.8
  57.5 3.5 %collective-permute-done.7.rb_ref = f32[64,512]{1,0:T(8,128)S(1)} collective-permute-done((f32[64,512]{1,0:T(8,128)S(1)}, f32[64,512]{1,0:T(8,128)S(1)}, u32[]{:S(2)}, u32[]{:S(2)}) %collective-permute-start.7) | collective-permute-done | bytes 131104 | tf_op jit(solution)/shard_map/ppermute | solution.py:569
  61.2 1.6 %collective-permute-start.10 = (f32[64,512]{1,0:T(8,128)S(1)}, f32[64,512]{1,0:T(8,128)S(1)}, u32[]{:S(2)}, u32[]{:S(2)}) collective-permute-start(f32[64,512]{1,0:T(8,128)S(1)} %pad_maximum_fusion.2), channel_id=1, source_target_pairs={{0,1},{1,0},{2,3},{3,2},{4,5},{5,4},{6,7},{7,6},{8,9},{9,8},{10,11... | collective-permute-start | bytes 393224 | tf_op jit(solution)/shard_map/ppermute | solution.py:577
  63.0 1.2 %sides.4.sum_ref = f32[64,1024]{1,0:T(8,128)S(1)} custom-call(f32[64,1024]{1,0:T(8,128)S(1)} %get-tuple-element.41.v_ref.v1_ref, f32[8,1024]{1,0:T(8,128)S(1)} %get-tuple-element.30.mask_ref, f32[64,512]{1,0:T(8,128)S(1)} %collective-permute-done.6.ra_ref, f32[64,512]{1,0:T(8,128)S(1)} %collective-permute-done.7.rb_ref, ...), custom_call_target="tpu_custom_call" | custom-call | flops 1500000000 | bytes 2000000 | tf_op jit(solution)/shard_map/sides/pallas_call | solution.py:425
  64.2 3.4 %collective-permute-done.11.cb_ref = f32[64,512]{1,0:T(8,128)S(1)} collective-permute-done((f32[64,512]{1,0:T(8,128)S(1)}, f32[64,512]{1,0:T(8,128)S(1)}, u32[]{:S(2)}, u32[]{:S(2)}) %collective-permute-start.11) | collective-permute-done | bytes 131104 | tf_op jit(solution)/shard_map/ppermute | solution.py:576
  67.5 0.6 corners.4
  68.1 1.3 %collective-permute-start.13 = (f32[64,512]{1,0:T(8,128)S(1)}, f32[64,512]{1,0:T(8,128)S(1)}, u32[]{:S(2)}, u32[]{:S(2)}) collective-permute-start(f32[64,512]{1,0:T(8,128)S(1)} %get-tuple-element.49), channel_id=1, source_target_pairs={{0,96},{32,64},{64,32},{96,0},{1,97},{33,65},{65,33},{97,1},{2,98}... | collective-permute-start | bytes 393224 | tf_op jit(solution)/shard_map/ppermute | solution.py:569
  69.4 0.7 collective-permute-start.14
  70.1 3.9 %collective-permute-done.13.rb_ref = f32[64,512]{1,0:T(8,128)S(1)} collective-permute-done((f32[64,512]{1,0:T(8,128)S(1)}, f32[64,512]{1,0:T(8,128)S(1)}, u32[]{:S(2)}, u32[]{:S(2)}) %collective-permute-start.13) | collective-permute-done | bytes 131104 | tf_op jit(solution)/shard_map/ppermute | solution.py:569
  74.1 1.3 %collective-permute-start.16 = (f32[64,512]{1,0:T(8,128)S(1)}, f32[64,512]{1,0:T(8,128)S(1)}, u32[]{:S(2)}, u32[]{:S(2)}) collective-permute-start(f32[64,512]{1,0:T(8,128)S(1)} %pad_maximum_fusion.4), channel_id=1, source_target_pairs={{0,1},{1,0},{2,3},{3,2},{4,5},{5,4},{6,7},{7,6},{8,9},{9,8},{10,11... | collective-permute-start | bytes 393224 | tf_op jit(solution)/shard_map/ppermute | solution.py:577
  75.8 2.1 %sides.5 = (f32[64,1024]{1,0:T(8,128)S(1)}, f32[128,128]{1,0:T(8,128)}) custom-call(f32[64,1024]{1,0:T(8,128)S(1)} %get-tuple-element.47.v_ref.v2_ref, f32[8,1024]{1,0:T(8,128)S(1)} %get-tuple-element.30.mask_ref, f32[64,512]{1,0:T(8,128)S(1)} %collective-permute-done.12.ra_ref, f32[64,512]{1,0:T(8,128)S(1)} %collective-permute-done.13.rb_ref, ...), custom_call_target="tpu_custom_call" | custom-call | flops 1500000000 | bytes 2000000 | tf_op jit(solution)/shard_map/sides/pallas_call | solution.py:425
  77.9 8.6 %all-to-all-start.1 = ((f32[128,1,128]{2,1,0:T(1,128)}), f32[128,1,128]{2,1,0:T(1,128)S(1)}, u32[]{:S(2)}, u32[]{:S(2)}) async-start(f32[128,1,128]{2,1,0:T(1,128)} %bitcast.6), calls=%async_computation.1 | async-start | bytes 131072 | tf_op jit(solution)/shard_map/all_to_all | solution.py:593
  86.9 9.1 %all-to-all-done.1 = f32[128,1,128]{2,1,0:T(1,128)S(1)} async-done(((f32[128,1,128]{2,1,0:T(1,128)}), f32[128,1,128]{2,1,0:T(1,128)S(1)}, u32[]{:S(2)}, u32[]{:S(2)}) %all-to-all-start.1) | async-done | bytes 65568 | tf_op jit(solution)/shard_map/all_to_all | solution.py:593
  96.0 1.4 %finish.1 = (f32[64,8,128]{2,1,0:T(8,128)}, f32[64,8,128]{2,1,0:T(8,128)}) custom-call(f32[128,128]{1,0:T(8,128)S(1)} %bitcast.20, f32[8,128]{1,0:T(8,128)S(1)} %get-tuple-element.52.rest_3_.c_ref, f32[64,1024]{1,0:T(8,128)S(1)} %get-tuple-element.32.v_ref.v0_ref, f32[64,1024]{1,0:T(8,128)S(1)} %get-tuple-element.41.v_ref.v1_ref, ...), custom_call_target="tpu_custom_call" | custom-call | tf_op jit(solution)/shard_map/finish/pallas_call | solution.py:539
  (42 shorter events, 3.4 us)
Async XLA Ops:
  0.6 26.5 %copy-start = (f32[27,64,64]{2,1,0:T(8,128)S(1)}, f32[27,64,64]{2,1,0:T(8,128)}, u32[]{:S(2)}) copy-start(f32[27,64,64]{2,1,0:T(8,128)} %coupling_ref.1) | copy-start | bytes 1327108
  0.6 26.5 %copy-start.1 = (s32[2,2,256]{2,1,0:T(2,128)S(1)}, s32[2,2,256]{2,1,0:T(2,128)}, u32[]{:S(2)}) copy-start(s32[2,2,256]{2,1,0:T(2,128)} %occ_ref.1) | copy-start | bytes 12292
  15.6 25.8 %all-to-all-start = ((f32[128,1,1152]{2,1,0:T(1,128)}), f32[128,1,1152]{2,1,0:T(1,128)S(1)}, u32[]{:S(2)}, u32[]{:S(2)}) async-start(f32[128,1,1152]{2,1,0:T(1,128)} %bitcast.3), calls=%async_computation | async-start | bytes 1179648 | tf_op jit(solution)/shard_map/all_to_all | solution.py:583
  42.4 5.1 %collective-permute-start.1 = (f32[64,512]{1,0:T(8,128)S(1)}, f32[64,512]{1,0:T(8,128)S(1)}, u32[]{:S(2)}, u32[]{:S(2)}) collective-permute-start(f32[64,512]{1,0:T(8,128)S(1)} %get-tuple-element.34), channel_id=1, source_target_pairs={{0,96},{32,64},{64,32},{96,0},{1,97},{33,65},{65,33},{97,1},{2,98}... | collective-permute-start | bytes 393224 | tf_op jit(solution)/shard_map/ppermute | solution.py:569
  42.8 4.7 %collective-permute-start = (f32[64,512]{1,0:T(8,128)S(1)}, f32[64,512]{1,0:T(8,128)S(1)}, u32[]{:S(2)}, u32[]{:S(2)}) collective-permute-start(f32[64,512]{1,0:T(8,128)S(1)} %get-tuple-element.33), channel_id=1, source_target_pairs={{0,32},{32,0},{64,96},{96,64},{1,33},{33,1},{65,97},{97,65},{2,34}... | collective-permute-start | bytes 393224 | tf_op jit(solution)/shard_map/ppermute | solution.py:568
  43.1 6.9 %collective-permute-start.2 = (f32[64,512]{1,0:T(8,128)S(1)}, f32[64,512]{1,0:T(8,128)S(1)}, u32[]{:S(2)}, u32[]{:S(2)}) collective-permute-start(f32[64,512]{1,0:T(8,128)S(1)} %get-tuple-element.35), channel_id=1, source_target_pairs={{0,1},{1,0},{2,3},{3,2},{4,5},{5,4},{6,7},{7,6},{8,9},{9,8},{10,11... | collective-permute-start | bytes 393224 | tf_op jit(solution)/shard_map/ppermute | solution.py:570
  44.1 6.0 %collective-permute-start.3 = (f32[64,512]{1,0:T(8,128)S(1)}, f32[64,512]{1,0:T(8,128)S(1)}, u32[]{:S(2)}, u32[]{:S(2)}) collective-permute-start(f32[64,512]{1,0:T(8,128)S(1)} %get-tuple-element.36), channel_id=1, source_target_pairs={{0,32},{1,2},{2,1},{3,4},{4,3},{5,6},{6,5},{7,8},{8,7},{9,10},{10,... | collective-permute-start | bytes 393224 | tf_op jit(solution)/shard_map/ppermute | solution.py:567
  47.5 3.7 %collective-permute-start.4 = (f32[64,512]{1,0:T(8,128)S(1)}, f32[64,512]{1,0:T(8,128)S(1)}, u32[]{:S(2)}, u32[]{:S(2)}) collective-permute-start(f32[64,512]{1,0:T(8,128)S(1)} %pad_maximum_fusion), channel_id=1, source_target_pairs={{0,1},{1,0},{2,3},{3,2},{4,5},{5,4},{6,7},{7,6},{8,9},{9,8},{10,11... | collective-permute-start | bytes 393224 | tf_op jit(solution)/shard_map/ppermute | solution.py:577
  49.8 4.7 %collective-permute-start.5 = (f32[64,512]{1,0:T(8,128)S(1)}, f32[64,512]{1,0:T(8,128)S(1)}, u32[]{:S(2)}, u32[]{:S(2)}) collective-permute-start(f32[64,512]{1,0:T(8,128)S(1)} %pad_maximum_fusion.1), channel_id=1, source_target_pairs={{0,32},{1,2},{2,1},{3,4},{4,3},{5,6},{6,5},{7,8},{8,7},{9,10},{10,... | collective-permute-start | bytes 393224 | tf_op jit(solution)/shard_map/ppermute | solution.py:576
  55.0 5.9 %collective-permute-start.7 = (f32[64,512]{1,0:T(8,128)S(1)}, f32[64,512]{1,0:T(8,128)S(1)}, u32[]{:S(2)}, u32[]{:S(2)}) collective-permute-start(f32[64,512]{1,0:T(8,128)S(1)} %get-tuple-element.43), channel_id=1, source_target_pairs={{0,96},{32,64},{64,32},{96,0},{1,97},{33,65},{65,33},{97,1},{2,98}... | collective-permute-start | bytes 393224 | tf_op jit(solution)/shard_map/ppermute | solution.py:569
  56.8 4.4 %collective-permute-start.6 = (f32[64,512]{1,0:T(8,128)S(1)}, f32[64,512]{1,0:T(8,128)S(1)}, u32[]{:S(2)}, u32[]{:S(2)}) collective-permute-start(f32[64,512]{1,0:T(8,128)S(1)} %get-tuple-element.42), channel_id=1, source_target_pairs={{0,32},{32,0},{64,96},{96,64},{1,33},{33,1},{65,97},{97,65},{2,34}... | collective-permute-start | bytes 393224 | tf_op jit(solution)/shard_map/ppermute | solution.py:568
  56.8 6.1 %collective-permute-start.8 = (f32[64,512]{1,0:T(8,128)S(1)}, f32[64,512]{1,0:T(8,128)S(1)}, u32[]{:S(2)}, u32[]{:S(2)}) collective-permute-start(f32[64,512]{1,0:T(8,128)S(1)} %get-tuple-element.44), channel_id=1, source_target_pairs={{0,1},{1,0},{2,3},{3,2},{4,5},{5,4},{6,7},{7,6},{8,9},{9,8},{10,11... | collective-permute-start | bytes 393224 | tf_op jit(solution)/shard_map/ppermute | solution.py:570
  57.5 5.5 %collective-permute-start.9 = (f32[64,512]{1,0:T(8,128)S(1)}, f32[64,512]{1,0:T(8,128)S(1)}, u32[]{:S(2)}, u32[]{:S(2)}) collective-permute-start(f32[64,512]{1,0:T(8,128)S(1)} %get-tuple-element.45), channel_id=1, source_target_pairs={{0,32},{1,2},{2,1},{3,4},{4,3},{5,6},{6,5},{7,8},{8,7},{9,10},{10,... | collective-permute-start | bytes 393224 | tf_op jit(solution)/shard_map/ppermute | solution.py:567
  61.2 2.9 %collective-permute-start.10 = (f32[64,512]{1,0:T(8,128)S(1)}, f32[64,512]{1,0:T(8,128)S(1)}, u32[]{:S(2)}, u32[]{:S(2)}) collective-permute-start(f32[64,512]{1,0:T(8,128)S(1)} %pad_maximum_fusion.2), channel_id=1, source_target_pairs={{0,1},{1,0},{2,3},{3,2},{4,5},{5,4},{6,7},{7,6},{8,9},{9,8},{10,11... | collective-permute-start | bytes 393224 | tf_op jit(solution)/shard_map/ppermute | solution.py:577
  62.8 4.7 %collective-permute-start.11 = (f32[64,512]{1,0:T(8,128)S(1)}, f32[64,512]{1,0:T(8,128)S(1)}, u32[]{:S(2)}, u32[]{:S(2)}) collective-permute-start(f32[64,512]{1,0:T(8,128)S(1)} %pad_maximum_fusion.3), channel_id=1, source_target_pairs={{0,32},{1,2},{2,1},{3,4},{4,3},{5,6},{6,5},{7,8},{8,7},{9,10},{10,... | collective-permute-start | bytes 393224 | tf_op jit(solution)/shard_map/ppermute | solution.py:576
  68.1 5.9 %collective-permute-start.13 = (f32[64,512]{1,0:T(8,128)S(1)}, f32[64,512]{1,0:T(8,128)S(1)}, u32[]{:S(2)}, u32[]{:S(2)}) collective-permute-start(f32[64,512]{1,0:T(8,128)S(1)} %get-tuple-element.49), channel_id=1, source_target_pairs={{0,96},{32,64},{64,32},{96,0},{1,97},{33,65},{65,33},{97,1},{2,98}... | collective-permute-start | bytes 393224 | tf_op jit(solution)/shard_map/ppermute | solution.py:569
  69.4 4.6 %collective-permute-start.12 = (f32[64,512]{1,0:T(8,128)S(1)}, f32[64,512]{1,0:T(8,128)S(1)}, u32[]{:S(2)}, u32[]{:S(2)}) collective-permute-start(f32[64,512]{1,0:T(8,128)S(1)} %get-tuple-element.48), channel_id=1, source_target_pairs={{0,32},{32,0},{64,96},{96,64},{1,33},{33,1},{65,97},{97,65},{2,34}... | collective-permute-start | bytes 393224 | tf_op jit(solution)/shard_map/ppermute | solution.py:568
  69.4 6.3 %collective-permute-start.14 = (f32[64,512]{1,0:T(8,128)S(1)}, f32[64,512]{1,0:T(8,128)S(1)}, u32[]{:S(2)}, u32[]{:S(2)}) collective-permute-start(f32[64,512]{1,0:T(8,128)S(1)} %get-tuple-element.50), channel_id=1, source_target_pairs={{0,1},{1,0},{2,3},{3,2},{4,5},{5,4},{6,7},{7,6},{8,9},{9,8},{10,11... | collective-permute-start | bytes 393224 | tf_op jit(solution)/shard_map/ppermute | solution.py:570
  70.1 5.7 %collective-permute-start.15 = (f32[64,512]{1,0:T(8,128)S(1)}, f32[64,512]{1,0:T(8,128)S(1)}, u32[]{:S(2)}, u32[]{:S(2)}) collective-permute-start(f32[64,512]{1,0:T(8,128)S(1)} %get-tuple-element.51), channel_id=1, source_target_pairs={{0,32},{1,2},{2,1},{3,4},{4,3},{5,6},{6,5},{7,8},{8,7},{9,10},{10,... | collective-permute-start | bytes 393224 | tf_op jit(solution)/shard_map/ppermute | solution.py:567
  74.1 12.3 %collective-permute-start.16 = (f32[64,512]{1,0:T(8,128)S(1)}, f32[64,512]{1,0:T(8,128)S(1)}, u32[]{:S(2)}, u32[]{:S(2)}) collective-permute-start(f32[64,512]{1,0:T(8,128)S(1)} %pad_maximum_fusion.4), channel_id=1, source_target_pairs={{0,1},{1,0},{2,3},{3,2},{4,5},{5,4},{6,7},{7,6},{8,9},{9,8},{10,11... | collective-permute-start | bytes 393224 | tf_op jit(solution)/shard_map/ppermute | solution.py:577
  75.5 11.0 %collective-permute-start.17 = (f32[64,512]{1,0:T(8,128)S(1)}, f32[64,512]{1,0:T(8,128)S(1)}, u32[]{:S(2)}, u32[]{:S(2)}) collective-permute-start(f32[64,512]{1,0:T(8,128)S(1)} %pad_maximum_fusion.5), channel_id=1, source_target_pairs={{0,32},{1,2},{2,1},{3,4},{4,3},{5,6},{6,5},{7,8},{8,7},{9,10},{10,... | collective-permute-start | bytes 393224 | tf_op jit(solution)/shard_map/ppermute | solution.py:576
  77.9 18.1 %all-to-all-start.1 = ((f32[128,1,128]{2,1,0:T(1,128)}), f32[128,1,128]{2,1,0:T(1,128)S(1)}, u32[]{:S(2)}, u32[]{:S(2)}) async-start(f32[128,1,128]{2,1,0:T(1,128)} %bitcast.6), calls=%async_computation.1 | async-start | bytes 131072 | tf_op jit(solution)/shard_map/all_to_all | solution.py:593
